TPU v7x, 32 devices: a whole 2x2x4 slice. The times are simulated.
32 devices in a mesh: dp: 8 (over z, x), mp: 4 (over y, core).
Axes of the slice: x: 2, y: 2, z: 4, core: 2. Of those that a mesh axis runs over, the one named last changes fastest.
Arguments:
- tokens: bfloat16 [2, 8, 256, 2048], P(None, 'dp'), may hold values from -6 to 6
- cotangent: bfloat16 [2, 8, 256, 2048], P(None, 'dp'), may hold values from -6 to 6
- row_length: int32 [2, 8], P(None, 'dp'), may hold values from 64 to 256, as said below
- first_gain: bfloat16 [2048], P('dp'), may hold values from 0.5 to 1.5
- value_weight: bfloat16 [2048, 2816], P('dp', 'mp'), may hold values from -0.125 to 0.125
- gelu_weight: bfloat16 [2048, 2816], P('dp', 'mp'), may hold values from -0.125 to 0.125
- conv_weight: bfloat16 [4, 2816], P(None, 'mp'), may hold values from -3 to 3
- conv_bias: bfloat16 [2816], P('mp'), may hold values from -3 to 3
- input_gate: bfloat16 [2816, 176], P('mp'), may hold values from -0.4375 to 0.4375
- input_bias: bfloat16 [2816], P('mp'), may hold values from -4 to 4
- recur_gate: bfloat16 [2816, 176], P('mp'), may hold values from -0.4375 to 0.4375
- recur_bias: bfloat16 [2816], P('mp'), may hold values from -4 to 4
- decay_param: bfloat16 [2816], P('mp'), may hold values from 2 to 9
- output_weight: bfloat16 [2816, 2048], P('mp', 'dp'), may hold values from -0.21875 to 0.21875
- second_gain: bfloat16 [2048], P('dp'), may hold values from 0.5 to 1.5
- mlp_gate: bfloat16 [2048, 6144], P(None, 'mp'), may hold values from -0.125 to 0.125
- mlp_up: bfloat16 [2048, 6144], P(None, 'mp'), may hold values from -0.125 to 0.125
- mlp_down: bfloat16 [6144, 2048], P('mp'), may hold values from -0.15625 to 0.15625
Outputs:
- layer_out: float32 [2, 8, 256, 2048], P(None, 'dp')
- input_grad: float32 [2, 8, 256, 2048], P(None, 'dp')
- first_gain_grad: float32 [2048], P('dp')
- value_weight_grad: float32 [2048, 2816], P('dp', 'mp')
- gelu_weight_grad: float32 [2048, 2816], P('dp', 'mp')
- conv_weight_grad: float32 [4, 2816], P(None, 'mp')
- conv_bias_grad: float32 [2816], P('mp')
- input_gate_grad: float32 [2816, 176], P('mp')
- input_bias_grad: float32 [2816], P('mp')
- recur_gate_grad: float32 [2816, 176], P('mp')
- recur_bias_grad: float32 [2816], P('mp')
- decay_param_grad: float32 [2816], P('mp')
- output_weight_grad: float32 [2816, 2048], P('mp', 'dp')
- second_gain_grad: float32 [2048], P('dp')
- mlp_gate_grad: float32 [2048, 6144], P('dp', 'mp')
- mlp_up_grad: float32 [2048, 6144], P('dp', 'mp')
- mlp_down_grad: float32 [6144, 2048], P('mp', 'dp')
Inputs may be any that keep to these rules, and one draw needn't show every extreme that they name: `row_length`: every row's length is 256 or 64; both occur in every draw.
All inputs are finite; a program needn't handle non-finite values.
Results may differ from a plain program's by a relative error of at most 0.017.
Values may be sent and summed in bfloat16 or wider, within the bound.
No kernel may reach another device: no remote copies, remote signals or barrier semaphores. Data moves between devices by JAX's collectives and lax.ppermute only.
A program may use at most 320 MiB of HBM per device.

v0:
```python
import jax
import jax.numpy as jnp
from jax import lax
from jax.sharding import PartitionSpec as P

EPSILON = 1e-06
DECAY_SCALE = 8.0


def rms_scale(values, weights):
    return values * lax.rsqrt(jnp.mean(values * values, -1, keepdims=True) + EPSILON) * weights


def linear_combine(earlier, later):
    return (earlier[0] * later[0], later[0] * earlier[1] + later[1])


def run_forward(decay, inputs):
    return lax.associative_scan(linear_combine, (decay, inputs), axis=1)[1]


def run_reverse(decay, inputs):
    flipped = lax.associative_scan(
        linear_combine, (jnp.flip(decay, 1), jnp.flip(inputs, 1)), axis=1
    )[1]
    return jnp.flip(flipped, 1)


def shift_earlier(values, steps):
    length = values.shape[1]
    return jnp.pad(values, ((0, 0), (steps, 0), (0, 0)))[:, :length]


def shift_later(values, steps):
    length = values.shape[1]
    return jnp.pad(values, ((0, 0), (0, steps), (0, 0)))[:, steps : steps + length]


def gate_piece(linear_input, linear_recur, mixed, input_shift, recur_shift, decay_full):
    input_open = jax.nn.sigmoid(linear_input + input_shift)
    recur_open = jax.nn.sigmoid(linear_recur + recur_shift)
    log_decay = -DECAY_SCALE * recur_open * jax.nn.softplus(-decay_full)
    decay = jnp.exp(log_decay)
    scaler = jnp.sqrt(-jnp.expm1(2.0 * log_decay))
    return (decay, scaler * input_open * mixed)


def gelu_product(gate_act, upward):
    return jax.nn.gelu(gate_act, approximate=True) * upward


def gelu_tanh(values):
    return jax.nn.gelu(values, approximate=True)


def matmul(left, right):
    return jnp.einsum("bld,de->ble", left, right, preferred_element_type=jnp.float32)


def matmul_back(left, right):
    return jnp.einsum("ble,de->bld", left, right, preferred_element_type=jnp.float32)


def outer_sum(left, right):
    return jnp.einsum("bld,ble->de", left, right, preferred_element_type=jnp.float32)


def block_apply(values, blocks):
    batch, length, width = values.shape
    head_width = blocks.shape[1]
    split = values.reshape(batch, length, width // head_width, head_width)
    cube = blocks.reshape(width // head_width, head_width, head_width)
    return jnp.einsum("blhi,hij->blhj", split, cube, preferred_element_type=jnp.float32).reshape(
        batch, length, width
    )


def block_back(grads, blocks):
    batch, length, width = grads.shape
    head_width = blocks.shape[1]
    split = grads.reshape(batch, length, width // head_width, head_width)
    cube = blocks.reshape(width // head_width, head_width, head_width)
    return jnp.einsum("blhj,hij->blhi", split, cube, preferred_element_type=jnp.float32).reshape(
        batch, length, width
    )


def block_outer(values, grads, head_width):
    batch, length, width = values.shape
    left = values.reshape(batch, length, width // head_width, head_width)
    right = grads.reshape(batch, length, width // head_width, head_width)
    return jnp.einsum("blhi,blhj->hij", left, right, preferred_element_type=jnp.float32).reshape(
        width, head_width
    )


def own_quarter(array, axis_dim):
    count_mp = lax.axis_size("mp")
    piece = array.shape[axis_dim] // count_mp
    return lax.dynamic_slice_in_dim(array, lax.axis_index("mp") * piece, piece, axis_dim)


def rec_forward(weights, layer_in):
    (
        gain_first,
        value_full,
        gelu_full,
        conv_full,
        conv_shift,
        input_full,
        input_shift,
        recur_full,
        recur_shift,
        decay_full,
        output_full,
        gain_second,
    ) = weights
    normed = rms_scale(layer_in, gain_first.astype(jnp.float32)).astype(jnp.bfloat16)
    branch_value = matmul(normed, value_full)
    branch_gelu = matmul(normed, gelu_full)
    gelu_out = gelu_tanh(branch_gelu)
    conv_taps = conv_full.astype(jnp.float32)
    mixed = conv_shift.astype(jnp.float32) + sum(
        (conv_taps[k] * shift_earlier(branch_value, k) for k in range(conv_taps.shape[0]))
    )
    mixed_low = mixed.astype(jnp.bfloat16)
    linear_input = block_apply(mixed_low, input_full)
    linear_recur = block_apply(mixed_low, recur_full)
    decay, driven = gate_piece(
        linear_input,
        linear_recur,
        mixed_low.astype(jnp.float32),
        input_shift.astype(jnp.float32),
        recur_shift.astype(jnp.float32),
        decay_full.astype(jnp.float32),
    )
    hidden = run_forward(decay, driven)
    product = (hidden * gelu_out).astype(jnp.bfloat16)
    partial_rec = matmul(product, output_full)
    saved = (
        normed,
        branch_value,
        branch_gelu,
        gelu_out,
        mixed_low,
        linear_input,
        linear_recur,
        decay,
        hidden,
        product,
    )
    return (saved, partial_rec)


def mlp_forward(mlp_weights, gain_second, residual):
    gate_local, upward_local, downward_local = mlp_weights
    normed_two = rms_scale(residual, gain_second.astype(jnp.float32)).astype(jnp.bfloat16)
    gate_act = matmul(normed_two, gate_local)
    upward = matmul(normed_two, upward_local)
    inner = gelu_product(gate_act, upward).astype(jnp.bfloat16)
    partial_out = matmul(inner, downward_local)
    return ((normed_two, gate_act, upward, inner), partial_out)


def mlp_backward(mlp_weights, mlp_saved, grad_out):
    gate_local, upward_local, downward_local = mlp_weights
    normed_two, gate_act, upward, inner = mlp_saved
    grad_low = grad_out.astype(jnp.bfloat16)
    inner_grad = matmul_back(grad_low, downward_local)
    down_grad = outer_sum(inner, grad_low)
    gate_grad_act, up_grad_act = jax.vjp(gelu_product, gate_act, upward)[1](inner_grad)
    gate_low = gate_grad_act.astype(jnp.bfloat16)
    up_low = up_grad_act.astype(jnp.bfloat16)
    normed_part = matmul_back(gate_low, gate_local) + matmul_back(up_low, upward_local)
    gate_grad = outer_sum(normed_two, gate_low)
    up_grad = outer_sum(normed_two, up_low)
    return (normed_part, (gate_grad, up_grad, down_grad))


def rec_backward(weights, saved, resid_total):
    (
        gain_first,
        value_full,
        gelu_full,
        conv_full,
        conv_shift,
        input_full,
        input_shift,
        recur_full,
        recur_shift,
        decay_full,
        output_full,
        gain_second,
    ) = weights
    (
        normed,
        branch_value,
        branch_gelu,
        gelu_out,
        mixed_low,
        linear_input,
        linear_recur,
        decay,
        hidden,
        product,
    ) = saved
    resid_low = resid_total.astype(jnp.bfloat16)
    product_grad = matmul_back(resid_low, output_full)
    output_grad = outer_sum(product, resid_low)
    hidden_grad = product_grad * gelu_out
    gelu_in_grad = jax.vjp(gelu_tanh, branch_gelu)[1](product_grad * hidden)[0]
    gelu_low = gelu_in_grad.astype(jnp.bfloat16)
    carried = run_reverse(shift_later(decay, 1), hidden_grad)
    decay_grad = carried * shift_earlier(hidden, 1)
    gate_pull = jax.vjp(
        gate_piece,
        linear_input,
        linear_recur,
        mixed_low.astype(jnp.float32),
        input_shift.astype(jnp.float32),
        recur_shift.astype(jnp.float32),
        decay_full.astype(jnp.float32),
    )[1]
    input_lin_grad, recur_lin_grad, mixed_grad, input_bias_grad, recur_bias_grad, decay_raw_grad = (
        gate_pull((decay_grad, carried))
    )
    input_lin_low = input_lin_grad.astype(jnp.bfloat16)
    recur_lin_low = recur_lin_grad.astype(jnp.bfloat16)
    mixed_total = (
        mixed_grad + block_back(input_lin_low, input_full) + block_back(recur_lin_low, recur_full)
    )
    head_width = input_full.shape[1]
    input_gate_grad = block_outer(mixed_low, input_lin_low, head_width)
    recur_gate_grad = block_outer(mixed_low, recur_lin_low, head_width)
    conv_taps = conv_full.astype(jnp.float32)
    taps = conv_taps.shape[0]
    conv_grad = jnp.stack(
        [jnp.sum(mixed_total * shift_earlier(branch_value, k), (0, 1)) for k in range(taps)]
    )
    conv_bias_grad = jnp.sum(mixed_total, (0, 1))
    value_in_grad = sum((conv_taps[k] * shift_later(mixed_total, k) for k in range(taps)))
    value_low = value_in_grad.astype(jnp.bfloat16)
    normed_first = matmul_back(value_low, value_full) + matmul_back(gelu_low, gelu_full)
    value_grad = outer_sum(normed, value_low)
    gelu_grad = outer_sum(normed, gelu_low)
    grads = (
        value_grad,
        gelu_grad,
        conv_grad,
        conv_bias_grad,
        input_gate_grad,
        input_bias_grad,
        recur_gate_grad,
        recur_bias_grad,
        decay_raw_grad,
        output_grad,
    )
    return (normed_first, grads)


def assemble(row_part, unit_part):
    return (
        row_part[0],
        unit_part[0],
        unit_part[1],
        unit_part[2],
        unit_part[3],
        unit_part[4],
        unit_part[5],
        unit_part[6],
        unit_part[7],
        unit_part[8],
        unit_part[9],
        row_part[4],
    )


def local(
    tokens,
    cotangent,
    row_length,
    first_gain,
    value_weight,
    gelu_weight,
    conv_weight,
    conv_bias,
    input_gate,
    input_bias,
    recur_gate,
    recur_bias,
    decay_param,
    output_weight,
    second_gain,
    mlp_gate,
    mlp_up,
    mlp_down,
):
    row_part = (
        lax.all_gather(first_gain, "dp", axis=0, tiled=True),
        lax.all_gather(value_weight, "dp", axis=0, tiled=True),
        lax.all_gather(gelu_weight, "dp", axis=0, tiled=True),
        lax.all_gather(output_weight, "dp", axis=1, tiled=True),
        lax.all_gather(second_gain, "dp", axis=0, tiled=True),
    )
    unit_part = (
        row_part[1],
        row_part[2],
        conv_weight,
        conv_bias,
        input_gate,
        input_bias,
        recur_gate,
        recur_bias,
        decay_param,
        row_part[3],
    )
    unit_part = (
        lax.all_gather(unit_part[0], "mp", axis=1, tiled=True),
        lax.all_gather(unit_part[1], "mp", axis=1, tiled=True),
        lax.all_gather(unit_part[2], "mp", axis=1, tiled=True),
        lax.all_gather(unit_part[3], "mp", axis=0, tiled=True),
        lax.all_gather(unit_part[4], "mp", axis=0, tiled=True),
        lax.all_gather(unit_part[5], "mp", axis=0, tiled=True),
        lax.all_gather(unit_part[6], "mp", axis=0, tiled=True),
        lax.all_gather(unit_part[7], "mp", axis=0, tiled=True),
        lax.all_gather(unit_part[8], "mp", axis=0, tiled=True),
        lax.all_gather(unit_part[9], "mp", axis=0, tiled=True),
    )
    fetched = assemble(row_part, unit_part)
    mlp_weights = (mlp_gate, mlp_up, mlp_down)
    sub_count = tokens.shape[0]
    row_count = tokens.shape[1]
    length = tokens.shape[2]
    outputs = []
    stored = []
    for sub in range(sub_count):
        layer_in = tokens[sub].astype(jnp.float32)
        rec_saved, partial_rec = rec_forward(fetched, layer_in)
        residual = layer_in + partial_rec
        mlp_saved, partial_out = mlp_forward(mlp_weights, fetched[11], residual)
        summed = lax.psum(partial_out.astype(jnp.bfloat16), "mp").astype(jnp.float32)
        outputs.append(residual + summed)
        stored.append((rec_saved, residual, mlp_saved))
    row_again = (
        lax.all_gather(first_gain, "dp", axis=0, tiled=True),
        lax.all_gather(value_weight, "dp", axis=0, tiled=True),
        lax.all_gather(gelu_weight, "dp", axis=0, tiled=True),
        lax.all_gather(output_weight, "dp", axis=1, tiled=True),
        lax.all_gather(second_gain, "dp", axis=0, tiled=True),
    )
    unit_again = (
        row_again[1],
        row_again[2],
        conv_weight,
        conv_bias,
        input_gate,
        input_bias,
        recur_gate,
        recur_bias,
        decay_param,
        row_again[3],
    )
    unit_again = (
        lax.all_gather(unit_again[0], "mp", axis=1, tiled=True),
        lax.all_gather(unit_again[1], "mp", axis=1, tiled=True),
        lax.all_gather(unit_again[2], "mp", axis=1, tiled=True),
        lax.all_gather(unit_again[3], "mp", axis=0, tiled=True),
        lax.all_gather(unit_again[4], "mp", axis=0, tiled=True),
        lax.all_gather(unit_again[5], "mp", axis=0, tiled=True),
        lax.all_gather(unit_again[6], "mp", axis=0, tiled=True),
        lax.all_gather(unit_again[7], "mp", axis=0, tiled=True),
        lax.all_gather(unit_again[8], "mp", axis=0, tiled=True),
        lax.all_gather(unit_again[9], "mp", axis=0, tiled=True),
    )
    back_weights = assemble(row_again, unit_again)
    gain_first_full = back_weights[0].astype(jnp.float32)
    gain_second_full = back_weights[11].astype(jnp.float32)
    rec_totals = None
    mlp_totals = None
    first_total = None
    second_total = None
    input_grads = []
    for sub in range(sub_count):
        layer_in = tokens[sub].astype(jnp.float32)
        positions = lax.broadcasted_iota(jnp.int32, (row_count, length), 1)
        valid = (positions < row_length[sub][:, None]).astype(jnp.float32)
        grad_out = cotangent[sub].astype(jnp.float32) * valid[..., None]
        rec_saved, residual, mlp_saved = stored[sub]
        normed_part, mlp_grads = mlp_backward(mlp_weights, mlp_saved, grad_out)
        normed_grad = lax.psum(normed_part, "mp")
        resid_grad, second_grad = jax.vjp(rms_scale, residual, gain_second_full)[1](normed_grad)
        resid_total = grad_out + resid_grad
        first_part, rec_grads = rec_backward(back_weights, rec_saved, resid_total)
        input_part, first_grad = jax.vjp(rms_scale, layer_in, gain_first_full)[1](first_part)
        input_grads.append(resid_total + input_part)
        if rec_totals is None:
            rec_totals = rec_grads
            mlp_totals = mlp_grads
            first_total = first_grad
            second_total = second_grad
        else:
            rec_totals = tuple((left + right for left, right in zip(rec_totals, rec_grads)))
            mlp_totals = tuple((left + right for left, right in zip(mlp_totals, mlp_grads)))
            first_total = first_total + first_grad
            second_total = second_total + second_grad
    unit_dims = (1, 1, 1, 0, 0, 0, 0, 0, 0, 0)
    rec_totals = tuple((own_quarter(item, place) for item, place in zip(rec_totals, unit_dims)))
    row_reduced = (
        lax.psum_scatter(
            first_total.astype(jnp.bfloat16), "dp", scatter_dimension=0, tiled=True
        ).astype(jnp.float32),
        lax.psum_scatter(
            rec_totals[0].astype(jnp.bfloat16), "dp", scatter_dimension=0, tiled=True
        ).astype(jnp.float32),
        lax.psum_scatter(
            rec_totals[1].astype(jnp.bfloat16), "dp", scatter_dimension=0, tiled=True
        ).astype(jnp.float32),
        lax.psum_scatter(
            rec_totals[9].astype(jnp.bfloat16), "dp", scatter_dimension=1, tiled=True
        ).astype(jnp.float32),
        lax.psum_scatter(
            second_total.astype(jnp.bfloat16), "dp", scatter_dimension=0, tiled=True
        ).astype(jnp.float32),
    )
    small_reduced = lax.psum(
        (
            rec_totals[2],
            rec_totals[3],
            rec_totals[4],
            rec_totals[5],
            rec_totals[6],
            rec_totals[7],
            rec_totals[8],
        ),
        "dp",
    )
    mlp_reduced = (
        lax.psum_scatter(
            mlp_totals[0].astype(jnp.bfloat16), "dp", scatter_dimension=0, tiled=True
        ).astype(jnp.float32),
        lax.psum_scatter(
            mlp_totals[1].astype(jnp.bfloat16), "dp", scatter_dimension=0, tiled=True
        ).astype(jnp.float32),
        lax.psum_scatter(
            mlp_totals[2].astype(jnp.bfloat16), "dp", scatter_dimension=1, tiled=True
        ).astype(jnp.float32),
    )
    layer_out = jnp.stack(outputs)
    input_total = jnp.stack(input_grads)
    return (
        layer_out,
        input_total,
        row_reduced[0],
        row_reduced[1],
        row_reduced[2],
        small_reduced[0],
        small_reduced[1],
        small_reduced[2],
        small_reduced[3],
        small_reduced[4],
        small_reduced[5],
        small_reduced[6],
        row_reduced[3],
        row_reduced[4],
        mlp_reduced[0],
        mlp_reduced[1],
        mlp_reduced[2],
    )


def solution(mesh):
    placed = (
        P(None, "dp", None, None),
        P(None, "dp", None, None),
        P(None, "dp"),
        P("dp"),
        P("dp", "mp"),
        P("dp", "mp"),
        P(None, "mp"),
        P("mp"),
        P("mp", None),
        P("mp"),
        P("mp", None),
        P("mp"),
        P("mp"),
        P("mp", "dp"),
        P("dp"),
        P(None, "mp"),
        P(None, "mp"),
        P("mp", None),
    )
    return jax.shard_map(
        local,
        mesh=mesh,
        in_specs=placed,
        out_specs=(
            P(None, "dp", None, None),
            P(None, "dp", None, None),
            P("dp"),
            P("dp", "mp"),
            P("dp", "mp"),
            P(None, "mp"),
            P("mp"),
            P("mp", None),
            P("mp"),
            P("mp", None),
            P("mp"),
            P("mp"),
            P("mp", "dp"),
            P("dp"),
            P("dp", "mp"),
            P("dp", "mp"),
            P("mp", "dp"),
        ),
        check_vma=False,
    )
```

profile of v0, /device:TPU:0, one launch (start us, length us, event | category | flops | bytes accessed | tf_op | source)
XLA Modules:
  0.0 1954.3 jit_solution(10424799621571059719)
XLA Ops:
  9.5 63.4 %all-gather.12.cloned.1.call-done = bf16[2048,704]{0,1:T(8,128)(2,1)} async-done(((bf16[256,704]{0,1:T(8,128)(2,1)}), bf16[2048,704]{0,1:T(8,128)(2,1)}) %all-gather.12.cloned.1.call-update) | async-done | bytes 2883600 | tf_op jit(solution)/shard_map/all_gather | solution.py:300
  72.9 60.2 %all-gather.16.cloned.1.call-done = bf16[2048,704]{0,1:T(8,128)(2,1)} async-done(((bf16[256,704]{0,1:T(8,128)(2,1)}), bf16[2048,704]{0,1:T(8,128)(2,1)}) %all-gather.16.cloned.1.call-update) | async-done | bytes 2883600 | tf_op jit(solution)/shard_map/all_gather | solution.py:301
  133.2 17.8 all-gather.1
  151.1 10.5 all-gather.2
  178.4 12.5 all-reduce.90
  193.6 12.4 all-gather.3
  209.8 16.9 all-gather.4
  235.9 33.2 %all-gather.14.cloned.1.call-done = bf16[2048,2816]{0,1:T(8,128)(2,1)} async-done(((bf16[2048,704]{0,1:T(8,128)(2,1)}), bf16[2048,2816]{0,1:T(8,128)(2,1)}) %all-gather.14.cloned.1.call-update) | async-done | bytes 11534352 | tf_op jit(solution)/shard_map/all_gather | solution.py:318
  275.6 8.9 fusion.190
  314.7 12.4 multiply_exponential_fusion
  555.7 9.3 multiply_reduce_fusion.11
  594.2 9.3 pad.292
  618.5 7.6 multiply_reduce_fusion.10
  637.5 7.4 multiply_convert_fusion.2
  701.6 12.1 slice.1003
  713.7 7.3 slice.1012
  728.1 12.1 slice.1075
  740.2 12.1 slice.1084
  752.3 7.2 slice.1077
  764.2 38.2 %all-reduce.100.cloned.1.call-done = (bf16[1,256,2048]{2,1,0:T(8,128)(2,1)}, bf16[1,256,2048]{2,1,0:T(8,128)(2,1)}) async-done(((bf16[1,256,2048]{2,1,0:T(8,128)(2,1)}, bf16[1,256,2048]{2,1,0:T(8,128)(2,1)}), (bf16[1,256,2048]{2,1,0:T(8,128)(2,1)}, bf16[1,256,2048]{2,1,0:T(8,128)(2,1)})) %all-reduce.100.cloned.1.call-update) | async-done | bytes 2097168 | tf_op jit(solution)/shard_map/psum | solution.py:341
  809.0 7.2 fusion.151
  828.3 11.9 slice.1009
  840.2 7.3 slice.1007
  911.1 15.6 fusion.46
  938.5 11.9 slice.1081
  950.4 11.9 slice.1079
  1039.9 12.0 slice.1065
  1070.4 9.5 pad.310
  1083.6 22.8 %rev.11 = f32[1,256,2816]{2,1,0:T(8,128)} reverse(f32[1,256,2816]{2,1,0:T(8,128)} %add.1158), dimensions={1} | reverse | bytes 5767168 | tf_op jit(solution)/shard_map/jit(_flip)/rev | solution.py:26
  1106.4 7.2 slice.1137
  1131.5 9.3 pad.331
  1144.5 23.0 %rev.12 = f32[1,256,2816]{2,1,0:T(8,128)} reverse(f32[1,256,2816]{2,1,0:T(8,128)} %add.1191), dimensions={1} | reverse | bytes 5767168 | tf_op jit(solution)/shard_map/jit(_flip)/rev | solution.py:26
  1167.5 18.6 fusion.232
  1229.0 11.0 fusion.228
  1250.0 9.5 fusion.132
  1259.5 9.5 fusion.139
  1277.2 9.9 fusion.129
  1287.1 9.6 fusion.136
  1296.7 7.1 fusion.1
  1304.0 13.3 fusion.145
  1317.2 9.4 fusion.149
  1406.1 21.9 %all-reduce.89 = (bf16[2048]{0:T(1024)(128)(2,1)S(1)}, bf16[2048]{0:T(1024)(128)(2,1)S(1)}) all-reduce(bf16[2048]{0:T(1024)(128)(2,1)S(1)} %add_convert_fusion.4, bf16[2048]{0:T(1024)(128)(2,1)S(1)} %add_convert_fusion.3), channel_id=2, replica_groups=mesh['dp'=8,'mp'=4] {'dp'}, use_global_device_ids=true, to_apply=%region_14.16.clone | all-reduce | flops 4096 | bytes 16384
  1435.5 34.4 %all-reduce.86 = (f32[4,704]{1,0:T(4,128)}, f32[704]{0:T(1024)}, f32[704]{0:T(1024)}, f32[704]{0:T(1024)}, f32[704]{0:T(1024)}) all-reduce(f32[4,704]{1,0:T(4,128)S(1)} %fusion.203, f32[704]{0:T(1024)S(1)} %get-tuple-element.210, f32[704]{0:T(1024)S(1)} %get-tuple-element.209, ...), channel_id=1, replica_groups=mesh['dp'=8,'mp'=4] {'dp'}, use_global_device_ids=true, to_apply=%region_25.27 | all-reduce | flops 5632 | bytes 45056 | tf_op jit(solution)/shard_map/psum | solution.py:425
  1480.7 18.0 reduce-scatter.11.cloned.1.call-done
  1500.6 118.7 %reduce-scatter.13.cloned.1.call-done = bf16[256,1536]{1,0:T(8,128)(2,1)} async-done(((bf16[2048,1536]{1,0:T(8,128)(2,1)}), bf16[256,1536]{1,0:T(8,128)(2,1)}) %reduce-scatter.13.cloned.1.call-update) | async-done | bytes 786448 | tf_op jit(solution)/shard_map/reduce_scatter | solution.py:438
  1621.8 118.3 %reduce-scatter.15.cloned.1.call-done = bf16[256,1536]{1,0:T(8,128)(2,1)} async-done(((bf16[2048,1536]{1,0:T(8,128)(2,1)}), bf16[256,1536]{1,0:T(8,128)(2,1)}) %reduce-scatter.15.cloned.1.call-update) | async-done | bytes 786448 | tf_op jit(solution)/shard_map/reduce_scatter | solution.py:441
  1742.5 118.6 %reduce-scatter.17.cloned.1.call-done = bf16[1536,256]{1,0:T(8,128)(2,1)} async-done(((bf16[1536,2048]{1,0:T(8,128)(2,1)}), bf16[1536,256]{1,0:T(8,128)(2,1)}) %reduce-scatter.17.cloned.1.call-update) | async-done | bytes 786448 | tf_op jit(solution)/shard_map/reduce_scatter | solution.py:444
  1863.5 80.0 %all-reduce.96.cloned.1.call-done = (f32[704,176]{0,1:T(8,128)}, f32[704,176]{0,1:T(8,128)}) async-done(((f32[704,176]{0,1:T(8,128)}, f32[704,176]{0,1:T(8,128)}), (f32[704,176]{0,1:T(8,128)}, f32[704,176]{0,1:T(8,128)})) %all-reduce.96.cloned.1.call-update) | async-done | bytes 991248 | tf_op jit(solution)/shard_map/psum | solution.py:425
  (960 shorter events, 807.3 us)
Async XLA Ops:
  7.2 65.6 %all-gather.12.cloned.1.call-start = ((), (), s32[]{:S(2)}) async-start(), calls=%async_computation.6 | async-start | bytes 3244032 | tf_op jit(solution)/shard_map/all_gather | solution.py:300
  7.9 125.2 %all-gather.16.cloned.1.call-start = ((), (), s32[]{:S(2)}) async-start(), calls=%async_computation.8 | async-start | bytes 3244032 | tf_op jit(solution)/shard_map/all_gather | solution.py:301
  8.7 227.0 %all-gather.20.cloned.1.call-start = ((), (), s32[]{:S(2)}) async-start(), calls=%async_computation.10 | async-start | bytes 3244032 | tf_op jit(solution)/shard_map/all_gather | solution.py:302
  9.4 259.7 %all-gather.14.cloned.1.call-start = ((), (), s32[]{:S(2)}) async-start(), calls=%async_computation.7 | async-start | bytes 14417920 | tf_op jit(solution)/shard_map/all_gather | solution.py:318
  72.8 60.4 %copy-start.205 = (bf16[256]{0:T(256)(128)(2,1)S(1)}, bf16[256]{0:T(256)(128)(2,1)}, u32[]{:S(2)}) copy-start(bf16[256]{0:T(256)(128)(2,1)} %param.22) | copy-start | bytes 1540
  72.8 78.2 %copy-start.133 = (bf16[704,176]{0,1:T(8,128)(2,1)S(1)}, bf16[704,176]{0,1:T(8,128)(2,1)}, u32[]{:S(2)}) copy-start(bf16[704,176]{0,1:T(8,128)(2,1)} %param.29) | copy-start | bytes 743428
  72.8 472.2 %all-gather.18.cloned.1.call-start = ((), (), s32[]{:S(2)}) async-start(), calls=%async_computation.9 | async-start | bytes 14417920 | tf_op jit(solution)/shard_map/all_gather | solution.py:319
  133.1 30.3 %copy-start.194 = (bf16[4,704]{1,0:T(4,128)(2,1)S(1)}, bf16[4,704]{1,0:T(4,128)(2,1)}, u32[]{:S(2)}) copy-start(bf16[4,704]{1,0:T(4,128)(2,1)} %param.25) | copy-start | bytes 16900
  133.1 422.6 %all-gather.22.cloned.1.call-start = ((), (), s32[]{:S(2)}) async-start(), calls=%async_computation.11 | async-start | bytes 14417920 | tf_op jit(solution)/shard_map/all_gather | solution.py:327
  151.1 457.9 %copy-start.92 = (f32[8,1,256]{2,1,0:T(1,128)}, f32[8,1,256]{2,1,0:T(1,128)S(1)}, u32[]{:S(2)}) copy-start(f32[8,1,256]{2,1,0:T(1,128)S(1)} %convert_element_type.478) | copy-start | bytes 24580
  161.6 70.5 %copy-start.8 = (bf16[2,1,256,2048]{3,2,1,0:T(8,128)(2,1)S(1)}, bf16[2,1,256,2048]{3,2,1,0:T(8,128)(2,1)}, u32[]{:S(2)}) copy-start(bf16[2,1,256,2048]{3,2,1,0:T(8,128)(2,1)} %param.19) | copy-start | bytes 6291460
  163.4 137.4 %copy-start.15 = (bf16[4,704,176]{2,1,0:T(8,128)(2,1)}, bf16[4,704,176]{2,1,0:T(8,128)(2,1)S(1)}, u32[]{:S(2)}) copy-start(bf16[4,704,176]{2,1,0:T(8,128)(2,1)S(1)} %copy.121) | copy-start | bytes 2973700
  191.0 17.5 copy-start.193
  235.7 523.8 %all-reduce.98.cloned.1.call-start = ((), (), s32[]{:S(2)}) async-start(), calls=%async_computation.19 | async-start | bytes 8388608 | tf_op jit(solution)/shard_map/psum | solution.py:390
  365.2 19.5 copy-start.17
  477.6 31.4 %copy-start.55 = (f32[1,128,2816]{2,1,0:T(8,128)S(1)}, f32[1,128,2816]{2,1,0:T(8,128)}, u32[]{:S(2)}) copy-start(f32[1,128,2816]{2,1,0:T(8,128)} %get-tuple-element.119) | copy-start | bytes 4325380
  662.2 140.2 %all-reduce.100.cloned.1.call-start = ((), (), s32[]{:S(2)}) async-start(), calls=%async_computation.20 | async-start | bytes 4194304 | tf_op jit(solution)/shard_map/psum | solution.py:341
  675.6 801.3 %reduce-scatter.7.cloned.1.call-start = ((), (), s32[]{:S(2)}) async-start(), calls=%async_computation.12 | async-start | bytes 3244032 | tf_op jit(solution)/shard_map/reduce_scatter | solution.py:412
  701.6 19.4 copy-start.79
  728.1 24.2 %copy-start.76 = (f32[1,128,2816]{2,1,0:T(8,128)S(1)}, f32[1,128,2816]{2,1,0:T(8,128)}, u32[]{:S(2)}) copy-start(f32[1,128,2816]{2,1,0:T(8,128)} %slice.1076) | copy-start | bytes 4325380
  740.2 19.3 copy-start.25
  759.5 42.9 %copy-start.196 = (f32[256]{0:T(256)S(1)}, f32[256]{0:T(256)}, u32[]{:S(2)}) copy-start(f32[256]{0:T(256)} %compare_convert_fusion.1) | copy-start | bytes 3076
  759.5 42.9 %copy-start.203 = (f32[256]{0:T(256)S(1)}, f32[256]{0:T(256)}, u32[]{:S(2)}) copy-start(f32[256]{0:T(256)} %compare_convert_fusion) | copy-start | bytes 3076
  871.7 39.4 %copy-start.29 = (f32[1,256,2048]{2,1,0:T(8,128)S(1)}, f32[1,256,2048]{2,1,0:T(8,128)}, u32[]{:S(2)}) copy-start(f32[1,256,2048]{2,1,0:T(8,128)} %get-tuple-element.110) | copy-start | bytes 6291460
  911.1 15.6 copy-start.41
  1031.9 20.0 %copy-start.174 = (f32[1,1,2816]{2,1,0:T(1,128)S(1)}, f32[1,1,2816]{2,1,0:T(1,128)}, u32[]{:S(2)}) copy-start(f32[1,1,2816]{2,1,0:T(1,128)} %get-tuple-element.161) | copy-start | bytes 33796
  1031.9 20.0 %copy-start.175 = (f32[1,1,2816]{2,1,0:T(1,128)S(1)}, f32[1,1,2816]{2,1,0:T(1,128)}, u32[]{:S(2)}) copy-start(f32[1,1,2816]{2,1,0:T(1,128)} %get-tuple-element.162) | copy-start | bytes 33796
  1031.9 20.1 %copy-start.151 = (f32[1,2,2816]{2,1,0:T(2,128)S(1)}, f32[1,2,2816]{2,1,0:T(2,128)}, u32[]{:S(2)}) copy-start(f32[1,2,2816]{2,1,0:T(2,128)} %pad_add_fusion.1) | copy-start | bytes 67588
  1031.9 20.2 %copy-start.134 = (f32[1,3,2816]{2,1,0:T(4,128)S(1)}, f32[1,3,2816]{2,1,0:T(4,128)}, u32[]{:S(2)}) copy-start(f32[1,3,2816]{2,1,0:T(4,128)} %slice.1054) | copy-start | bytes 101380
  1031.9 20.2 %copy-start.135 = (f32[1,3,2816]{2,1,0:T(4,128)S(1)}, f32[1,3,2816]{2,1,0:T(4,128)}, u32[]{:S(2)}) copy-start(f32[1,3,2816]{2,1,0:T(4,128)} %slice.1037) | copy-start | bytes 101380
  1035.4 16.7 copy-start.164
  1035.4 16.8 copy-start.122
  1035.4 16.8 copy-start.123
  1083.6 22.8 %copy-start.75 = (f32[1,127,2816]{2,1,0:T(8,128)S(1)}, f32[1,127,2816]{2,1,0:T(8,128)}, u32[]{:S(2)}) copy-start(f32[1,127,2816]{2,1,0:T(8,128)} %slice.1136) | copy-start | bytes 4291588
  1144.4 23.0 %copy-start.1 = (f32[1,256,2816]{2,1,0:T(8,128)S(1)}, f32[1,256,2816]{2,1,0:T(8,128)}, u32[]{:S(2)}) copy-start(f32[1,256,2816]{2,1,0:T(8,128)} %copy-done) | copy-start | bytes 8650756
  1144.5 23.0 %copy-start.121 = (f32[2816]{0:T(1024)S(1)}, f32[2816]{0:T(1024)}, u32[]{:S(2)}) copy-start(f32[2816]{0:T(1024)} %convert_element_type.402) | copy-start | bytes 33796
  1144.5 23.0 %copy-start.129 = (f32[2816]{0:T(1024)S(1)}, f32[2816]{0:T(1024)}, u32[]{:S(2)}) copy-start(f32[2816]{0:T(1024)} %convert_element_type.404) | copy-start | bytes 33796
  1144.5 23.0 %copy-start.131 = (f32[2816]{0:T(1024)S(1)}, f32[2816]{0:T(1024)}, u32[]{:S(2)}) copy-start(f32[2816]{0:T(1024)} %get-tuple-element.192) | copy-start | bytes 33796
  1144.5 23.0 %copy-start.142 = (f32[2816]{0:T(1024)S(1)}, f32[2816]{0:T(1024)}, u32[]{:S(2)}) copy-start(f32[2816]{0:T(1024)} %get-tuple-element.193) | copy-start | bytes 33796
  1167.5 18.6 copy-start.2
  1275.8 203.0 %reduce-scatter.9.cloned.1.call-start = ((), (), s32[]{:S(2)}) async-start(), calls=%async_computation.13 | async-start | bytes 3244032 | tf_op jit(solution)/shard_map/reduce_scatter | solution.py:415
  1303.9 194.8 %reduce-scatter.11.cloned.1.call-start = ((), (), s32[]{:S(2)}) async-start(), calls=%async_computation.14 | async-start | bytes 3244032 | tf_op jit(solution)/shard_map/reduce_scatter | solution.py:418
  1333.7 285.6 %reduce-scatter.13.cloned.1.call-start = ((), (), s32[]{:S(2)}) async-start(), calls=%async_computation.15 | async-start | bytes 7077888 | tf_op jit(solution)/shard_map/reduce_scatter | solution.py:438
  1342.5 397.5 %reduce-scatter.15.cloned.1.call-start = ((), (), s32[]{:S(2)}) async-start(), calls=%async_computation.16 | async-start | bytes 7077888 | tf_op jit(solution)/shard_map/reduce_scatter | solution.py:441
  1350.3 510.8 %reduce-scatter.17.cloned.1.call-start = ((), (), s32[]{:S(2)}) async-start(), calls=%async_computation.17 | async-start | bytes 7077888 | tf_op jit(solution)/shard_map/reduce_scatter | solution.py:444
  1359.4 584.1 %all-reduce.96.cloned.1.call-start = ((), (), s32[]{:S(2)}) async-start(), calls=%async_computation.18 | async-start | bytes 2162688 | tf_op jit(solution)/shard_map/psum | solution.py:425
  1401.0 27.6 %copy-start.190 = (f32[256]{0:T(256)S(1)}, f32[256]{0:T(256)}, u32[]{:S(2)}) copy-start(f32[256]{0:T(256)} %copy-done.189) | copy-start | bytes 3076
  1401.0 27.6 %copy-start.192 = (f32[256]{0:T(256)S(1)}, f32[256]{0:T(256)}, u32[]{:S(2)}) copy-start(f32[256]{0:T(256)} %copy-done.191) | copy-start | bytes 3076
  (184 other events, 1032.3 us)
Sparse Core Ops, SparseCore 0:
  10.1 62.7 all-gather.11
  74.9 58.1 all-gather.15
  135.1 58.1 all-gather.19
  194.8 74.3 all-gather.13
  270.6 76.1 all-gather.17
  348.2 76.1 all-gather.21
  662.3 85.7 all-reduce.97
  750.6 51.6 all-reduce.99
  1276.0 72.4 reduce-scatter.6
  1351.8 71.9 reduce-scatter.8
  1427.4 71.2 reduce-scatter.10
  1502.2 117.0 reduce-scatter.12
  1622.9 117.0 reduce-scatter.14
  1743.5 117.5 reduce-scatter.16
  1865.6 77.8 all-reduce.95
where the time goes:
time: 1980 us; the launch traced here: 1950 us
  local copies, waits for them, and re-layouts  660 us (33%)
  waiting for transfers between devices  651 us (33%)
  matrix products  246 us (12%)
  other arithmetic  245 us (12%)
  blocking collectives  132 us (7%)
    slice x104, local copies, waits for them, and re-layouts, run_reverse(): lax.associative_scan(linear_combine, (jnp.flip(decay, 1), jnp.flip(inputs...  272 us
    slice x92, local copies, waits for them, and re-layouts, run_forward(): return lax.associative_scan(linear_combine, (decay, inputs), axis=1)[1]  160 us
    reduce_scatter x1, waiting for transfers between devices, local(): lax.psum_scatter(mlp_totals[0].astype(jnp.bfloat16), 'dp', scatter_dimens...  119 us
    reduce_scatter x1, waiting for transfers between devices, local(): lax.psum_scatter(mlp_totals[2].astype(jnp.bfloat16), 'dp', scatter_dimens...  119 us
    reduce_scatter x1, waiting for transfers between devices, local(): lax.psum_scatter(mlp_totals[1].astype(jnp.bfloat16), 'dp', scatter_dimens...  118 us
    dot_general x12, matrix products, outer_sum(): jnp.einsum('bld,ble->de', left, right, preferred_element_type=jnp.float32)  84.3 us
    psum x1, waiting for transfers between devices, local(): lax.psum((rec_totals[2], rec_totals[3], rec_totals[4], rec_totals[5], rec...  80 us
    dot_general x12, matrix products, matmul_back(): jnp.einsum('ble,de->bld', left, right, preferred_element_type=jnp.float32)  67.5 us
  transfers between devices with their start and end apart: 15, of which 9 were waited for; matrix products, arithmetic and copies ran while one was open for 29% of the time, Pallas kernels for 0%

commit v1 on v0

v1 whole, which is shorter than its diff:
```python
import jax
import jax.numpy as jnp
from jax import lax
from jax.experimental import pallas as pl
from jax.experimental.pallas import tpu as pltpu
from jax.sharding import PartitionSpec as P

EPSILON = 1e-06
DECAY_SCALE = 8.0
GELU_A = 0.7978845608028654
GELU_B = 0.044715
BF16 = jnp.bfloat16
F32 = jnp.float32
STEP = 16
HALF = 8
SUMS = 8
TN = (((0,), (0,)), ((), ()))


def gelu(v):
    return 0.5 * v * (1.0 + jnp.tanh(GELU_A * (v + GELU_B * v * v * v)))


def gelu_both(v):
    squared = v * v
    bent = jnp.tanh(GELU_A * v * (1.0 + GELU_B * squared))
    value = 0.5 * v * (1.0 + bent)
    slope = 0.5 * (1.0 + bent) + 0.5 * v * (1.0 - bent * bent) * GELU_A * (
        1.0 + 3.0 * GELU_B * squared
    )
    return value, slope


def negative_expm1(z, exp_z):
    series = 1.0 + z * (1.0 / 7.0)
    for k in (6.0, 5.0, 4.0, 3.0, 2.0):
        series = 1.0 + z * (1.0 / k) * series
    return jnp.where(z > -0.25, -z * series, 1.0 - exp_z)


def rows_of(shape):
    return lax.broadcasted_iota(jnp.int32, shape, 0)


def earlier(now, before, k, rows):
    return jnp.where(rows < k, pltpu.roll(before, k, 0), pltpu.roll(now, k, 0))


def later(now, after, k, rows):
    size = now.shape[0]
    return jnp.where(
        rows >= size - k, pltpu.roll(after, size - k, 0), pltpu.roll(now, size - k, 0)
    )


def mixer_forward_kernel(
    seqs, bx, by, taps, tap_bias, blocks_i, blocks_r, bias_i, bias_r, soft, p_o, cx_o, lx_o, lr_o, h_o
):
    total, width = bx.shape
    length = total // seqs
    steps = length // STEP
    rows16 = rows_of((STEP, width))
    w = [jnp.broadcast_to(taps[k : k + 1, :], (STEP, width)) for k in range(taps.shape[0])]
    shift = jnp.broadcast_to(tap_bias[...], (STEP, width))
    for seq in range(seqs):

        def conv(i, before):
            at = pl.ds(pl.multiple_of(seq * length + i * STEP, STEP), STEP)
            now = bx[at, :]
            mixed = shift + w[0] * now
            for k in range(1, taps.shape[0]):
                mixed = mixed + w[k] * earlier(now, before, k, rows16)
            cx_o[at, :] = mixed.astype(BF16)
            return now

        lax.fori_loop(0, steps, conv, jnp.zeros((STEP, width), F32))
    lx_o[...] = jnp.dot(cx_o[...], blocks_i[...], preferred_element_type=F32) + bias_i[...]
    lr_o[...] = jnp.dot(cx_o[...], blocks_r[...], preferred_element_type=F32) + bias_r[...]
    rows8 = rows_of((HALF, width))
    soft8 = jnp.broadcast_to(-DECAY_SCALE * soft[...], (HALF, width))

    def scan(i, carries):
        out = []
        for seq in range(seqs):
            carry = carries[seq]
            base = seq * length + i * STEP
            at = pl.ds(pl.multiple_of(base, STEP), STEP)
            cx16 = cx_o[at, :].astype(F32)
            products = []
            for part in range(STEP // HALF):
                here = pl.ds(pl.multiple_of(base + part * HALF, HALF), HALF)
                cx = cx16[part * HALF : (part + 1) * HALF, :]
                ix = jax.nn.sigmoid(lx_o[here, :])
                la = soft8 * jax.nn.sigmoid(lr_o[here, :])
                a = jnp.exp(la)
                rest = negative_expm1(2.0 * la, a * a)
                m = jnp.where(rest > 0.0, rest * lax.rsqrt(rest), 0.0)
                u = m * ix * cx
                for s in (1, 2, 4):
                    keep = rows8 >= s
                    u = u + jnp.where(keep, a * pltpu.roll(u, s, 0), 0.0)
                    a = jnp.where(keep, a * pltpu.roll(a, s, 0), a)
                h = u + a * carry
                carry = jnp.broadcast_to(h[HALF - 1 : HALF, :], (HALF, width))
                h_o[here, :] = h
                products.append(h * gelu(by[here, :]))
            p_o[at, :] = jnp.concatenate(products, 0).astype(BF16)
            out.append(carry)
        return tuple(out)

    lax.fori_loop(0, steps, scan, tuple(jnp.zeros((HALF, width), F32) for _ in range(seqs)))


def mixer_forward(seqs, bx, by, taps, tap_bias, blocks_i, blocks_r, bias_i, bias_r, soft):
    total, width = bx.shape
    low = jax.ShapeDtypeStruct((total, width), BF16)
    full = jax.ShapeDtypeStruct((total, width), F32)
    return pl.pallas_call(
        lambda *refs: mixer_forward_kernel(seqs, *refs),
        out_shape=(low, low, full, full, full),
        compiler_params=pltpu.CompilerParams(vmem_limit_bytes=40 << 20),
        cost_estimate=pl.CostEstimate(
            flops=4 * total * width * width, bytes_accessed=total * width * 24, transcendentals=6 * total * width
        ),
        name="mixer_forward",
    )(bx, by, taps, tap_bias, blocks_i, blocks_r, bias_i, bias_r, soft)


def mixer_backward_kernel(seqs, head, ring_size, dhr, *refs):
    outputs = refs[:ring_size]
    bx, by, cx_i, lx_i, lr_i, h_i, taps, blocks_i, blocks_r, soft, gate_soft = refs[ring_size : ring_size + 11]
    dbx_o, dby_o, gate_i_o, gate_r_o, dlx_o, dlr_o, dcx_s, dp = refs[ring_size + 11 :]
    for o in range(ring_size):
        part = jnp.dot(dhr[o], outputs[o][...], preferred_element_type=F32)
        dp[...] = part if o == 0 else dp[...] + part
    total, width = bx.shape
    length = total // seqs
    steps = length // STEP
    rows8 = rows_of((HALF, width))
    soft8 = jnp.broadcast_to(-DECAY_SCALE * soft[...], (HALF, width))
    zero = jnp.zeros((HALF, width), F32)

    def scan(j, state):
        i = steps - 1 - j
        sums_i, sums_r, sums_d = state[0]
        out = []
        for seq in range(seqs):
            a_after, e_after = state[1][seq]
            base = seq * length + i * STEP
            at = pl.ds(pl.multiple_of(base, STEP), STEP)
            cx16 = cx_i[at, :].astype(F32)
            dby_parts, dlx_parts, dlr_parts = [None, None], [None, None], [None, None]
            for part in (1, 0):
                start = base + part * HALF
                here = pl.ds(pl.multiple_of(start, HALF), HALF)
                cx = cx16[part * HALF : (part + 1) * HALF, :]
                ix = jax.nn.sigmoid(lx_i[here, :])
                ra = jax.nn.sigmoid(lr_i[here, :])
                la = soft8 * ra
                a = jnp.exp(la)
                rest = negative_expm1(2.0 * la, a * a)
                inverse = lax.rsqrt(rest)
                m = rest * inverse
                h = h_i[here, :]
                first = (i == 0) if part == 0 else False
                back = jnp.maximum(start - HALF, 0)
                before = h_i[pl.ds(pl.multiple_of(back, HALF), HALF), :]
                if part == 0:
                    before = jnp.where(i == 0, 0.0, before)
                h_prev = earlier(h, before, 1, rows8)
                gy, slope = gelu_both(by[here, :])
                grad = dp[here, :]
                dby_parts[part] = grad * h * slope
                e = grad * gy
                f = later(a, a_after, 1, rows8)
                for s in (1, 2, 4):
                    keep = rows8 < HALF - s
                    e = e + jnp.where(keep, f * pltpu.roll(e, HALF - s, 0), 0.0)
                    f = jnp.where(keep, f * pltpu.roll(f, HALF - s, 0), f)
                e = e + f * e_after
                e_after = jnp.broadcast_to(e[0:1, :], (HALF, width))
                a_after = a
                eix = e * ix
                dla = (e * h_prev - eix * cx * a * inverse) * a
                dlx = eix * m * cx * (1.0 - ix)
                dlr = dla * la * (1.0 - ra)
                sums_i = sums_i + dlx
                sums_r = sums_r + dlr
                sums_d = sums_d + dla * ra
                dlx_parts[part], dlr_parts[part] = dlx, dlr
                dcx_s[here, :] = eix * m
            dby_o[at, :] = jnp.concatenate(dby_parts, 0).astype(BF16)
            dlx_o[at, :] = jnp.concatenate(dlx_parts, 0).astype(BF16)
            dlr_o[at, :] = jnp.concatenate(dlr_parts, 0).astype(BF16)
            out.append((a_after, e_after))
        return (sums_i, sums_r, sums_d), tuple(out)

    (sums_i, sums_r, sums_d), _ = lax.fori_loop(
        0, steps, scan, ((zero, zero, zero), tuple((zero, zero) for _ in range(seqs)))
    )
    transposed = (((1,), (1,)), ((), ()))
    dcx_s[...] += lax.dot_general(
        dlx_o[...], blocks_i[...], transposed, preferred_element_type=F32
    ) + lax.dot_general(dlr_o[...], blocks_r[...], transposed, preferred_element_type=F32)
    count = taps.shape[0]
    rows16 = rows_of((STEP, width))
    w = [jnp.broadcast_to(taps[k : k + 1, :], (STEP, width)) for k in range(count)]
    zero16 = jnp.zeros((STEP, width), F32)
    sums_t = tuple(zero16 for _ in range(count))
    sums_b = zero16
    for seq in range(seqs):

        def conv(j, state):
            after, tap_sums, shift_sum = state
            at = pl.ds(pl.multiple_of(seq * length + (steps - 1 - j) * STEP, STEP), STEP)
            now = dcx_s[at, :]
            source = bx[at, :]
            grad = w[0] * now
            new_sums = [tap_sums[0] + now * source]
            for k in range(1, count):
                moved = later(now, after, k, rows16)
                grad = grad + w[k] * moved
                new_sums.append(tap_sums[k] + moved * source)
            dbx_o[at, :] = grad.astype(BF16)
            return now, tuple(new_sums), shift_sum + now

        _, sums_t, sums_b = lax.fori_loop(0, steps, conv, (zero16, sums_t, sums_b))
    lines = [jnp.sum(item, 0, keepdims=True) for item in (*sums_t, sums_b, sums_i, sums_r)]
    lines.append(DECAY_SCALE * gate_soft[...] * jnp.sum(sums_d, 0, keepdims=True))
    for place, line in enumerate(lines):
        for i in range(width // head):
            gate_i_o[width + i * SUMS + place : width + i * SUMS + place + 1, :] = line[:, i * head : (i + 1) * head]
    for grads, out in ((dlx_o, gate_i_o), (dlr_o, gate_r_o)):
        whole = lax.dot_general(cx_i[...], grads[...], TN, preferred_element_type=F32)
        for i in range(width // head):
            at = slice(i * head, (i + 1) * head)
            out[at, :] = whole[at, at]


def mixer_backward(
    seqs, dhr, outputs, bx, by, cx, lx, lr, h, taps, blocks_i, blocks_r, soft, gate_soft, head
):
    total, width = bx.shape
    ring_size = len(outputs)
    low = jax.ShapeDtypeStruct((total, width), BF16)
    gate = jax.ShapeDtypeStruct((width, head), F32)
    gate_sums = jax.ShapeDtypeStruct((width + SUMS * (width // head), head), F32)
    return pl.pallas_call(
        lambda *refs: mixer_backward_kernel(seqs, head, ring_size, *refs),
        out_shape=(low, low, gate_sums, gate),
        scratch_shapes=[
            pltpu.VMEM((total, width), BF16),
            pltpu.VMEM((total, width), BF16),
            pltpu.VMEM((total, width), F32),
            pltpu.VMEM((total, width), F32),
        ],
        compiler_params=pltpu.CompilerParams(vmem_limit_bytes=40 << 20),
        cost_estimate=pl.CostEstimate(
            flops=14 * total * width * width, bytes_accessed=total * width * 36, transcendentals=8 * total * width
        ),
        name="mixer_backward",
    )(dhr, *outputs, bx, by, cx, lx, lr, h, taps, blocks_i, blocks_r, soft, gate_soft)


def smem():
    return pl.BlockSpec(memory_space=pltpu.SMEM)


def vmem(count):
    return [pl.BlockSpec(memory_space=pltpu.VMEM)] * count


def params():
    return pltpu.CompilerParams(vmem_limit_bytes=40 << 20)


def cost(flops, bytes_accessed, transcendentals=0):
    return pl.CostEstimate(flops=flops, bytes_accessed=bytes_accessed, transcendentals=transcendentals)


def shaped(shape, dtype):
    return jax.ShapeDtypeStruct(shape, dtype)


def prepare_kernel(scalars, slots, tokens, cotangent, x_o, g_o, flat_o, r_o):
    ring_size, total, block = x_o.shape
    half = total // 2
    row_count = (scalars.shape[0] - 1) // 2
    length = half // row_count
    rows = lax.broadcasted_iota(jnp.int32, (length, block), 0)
    for place in range(2):
        sub = scalars[0] if place == 0 else 1 - scalars[0]
        for row in range(row_count):
            at = slice(place * half + row * length, place * half + (row + 1) * length)
            source = pl.ds(row * length, length)
            valid = jnp.where(rows < scalars[1 + sub * row_count + row], 1.0, 0.0)
            squares = jnp.zeros((length, block), F32)
            for k in range(ring_size):
                columns = slice(k * block, (k + 1) * block)
                piece = tokens[sub, source, columns]
                wide = piece.astype(F32)
                squares = squares + wide * wide
                x_o[slots[k], at, :] = piece
                masked = (cotangent[sub, source, columns].astype(F32) * valid).astype(BF16)
                g_o[slots[k], at, :] = masked
                flat_o[at, columns] = masked
            mean = jnp.sum(squares, 1, keepdims=True) * (1.0 / (ring_size * block))
            r_o[at, :] = lax.rsqrt(mean + EPSILON)


def prepare(scalars, slots, tokens, cotangent, ring_size):
    subs, half, model = tokens.shape
    total = subs * half
    rel = shaped((ring_size, total, model // ring_size), BF16)
    return pl.pallas_call(
        prepare_kernel,
        in_specs=[smem(), smem(), *vmem(2)],
        out_shape=(rel, rel, shaped((total, model), BF16), shaped((total, 1), F32)),
        compiler_params=params(),
        cost_estimate=cost(8 * total * model, 10 * total * model),
        name="prepare",
    )(scalars, slots, tokens, cotangent)


def project_kernel(offsets, first, width, *refs):
    count = len(offsets)
    x, r1 = refs[:2]
    value, gelu_w = refs[2 : 2 + count], refs[2 + count : 2 + 2 * count]
    rest = refs[2 + 2 * count :]
    if not first:
        before = rest[:2]
        rest = rest[2:]
    bx, by, n1_o, gains_o = rest
    block = x.shape[2]
    spare = value[0].shape[1] - width
    lines = block // spare
    scale = r1[...]
    for i, o in enumerate(offsets):
        slab = value[i][0:16, width:].astype(F32)
        gains = [
            jnp.concatenate([slab[g * lines + k : g * lines + k + 1, :] for k in range(lines)], 1)
            for g in range(2)
        ]
        gains_o[i, 0:1, :] = gains[0]
        gains_o[i, 1:2, :] = gains[1]
        n1 = (x[o].astype(F32) * scale * gains[0]).astype(BF16)
        n1_o[i] = n1
        for out, weight, place in ((bx, value[i][:, :width], 0), (by, gelu_w[i][...], 1)):
            part = jnp.dot(n1, weight, preferred_element_type=F32)
            if i == 0:
                out[...] = part if first else before[place][...] + part
            else:
                out[...] += part


def project(offsets, x, r1, value, gelu_w, before, width):
    total, block = x.shape[1:]
    count = len(offsets)
    first = before is None
    full = shaped((total, width), F32)
    extra = () if first else before
    at = 2 + 2 * count
    return pl.pallas_call(
        lambda *refs: project_kernel(offsets, first, width, *refs),
        in_specs=vmem(2 + 2 * count + len(extra)),
        out_shape=(full, full, shaped((count, total, block), BF16), shaped((count, 2, block), F32)),
        input_output_aliases={} if first else {at: 0, at + 1: 1},
        compiler_params=params(),
        cost_estimate=cost(4 * count * total * block * width, count * block * (4 * width + 4 * total)),
        name="project",
    )(x, r1, *value, *gelu_w, *extra)


NT = (((1,), (1,)), ((), ()))


def emit_kernel(ring_size, factors, *refs):
    half = refs[-1].shape[1]
    left = refs[:factors]
    own_o, other_o = refs[-2:]
    for o in range(ring_size):
        part = None
        for f in range(factors):
            weight = refs[factors + f * ring_size + o]
            width = left[f].shape[1]
            term = lax.dot_general(left[f][...], weight[:, :width], NT, preferred_element_type=F32)
            part = term if part is None else part + term
        own_o[o] = part[:half]
        other_o[o] = part[half:].astype(BF16)


def emit(lefts, weights, name):
    total, width = lefts[0].shape
    ring_size = len(weights[0])
    block = weights[0][0].shape[0]
    half = total // 2
    flat = [item for group in weights for item in group]
    return pl.pallas_call(
        lambda *refs: emit_kernel(ring_size, len(lefts), *refs),
        in_specs=vmem(len(lefts) + len(flat)),
        out_shape=(shaped((ring_size, half, block), F32), shaped((ring_size, half, block), BF16)),
        compiler_params=params(),
        cost_estimate=cost(
            2 * len(lefts) * total * width * ring_size * block, ring_size * block * (2 * width + 3 * total)
        ),
        name=name,
    )(*lefts, *flat)


def norm_kernel(x, pair, other, gains, h_o, n_o, r_o):
    ring_size, half, block = h_o.shape
    squares = jnp.zeros((half, block), F32)
    for o in range(ring_size):
        h = x[o, 0:half, :].astype(F32) + (pair[o].astype(F32) + other[o].astype(F32))
        h_o[o] = h
        squares = squares + h * h
    mean = jnp.sum(squares, 1, keepdims=True) * (1.0 / (ring_size * block))
    scale = lax.rsqrt(mean + EPSILON)
    r_o[...] = scale
    for o in range(ring_size):
        n_o[o] = (h_o[o] * scale * gains[o, 1:2, :]).astype(BF16)


def norm(x, pair, other, gains):
    ring_size, half, block = pair.shape
    return pl.pallas_call(
        norm_kernel,
        in_specs=vmem(4),
        out_shape=(shaped(pair.shape, F32), shaped(pair.shape, BF16), shaped((half, 1), F32)),
        compiler_params=params(),
        cost_estimate=cost(8 * pair.size, 12 * pair.size),
        name="norm",
    )(x, pair, other, gains)


def norm_back_kernel(pair, other, h1, r2, gains, g, dh_o, dhr_o, grad_o):
    ring_size, half, block = h1.shape
    dots = jnp.zeros((half, block), F32)
    scale = r2[...]
    for o in range(ring_size):
        grad = pair[o].astype(F32) + other[o].astype(F32)
        h = h1[o]
        product = grad * h
        dots = dots + product * gains[o, 1:2, :]
        grad_o[o] = jnp.sum(product * scale, 0, keepdims=True)
    mean = jnp.sum(dots, 1, keepdims=True) * (1.0 / (ring_size * block))
    bend = scale * scale * scale * mean
    for o in range(ring_size):
        grad = pair[o].astype(F32) + other[o].astype(F32)
        dh = g[o, 0:half, :].astype(F32) + scale * (grad * gains[o, 1:2, :]) - h1[o] * bend
        dh_o[o] = dh
        dhr_o[o] = dh.astype(BF16)


def norm_back(pair, other, h1, r2, gains, g):
    ring_size, half, block = pair.shape
    return pl.pallas_call(
        norm_back_kernel,
        in_specs=vmem(6),
        out_shape=(shaped(pair.shape, F32), shaped(pair.shape, BF16), shaped((ring_size, 1, block), F32)),
        compiler_params=params(),
        cost_estimate=cost(12 * pair.size, 16 * pair.size),
        name="norm_back",
    )(pair, other, h1, r2, gains, g)


def input_back_kernel(slots, pair, other, x, r1, gains, dh1, out_o, grad_o):
    ring_size, half, block = dh1.shape
    dots = jnp.zeros((half, block), F32)
    scale = r1[0:half, :]
    for o in range(ring_size):
        product = (pair[o].astype(F32) + other[o].astype(F32)) * x[o, 0:half, :].astype(F32)
        dots = dots + product * gains[o, 0:1, :]
        grad_o[o] = jnp.sum(product * scale, 0, keepdims=True)
    mean = jnp.sum(dots, 1, keepdims=True) * (1.0 / (ring_size * block))
    bend = scale * scale * scale * mean
    for k in range(ring_size):
        o = slots[k]
        grad = pair[o].astype(F32) + other[o].astype(F32)
        out_o[:, k * block : (k + 1) * block] = (
            dh1[o] + scale * (grad * gains[o, 0:1, :]) - x[o, 0:half, :].astype(F32) * bend
        )


def input_back(slots, pair, other, x, r1, gains, dh1):
    ring_size, half, block = pair.shape
    return pl.pallas_call(
        input_back_kernel,
        in_specs=[smem(), *vmem(6)],
        out_shape=(shaped((half, ring_size * block), F32), shaped((ring_size, 1, block), F32)),
        compiler_params=params(),
        cost_estimate=cost(12 * pair.size, 16 * pair.size),
        name="input_back",
    )(slots, pair, other, x, r1, gains, dh1)


def finish_kernel(slots, h1, pair, other, out_o):
    ring_size, half, block = h1.shape
    for k in range(ring_size):
        columns = slice(k * block, (k + 1) * block)
        out_o[:, columns] = h1[slots[k]] + (pair[:, columns].astype(F32) + other[:, columns].astype(F32))


def finish(slots, h1, pair, other):
    return pl.pallas_call(
        finish_kernel,
        in_specs=[smem(), *vmem(3)],
        out_shape=shaped(pair.shape, F32),
        compiler_params=params(),
        cost_estimate=cost(2 * pair.size, 12 * pair.size),
        name="finish",
    )(slots, h1, pair, other)


def unit_kernel(owners, n2, gate, up, dq, q_o, dga_o, dup_o):
    ring_size, total, block = n2.shape
    ga = upward = None
    for o in range(ring_size):
        at = pl.ds(pl.multiple_of(owners[o] * block, block), block)
        left = n2[o]
        term_g = jnp.dot(left, gate[at, :], preferred_element_type=F32)
        term_u = jnp.dot(left, up[at, :], preferred_element_type=F32)
        ga = term_g if ga is None else ga + term_g
        upward = term_u if upward is None else upward + term_u
    value, slope = gelu_both(ga)
    grad = dq[...]
    q_o[...] = (value * upward).astype(BF16)
    dga_o[...] = (grad * upward * slope).astype(BF16)
    dup_o[...] = (grad * value).astype(BF16)


def unit_pass(owners, n2, gate, up, dq):
    ring_size, total, block = n2.shape
    model, units = gate.shape
    tile = 256
    wide = pl.BlockSpec((total, tile), lambda i: (0, i))
    tall = pl.BlockSpec((model, tile), lambda i: (0, i))
    out = shaped((total, units), BF16)
    return pl.pallas_call(
        unit_kernel,
        grid=(units // tile,),
        in_specs=[smem(), pl.BlockSpec(n2.shape, lambda i: (0, 0, 0)), tall, tall, wide],
        out_specs=[wide, wide, wide],
        out_shape=(out, out, out),
        compiler_params=params(),
        cost_estimate=cost(4 * total * model * units, 4 * model * units + 10 * total * units, total * units),
        name="unit_pass",
    )(owners, n2, gate, up, dq)


def unit_back_kernel(owners, dga, dup, gate, up, own_o, other_o):
    half = other_o.shape[1]
    part = lax.dot_general(dga[...], gate[...], NT, preferred_element_type=F32)
    part = part + lax.dot_general(dup[...], up[...], NT, preferred_element_type=F32)
    own_o[0] = part[:half]
    other_o[0] = part[half:].astype(BF16)


def unit_back(owners, dga, dup, gate, up):
    ring_size = owners.shape[0]
    total, units = dga.shape
    half = total // 2
    block = gate.shape[0] // ring_size
    left = pl.BlockSpec((total, units), lambda o, owners: (0, 0))
    weight = pl.BlockSpec((block, units), lambda o, owners: (owners[o], 0))
    out = pl.BlockSpec((1, half, block), lambda o, owners: (o, 0, 0))
    return pl.pallas_call(
        unit_back_kernel,
        grid_spec=pltpu.PrefetchScalarGridSpec(
            num_scalar_prefetch=1,
            grid=(ring_size,),
            in_specs=[left, left, weight, weight],
            out_specs=[out, out],
        ),
        out_shape=(shaped((ring_size, half, block), F32), shaped((ring_size, half, block), BF16)),
        compiler_params=params(),
        cost_estimate=cost(4 * total * units * gate.shape[0], 4 * units * gate.shape[0] + 6 * total * gate.shape[0]),
        name="unit_back",
    )(owners, dga, dup, gate, up)


def local(
    tokens,
    cotangent,
    row_length,
    first_gain,
    value_weight,
    gelu_weight,
    conv_weight,
    conv_bias,
    input_gate,
    input_bias,
    recur_gate,
    recur_bias,
    decay_param,
    output_weight,
    second_gain,
    mlp_gate,
    mlp_up,
    mlp_down,
):
    ring_size = lax.axis_size("dp")
    middle = ring_size // 2
    ring = [2 * i if i < middle else 2 * (ring_size - 1 - i) + 1 for i in range(ring_size)]
    onward = [(ring[i], ring[(i + 1) % ring_size]) for i in range(ring_size)]
    backward = [(b, a) for a, b in onward]
    me = lax.axis_index("dp")
    core = lax.axis_index("mp") % 2
    core_pair = [(i, i ^ 1) for i in range(4)]
    chip_pair = [(i, i ^ 2) for i in range(4)]
    count = jnp.arange(ring_size, dtype=jnp.int32)

    def spot_of(index):
        return jnp.where(index % 2 == 0, index // 2, ring_size - 1 - index // 2)

    spots = (spot_of(me) + count) % ring_size
    owners = jnp.where(spots < middle, 2 * spots, 2 * (ring_size - 1 - spots) + 1).astype(jnp.int32)
    slots = ((spot_of(count) - spot_of(me) + ring_size) % ring_size).astype(jnp.int32)

    def hops(long_way_on):
        return (middle, ring_size - 1 - middle) if long_way_on else (ring_size - 1 - middle, middle)

    def ring_gather(shard, long_way_on):
        on, back = hops(long_way_on)
        got = [shard] + [None] * (ring_size - 1)
        moving = shard
        for s in range(1, on + 1):
            moving = lax.ppermute(moving, "dp", onward)
            got[ring_size - s] = moving
        moving = shard
        for s in range(1, back + 1):
            moving = lax.ppermute(moving, "dp", backward)
            got[s] = moving
        return got

    def ring_scatter(term, long_way_on, sent=BF16):
        on, back = hops(long_way_on)
        arrived = []
        for far, sign, way in ((on, 1, onward), (back, -1, backward)):
            moving = None
            for j in range(far, 0, -1):
                part = term(j if sign > 0 else ring_size - j)
                if moving is not None:
                    part = part + moving.astype(F32)
                moving = lax.ppermute(part.astype(sent), "dp", way)
            if moving is not None:
                arrived.append(moving)
        out = term(0)
        for item in arrived:
            out = out + item.astype(F32)
        return out

    def outer(left, right):
        return jnp.einsum("tb,tf->bf", left, right, preferred_element_type=F32)

    subs, row_count, length, model = tokens.shape
    half = row_count * length
    total = subs * half
    seqs = subs * row_count
    width, head = input_gate.shape
    block = model // ring_size
    lanes = (width + 128) // 128 * 128
    spare = lanes - width

    def mp_sum(own, other):
        got = lax.ppermute(other, "mp", core_pair)
        pair = (own + got.astype(F32)).astype(BF16)
        return pair, lax.ppermute(pair, "mp", chip_pair)

    def both_halves(own):
        return jnp.concatenate([own, lax.ppermute(own, "mp", core_pair)], 1)

    def in_order(own):
        got = lax.ppermute(own, "mp", core_pair)
        lower = jnp.where(core == 0, own, got)
        upper = jnp.where(core == 0, got, own)
        return jnp.stack([lower, upper]).reshape(subs, row_count, length, model)

    gain_lines = jnp.concatenate([first_gain.reshape(-1, spare), second_gain.reshape(-1, spare)])
    gain_lines = jnp.pad(gain_lines, ((0, block - gain_lines.shape[0]), (0, 0)))
    value_all = ring_gather(jnp.concatenate([value_weight, gain_lines], 1), True)
    gelu_all = ring_gather(gelu_weight, False)
    output_all = ring_gather(output_weight.T, True)

    scalars = jnp.concatenate([core[None], row_length.reshape(-1)]).astype(jnp.int32)
    x, g, g_flat, r1 = prepare(
        scalars, slots, tokens.reshape(subs, half, model), cotangent.reshape(subs, half, model), ring_size
    )
    dq = jnp.einsum("td,fd->tf", g_flat, mlp_down, preferred_element_type=F32)

    heads = width // head
    row_head = lax.broadcasted_iota(jnp.int32, (width, width), 0) // head
    column_head = lax.broadcasted_iota(jnp.int32, (width, width), 1) // head

    def block_matrix(gate):
        return jnp.where(row_head == column_head, jnp.tile(gate, (1, heads)), 0).astype(BF16)

    blocks_i, blocks_r = block_matrix(input_gate), block_matrix(recur_gate)
    decay_wide = decay_param.astype(F32)
    soft = jax.nn.softplus(-decay_wide)[None]
    gate_soft = jax.nn.sigmoid(-decay_wide)[None]
    taps = conv_weight.astype(F32)
    tap_bias = conv_bias.astype(F32)[None]
    bias_i, bias_r = input_bias.astype(F32)[None], recur_bias.astype(F32)[None]

    near = [o for o in range(ring_size) if min(o, ring_size - o) <= ring_size // 4]
    far = [o for o in range(ring_size) if o not in near]
    bx, by, n1_near, gains_near = project(
        near, x, r1, [value_all[o] for o in near], [gelu_all[o] for o in near], None, width
    )
    bx, by, n1_far, gains_far = project(
        far, x, r1, [value_all[o] for o in far], [gelu_all[o] for o in far], (bx, by), width
    )
    n1 = {o: n1_near[i] for i, o in enumerate(near)} | {o: n1_far[i] for i, o in enumerate(far)}
    gains = {o: gains_near[i] for i, o in enumerate(near)} | {o: gains_far[i] for i, o in enumerate(far)}
    gains = jnp.stack([gains[o] for o in range(ring_size)])

    p, cx, lx, lr, h = mixer_forward(
        seqs, bx, by, taps, tap_bias, blocks_i, blocks_r, bias_i, bias_r, soft
    )
    h1, n2_own, r2 = norm(x, *mp_sum(*emit([p], [output_all], "mixer_out")), gains)
    n2 = both_halves(n2_own)
    q, dga, dup = unit_pass(owners, n2, mlp_gate, mlp_up, dq)

    gate_grad = ring_scatter(lambda o: outer(n2[o], dga), True)
    up_grad = ring_scatter(lambda o: outer(n2[o], dup), False)
    down_grad = ring_scatter(lambda o: outer(g[o], q), True).T

    dh1, dhr_own, second_grad = norm_back(
        *mp_sum(*unit_back(owners, dga, dup, mlp_gate, mlp_up)), h1, r2, gains, g
    )
    dhr = both_halves(dhr_own)
    dbx, dby, gate_i, gate_r = mixer_backward(
        seqs, dhr, output_all, bx, by, cx, lx, lr, h, taps, blocks_i, blocks_r, soft, gate_soft, head
    )
    output_grad = ring_scatter(lambda o: outer(dhr[o], p), True).T
    value_grad = ring_scatter(lambda o: outer(n1[o], dbx), False)
    gelu_grad = ring_scatter(lambda o: outer(n1[o], dby), True)
    gate_i, gate_r = lax.psum((gate_i, gate_r), "dp")
    sums = jnp.concatenate(
        [gate_i[width + i * SUMS : width + (i + 1) * SUMS] for i in range(heads)], 1
    )

    input_own, first_grad = input_back(
        slots, *mp_sum(*emit([dbx, dby], [value_all, gelu_all], "input_out")), x, r1, gains, dh1
    )
    input_grad = in_order(input_own)
    gain_grads = jnp.concatenate([first_grad, second_grad], 1)
    gain_grads = gain_grads + lax.ppermute(gain_grads, "mp", core_pair)
    gain_grads = ring_scatter(lambda o: gain_grads[o], True, F32)

    out_own = jnp.dot(q[:half], mlp_down, preferred_element_type=F32)
    out_other = jnp.dot(q[half:], mlp_down, preferred_element_type=F32).astype(BF16)
    layer_out = in_order(finish(slots, h1, *mp_sum(out_own, out_other)))

    count = conv_weight.shape[0]
    return (
        layer_out,
        input_grad,
        gain_grads[0],
        value_grad,
        gelu_grad,
        sums[:count],
        sums[count],
        gate_i[:width],
        sums[count + 1],
        gate_r,
        sums[count + 2],
        sums[count + 3],
        output_grad,
        gain_grads[1],
        gate_grad,
        up_grad,
        down_grad,
    )


def solution(mesh):
    placed = (
        P(None, "dp", None, None),
        P(None, "dp", None, None),
        P(None, "dp"),
        P("dp"),
        P("dp", "mp"),
        P("dp", "mp"),
        P(None, "mp"),
        P("mp"),
        P("mp", None),
        P("mp"),
        P("mp", None),
        P("mp"),
        P("mp"),
        P("mp", "dp"),
        P("dp"),
        P(None, "mp"),
        P(None, "mp"),
        P("mp", None),
    )
    return jax.shard_map(
        local,
        mesh=mesh,
        in_specs=placed,
        out_specs=(
            P(None, "dp", None, None),
            P(None, "dp", None, None),
            P("dp"),
            P("dp", "mp"),
            P("dp", "mp"),
            P(None, "mp"),
            P("mp"),
            P("mp", None),
            P("mp"),
            P("mp", None),
            P("mp"),
            P("mp"),
            P("mp", "dp"),
            P("dp"),
            P("dp", "mp"),
            P("dp", "mp"),
            P("mp", "dp"),
        ),
        check_vma=False,
    )
```

time: 1980 us -> 565 us (0.29)
  local copies, waits for them, and re-layouts: 660 us -> 45.9 us
  waiting for transfers between devices: 651 us -> 226 us
  other arithmetic: 245 us -> 13.9 us
  matrix products: 246 us -> 83.9 us
  blocking collectives: 132 us -> 0 us
  starting transfers between devices: 1.28 us -> 101 us
  Pallas kernels: 0 us -> 70.2 us
    slice x200 -> x6, local copies, waits for them, and re-layouts: 438 us -> 2.83 us  [the longest x1 0.91 us: local(): gate_i[:width]]
    reduce_scatter x6 -> x0, waiting for transfers between devices: 374 us -> none  [the longest x1 119 us: local(): lax.psum_scatter(mlp_totals[0].astype(jnp.bfloat16), 'dp', scatter_dimens...]
    ppermute x0 -> x83, waiting for transfers between devices: none -> 201 us  [the longest x49 119 us: ring_scatter(): moving = lax.ppermute(part.astype(sent), 'dp', way)]
    dot_general x48 -> x51, matrix products: 246 us -> 83.9 us  [the longest x48 70.5 us: outer(): return jnp.einsum('tb,tf->bf', left, right, preferred_element_type=F32)]
    all_gather x6 -> x0, waiting for transfers between devices: 157 us -> none  [the longest x1 63.4 us: local(): lax.all_gather(value_weight, 'dp', axis=0, tiled=True)]
    ppermute x0 -> x83, starting transfers between devices: none -> 101 us  [the longest x49 63.9 us: ring_scatter(): moving = lax.ppermute(part.astype(sent), 'dp', way)]
    psum x3 -> x1, waiting for transfers between devices: 118 us -> 24.4 us  [local(): gate_i, gate_r = lax.psum((gate_i, gate_r), 'dp')]
    pad x56 -> x0, local copies, waits for them, and re-layouts: 80 us -> none  [the longest x28 42.3 us: run_forward(): return lax.associative_scan(linear_combine, (decay, inputs), axis=1)[1]]
  transfers between devices with their start and end apart: 15 -> 84, of which waited for: 9 -> 38; matrix products, arithmetic and copies ran while one was open for 29% -> 20% of each run, Pallas kernels for 0% -> 10%
where the time goes in v1:
time: 565 us; the launch traced here: 557 us
  waiting for transfers between devices  226 us (40%)
  starting transfers between devices  101 us (18%)
  matrix products  83.9 us (15%)
  Pallas kernels  70.2 us (12%)
  local copies, waits for them, and re-layouts  45.9 us (8%)
  between operations  16.1 us (3%)
  other arithmetic  13.9 us (2%)
    ppermute x49, waiting for transfers between devices, ring_scatter(): moving = lax.ppermute(part.astype(sent), 'dp', way)  119 us
    dot_general x48, matrix products, outer(): return jnp.einsum('tb,tf->bf', left, right, preferred_element_type=F32)  70.5 us
    ppermute x49, starting transfers between devices, ring_scatter(): moving = lax.ppermute(part.astype(sent), 'dp', way)  63.9 us
    ppermute x4, waiting for transfers between devices, mp_sum(): return (pair, lax.ppermute(pair, 'mp', chip_pair))  44 us
    unnamed x236, local copies, waits for them, and re-layouts  30.7 us
    psum x1, waiting for transfers between devices, local(): gate_i, gate_r = lax.psum((gate_i, gate_r), 'dp')  24.4 us
    ppermute x11, waiting for transfers between devices, ring_gather(): moving = lax.ppermute(moving, 'dp', onward)  22.6 us
    ppermute x11, starting transfers between devices, ring_gather(): moving = lax.ppermute(moving, 'dp', onward)  18.6 us
  transfers between devices with their start and end apart: 84, of which 38 were waited for; matrix products, arithmetic and copies ran while one was open for 20% of the time, Pallas kernels for 10%

profile of v1, /device:TPU:0, one launch (start us, length us, event | category | flops | bytes accessed | tf_op | source)
XLA Modules:
  0.0 557.1 jit_solution(8618541439216452265)
XLA Ops:
  8.6 3.1 collective-permute-start.17
  18.7 2.8 collective-permute-done.17.refs_8_
  23.6 6.3 %collective-permute-done.3.refs_6_.refs_9_ = bf16[256,768]{1,0:T(8,128)(2,1)S(1)} collective-permute-done((bf16[256,768]{1,0:T(8,128)(2,1)S(1)}, bf16[256,768]{1,0:T(8,128)(2,1)S(1)}, u32[]{:S(2)}, u32[]{:S(2)}) %collective-permute-start.3) | collective-permute-done | bytes 393248 | tf_op jit(solution)/shard_map/ppermute | solution.py:628
  40.5 4.4 collective-permute-done.refs_3_
  47.3 8.0 %collective-permute-done.18.refs_7_ = bf16[256,704]{1,0:T(8,128)(2,1)} collective-permute-done((bf16[256,704]{1,0:T(8,128)(2,1)S(1)}, bf16[256,704]{1,0:T(8,128)(2,1)}, u32[]{:S(2)}, u32[]{:S(2)}) %collective-permute-start.18) | collective-permute-done | bytes 360480 | tf_op jit(solution)/shard_map/ppermute | solution.py:628
  84.7 4.3 collective-permute-done.13.refs_7_.refs_15_
  91.2 3.8 project.2
  96.1 4.3 collective-permute-done.10.refs_6_.refs_14_
  100.4 3.4 project.3
  104.8 7.2 %mixer_forward.1 = (bf16[512,704]{1,0:T(8,128)(2,1)S(1)}, bf16[512,704]{1,0:T(8,128)(2,1)S(1)}, f32[512,704]{1,0:T(8,128)S(1)}, f32[512,704]{1,0:T(8,128)S(1)}, f32[512,704]{1,0:T(8,128)S(1)}) custom-call(f32[512,704]{1,0:T(8,128)S(1)} %get-tuple-element.59.refs_0_.refs_9_, f32[512,704]{1,0:T(8,128)S(1)} %get-tuple-element.60.refs_1_.refs_10_, ...), custom_call_target="tpu_custom_call" | custom-call | flops 1015021568 | bytes 8650752 | tf_op jit(solution)/shard_map/mixer_forward/pallas_call | solution.py:118
  115.5 3.5 mixer_out.1
  119.1 2.6 collective-permute-done.21
  123.7 23.6 %collective-permute-done.22.other = bf16[8,256,256]{2,1,0:T(8,128)(2,1)S(1)} collective-permute-done((bf16[8,256,256]{2,1,0:T(8,128)(2,1)S(1)}, bf16[8,256,256]{2,1,0:T(8,128)(2,1)S(1)}, u32[]{:S(2)}, u32[]{:S(2)}) %collective-permute-start.22) | collective-permute-done | bytes 1048608 | tf_op jit(solution)/shard_map/ppermute | solution.py:668
  151.4 5.6 %fusion.119.dq = f32[512,1536]{1,0:T(8,128)S(1)} fusion(bf16[512,2048]{1,0:T(8,128)(2,1)S(1)} %copy-done.80, bf16[1536,2048]{1,0:T(8,128)(2,1)} %param.35), kind=kOutput, calls=%fused_computation.237 | convolution fusion | flops 3221225472 | bytes 11534336 | tf_op jit(solution)/shard_map/td,fd->tf/dot_general | solution.py:689
  158.4 12.2 %unit_pass.1 = (bf16[512,1536]{1,0:T(8,128)(2,1)S(1)}, bf16[512,1536]{1,0:T(8,128)(2,1)S(1)}, bf16[512,1536]{1,0:T(8,128)(2,1)S(1)}) custom-call(s32[8]{0:T(128)S(1)} %copy-done.92, bf16[8,512,256]{2,1,0:T(8,128)(2,1)S(1)} %constant_dynamic-update-slice_fusion.n2, bf16[2048,1536]{1,0:T(8,128)(2,1)} %gate.3, bf16[2048,1536]{1,0:T(8,128)(2,1)} %up.3, ...), custom_call_target="tpu_custom_call" | custom-call | flops 6442450944 | bytes 20447232 | tf_op jit(solution)/shard_map/unit_pass/pallas_call | solution.py:539
  171.9 5.9 %convolution_convert_fusion.6 = bf16[256,2048]{1,0:T(8,128)(2,1)} fusion(bf16[1536,2048]{1,0:T(8,128)(2,1)} %param.35, bf16[512,1536]{1,0:T(8,128)(2,1)S(1)} %get-tuple-element.69), kind=kOutput, calls=%fused_computation.47 | convolution fusion | flops 1611137024 | bytes 8126464 | tf_op jit(solution)/shard_map/dot_general | solution.py:753
  182.0 10.3 %unit_back.1 = (f32[8,256,256]{2,1,0:T(8,128)S(1)}, bf16[8,256,256]{2,1,0:T(8,128)(2,1)S(1)}) custom-call(s32[8]{0:T(128)S(1)} %copy-done.92, bf16[512,1536]{1,0:T(8,128)(2,1)S(1)} %get-tuple-element.70.dga, bf16[512,1536]{1,0:T(8,128)(2,1)S(1)} %get-tuple-element.71.dup, bf16[2048,1536]{1,0:T(8,128)(2,1)S(1)} %bitcast.238, bf16[2048,1536]{1,0:T(8,128)(2,1)} %up.3), custom_call_target="tpu_custom_call" | custom-call | flops 6442450944 | bytes 18874368 | tf_op jit(solution)/shard_map/unit_back/pallas_call | solution.py:567
  196.2 2.6 collective-permute-done.76
  203.9 11.7 %collective-permute-done.69 = bf16[256,1536]{1,0:T(8,128)(2,1)} collective-permute-done((bf16[256,1536]{1,0:T(8,128)(2,1)S(1)}, bf16[256,1536]{1,0:T(8,128)(2,1)}, u32[]{:S(2)}, u32[]{:S(2)}) %collective-permute-start.69) | collective-permute-done | bytes 786464 | tf_op jit(solution)/shard_map/ppermute | solution.py:645
  219.6 12.8 %collective-permute-done.62 = bf16[256,1536]{1,0:T(8,128)(2,1)S(1)} collective-permute-done((bf16[256,1536]{1,0:T(8,128)(2,1)S(1)}, bf16[256,1536]{1,0:T(8,128)(2,1)S(1)}, u32[]{:S(2)}, u32[]{:S(2)}) %collective-permute-start.62) | collective-permute-done | bytes 786464 | tf_op jit(solution)/shard_map/ppermute | solution.py:645
  240.1 9.2 %collective-permute-done.77 = bf16[256,1536]{1,0:T(8,128)(2,1)S(1)} collective-permute-done((bf16[256,1536]{1,0:T(8,128)(2,1)S(1)}, bf16[256,1536]{1,0:T(8,128)(2,1)S(1)}, u32[]{:S(2)}, u32[]{:S(2)}) %collective-permute-start.77) | collective-permute-done | bytes 786464 | tf_op jit(solution)/shard_map/ppermute | solution.py:645
  250.1 2.8 collective-permute-done.81
  255.9 10.2 %collective-permute-done.70 = bf16[256,1536]{1,0:T(8,128)(2,1)S(1)} collective-permute-done((bf16[256,1536]{1,0:T(8,128)(2,1)S(1)}, bf16[256,1536]{1,0:T(8,128)(2,1)S(1)}, u32[]{:S(2)}, u32[]{:S(2)}) %collective-permute-start.70) | collective-permute-done | bytes 786464 | tf_op jit(solution)/shard_map/ppermute | solution.py:645
  272.8 10.1 %collective-permute-done.63 = bf16[256,1536]{1,0:T(8,128)(2,1)S(1)} collective-permute-done((bf16[256,1536]{1,0:T(8,128)(2,1)S(1)}, bf16[256,1536]{1,0:T(8,128)(2,1)S(1)}, u32[]{:S(2)}, u32[]{:S(2)}) %collective-permute-start.63) | collective-permute-done | bytes 786464 | tf_op jit(solution)/shard_map/ppermute | solution.py:645
  288.0 9.2 %collective-permute-done.28.other = bf16[8,256,256]{2,1,0:T(8,128)(2,1)S(1)} collective-permute-done((bf16[8,256,256]{2,1,0:T(8,128)(2,1)S(1)}, bf16[8,256,256]{2,1,0:T(8,128)(2,1)S(1)}, u32[]{:S(2)}, u32[]{:S(2)}) %collective-permute-start.28) | collective-permute-done | bytes 1048608 | tf_op jit(solution)/shard_map/ppermute | solution.py:668
  304.3 2.7 fusion.15
  308.4 2.8 fusion.12
  311.2 5.6 %collective-permute-done.64 = bf16[256,1536]{1,0:T(8,128)(2,1)} collective-permute-done((bf16[256,1536]{1,0:T(8,128)(2,1)}, bf16[256,1536]{1,0:T(8,128)(2,1)}, u32[]{:S(2)}, u32[]{:S(2)}) %collective-permute-start.64) | collective-permute-done | bytes 786464 | tf_op jit(solution)/shard_map/ppermute | solution.py:645
  318.5 2.8 fusion.5
  323.4 16.6 %mixer_backward.1 = (bf16[512,704]{1,0:T(8,128)(2,1)S(1)}, bf16[512,704]{1,0:T(8,128)(2,1)S(1)}, f32[736,176]{1,0:T(8,128)S(1)}, f32[704,176]{1,0:T(8,128)S(1)}) custom-call(bf16[8,512,256]{2,1,0:T(8,128)(2,1)} %copy-done.93, bf16[256,704]{1,0:T(8,128)(2,1)S(1)} %bitcast.236, bf16[256,704]{1,0:T(8,128)(2,1)S(1)} %copy-done.54, ...), custom_call_target="tpu_custom_call" | custom-call | flops 3552575488 | bytes 12976128 | tf_op jit(solution)/shard_map/mixer_backward/pallas_call | solution.py:248
  343.1 5.3 input_out.1
  359.3 3.7 fusion.3
  365.2 3.2 fusion.1
  369.9 16.6 %collective-permute-done.65 = bf16[256,1536]{1,0:T(8,128)(2,1)} collective-permute-done((bf16[256,1536]{1,0:T(8,128)(2,1)}, bf16[256,1536]{1,0:T(8,128)(2,1)}, u32[]{:S(2)}, u32[]{:S(2)}) %collective-permute-start.65) | collective-permute-done | bytes 786464 | tf_op jit(solution)/shard_map/ppermute | solution.py:645
  386.5 4.0 collective-permute-start.52
  390.5 3.2 fusion.2
  393.7 3.1 copy.62
  404.6 3.3 collective-permute-done.48
  413.4 5.0 collective-permute-done.41
  421.7 5.3 collective-permute-done.56
  433.9 3.9 collective-permute-done.49
  450.6 24.4 %all-reduce.4.cloned.1.call-done = (f32[736,176]{1,0:T(8,128)}, f32[704,176]{1,0:T(8,128)}) async-done(((f32[736,176]{1,0:T(8,128)}, f32[704,176]{1,0:T(8,128)}), (f32[736,176]{1,0:T(8,128)}, f32[704,176]{1,0:T(8,128)})) %all-reduce.4.cloned.1.call-update) | async-done | bytes 1013776 | tf_op jit(solution)/shard_map/psum | solution.py:739
  486.5 2.8 select_bitcast_fusion.3
  489.4 2.6 maximum_bitcast_fusion
  492.0 11.2 %collective-permute-done.31.other = bf16[8,256,256]{2,1,0:T(8,128)(2,1)} collective-permute-done((bf16[8,256,256]{2,1,0:T(8,128)(2,1)S(1)}, bf16[8,256,256]{2,1,0:T(8,128)(2,1)}, u32[]{:S(2)}, u32[]{:S(2)}) %collective-permute-start.31) | collective-permute-done | bytes 1048608 | tf_op jit(solution)/shard_map/ppermute | solution.py:668
  508.0 2.7 collective-permute-start.58
  514.3 6.1 %collective-permute-done.34 = f32[2,256]{1,0:T(2,128)S(1)} collective-permute-done((f32[2,256]{1,0:T(2,128)S(1)}, f32[2,256]{1,0:T(2,128)S(1)}, u32[]{:S(2)}, u32[]{:S(2)}) %collective-permute-start.34) | collective-permute-done | bytes 2080 | tf_op jit(solution)/shard_map/ppermute | solution.py:645
  531.6 3.8 collective-permute-done.36
  (470 shorter events, 220.3 us)
Async XLA Ops:
  7.3 467.7 %all-reduce.4.cloned.1.call-start = ((), (), s32[]{:S(2)}) async-start(), calls=%async_computation | async-start | bytes 2949120 | tf_op jit(solution)/shard_map/psum | solution.py:739
  16.7 28.2 %collective-permute-start = (bf16[256,768]{1,0:T(8,128)(2,1)S(1)}, bf16[256,768]{1,0:T(8,128)(2,1)S(1)}, u32[]{:S(2)}, u32[]{:S(2)}) collective-permute-start(bf16[256,768]{1,0:T(8,128)(2,1)S(1)} %pad_maximum_fusion.refs_2_), channel_id=1, source_target_pairs={{8,0},{16,8},{24,16},{28,24},{20,28},{12,20},{4,12},{0,4},{9,1},{1... | collective-permute-start | bytes 1179656 | tf_op jit(solution)/shard_map/ppermute | solution.py:632
  29.9 29.0 %collective-permute-start.4 = (bf16[256,768]{1,0:T(8,128)(2,1)S(1)}, bf16[256,768]{1,0:T(8,128)(2,1)}, u32[]{:S(2)}, u32[]{:S(2)}) collective-permute-start(bf16[256,768]{1,0:T(8,128)(2,1)S(1)} %collective-permute-done.3.refs_6_.refs_9_), channel_id=1, source_target_pairs={{0,8},{8,16},{16,24},{24,28},{28,20},{20,12},{12,4},{4,0},{1,9},{9... | collective-permute-start | bytes 1179656 | tf_op jit(solution)/shard_map/ppermute | solution.py:628
  32.8 22.5 %collective-permute-start.18 = (bf16[256,704]{1,0:T(8,128)(2,1)S(1)}, bf16[256,704]{1,0:T(8,128)(2,1)}, u32[]{:S(2)}, u32[]{:S(2)}) collective-permute-start(bf16[256,704]{1,0:T(8,128)(2,1)S(1)} %collective-permute-done.17.refs_8_), channel_id=1, source_target_pairs={{0,8},{8,16},{16,24},{24,28},{28,20},{20,12},{12,4},{4,0},{1,9},{9... | collective-permute-start | bytes 1081352 | tf_op jit(solution)/shard_map/ppermute | solution.py:628
  38.4 23.3 %collective-permute-start.15 = (bf16[256,704]{1,0:T(8,128)(2,1)S(1)}, bf16[256,704]{1,0:T(8,128)(2,1)S(1)}, u32[]{:S(2)}, u32[]{:S(2)}) collective-permute-start(bf16[256,704]{1,0:T(8,128)(2,1)S(1)} %collective-permute-done.14.refs_2_), channel_id=1, source_target_pairs={{8,0},{16,8},{24,16},{28,24},{20,28},{12,20},{4,12},{0,4},{9,1},{1... | collective-permute-start | bytes 1081352 | tf_op jit(solution)/shard_map/ppermute | solution.py:632
  55.3 24.4 %collective-permute-start.1 = (bf16[256,768]{1,0:T(8,128)(2,1)}, bf16[256,768]{1,0:T(8,128)(2,1)}, u32[]{:S(2)}, u32[]{:S(2)}) collective-permute-start(bf16[256,768]{1,0:T(8,128)(2,1)} %copy-done.89), channel_id=1, source_target_pairs={{8,0},{16,8},{24,16},{28,24},{20,28},{12,20},{4,12},{0,4},{9,1},{1... | collective-permute-start | bytes 1179656 | tf_op jit(solution)/shard_map/ppermute | solution.py:632
  57.4 22.4 %collective-permute-start.9 = (bf16[256,704]{1,0:T(8,128)(2,1)}, bf16[256,704]{1,0:T(8,128)(2,1)}, u32[]{:S(2)}, u32[]{:S(2)}) collective-permute-start(bf16[256,704]{1,0:T(8,128)(2,1)} %collective-permute-done.8.refs_9_.refs_12_), channel_id=1, source_target_pairs={{8,0},{16,8},{24,16},{28,24},{20,28},{12,20},{4,12},{0,4},{9,1},{1... | collective-permute-start | bytes 1081352 | tf_op jit(solution)/shard_map/ppermute | solution.py:632
  58.9 22.7 %collective-permute-start.5 = (bf16[256,768]{1,0:T(8,128)(2,1)}, bf16[256,768]{1,0:T(8,128)(2,1)}, u32[]{:S(2)}, u32[]{:S(2)}) collective-permute-start(bf16[256,768]{1,0:T(8,128)(2,1)} %collective-permute-done.4.refs_5_.refs_8_), channel_id=1, source_target_pairs={{0,8},{8,16},{16,24},{24,28},{28,20},{20,12},{12,4},{4,0},{1,9},{9... | collective-permute-start | bytes 1179656 | tf_op jit(solution)/shard_map/ppermute | solution.py:628
  61.8 21.0 %collective-permute-start.19 = (bf16[256,704]{1,0:T(8,128)(2,1)}, bf16[256,704]{1,0:T(8,128)(2,1)}, u32[]{:S(2)}, u32[]{:S(2)}) collective-permute-start(bf16[256,704]{1,0:T(8,128)(2,1)} %collective-permute-done.18.refs_7_), channel_id=1, source_target_pairs={{0,8},{8,16},{16,24},{24,28},{28,20},{20,12},{12,4},{4,0},{1,9},{9... | collective-permute-start | bytes 1081352 | tf_op jit(solution)/shard_map/ppermute | solution.py:628
  63.7 25.3 %collective-permute-start.13 = (bf16[256,704]{1,0:T(8,128)(2,1)}, bf16[256,704]{1,0:T(8,128)(2,1)}, u32[]{:S(2)}, u32[]{:S(2)}) collective-permute-start(bf16[256,704]{1,0:T(8,128)(2,1)} %collective-permute-done.12.refs_10_.refs_16_), channel_id=1, source_target_pairs={{0,8},{8,16},{16,24},{24,28},{28,20},{20,12},{12,4},{4,0},{1,9},{9... | collective-permute-start | bytes 1081352 | tf_op jit(solution)/shard_map/ppermute | solution.py:628
  82.8 32.6 %collective-permute-start.16 = (bf16[256,704]{1,0:T(8,128)(2,1)S(1)}, bf16[256,704]{1,0:T(8,128)(2,1)S(1)}, u32[]{:S(2)}, u32[]{:S(2)}) collective-permute-start(bf16[256,704]{1,0:T(8,128)(2,1)S(1)} %copy-done.56), channel_id=1, source_target_pairs={{8,0},{16,8},{24,16},{28,24},{20,28},{12,20},{4,12},{0,4},{9,1},{1... | collective-permute-start | bytes 1081352 | tf_op jit(solution)/shard_map/ppermute | solution.py:632
  89.0 26.5 %collective-permute-start.20 = (bf16[256,704]{1,0:T(8,128)(2,1)}, bf16[256,704]{1,0:T(8,128)(2,1)S(1)}, u32[]{:S(2)}, u32[]{:S(2)}) collective-permute-start(bf16[256,704]{1,0:T(8,128)(2,1)} %collective-permute-done.19.refs_6_), channel_id=1, source_target_pairs={{0,8},{8,16},{16,24},{24,28},{28,20},{20,12},{12,4},{4,0},{1,9},{9... | collective-permute-start | bytes 1081352 | tf_op jit(solution)/shard_map/ppermute | solution.py:628
  122.0 25.3 %collective-permute-start.22 = (bf16[8,256,256]{2,1,0:T(8,128)(2,1)S(1)}, bf16[8,256,256]{2,1,0:T(8,128)(2,1)S(1)}, u32[]{:S(2)}, u32[]{:S(2)}) collective-permute-start(bf16[8,256,256]{2,1,0:T(8,128)(2,1)S(1)} %add_convert_fusion.2.pair), channel_id=1, source_target_pairs={{0,2},{1,3},{2,0},{3,1},{4,6},{5,7},{6,4},{7,5},{8,10},{9,11},{10,... | collective-permute-start | bytes 3145736 | tf_op jit(solution)/shard_map/ppermute | solution.py:668
  179.9 21.2 %collective-permute-start.80 = (bf16[256,1536]{1,0:T(8,128)(2,1)S(1)}, bf16[256,1536]{1,0:T(8,128)(2,1)S(1)}, u32[]{:S(2)}, u32[]{:S(2)}) collective-permute-start(bf16[256,1536]{1,0:T(8,128)(2,1)S(1)} %convolution_convert_fusion), channel_id=1, source_target_pairs={{8,0},{16,8},{24,16},{28,24},{20,28},{12,20},{4,12},{0,4},{9,1},{1... | collective-permute-start | bytes 2359304 | tf_op jit(solution)/shard_map/ppermute | solution.py:645
  180.4 35.3 %collective-permute-start.69 = (bf16[256,1536]{1,0:T(8,128)(2,1)S(1)}, bf16[256,1536]{1,0:T(8,128)(2,1)}, u32[]{:S(2)}, u32[]{:S(2)}) collective-permute-start(bf16[256,1536]{1,0:T(8,128)(2,1)S(1)} %convolution_convert_fusion.3), channel_id=1, source_target_pairs={{0,8},{8,16},{16,24},{24,28},{28,20},{20,12},{12,4},{4,0},{1,9},{9... | collective-permute-start | bytes 2359304 | tf_op jit(solution)/shard_map/ppermute | solution.py:645
  192.8 24.5 %collective-permute-start.72 = (bf16[256,1536]{1,0:T(8,128)(2,1)S(1)}, bf16[256,1536]{1,0:T(8,128)(2,1)S(1)}, u32[]{:S(2)}, u32[]{:S(2)}) collective-permute-start(bf16[256,1536]{1,0:T(8,128)(2,1)S(1)} %convolution_convert_fusion.2), channel_id=1, source_target_pairs={{8,0},{16,8},{24,16},{28,24},{20,28},{12,20},{4,12},{0,4},{9,1},{1... | collective-permute-start | bytes 2359304 | tf_op jit(solution)/shard_map/ppermute | solution.py:645
  193.9 38.4 %collective-permute-start.62 = (bf16[256,1536]{1,0:T(8,128)(2,1)S(1)}, bf16[256,1536]{1,0:T(8,128)(2,1)S(1)}, u32[]{:S(2)}, u32[]{:S(2)}) collective-permute-start(bf16[256,1536]{1,0:T(8,128)(2,1)S(1)} %convolution_convert_fusion.5), channel_id=1, source_target_pairs={{0,8},{8,16},{16,24},{24,28},{28,20},{20,12},{12,4},{4,0},{1,9},{9... | collective-permute-start | bytes 2359304 | tf_op jit(solution)/shard_map/ppermute | solution.py:645
  198.8 34.5 %collective-permute-start.66 = (bf16[256,1536]{1,0:T(8,128)(2,1)S(1)}, bf16[256,1536]{1,0:T(8,128)(2,1)S(1)}, u32[]{:S(2)}, u32[]{:S(2)}) collective-permute-start(bf16[256,1536]{1,0:T(8,128)(2,1)S(1)} %convolution_convert_fusion.4), channel_id=1, source_target_pairs={{8,0},{16,8},{24,16},{28,24},{20,28},{12,20},{4,12},{0,4},{9,1},{1... | collective-permute-start | bytes 2359304 | tf_op jit(solution)/shard_map/ppermute | solution.py:645
  202.1 33.6 %collective-permute-start.24 = (bf16[256,2048]{1,0:T(8,128)(2,1)S(1)}, bf16[256,2048]{1,0:T(8,128)(2,1)S(1)}, u32[]{:S(2)}, u32[]{:S(2)}) collective-permute-start(bf16[256,2048]{1,0:T(8,128)(2,1)S(1)} %copy-done.108), channel_id=1, source_target_pairs={{0,1},{1,0},{2,3},{3,2},{4,5},{5,4},{6,7},{7,6},{8,9},{9,8},{10,11... | collective-permute-start | bytes 3145736 | tf_op jit(solution)/shard_map/ppermute | solution.py:666
  215.6 22.3 %collective-permute-start.27 = (bf16[8,256,256]{2,1,0:T(8,128)(2,1)S(1)}, bf16[8,256,256]{2,1,0:T(8,128)(2,1)S(1)}, u32[]{:S(2)}, u32[]{:S(2)}) collective-permute-start(bf16[8,256,256]{2,1,0:T(8,128)(2,1)S(1)} %get-tuple-element.73), channel_id=1, source_target_pairs={{0,1},{1,0},{2,3},{3,2},{4,5},{5,4},{6,7},{7,6},{8,9},{9,8},{10,11... | collective-permute-start | bytes 3145736 | tf_op jit(solution)/shard_map/ppermute | solution.py:666
  217.4 31.8 %collective-permute-start.77 = (bf16[256,1536]{1,0:T(8,128)(2,1)S(1)}, bf16[256,1536]{1,0:T(8,128)(2,1)S(1)}, u32[]{:S(2)}, u32[]{:S(2)}) collective-permute-start(bf16[256,1536]{1,0:T(8,128)(2,1)S(1)} %fusion.17), channel_id=1, source_target_pairs={{0,8},{8,16},{16,24},{24,28},{28,20},{20,12},{12,4},{4,0},{1,9},{9... | collective-permute-start | bytes 2359304 | tf_op jit(solution)/shard_map/ppermute | solution.py:645
  233.3 32.8 %collective-permute-start.70 = (bf16[256,1536]{1,0:T(8,128)(2,1)S(1)}, bf16[256,1536]{1,0:T(8,128)(2,1)S(1)}, u32[]{:S(2)}, u32[]{:S(2)}) collective-permute-start(bf16[256,1536]{1,0:T(8,128)(2,1)S(1)} %fusion.11), channel_id=1, source_target_pairs={{0,8},{8,16},{16,24},{24,28},{28,20},{20,12},{12,4},{4,0},{1,9},{9... | collective-permute-start | bytes 2359304 | tf_op jit(solution)/shard_map/ppermute | solution.py:645
  235.7 34.0 %collective-permute-start.73 = (bf16[256,1536]{1,0:T(8,128)(2,1)S(1)}, bf16[256,1536]{1,0:T(8,128)(2,1)S(1)}, u32[]{:S(2)}, u32[]{:S(2)}) collective-permute-start(bf16[256,1536]{1,0:T(8,128)(2,1)S(1)} %fusion.14), channel_id=1, source_target_pairs={{8,0},{16,8},{24,16},{28,24},{20,28},{12,20},{4,12},{0,4},{9,1},{1... | collective-permute-start | bytes 2359304 | tf_op jit(solution)/shard_map/ppermute | solution.py:645
  237.9 45.0 %collective-permute-start.63 = (bf16[256,1536]{1,0:T(8,128)(2,1)S(1)}, bf16[256,1536]{1,0:T(8,128)(2,1)S(1)}, u32[]{:S(2)}, u32[]{:S(2)}) collective-permute-start(bf16[256,1536]{1,0:T(8,128)(2,1)S(1)} %fusion.7), channel_id=1, source_target_pairs={{0,8},{8,16},{16,24},{24,28},{28,20},{20,12},{12,4},{4,0},{1,9},{9... | collective-permute-start | bytes 2359304 | tf_op jit(solution)/shard_map/ppermute | solution.py:645
  249.2 35.6 %collective-permute-start.67 = (bf16[256,1536]{1,0:T(8,128)(2,1)S(1)}, bf16[256,1536]{1,0:T(8,128)(2,1)S(1)}, u32[]{:S(2)}, u32[]{:S(2)}) collective-permute-start(bf16[256,1536]{1,0:T(8,128)(2,1)S(1)} %fusion.9), channel_id=1, source_target_pairs={{8,0},{16,8},{24,16},{28,24},{20,28},{12,20},{4,12},{0,4},{9,1},{1... | collective-permute-start | bytes 2359304 | tf_op jit(solution)/shard_map/ppermute | solution.py:645
  252.9 48.7 %collective-permute-start.25 = (bf16[256,2048]{1,0:T(8,128)(2,1)S(1)}, bf16[256,2048]{1,0:T(8,128)(2,1)S(1)}, u32[]{:S(2)}, u32[]{:S(2)}) collective-permute-start(bf16[256,2048]{1,0:T(8,128)(2,1)S(1)} %fusion.4.pair), channel_id=1, source_target_pairs={{0,2},{1,3},{2,0},{3,1},{4,6},{5,7},{6,4},{7,5},{8,10},{9,11},{10,... | collective-permute-start | bytes 3145736 | tf_op jit(solution)/shard_map/ppermute | solution.py:668
  266.1 31.0 %collective-permute-start.28 = (bf16[8,256,256]{2,1,0:T(8,128)(2,1)S(1)}, bf16[8,256,256]{2,1,0:T(8,128)(2,1)S(1)}, u32[]{:S(2)}, u32[]{:S(2)}) collective-permute-start(bf16[8,256,256]{2,1,0:T(8,128)(2,1)S(1)} %add_convert_fusion.1.pair), channel_id=1, source_target_pairs={{0,2},{1,3},{2,0},{3,1},{4,6},{5,7},{6,4},{7,5},{8,10},{9,11},{10,... | collective-permute-start | bytes 3145736 | tf_op jit(solution)/shard_map/ppermute | solution.py:668
  269.7 32.8 %collective-permute-start.78 = (bf16[256,1536]{1,0:T(8,128)(2,1)S(1)}, bf16[256,1536]{1,0:T(8,128)(2,1)S(1)}, u32[]{:S(2)}, u32[]{:S(2)}) collective-permute-start(bf16[256,1536]{1,0:T(8,128)(2,1)S(1)} %fusion.16), channel_id=1, source_target_pairs={{0,8},{8,16},{16,24},{24,28},{28,20},{20,12},{12,4},{4,0},{1,9},{9... | collective-permute-start | bytes 2359304 | tf_op jit(solution)/shard_map/ppermute | solution.py:645
  283.0 24.1 %collective-permute-start.74 = (bf16[256,1536]{1,0:T(8,128)(2,1)}, bf16[256,1536]{1,0:T(8,128)(2,1)}, u32[]{:S(2)}, u32[]{:S(2)}) collective-permute-start(bf16[256,1536]{1,0:T(8,128)(2,1)} %fusion.13), channel_id=1, source_target_pairs={{8,0},{16,8},{24,16},{28,24},{20,28},{12,20},{4,12},{0,4},{9,1},{1... | collective-permute-start | bytes 2359304 | tf_op jit(solution)/shard_map/ppermute | solution.py:645
  284.9 31.9 %collective-permute-start.64 = (bf16[256,1536]{1,0:T(8,128)(2,1)}, bf16[256,1536]{1,0:T(8,128)(2,1)}, u32[]{:S(2)}, u32[]{:S(2)}) collective-permute-start(bf16[256,1536]{1,0:T(8,128)(2,1)} %fusion.6), channel_id=1, source_target_pairs={{0,8},{8,16},{16,24},{24,28},{28,20},{20,12},{12,4},{4,0},{1,9},{9... | collective-permute-start | bytes 2359304 | tf_op jit(solution)/shard_map/ppermute | solution.py:645
  297.1 58.2 %collective-permute-start.82 = (bf16[256,1536]{1,0:T(8,128)(2,1)}, bf16[256,1536]{1,0:T(8,128)(2,1)S(1)}, u32[]{:S(2)}, u32[]{:S(2)}) collective-permute-start(bf16[256,1536]{1,0:T(8,128)(2,1)} %fusion.18), channel_id=1, source_target_pairs={{8,0},{16,8},{24,16},{28,24},{20,28},{12,20},{4,12},{0,4},{9,1},{1... | collective-permute-start | bytes 2359304 | tf_op jit(solution)/shard_map/ppermute | solution.py:645
  303.6 59.3 %collective-permute-start.71 = (bf16[256,1536]{1,0:T(8,128)(2,1)}, bf16[256,1536]{1,0:T(8,128)(2,1)}, u32[]{:S(2)}, u32[]{:S(2)}) collective-permute-start(bf16[256,1536]{1,0:T(8,128)(2,1)} %fusion.10), channel_id=1, source_target_pairs={{0,8},{8,16},{16,24},{24,28},{28,20},{20,12},{12,4},{4,0},{1,9},{9... | collective-permute-start | bytes 2359304 | tf_op jit(solution)/shard_map/ppermute | solution.py:645
  307.0 61.3 %collective-permute-start.68 = (bf16[256,1536]{1,0:T(8,128)(2,1)}, bf16[256,1536]{1,0:T(8,128)(2,1)}, u32[]{:S(2)}, u32[]{:S(2)}) collective-permute-start(bf16[256,1536]{1,0:T(8,128)(2,1)} %fusion.8), channel_id=1, source_target_pairs={{8,0},{16,8},{24,16},{28,24},{20,28},{12,20},{4,12},{0,4},{9,1},{1... | collective-permute-start | bytes 2359304 | tf_op jit(solution)/shard_map/ppermute | solution.py:645
  316.8 42.4 %collective-permute-start.79 = (bf16[256,1536]{1,0:T(8,128)(2,1)}, bf16[256,1536]{1,0:T(8,128)(2,1)}, u32[]{:S(2)}, u32[]{:S(2)}) collective-permute-start(bf16[256,1536]{1,0:T(8,128)(2,1)} %fusion.15), channel_id=1, source_target_pairs={{0,8},{8,16},{16,24},{24,28},{28,20},{20,12},{12,4},{4,0},{1,9},{9... | collective-permute-start | bytes 2359304 | tf_op jit(solution)/shard_map/ppermute | solution.py:645
  321.3 43.2 %collective-permute-start.75 = (bf16[256,1536]{1,0:T(8,128)(2,1)}, bf16[256,1536]{1,0:T(8,128)(2,1)}, u32[]{:S(2)}, u32[]{:S(2)}) collective-permute-start(bf16[256,1536]{1,0:T(8,128)(2,1)} %fusion.12), channel_id=1, source_target_pairs={{8,0},{16,8},{24,16},{28,24},{20,28},{12,20},{4,12},{0,4},{9,1},{1... | collective-permute-start | bytes 2359304 | tf_op jit(solution)/shard_map/ppermute | solution.py:645
  355.4 31.2 %collective-permute-start.65 = (bf16[256,1536]{1,0:T(8,128)(2,1)}, bf16[256,1536]{1,0:T(8,128)(2,1)}, u32[]{:S(2)}, u32[]{:S(2)}) collective-permute-start(bf16[256,1536]{1,0:T(8,128)(2,1)} %fusion.5), channel_id=1, source_target_pairs={{0,8},{8,16},{16,24},{24,28},{28,20},{20,12},{12,4},{4,0},{1,9},{9... | collective-permute-start | bytes 2359304 | tf_op jit(solution)/shard_map/ppermute | solution.py:645
  359.2 126.8 %collective-permute-start.26 = (f32[256,2048]{1,0:T(8,128)}, f32[256,2048]{1,0:T(8,128)}, u32[]{:S(2)}, u32[]{:S(2)}) collective-permute-start(f32[256,2048]{1,0:T(8,128)} %copy-done.23), channel_id=1, source_target_pairs={{0,1},{1,0},{2,3},{3,2},{4,5},{5,4},{6,7},{7,6},{8,9},{9,8},{10,11... | collective-permute-start | bytes 6291464 | tf_op jit(solution)/shard_map/ppermute | solution.py:674
  362.9 36.0 %collective-permute-start.55 = (bf16[256,704]{0,1:T(8,128)(2,1)}, bf16[256,704]{0,1:T(8,128)(2,1)}, u32[]{:S(2)}, u32[]{:S(2)}) collective-permute-start(bf16[256,704]{0,1:T(8,128)(2,1)} %convolution_convert_fusion.8), channel_id=1, source_target_pairs={{0,8},{8,16},{16,24},{24,28},{28,20},{20,12},{12,4},{4,0},{1,9},{9... | collective-permute-start | bytes 1081352 | tf_op jit(solution)/shard_map/ppermute | solution.py:645
  364.5 38.4 %collective-permute-start.59 = (bf16[256,704]{0,1:T(8,128)(2,1)}, bf16[256,704]{0,1:T(8,128)(2,1)}, u32[]{:S(2)}, u32[]{:S(2)}) collective-permute-start(bf16[256,704]{0,1:T(8,128)(2,1)} %convolution_convert_fusion.7), channel_id=1, source_target_pairs={{8,0},{16,8},{24,16},{28,24},{20,28},{12,20},{4,12},{0,4},{9,1},{1... | collective-permute-start | bytes 1081352 | tf_op jit(solution)/shard_map/ppermute | solution.py:645
  368.3 39.5 %collective-permute-start.48 = (bf16[256,704]{0,1:T(8,128)(2,1)}, bf16[256,704]{0,1:T(8,128)(2,1)}, u32[]{:S(2)}, u32[]{:S(2)}) collective-permute-start(bf16[256,704]{0,1:T(8,128)(2,1)} %convolution_convert_fusion.10), channel_id=1, source_target_pairs={{0,8},{8,16},{16,24},{24,28},{28,20},{20,12},{12,4},{4,0},{1,9},{9... | collective-permute-start | bytes 1081352 | tf_op jit(solution)/shard_map/ppermute | solution.py:645
  386.5 22.8 %collective-permute-start.52 = (bf16[256,704]{0,1:T(8,128)(2,1)}, bf16[256,704]{0,1:T(8,128)(2,1)}, u32[]{:S(2)}, u32[]{:S(2)}) collective-permute-start(bf16[256,704]{0,1:T(8,128)(2,1)} %convolution_convert_fusion.9), channel_id=1, source_target_pairs={{8,0},{16,8},{24,16},{28,24},{20,28},{12,20},{4,12},{0,4},{9,1},{1... | collective-permute-start | bytes 1081352 | tf_op jit(solution)/shard_map/ppermute | solution.py:645
  407.9 67.8 %collective-permute-start.30 = (bf16[8,256,256]{2,1,0:T(8,128)(2,1)S(1)}, bf16[8,256,256]{2,1,0:T(8,128)(2,1)}, u32[]{:S(2)}, u32[]{:S(2)}) collective-permute-start(bf16[8,256,256]{2,1,0:T(8,128)(2,1)S(1)} %copy-done.82), channel_id=1, source_target_pairs={{0,1},{1,0},{2,3},{3,2},{4,5},{5,4},{6,7},{7,6},{8,9},{9,8},{10,11... | collective-permute-start | bytes 3145736 | tf_op jit(solution)/shard_map/ppermute | solution.py:666
  440.0 66.3 %collective-permute-start.57 = (bf16[256,704]{0,1:T(8,128)(2,1)}, bf16[256,704]{0,1:T(8,128)(2,1)}, u32[]{:S(2)}, u32[]{:S(2)}) collective-permute-start(bf16[256,704]{0,1:T(8,128)(2,1)} %fusion.37), channel_id=1, source_target_pairs={{0,8},{8,16},{16,24},{24,28},{28,20},{20,12},{12,4},{4,0},{1,9},{9... | collective-permute-start | bytes 1081352 | tf_op jit(solution)/shard_map/ppermute | solution.py:645
  445.7 79.5 %collective-permute-start.61 = (bf16[256,704]{0,1:T(8,128)(2,1)}, bf16[256,704]{0,1:T(8,128)(2,1)}, u32[]{:S(2)}, u32[]{:S(2)}) collective-permute-start(bf16[256,704]{0,1:T(8,128)(2,1)} %fusion.39), channel_id=1, source_target_pairs={{8,0},{16,8},{24,16},{28,24},{20,28},{12,20},{4,12},{0,4},{9,1},{1... | collective-permute-start | bytes 1081352 | tf_op jit(solution)/shard_map/ppermute | solution.py:645
  447.8 62.9 %collective-permute-start.50 = (bf16[256,704]{0,1:T(8,128)(2,1)}, bf16[256,704]{0,1:T(8,128)(2,1)}, u32[]{:S(2)}, u32[]{:S(2)}) collective-permute-start(bf16[256,704]{0,1:T(8,128)(2,1)} %fusion.32), channel_id=1, source_target_pairs={{0,8},{8,16},{16,24},{24,28},{28,20},{20,12},{12,4},{4,0},{1,9},{9... | collective-permute-start | bytes 1081352 | tf_op jit(solution)/shard_map/ppermute | solution.py:645
  477.9 25.3 %collective-permute-start.31 = (bf16[8,256,256]{2,1,0:T(8,128)(2,1)S(1)}, bf16[8,256,256]{2,1,0:T(8,128)(2,1)}, u32[]{:S(2)}, u32[]{:S(2)}) collective-permute-start(bf16[8,256,256]{2,1,0:T(8,128)(2,1)S(1)} %add_convert_fusion.pair), channel_id=1, source_target_pairs={{0,2},{1,3},{2,0},{3,1},{4,6},{5,7},{6,4},{7,5},{8,10},{9,11},{10,... | collective-permute-start | bytes 3145736 | tf_op jit(solution)/shard_map/ppermute | solution.py:668
  486.0 51.1 %collective-permute-start.54 = (bf16[256,704]{0,1:T(8,128)(2,1)}, bf16[256,704]{0,1:T(8,128)(2,1)S(1)}, u32[]{:S(2)}, u32[]{:S(2)}) collective-permute-start(bf16[256,704]{0,1:T(8,128)(2,1)} %fusion.34), channel_id=1, source_target_pairs={{8,0},{16,8},{24,16},{28,24},{20,28},{12,20},{4,12},{0,4},{9,1},{1... | collective-permute-start | bytes 1081352 | tf_op jit(solution)/shard_map/ppermute | solution.py:645
  520.4 26.7 %collective-permute-start.32 = (f32[256,2048]{1,0:T(8,128)S(1)}, f32[256,2048]{1,0:T(8,128)S(1)}, u32[]{:S(2)}, u32[]{:S(2)}) collective-permute-start(f32[256,2048]{1,0:T(8,128)S(1)} %get-tuple-element.86), channel_id=1, source_target_pairs={{0,1},{1,0},{2,3},{3,2},{4,5},{5,4},{6,7},{7,6},{8,9},{9,8},{10,11... | collective-permute-start | bytes 6291464 | tf_op jit(solution)/shard_map/ppermute | solution.py:674
  (150 other events, 2378.7 us)
Sparse Core Ops, SparseCore 0:
  359.3 115.6 all-reduce.3

commit v2 on v1

v2 whole, which is shorter than its diff:
```python
import jax
import jax.numpy as jnp
from jax import lax
from jax.experimental import pallas as pl
from jax.experimental.pallas import tpu as pltpu
from jax.sharding import PartitionSpec as P

EPSILON = 1e-06
DECAY_SCALE = 8.0
GELU_A = 0.7978845608028654
GELU_B = 0.044715
BF16 = jnp.bfloat16
F32 = jnp.float32
STEP = 16
HALF = 8
SUMS = 8
TN = (((0,), (0,)), ((), ()))
NT = (((1,), (1,)), ((), ()))


def gelu(v):
    return 0.5 * v * (1.0 + jnp.tanh(GELU_A * (v + GELU_B * v * v * v)))


def gelu_both(v):
    squared = v * v
    bent = jnp.tanh(GELU_A * v * (1.0 + GELU_B * squared))
    value = 0.5 * v * (1.0 + bent)
    slope = 0.5 * (1.0 + bent) + 0.5 * v * (1.0 - bent * bent) * GELU_A * (
        1.0 + 3.0 * GELU_B * squared
    )
    return value, slope


def negative_expm1(z, exp_z):
    series = 1.0 + z * (1.0 / 7.0)
    for k in (6.0, 5.0, 4.0, 3.0, 2.0):
        series = 1.0 + z * (1.0 / k) * series
    return jnp.where(z > -0.25, -z * series, 1.0 - exp_z)


def rows_of(shape):
    return lax.broadcasted_iota(jnp.int32, shape, 0)


def earlier(now, before, k, rows):
    return jnp.where(rows < k, pltpu.roll(before, k, 0), pltpu.roll(now, k, 0))


def later(now, after, k, rows):
    size = now.shape[0]
    return jnp.where(
        rows >= size - k, pltpu.roll(after, size - k, 0), pltpu.roll(now, size - k, 0)
    )


def shaped(shape, dtype):
    return jax.ShapeDtypeStruct(shape, dtype)


def launch(
    kernel, inputs, out_shape, name, scalars=0, after=(), mib=20, scratch=(), aliases=None, grid=None, flops=1
):
    count, extra = len(inputs), len(after)
    waits = [pl.BlockSpec(memory_space=pl.ANY)] * extra
    in_specs = [pl.BlockSpec(memory_space=pltpu.SMEM)] * scalars
    more = {}
    if grid is None:
        in_specs += [pl.BlockSpec(memory_space=pltpu.VMEM)] * (count - scalars)
    else:
        in_specs += grid[1]
        more = {"grid": grid[0], "out_specs": grid[2]}
    return pl.pallas_call(
        lambda *refs: kernel(*refs[:count], *refs[count + extra :]),
        in_specs=in_specs + waits,
        out_shape=out_shape,
        scratch_shapes=list(scratch),
        input_output_aliases=aliases or {},
        compiler_params=pltpu.CompilerParams(vmem_limit_bytes=mib << 20),
        cost_estimate=pl.CostEstimate(flops=flops, bytes_accessed=1, transcendentals=0),
        name=name,
        **more,
    )(*inputs, *after)


def in_hbm(array):
    return pltpu.with_memory_space_constraint(array, pltpu.HBM)


def mixer_forward_kernel(
    seqs, count, bx, by, lines, blocks_i, blocks_r, p_o, cx_o, lx_o, lr_o, h_o
):
    total, width = bx.shape
    length = total // seqs
    steps = length // STEP
    rows16 = rows_of((STEP, width))
    w = [jnp.broadcast_to(lines[k : k + 1, :], (STEP, width)) for k in range(count)]
    shift = jnp.broadcast_to(lines[count : count + 1, :], (STEP, width))
    bias_i, bias_r = lines[count + 1 : count + 2, :], lines[count + 2 : count + 3, :]
    soft = lines[count + 3 : count + 4, :]
    for seq in range(seqs):

        def conv(i, before):
            at = pl.ds(pl.multiple_of(seq * length + i * STEP, STEP), STEP)
            now = bx[at, :]
            mixed = shift + w[0] * now
            for k in range(1, count):
                mixed = mixed + w[k] * earlier(now, before, k, rows16)
            cx_o[at, :] = mixed.astype(BF16)
            return now

        lax.fori_loop(0, steps, conv, jnp.zeros((STEP, width), F32))
    lx_o[...] = lax.dot_general(cx_o[...], blocks_i[...], NT, preferred_element_type=F32) + bias_i
    lr_o[...] = lax.dot_general(cx_o[...], blocks_r[...], NT, preferred_element_type=F32) + bias_r
    rows8 = rows_of((HALF, width))
    soft8 = jnp.broadcast_to(-DECAY_SCALE * soft, (HALF, width))

    def scan(i, carries):
        out = []
        for seq in range(seqs):
            carry = carries[seq]
            base = seq * length + i * STEP
            at = pl.ds(pl.multiple_of(base, STEP), STEP)
            cx16 = cx_o[at, :].astype(F32)
            products = []
            for part in range(STEP // HALF):
                here = pl.ds(pl.multiple_of(base + part * HALF, HALF), HALF)
                cx = cx16[part * HALF : (part + 1) * HALF, :]
                ix = jax.nn.sigmoid(lx_o[here, :])
                la = soft8 * jax.nn.sigmoid(lr_o[here, :])
                a = jnp.exp(la)
                rest = negative_expm1(2.0 * la, a * a)
                m = jnp.where(rest > 0.0, rest * lax.rsqrt(rest), 0.0)
                u = m * ix * cx
                for s in (1, 2, 4):
                    keep = rows8 >= s
                    u = u + jnp.where(keep, a * pltpu.roll(u, s, 0), 0.0)
                    a = jnp.where(keep, a * pltpu.roll(a, s, 0), a)
                h = u + a * carry
                carry = jnp.broadcast_to(h[HALF - 1 : HALF, :], (HALF, width))
                h_o[here, :] = h
                products.append(h * gelu(by[here, :]))
            p_o[at, :] = jnp.concatenate(products, 0).astype(BF16)
            out.append(carry)
        return tuple(out)

    lax.fori_loop(0, steps, scan, tuple(jnp.zeros((HALF, width), F32) for _ in range(seqs)))


def mixer_forward(seqs, count, bx, by, lines, blocks_i, blocks_r):
    low, full = shaped(bx.shape, BF16), shaped(bx.shape, F32)
    return launch(
        lambda *refs: mixer_forward_kernel(seqs, count, *refs),
        (bx, by, lines, blocks_i, blocks_r),
        (low, low, full, full, full),
        "mixer_forward",
    )


def mixer_backward_kernel(seqs, head, count, split, dhr, *refs):
    ring_size = dhr.shape[0]
    second = refs[:ring_size]
    bx, by, cx_i, lx_i, lr_i, h_i, lines, blocks_i, blocks_r = refs[ring_size : ring_size + 9]
    dbx_o, dby_o, small_o, dlx_o, dlr_o, dcx_s, dp = refs[ring_size + 9 :]
    skip = bx.shape[1] - split
    soft, gate_soft = lines[count + 3 : count + 4, :], lines[count + 4 : count + 5, :]
    for o in range(ring_size):
        part = lax.dot_general(dhr[o], second[o][skip:, :], NT, preferred_element_type=F32)
        dp[...] = part if o == 0 else dp[...] + part
    total, width = bx.shape
    length = total // seqs
    steps = length // STEP
    rows8 = rows_of((HALF, width))
    soft8 = jnp.broadcast_to(-DECAY_SCALE * soft, (HALF, width))
    zero = jnp.zeros((HALF, width), F32)

    def scan(j, state):
        i = steps - 1 - j
        sums_i, sums_r, sums_d = state[0]
        out = []
        for seq in range(seqs):
            a_after, e_after = state[1][seq]
            base = seq * length + i * STEP
            at = pl.ds(pl.multiple_of(base, STEP), STEP)
            cx16 = cx_i[at, :].astype(F32)
            dby_parts, dlx_parts, dlr_parts = [None, None], [None, None], [None, None]
            for part in (1, 0):
                start = base + part * HALF
                here = pl.ds(pl.multiple_of(start, HALF), HALF)
                cx = cx16[part * HALF : (part + 1) * HALF, :]
                ix = jax.nn.sigmoid(lx_i[here, :])
                ra = jax.nn.sigmoid(lr_i[here, :])
                la = soft8 * ra
                a = jnp.exp(la)
                rest = negative_expm1(2.0 * la, a * a)
                inverse = lax.rsqrt(rest)
                m = rest * inverse
                h = h_i[here, :]
                first = (i == 0) if part == 0 else False
                back = jnp.maximum(start - HALF, 0)
                before = h_i[pl.ds(pl.multiple_of(back, HALF), HALF), :]
                if part == 0:
                    before = jnp.where(i == 0, 0.0, before)
                h_prev = earlier(h, before, 1, rows8)
                gy, slope = gelu_both(by[here, :])
                grad = dp[here, :]
                dby_parts[part] = grad * h * slope
                e = grad * gy
                f = later(a, a_after, 1, rows8)
                for s in (1, 2, 4):
                    keep = rows8 < HALF - s
                    e = e + jnp.where(keep, f * pltpu.roll(e, HALF - s, 0), 0.0)
                    f = jnp.where(keep, f * pltpu.roll(f, HALF - s, 0), f)
                e = e + f * e_after
                e_after = jnp.broadcast_to(e[0:1, :], (HALF, width))
                a_after = a
                eix = e * ix
                dla = (e * h_prev - eix * cx * a * inverse) * a
                dlx = eix * m * cx * (1.0 - ix)
                dlr = dla * la * (1.0 - ra)
                sums_i = sums_i + dlx
                sums_r = sums_r + dlr
                sums_d = sums_d + dla * ra
                dlx_parts[part], dlr_parts[part] = dlx, dlr
                dcx_s[here, :] = eix * m
            dby_o[at, :] = jnp.concatenate(dby_parts, 0).astype(BF16)
            dlx_o[at, :] = jnp.concatenate(dlx_parts, 0).astype(BF16)
            dlr_o[at, :] = jnp.concatenate(dlr_parts, 0).astype(BF16)
            out.append((a_after, e_after))
        return (sums_i, sums_r, sums_d), tuple(out)

    (sums_i, sums_r, sums_d), _ = lax.fori_loop(
        0, steps, scan, ((zero, zero, zero), tuple((zero, zero) for _ in range(seqs)))
    )
    dcx_s[...] += jnp.dot(dlx_o[...], blocks_i[...], preferred_element_type=F32) + jnp.dot(
        dlr_o[...], blocks_r[...], preferred_element_type=F32
    )
    rows16 = rows_of((STEP, width))
    w = [jnp.broadcast_to(lines[k : k + 1, :], (STEP, width)) for k in range(count)]
    zero16 = jnp.zeros((STEP, width), F32)
    sums_t = tuple(zero16 for _ in range(count))
    sums_b = zero16
    for seq in range(seqs):

        def conv(j, state):
            after, tap_sums, shift_sum = state
            at = pl.ds(pl.multiple_of(seq * length + (steps - 1 - j) * STEP, STEP), STEP)
            now = dcx_s[at, :]
            source = bx[at, :]
            grad = w[0] * now
            new_sums = [tap_sums[0] + now * source]
            for k in range(1, count):
                moved = later(now, after, k, rows16)
                grad = grad + w[k] * moved
                new_sums.append(tap_sums[k] + moved * source)
            dbx_o[at, :] = grad.astype(BF16)
            return now, tuple(new_sums), shift_sum + now

        _, sums_t, sums_b = lax.fori_loop(0, steps, conv, (zero16, sums_t, sums_b))
    rows = [jnp.sum(item, 0, keepdims=True) for item in (*sums_t, sums_b, sums_i, sums_r)]
    rows.append(DECAY_SCALE * gate_soft * jnp.sum(sums_d, 0, keepdims=True))
    spare = small_o.shape[0] - 2 * head - SUMS
    if spare:
        rows.append(jnp.zeros((spare, width), F32))
    small_o[2 * head :, :] = jnp.concatenate(rows, 0).astype(BF16)
    lanes = lax.broadcasted_iota(jnp.int32, (head, width), 1)
    for gate, grads in enumerate((dlx_o, dlr_o)):
        whole = lax.dot_general(grads[...], cx_i[...], TN, preferred_element_type=F32)
        picked = whole[:head]
        for i in range(1, width // head):
            picked = jnp.where(lanes < i * head, picked, whole[i * head : (i + 1) * head])
        small_o[gate * head : (gate + 1) * head, :] = picked.astype(BF16)


def mixer_backward(seqs, head, count, split, small_rows, dhr, second, saved, after):
    total, width = saved[0].shape
    low = shaped((total, width), BF16)
    return launch(
        lambda *refs: mixer_backward_kernel(seqs, head, count, split, *refs),
        (dhr, *second, *saved),
        (low, low, shaped((small_rows, width), BF16)),
        "mixer_backward",
        after=after,
        mib=32,
        scratch=[
            pltpu.VMEM((total, width), BF16),
            pltpu.VMEM((total, width), BF16),
            pltpu.VMEM((total, width), F32),
            pltpu.VMEM((total, width), F32),
        ],
    )


def prepare_kernel(scalars, slots, tokens, cotangent, gate_i, gate_r, x_o, g_o, flat_o, r_o, blocks_i, blocks_r):
    ring_size, total, block = x_o.shape
    half = total // 2
    row_count = (scalars.shape[0] - 1) // 2
    length = half // row_count
    rows = lax.broadcasted_iota(jnp.int32, (length, block), 0)
    for place in range(2):
        sub = scalars[0] if place == 0 else 1 - scalars[0]
        for row in range(row_count):
            at = slice(place * half + row * length, place * half + (row + 1) * length)
            source = pl.ds(row * length, length)
            valid = jnp.where(rows < scalars[1 + sub * row_count + row], 1.0, 0.0)
            squares = jnp.zeros((length, block), F32)
            for k in range(ring_size):
                columns = slice(k * block, (k + 1) * block)
                piece = tokens[sub, source, columns]
                wide = piece.astype(F32)
                squares = squares + wide * wide
                x_o[slots[k], at, :] = piece
                masked = (cotangent[sub, source, columns].astype(F32) * valid).astype(BF16)
                g_o[slots[k], at, :] = masked
                flat_o[at, columns] = masked
            mean = jnp.sum(squares, 1, keepdims=True) * (1.0 / (ring_size * block))
            r_o[at, :] = lax.rsqrt(mean + EPSILON)
    head, width = gate_i.shape
    lanes = lax.broadcasted_iota(jnp.int32, (head, width), 1)
    for source, out in ((gate_i, blocks_i), (gate_r, blocks_r)):
        wide = source[...].astype(F32)
        for i in range(width // head):
            inside = (lanes >= i * head) & (lanes < (i + 1) * head)
            out[i * head : (i + 1) * head, :] = jnp.where(inside, wide, 0.0).astype(BF16)


def prepare(scalars, slots, tokens, cotangent, gate_i, gate_r, after):
    subs, half, model = tokens.shape
    total, ring_size, width = subs * half, slots.shape[0], gate_i.shape[1]
    rel = shaped((ring_size, total, model // ring_size), BF16)
    blocks = shaped((width, width), BF16)
    return launch(
        prepare_kernel,
        (scalars, slots, tokens, cotangent, gate_i, gate_r),
        (rel, rel, shaped((total, model), BF16), shaped((total, 1), F32), blocks, blocks),
        "prepare",
        scalars=2,
        after=after,
    )


def project_kernel(offsets, first, width, split, x, r1, *refs):
    count = len(offsets)
    one, two = refs[:count], refs[count : 2 * count]
    rest = refs[2 * count :]
    if not first:
        before = rest[:2]
        rest = rest[2:]
    bx, by, n1_o = rest
    scale = r1[...]
    for i, o in enumerate(offsets):
        gain = one[i][width : width + 16, :].astype(F32)[0:1, :]
        n1 = (x[o].astype(F32) * scale * gain).astype(BF16)
        n1_o[i] = n1
        for out, place, columns, weight in (
            (bx, 0, slice(0, width), one[i][:width, :]),
            (by, 1, slice(0, split), one[i][width + 16 :, :]),
            (by, 1, slice(split, width), two[i][: width - split, :]),
        ):
            part = lax.dot_general(n1, weight, NT, preferred_element_type=F32)
            if i > 0:
                out[:, columns] += part
            elif first:
                out[:, columns] = part
            else:
                out[:, columns] = before[place][:, columns] + part


def project(offsets, x, r1, one, two, before, width, split):
    total, block = x.shape[1:]
    count = len(offsets)
    full = shaped((total, width), F32)
    at = 2 + 2 * count
    return launch(
        lambda *refs: project_kernel(offsets, before is None, width, split, *refs),
        (x, r1, *one, *two, *(before or ())),
        (full, full, shaped((count, total, block), BF16)),
        "project",
        aliases={} if before is None else {at: 0, at + 1: 1},
    )


def mixer_out_kernel(skip, p, *refs):
    own_o, other_o, gains_o = refs[-3:]
    count, half = own_o.shape[:2]
    width = p.shape[1]
    for o in range(count):
        part = jnp.dot(p[...], refs[count + o][skip:, :], preferred_element_type=F32)
        own_o[o] = part[:half]
        other_o[o] = part[half:].astype(BF16)
        gains_o[o] = refs[o][width : width + 16, :].astype(F32)[0:2, :]


def mixer_out(p, one, two, split):
    total, width = p.shape
    count, block = len(one), one[0].shape[1]
    shape = (count, total // 2, block)
    return launch(
        lambda *refs: mixer_out_kernel(width - split, *refs),
        (p, *one, *two),
        (shaped(shape, F32), shaped(shape, BF16), shaped((count, 2, block), F32)),
        "mixer_out",
        mib=24,
    )


def input_out_kernel(split, dbx, dby, *refs):
    own_o, other_o = refs[-2:]
    count, half = own_o.shape[:2]
    width = dbx.shape[1]
    for o in range(count):
        one, two = refs[o], refs[count + o]
        part = (
            jnp.dot(dbx[...], one[:width, :], preferred_element_type=F32)
            + jnp.dot(dby[:, :split], one[width + 16 :, :], preferred_element_type=F32)
            + jnp.dot(dby[:, split:], two[: width - split, :], preferred_element_type=F32)
        )
        own_o[o] = part[:half]
        other_o[o] = part[half:].astype(BF16)


def input_out(dbx, dby, one, two, split, after):
    shape = (len(one), dbx.shape[0] // 2, one[0].shape[1])
    return launch(
        lambda *refs: input_out_kernel(split, *refs),
        (dbx, dby, *one, *two),
        (shaped(shape, F32), shaped(shape, BF16)),
        "input_out",
        after=after,
        mib=24,
    )


def pair_kernel(own, got, out):
    out[...] = (own[...] + got[...].astype(F32)).astype(BF16)


def pair_sum(own, got, after):
    return launch(pair_kernel, (own, got), shaped(own.shape, BF16), "pair_sum", after=after)


def norm_kernel(slots, x, gains, pair, other, h_o, n_o, r_o):
    ring_size, half, block = h_o.shape
    squares = jnp.zeros((half, block), F32)
    for o in range(ring_size):
        h = x[o, 0:half, :].astype(F32) + (pair[o].astype(F32) + other[o].astype(F32))
        h_o[o] = h
        squares = squares + h * h
    mean = jnp.sum(squares, 1, keepdims=True) * (1.0 / (ring_size * block))
    scale = lax.rsqrt(mean + EPSILON)
    r_o[...] = scale
    for k in range(ring_size):
        o = slots[k]
        n_o[:, k * block : (k + 1) * block] = (h_o[o] * scale * gains[o, 1:2, :]).astype(BF16)


def norm(slots, x, gains, pair, other, after):
    ring_size, half, block = pair.shape
    return launch(
        norm_kernel,
        (slots, x, gains, pair, other),
        (shaped(pair.shape, F32), shaped((half, ring_size * block), BF16), shaped((half, 1), F32)),
        "norm",
        scalars=1,
        after=after,
    )


def norm_back_kernel(pair, other, h1, r2, gains, g, dh_o, dhr_o, grad_o):
    ring_size, half, block = h1.shape
    dots = jnp.zeros((half, block), F32)
    scale = r2[...]
    for o in range(ring_size):
        product = (pair[o].astype(F32) + other[o].astype(F32)) * h1[o]
        dots = dots + product * gains[o, 1:2, :]
        grad_o[o] = jnp.sum(product * scale, 0, keepdims=True)
    mean = jnp.sum(dots, 1, keepdims=True) * (1.0 / (ring_size * block))
    bend = scale * scale * scale * mean
    for o in range(ring_size):
        grad = pair[o].astype(F32) + other[o].astype(F32)
        dh = g[o, 0:half, :].astype(F32) + scale * (grad * gains[o, 1:2, :]) - h1[o] * bend
        dh_o[o] = dh
        dhr_o[o] = dh.astype(BF16)


def norm_back(pair, other, h1, r2, gains, g, after):
    ring_size, half, block = pair.shape
    return launch(
        norm_back_kernel,
        (pair, other, h1, r2, gains, g),
        (shaped(pair.shape, F32), shaped(pair.shape, BF16), shaped((ring_size, 1, block), F32)),
        "norm_back",
        after=after,
    )


def input_back_kernel(slots, pair, other, x, r1, gains, dh1, second, out_o, grad_o):
    ring_size, half, block = dh1.shape
    dots = jnp.zeros((half, block), F32)
    scale = r1[0:half, :]
    for o in range(ring_size):
        product = (pair[o].astype(F32) + other[o].astype(F32)) * x[o, 0:half, :].astype(F32)
        dots = dots + product * gains[o, 0:1, :]
        grad_o[o, 0:1, :] = jnp.sum(product * scale, 0, keepdims=True)
        grad_o[o, 1:2, :] = second[o]
    mean = jnp.sum(dots, 1, keepdims=True) * (1.0 / (ring_size * block))
    bend = scale * scale * scale * mean
    for k in range(ring_size):
        o = slots[k]
        grad = pair[o].astype(F32) + other[o].astype(F32)
        out_o[:, k * block : (k + 1) * block] = (
            dh1[o] + scale * (grad * gains[o, 0:1, :]) - x[o, 0:half, :].astype(F32) * bend
        )


def input_back(slots, pair, other, x, r1, gains, dh1, second, after):
    ring_size, half, block = pair.shape
    return launch(
        input_back_kernel,
        (slots, pair, other, x, r1, gains, dh1, second),
        (shaped((half, ring_size * block), F32), shaped((ring_size, 2, block), F32)),
        "input_back",
        scalars=1,
        after=after,
    )


def finish_kernel(slots, h1, pair, other, out_o):
    ring_size, half, block = h1.shape
    for k in range(ring_size):
        columns = slice(k * block, (k + 1) * block)
        out_o[:, columns] = h1[slots[k]] + (pair[:, columns].astype(F32) + other[:, columns].astype(F32))


def finish(slots, h1, pair, other, after):
    return launch(
        finish_kernel, (slots, h1, pair, other), shaped(pair.shape, F32), "finish", scalars=1, after=after
    )


def arrange_kernel(scalars, own, got, out):
    core = scalars[0]
    out[core] = own[...]
    out[1 - core] = got[...]


def arrange(scalars, own, got, after):
    return launch(
        arrange_kernel, (scalars, own, got), shaped((2, *own.shape), own.dtype), "arrange", scalars=1, after=after
    )


def unit_grad_kernel(g, down, dq_o):
    dq_o[...] = lax.dot_general(g[...], down[...], NT, preferred_element_type=F32)


def unit_grad(g, down, after):
    total, model = g.shape
    units = down.shape[0]
    tile = 256
    grid = (
        (units // tile,),
        [pl.BlockSpec((total, model), lambda i: (0, 0)), pl.BlockSpec((tile, model), lambda i: (i, 0))],
        pl.BlockSpec((total, tile), lambda i: (0, i)),
    )
    return launch(unit_grad_kernel, (g, in_hbm(down)), shaped((total, units), F32), "unit_grad", after=after, grid=grid)


def unit_kernel(slots, n2, gate, up, dq, q_o, dga_o, dup_o, rel_o):
    ring_size, total, block = rel_o.shape

    @pl.when(pl.program_id(0) == 0)
    def _():
        for k in range(ring_size):
            rel_o[slots[k]] = n2[:, k * block : (k + 1) * block]

    ga = jnp.dot(n2[...], gate[...], preferred_element_type=F32)
    upward = jnp.dot(n2[...], up[...], preferred_element_type=F32)
    value, slope = gelu_both(ga)
    grad = dq[...]
    q_o[...] = (value * upward).astype(BF16)
    dga_o[...] = (grad * upward * slope).astype(BF16)
    dup_o[...] = (grad * value).astype(BF16)


def unit_pass(slots, n2, gate, up, dq):
    total, model = n2.shape
    ring_size = slots.shape[0]
    units = gate.shape[1]
    tile = 256
    rel = (ring_size, total, model // ring_size)
    wide = pl.BlockSpec((total, tile), lambda i: (0, i))
    tall = pl.BlockSpec((model, tile), lambda i: (0, i))
    out = shaped((total, units), BF16)
    grid = (
        (units // tile,),
        [pl.BlockSpec((total, model), lambda i: (0, 0)), tall, tall, wide],
        [wide, wide, wide, pl.BlockSpec(rel, lambda i: (0, 0, 0))],
    )
    return launch(
        unit_kernel,
        (slots, n2, in_hbm(gate), in_hbm(up), dq),
        (out, out, out, shaped(rel, BF16)),
        "unit_pass",
        scalars=1,
        mib=28,
        grid=grid,
    )


def unit_out_kernel(q, down, own_o, other_o):
    half = own_o.shape[0]
    part = jnp.dot(q[...], down[...], preferred_element_type=F32)
    own_o[...] = part[:half]
    other_o[...] = part[half:].astype(BF16)


def unit_out(q, down, after):
    total, units = q.shape
    model = down.shape[1]
    half = total // 2
    tile = 256
    out = pl.BlockSpec((half, tile), lambda i: (0, i))
    grid = (
        (model // tile,),
        [pl.BlockSpec((total, units), lambda i: (0, 0)), pl.BlockSpec((units, tile), lambda i: (0, i))],
        [out, out],
    )
    return launch(
        unit_out_kernel,
        (q, in_hbm(down)),
        (shaped((half, model), F32), shaped((half, model), BF16)),
        "unit_out",
        after=after,
        grid=grid,
    )


def unit_back_kernel(owners, dga, dup, gate, up, *refs):
    own_o, other_o = refs[-2:]
    half = other_o.shape[1]
    part = lax.dot_general(dga[...], gate[...], NT, preferred_element_type=F32)
    part = part + lax.dot_general(dup[...], up[...], NT, preferred_element_type=F32)
    own_o[0] = part[:half]
    other_o[0] = part[half:].astype(BF16)


def unit_back(owners, dga, dup, gate, up, after):
    ring_size = owners.shape[0]
    total, units = dga.shape
    half = total // 2
    block = gate.shape[0] // ring_size
    left = pl.BlockSpec((total, units), lambda o, owners: (0, 0))
    weight = pl.BlockSpec((block, units), lambda o, owners: (owners[o], 0))
    out = pl.BlockSpec((1, half, block), lambda o, owners: (o, 0, 0))
    return pl.pallas_call(
        unit_back_kernel,
        grid_spec=pltpu.PrefetchScalarGridSpec(
            num_scalar_prefetch=1,
            grid=(ring_size,),
            in_specs=[left, left, weight, weight, *[pl.BlockSpec(memory_space=pl.ANY)] * len(after)],
            out_specs=[out, out],
        ),
        out_shape=(shaped((ring_size, half, block), F32), shaped((ring_size, half, block), BF16)),
        compiler_params=pltpu.CompilerParams(vmem_limit_bytes=24 << 20),
        cost_estimate=pl.CostEstimate(flops=1, bytes_accessed=1, transcendentals=0),
        name="unit_back",
    )(owners, dga, dup, in_hbm(gate), in_hbm(up), *after)


def unit_term_kernel(part, turns, fold, n2, g, right, q, *refs):
    units = right.shape[1]
    share = units // 2
    columns = slice(part * share, (part + 1) * share)
    rest = list(refs)
    outs = rest[len(rest) - len(turns) - (2 if fold else 0) :]
    for (o, has), out in zip(turns, outs):
        recv = rest.pop(0) if has else None
        grad = lax.dot_general(n2[o], right[...], TN, preferred_element_type=F32)
        down = lax.dot_general(g[o], q[:, columns], TN, preferred_element_type=F32)
        if recv is not None:
            grad = grad + recv[:, :units].astype(F32)
            down = down + recv[:, units:].astype(F32)
        out[:, :units] = grad.astype(BF16)
        out[:, units:] = down.astype(BF16)
    if fold:
        recv = rest.pop(0)
        grad_o, down_o = outs[len(turns) :]
        grad = lax.dot_general(n2[0], right[...], TN, preferred_element_type=F32)
        grad_o[...] = grad + recv[:, :units].astype(F32)
        down = lax.dot_general(q[:, columns], g[0], TN, preferred_element_type=F32)
        down_o[...] = down + recv[:, units:].astype(F32).T


def unit_term(part, n2, g, right, q, turns, fold, after):
    block, units = n2.shape[2], right.shape[1]
    arrived = [item for _, item in turns if item is not None] + ([] if fold is None else [fold])
    plan = [(o, item is not None) for o, item in turns]
    out = [shaped((block, units + units // 2), BF16) for _ in turns]
    if fold is not None:
        out += [shaped((block, units), F32), shaped((units // 2, block), F32)]
    return launch(
        lambda *refs: unit_term_kernel(part, plan, fold is not None, *refs),
        (n2, g, right, q, *arrived),
        tuple(out),
        "unit_term",
        after=after,
        mib=24,
        flops=10**9,
    )


def unit_end_kernel(grad, down, item, grad_o, down_o):
    units = grad.shape[1]
    grad_o[...] = grad[...] + item[:, :units].astype(F32)
    down_o[...] = down[...] + item[:, units:].astype(F32).T


def unit_end(own, item, after):
    grad, down = own
    return launch(
        unit_end_kernel,
        (grad, down, item),
        (shaped(grad.shape, F32), shaped(down.shape, F32)),
        "unit_end",
        after=after,
        flops=10**9,
    )


def small_pieces(width, block):
    return [slice(i, min(i + block, width)) for i in range(0, width, block)]


def mixer_term_kernel(part, places, groups, split, chunk, turns, fold, owners, *refs):
    n1_all = refs[:groups]
    dhr, grads, p = refs[groups : groups + 3]
    rest = list(refs[groups + 3 :])
    extra = rest.pop(0) if part == 0 else None
    outs = rest[len(rest) - len(turns) - (3 - part if fold else 0) :]
    width, block = grads.shape[1], dhr.shape[2]
    columns = slice(0, split) if part == 0 else slice(split, width)
    size = columns.stop - columns.start
    at = width + size
    pieces = small_pieces(width, block)

    def terms(o, recv):
        group, i = places[o]
        grad = lax.dot_general(grads[...], n1_all[group][i], TN, preferred_element_type=F32)
        out = lax.dot_general(p[:, columns], dhr[o], TN, preferred_element_type=F32)
        if recv is not None:
            grad = grad + recv[:width, :].astype(F32)
            out = out + recv[width:at, :].astype(F32)
        return grad, out

    def small(o, recv):
        own = extra[pl.ds(pl.multiple_of(owners[o] * chunk, 16), chunk), :].astype(F32)
        out = []
        for i, piece in enumerate(pieces):
            total = own[:, piece]
            if recv is not None:
                total = total + recv[at + i * chunk : at + (i + 1) * chunk, : piece.stop - piece.start].astype(F32)
            out.append(total)
        return out

    for (o, has), out_ref in zip(turns, outs):
        recv = rest.pop(0) if has else None
        grad, out = terms(o, recv)
        out_ref[:width, :] = grad.astype(BF16)
        out_ref[width:at, :] = out.astype(BF16)
        if part == 0:
            for i, total in enumerate(small(o, recv)):
                rows = slice(at + i * chunk, at + (i + 1) * chunk)
                wide = total.shape[1]
                out_ref[rows, :wide] = total.astype(BF16)
                if wide < block:
                    out_ref[rows, wide:] = jnp.zeros((chunk, block - wide), BF16)
    if fold:
        recv = rest.pop(0)
        outs[len(turns)][...], outs[len(turns) + 1][...] = terms(0, recv)
        if part == 0:
            for piece, total in zip(pieces, small(0, recv)):
                outs[len(turns) + 2][:, piece] = total


def mixer_term(part, places, split, chunk, owners, n1, dhr, grads, p, extra, turns, fold, after):
    block, width = dhr.shape[2], grads.shape[1]
    size = split if part == 0 else width - split
    arrived = [item for _, item in turns if item is not None] + ([] if fold is None else [fold])
    more = 0 if part == 1 else chunk * len(small_pieces(width, block))
    out = [shaped((width + size + more, block), BF16) for _ in turns]
    if fold is not None:
        out += [shaped((width, block), F32), shaped((size, block), F32)]
        out += [shaped((chunk, width), F32)] if part == 0 else []
    plan = [(o, item is not None) for o, item in turns]
    return launch(
        lambda *refs: mixer_term_kernel(part, places, len(n1), split, chunk, plan, fold is not None, *refs),
        (owners, *n1, dhr, grads, p, *([extra] if part == 0 else []), *arrived),
        tuple(out),
        "mixer_term",
        scalars=1,
        after=after,
        mib=24,
        flops=10**9,
    )


def mixer_end_kernel(part, *refs):
    own, item, outs = refs[: 3 - part], refs[3 - part], refs[4 - part :]
    width, block = own[0].shape
    at = width + own[1].shape[0]
    outs[0][...] = own[0][...] + item[:width, :].astype(F32)
    outs[1][...] = own[1][...] + item[width:at, :].astype(F32)
    if part == 0:
        chunk = own[2].shape[0]
        for i, piece in enumerate(small_pieces(width, block)):
            rows = slice(at + i * chunk, at + (i + 1) * chunk)
            total = own[2][:, piece] + item[rows, : piece.stop - piece.start].astype(F32)
            outs[2][:, piece] = total.astype(BF16)


def mixer_end(part, own, item, after):
    shapes = [shaped(own[0].shape, F32), shaped(own[1].shape, F32)]
    if part == 0:
        shapes.append(shaped(own[2].shape, BF16))
    return launch(
        lambda *refs: mixer_end_kernel(part, *refs), (*own, item), tuple(shapes), "mixer_end", after=after, flops=10**9
    )


def spread_kernel(head, owners, *refs):
    ring_size = owners.shape[0]
    gate_i, gate_r, sums, gain_o, whole = refs[ring_size:]
    block = gain_o.shape[1]
    chunk = refs[0].shape[0] - 2 * ring_size
    gain = jnp.zeros((2, block), F32)
    for o in range(ring_size):
        at = pl.ds(pl.multiple_of(owners[o] * chunk, 16), chunk)
        whole[at, :] = refs[o][:chunk, :].astype(F32)
        mine = 2 * ((ring_size - o) % ring_size)
        gain = gain + refs[o][chunk:, :block].astype(F32)[mine : mine + 2, :]
    gate_i[...] = whole[:head, :]
    gate_r[...] = whole[head : 2 * head, :]
    sums[...] = whole[2 * head : 2 * head + SUMS, :]
    gain_o[...] = gain


def spread(head, block, owners, chunks, after):
    ring_size = len(chunks)
    rows, width = chunks[0].shape
    gate = shaped((head, width), F32)
    return launch(
        lambda *refs: spread_kernel(head, *refs),
        (owners, *chunks),
        (gate, gate, shaped((SUMS, width), F32), shaped((2, block), F32)),
        "spread",
        scalars=1,
        after=after,
        scratch=[pltpu.VMEM(((rows - 2 * ring_size) * ring_size, width), F32)],
    )


def local(
    tokens,
    cotangent,
    row_length,
    first_gain,
    value_weight,
    gelu_weight,
    conv_weight,
    conv_bias,
    input_gate,
    input_bias,
    recur_gate,
    recur_bias,
    decay_param,
    output_weight,
    second_gain,
    mlp_gate,
    mlp_up,
    mlp_down,
):
    ring_size = lax.axis_size("dp")
    middle = ring_size // 2
    ring = [2 * i if i < middle else 2 * (ring_size - 1 - i) + 1 for i in range(ring_size)]
    onward = [(ring[i], ring[(i + 1) % ring_size]) for i in range(ring_size)]
    backward = [(b, a) for a, b in onward]
    me = lax.axis_index("dp")
    core = lax.axis_index("mp") % 2
    core_pair = [(i, i ^ 1) for i in range(4)]
    chip_pair = [(i, i ^ 2) for i in range(4)]
    index = jnp.arange(ring_size, dtype=jnp.int32)

    def spot_of(place):
        return jnp.where(place % 2 == 0, place // 2, ring_size - 1 - place // 2)

    spots = (spot_of(me) + index) % ring_size
    owners = jnp.where(spots < middle, 2 * spots, 2 * (ring_size - 1 - spots) + 1).astype(jnp.int32)
    slots = ((spot_of(index) - spot_of(me) + ring_size) % ring_size).astype(jnp.int32)

    subs, row_count, length, model = tokens.shape
    half = row_count * length
    seqs = subs * row_count
    block = model // ring_size
    width, head = input_gate.shape
    count = conv_weight.shape[0]
    split = (width // 2 + 127) // 128 * 128
    chunk = -(-(2 * head + SUMS) // (16 * ring_size)) * 16
    small_rows = chunk * ring_size

    def hops(long_way_on):
        return (middle, ring_size - 1 - middle) if long_way_on else (ring_size - 1 - middle, middle)

    token = []

    def mark(*values):
        token[:] = values

    class Gather:
        def __init__(self, shard, long_way_on):
            self.hops = hops(long_way_on)
            self.moving = [shard, shard]
            self.got = [shard] + [None] * (ring_size - 1)

        def step(self, s):
            for d, way in enumerate((onward, backward)):
                if s <= self.hops[d]:
                    self.moving[d] = lax.ppermute(self.moving[d], "dp", way)
                    self.got[ring_size - s if d == 0 else s] = self.moving[d]

    class Scatter:
        def __init__(self, term, end, long_way_on):
            self.term, self.ending = term, end
            self.hops = hops(long_way_on)
            self.moving = [None, None]
            self.own = None

        def step(self, s):
            turns, ways, fold = [], [], None
            for d in range(2):
                far = self.hops[d] - s
                if far > 0:
                    turns.append((far if d == 0 else ring_size - far, self.moving[d]))
                    ways.append(d)
                elif far == 0:
                    fold = self.moving[d]
            parts = self.term(turns, fold, tuple(token))
            if fold is not None:
                self.own = parts[len(turns) :]
            mark(parts[0])
            for d, part in zip(ways, parts):
                self.moving[d] = lax.ppermute(part, "dp", (onward, backward)[d])

        def end(self):
            last = 0 if self.hops[0] > self.hops[1] else 1
            out = self.ending(self.own, self.moving[last], tuple(token))
            mark(out[0])
            return out

    def core_swap(other):
        return lax.ppermute(other, "mp", core_pair)

    def chip_swap(own, got, after):
        pair = pair_sum(own, got, after)
        mark(pair)
        return pair, lax.ppermute(pair, "mp", chip_pair)

    def both_halves(own, dim):
        return jnp.concatenate([own, lax.ppermute(own, "mp", core_pair)], dim)

    scalars = jnp.concatenate([core[None], row_length.reshape(-1)]).astype(jnp.int32)
    gain_lines = jnp.pad(jnp.stack([first_gain, second_gain]), ((0, 14), (0, 0)))
    gelu_t = gelu_weight.T
    ring_one = Gather(jnp.concatenate([value_weight.T, gain_lines, gelu_t[:split]]), True)
    ring_two = Gather(jnp.concatenate([gelu_t[split:], output_weight]), False)
    ring_one.step(1)
    ring_two.step(1)

    decay_wide = decay_param.astype(F32)
    lines = jnp.concatenate(
        [
            conv_weight.astype(F32),
            jnp.stack(
                [
                    conv_bias.astype(F32),
                    input_bias.astype(F32),
                    recur_bias.astype(F32),
                    jax.nn.softplus(-decay_wide),
                    jax.nn.sigmoid(-decay_wide),
                ]
            ),
        ]
    )
    x, g, g_flat, r1, blocks_i, blocks_r = prepare(
        scalars,
        slots,
        tokens.reshape(subs, half, model),
        cotangent.reshape(subs, half, model),
        input_gate.T,
        recur_gate.T,
        (lines,),
    )
    x, *moved = lax.optimization_barrier((x, *ring_one.moving, *ring_two.moving))
    ring_one.moving, ring_two.moving = moved[:2], moved[2:]
    for s in range(2, middle + 1):
        ring_one.step(s)
        ring_two.step(s)
    one, two = ring_one.got, ring_two.got

    hop_groups = [[0, 1, ring_size - 1]] + [[s, ring_size - s] for s in range(2, middle)] + [[middle]]
    places, n1, sums_so_far = {}, [], None
    for place, offsets in enumerate(hop_groups):
        bx, by, n1_part = project(
            offsets, x, r1, [one[o] for o in offsets], [two[o] for o in offsets], sums_so_far, width, split
        )
        sums_so_far = (bx, by)
        n1.append(n1_part)
        places |= {o: (place, i) for i, o in enumerate(offsets)}

    p, cx, lx, lr, h = mixer_forward(seqs, count, bx, by, lines, blocks_i, blocks_r)
    own, other, gains = mixer_out(p, one, two, split)
    pair, other = chip_swap(own, core_swap(other), ())
    dq = unit_grad(g_flat, mlp_down, (pair,))
    h1, n2_own, r2 = norm(slots, x, gains, pair, other, (dq,))
    q, dga, dup, n2 = unit_pass(slots, both_halves(n2_own, 0), mlp_gate, mlp_up, dq)

    unit_a = Scatter(lambda *a: unit_term(0, n2, g, dga, q, *a), unit_end, True)
    unit_b = Scatter(lambda *a: unit_term(1, n2, g, dup, q, *a), unit_end, False)
    last = middle - 1

    def now():
        return tuple(token)

    unit_a.step(0)
    unit_b.step(0)
    own, other = unit_back(owners, dga, dup, mlp_gate, mlp_up, now())
    mark(own)
    got = core_swap(other)
    for s in range(1, max(last - 1, 1)):
        unit_a.step(s)
        if s == 1:
            pair, other = chip_swap(own, got, now())
        unit_b.step(s)
    unit_a.step(last - 1)
    dh1, dhr_own, second_grad = norm_back(pair, other, h1, r2, gains, g, now())
    mark(dhr_own)
    dhr = both_halves(dhr_own, 1)
    unit_b.step(last - 1)
    dbx, dby, small = mixer_backward(
        seqs, head, count, split, small_rows, dhr, two, (bx, by, cx, lx, lr, h, lines, blocks_i, blocks_r), now()
    )
    mark(dbx)
    out_own, out_other = unit_out(q, mlp_down, now())
    mark(out_own)
    out_got = core_swap(out_other)
    unit_a.step(last)
    layer_pair = pair_sum(out_own, out_got, now())
    mark(layer_pair)
    layer_other = lax.ppermute(layer_pair, "mp", chip_pair)
    own, other = input_out(dbx, dby, one, two, split, now())
    mark(own)
    got = core_swap(other)
    unit_b.step(last)
    pair, other = chip_swap(own, got, now())

    half_split = width // 2 // 128 * 128
    mixer_a = Scatter(
        lambda *a: mixer_term(0, places, half_split, chunk, owners, n1, dhr, dbx, p, small, *a),
        lambda *a: mixer_end(0, *a),
        True,
    )
    mixer_b = Scatter(
        lambda *a: mixer_term(1, places, half_split, chunk, owners, n1, dhr, dby, p, None, *a),
        lambda *a: mixer_end(1, *a),
        False,
    )
    mixer_a.step(0)
    gate_grad, down_low = unit_a.end()
    up_grad, down_high = unit_b.end()
    mixer_b.step(0)
    input_own, gain_grads = input_back(slots, pair, other, x, r1, gains, dh1, second_grad, now())
    mark(input_own)
    input_got = core_swap(input_own)
    for s in range(1, middle):
        mixer_a.step(s)
        mixer_b.step(s)
        if s == 1:
            input_grad = arrange(scalars, input_own, input_got, now())
            mark(input_grad)
        elif s == 2:
            layer_own = finish(slots, h1, layer_pair, layer_other, now())
            mark(layer_own)
            layer_got = core_swap(layer_own)
        elif s == 3:
            layer_out = arrange(scalars, layer_own, layer_got, now())
            mark(layer_out)
    value_grad, output_low, small = mixer_a.end()
    gain_grads = gain_grads + core_swap(gain_grads)
    gain_rows = jnp.pad(gain_grads.reshape(2 * ring_size, block), ((0, 0), (0, width - block)))
    small_ring = Gather(jnp.concatenate([small, gain_rows.astype(BF16)]), True)
    for s in range(1, middle + 1):
        small_ring.step(s)
    gelu_grad, output_high = mixer_b.end()
    output_grad = jnp.concatenate([output_low, output_high], 0)
    down_grad = jnp.concatenate([down_low, down_high], 0)
    down_grad = jnp.concatenate([down_low, down_high], 0)
    gate_i, gate_r, sums, gain_grads = spread(head, block, owners, small_ring.got, now())

    return (
        layer_out.reshape(tokens.shape),
        input_grad.reshape(tokens.shape),
        gain_grads[0],
        value_grad.T,
        gelu_grad.T,
        sums[:count],
        sums[count],
        gate_i.T,
        sums[count + 1],
        gate_r.T,
        sums[count + 2],
        sums[count + 3],
        output_grad,
        gain_grads[1],
        gate_grad,
        up_grad,
        down_grad,
    )


def solution(mesh):
    placed = (
        P(None, "dp", None, None),
        P(None, "dp", None, None),
        P(None, "dp"),
        P("dp"),
        P("dp", "mp"),
        P("dp", "mp"),
        P(None, "mp"),
        P("mp"),
        P("mp", None),
        P("mp"),
        P("mp", None),
        P("mp"),
        P("mp"),
        P("mp", "dp"),
        P("dp"),
        P(None, "mp"),
        P(None, "mp"),
        P("mp", None),
    )
    return jax.shard_map(
        local,
        mesh=mesh,
        in_specs=placed,
        out_specs=(
            P(None, "dp", None, None),
            P(None, "dp", None, None),
            P("dp"),
            P("dp", "mp"),
            P("dp", "mp"),
            P(None, "mp"),
            P("mp"),
            P("mp", None),
            P("mp"),
            P("mp", None),
            P("mp"),
            P("mp"),
            P("mp", "dp"),
            P("dp"),
            P("dp", "mp"),
            P("dp", "mp"),
            P("mp", "dp"),
        ),
        check_vma=False,
    )
```

time: 565 us -> 488 us (0.86)
  matrix products: 83.9 us -> 0 us
  Pallas kernels: 70.2 us -> 125 us
  starting transfers between devices: 101 us -> 59.9 us
  waiting for transfers between devices: 226 us -> 261 us
  local copies, waits for them, and re-layouts: 45.9 us -> 28.9 us
  between operations: 16.1 us -> 2.42 us
  other arithmetic: 13.9 us -> 3.55 us
    dot_general x51 -> x0, matrix products: 83.9 us -> none  [the longest x48 70.5 us: outer(): return jnp.einsum('tb,tf->bf', left, right, preferred_element_type=F32)]
    ppermute x83 -> x62, waiting for transfers between devices: 201 us -> 261 us  [the longest x28 170 us: step(): self.moving[d] = lax.ppermute(part, 'dp', (onward, backward)[d])]
    pallas_call x12 -> x43, Pallas kernels: 59.9 us -> 114 us  [launch(): pl.pallas_call(lambda *refs: kernel(*refs[:count], *refs[count + extra:])...]
    ppermute x83 -> x62, starting transfers between devices: 101 us -> 59.9 us  [the longest x28 30.5 us: step(): self.moving[d] = lax.ppermute(part, 'dp', (onward, backward)[d])]
    psum x1 -> x0, waiting for transfers between devices: 24.4 us -> none  [local(): gate_i, gate_r = lax.psum((gate_i, gate_r), 'dp')]
    another operation x4 -> x7, local copies, waits for them, and re-layouts: 8.8 us -> 1.34 us  [the longest x2 1.32 us: local(): jnp.stack([first_gain, second_gain])]
    unnamed x236 -> x187, local copies, waits for them, and re-layouts: 30.7 us -> 23.6 us
  transfers between devices with their start and end apart: 84 -> 62, of which waited for: 38 -> 38; matrix products, arithmetic and copies ran while one was open for 20% -> 1% of each run, Pallas kernels for 10% -> 20%
where the time goes in v2:
time: 488 us; the launch traced here: 481 us
  waiting for transfers between devices  261 us (53%)
  Pallas kernels  125 us (26%)
  starting transfers between devices  59.9 us (12%)
  local copies, waits for them, and re-layouts  28.9 us (6%)
    ppermute x28, waiting for transfers between devices, step(): self.moving[d] = lax.ppermute(part, 'dp', (onward, backward)[d])  170 us
    pallas_call x43, Pallas kernels, launch(): pl.pallas_call(lambda *refs: kernel(*refs[:count], *refs[count + extra:])...  114 us
    ppermute x21, waiting for transfers between devices, step(): self.moving[d] = lax.ppermute(self.moving[d], 'dp', way)  69.3 us
    ppermute x28, starting transfers between devices, step(): self.moving[d] = lax.ppermute(part, 'dp', (onward, backward)[d])  30.5 us
    unnamed x187, local copies, waits for them, and re-layouts  23.6 us
    ppermute x21, starting transfers between devices, step(): self.moving[d] = lax.ppermute(self.moving[d], 'dp', way)  22.9 us
    ppermute x3, waiting for transfers between devices, chip_swap(): return (pair, lax.ppermute(pair, 'mp', chip_pair))  16.8 us
    pallas_call x1, Pallas kernels, unit_back(): pl.pallas_call(unit_back_kernel, grid_spec=pltpu.PrefetchScalarGridSpec(n...  11.4 us
  transfers between devices with their start and end apart: 62, of which 38 were waited for; matrix products, arithmetic and copies ran while one was open for 1% of the time, Pallas kernels for 20%

profile of v2, /device:TPU:0, one launch (start us, length us, event | category | flops | bytes accessed | tf_op | source)
XLA Modules:
  0.0 481.0 jit_solution(6111439311507664651)
XLA Ops:
  4.2 3.1 collective-permute-start
  8.3 2.1 collective-permute-start.2
  14.8 2.1 prepare.1
  16.9 14.3 %collective-permute-done.2.refs_7_.refs_16_.refs_8_.refs_17_ = bf16[1024,256]{1,0:T(8,128)(2,1)S(1)} collective-permute-done((bf16[1024,256]{1,0:T(8,128)(2,1)S(1)}, bf16[1024,256]{1,0:T(8,128)(2,1)S(1)}, u32[]{:S(2)}, u32[]{:S(2)}) %collective-permute-start.2) | collective-permute-done | bytes 524320 | tf_op jit(solution)/shard_map/ppermute | solution.py:928
  35.1 11.0 %collective-permute-done.4.refs_3_.refs_7_.refs_8_ = bf16[1104,256]{1,0:T(8,128)(2,1)S(1)} collective-permute-done((bf16[1104,256]{1,0:T(8,128)(2,1)S(1)}, bf16[1104,256]{1,0:T(8,128)(2,1)S(1)}, u32[]{:S(2)}, u32[]{:S(2)}) %collective-permute-start.4) | collective-permute-done | bytes 565280 | tf_op jit(solution)/shard_map/ppermute | solution.py:928
  49.8 11.6 %collective-permute-done.10.refs_2_.refs_3_.refs_4_ = bf16[1104,256]{1,0:T(8,128)(2,1)S(1)} collective-permute-done((bf16[1104,256]{1,0:T(8,128)(2,1)}, bf16[1104,256]{1,0:T(8,128)(2,1)S(1)}, u32[]{:S(2)}, u32[]{:S(2)}) %collective-permute-start.10) | collective-permute-done | bytes 565280 | tf_op jit(solution)/shard_map/ppermute | solution.py:928
  63.5 9.7 %collective-permute-done.12.refs_5_.refs_15_.refs_7_.refs_16_ = bf16[1024,256]{1,0:T(8,128)(2,1)S(1)} collective-permute-done((bf16[1024,256]{1,0:T(8,128)(2,1)S(1)}, bf16[1024,256]{1,0:T(8,128)(2,1)S(1)}, u32[]{:S(2)}, u32[]{:S(2)}) %collective-permute-start.12) | collective-permute-done | bytes 524320 | tf_op jit(solution)/shard_map/ppermute | solution.py:928
  75.2 2.9 project.4
  79.6 13.6 %collective-permute-done.13.refs_5_.refs_14_.refs_6_.refs_15_ = bf16[1024,256]{1,0:T(8,128)(2,1)S(1)} collective-permute-done((bf16[1024,256]{1,0:T(8,128)(2,1)S(1)}, bf16[1024,256]{1,0:T(8,128)(2,1)S(1)}, u32[]{:S(2)}, u32[]{:S(2)}) %collective-permute-start.13) | collective-permute-done | bytes 524320 | tf_op jit(solution)/shard_map/ppermute | solution.py:928
  95.7 7.5 %mixer_forward.1 = (bf16[512,704]{1,0:T(8,128)(2,1)S(1)}, bf16[512,704]{1,0:T(8,128)(2,1)S(1)}, f32[512,704]{1,0:T(8,128)S(1)}, f32[512,704]{1,0:T(8,128)S(1)}, f32[512,704]{1,0:T(8,128)S(1)}) custom-call(f32[512,704]{1,0:T(8,128)S(1)} %get-tuple-element.132.refs_0_.refs_9_, f32[512,704]{1,0:T(8,128)S(1)} %get-tuple-element.133.refs_1_.refs_10_, ...), custom_call_target="tpu_custom_call" | custom-call | flops 1 | bytes 1 | tf_op jit(solution)/shard_map/mixer_forward/pallas_call | solution.py:73
  103.3 3.0 mixer_out.1
  106.4 2.6 collective-permute-done.14.refs_1_
  110.8 6.9 %unit_grad.1.refs_5_.refs_4_ = f32[512,1536]{1,0:T(8,128)S(1)} custom-call(bf16[512,2048]{1,0:T(8,128)(2,1)S(1)} %get-tuple-element.140.refs_0_, bf16[1536,2048]{1,0:T(8,128)(2,1)} %refs_1_.3, bf16[8,256,256]{2,1,0:T(8,128)(2,1)S(1)} %pair_sum.4.refs_2_.refs_3_.refs_4_), custom_call_target="tpu_custom_call" | custom-call | flops 1 | bytes 1 | tf_op jit(solution)/shard_map/unit_grad/pallas_call | solution.py:73
  117.8 16.7 %collective-permute-done.15.refs_4_ = bf16[8,256,256]{2,1,0:T(8,128)(2,1)S(1)} collective-permute-done((bf16[8,256,256]{2,1,0:T(8,128)(2,1)S(1)}, bf16[8,256,256]{2,1,0:T(8,128)(2,1)S(1)}, u32[]{:S(2)}, u32[]{:S(2)}) %collective-permute-start.15) | collective-permute-done | bytes 1048608 | tf_op jit(solution)/shard_map/ppermute | solution.py:966
  136.0 2.6 collective-permute-done.16
  138.8 11.7 %unit_pass.1 = (bf16[512,1536]{1,0:T(8,128)(2,1)S(1)}, bf16[512,1536]{1,0:T(8,128)(2,1)S(1)}, bf16[512,1536]{1,0:T(8,128)(2,1)S(1)}, bf16[8,512,256]{2,1,0:T(8,128)(2,1)S(1)}) custom-call(s32[8]{0:T(128)S(1)} %and_select_fusion.1.refs_1_.refs_0_, bf16[512,2048]{1,0:T(8,128)(2,1)S(1)} %pad_maximum_fusion.refs_1_, bf16[2048,1536]{1,0:T(8,128)(2,1)} %gate.1, ...), custom_call_target="tpu_custom_call" | custom-call | flops 1 | bytes 1 | tf_op jit(solution)/shard_map/unit_pass/pallas_call | solution.py:73
  155.5 11.4 %unit_back.1 = (f32[8,256,256]{2,1,0:T(8,128)S(1)}, bf16[8,256,256]{2,1,0:T(8,128)(2,1)S(1)}) custom-call(s32[8]{0:T(128)S(1)} %compare_select_fusion.5.owners.refs_0_, bf16[512,1536]{1,0:T(8,128)(2,1)S(1)} %get-tuple-element.144.refs_2_.dga, bf16[512,1536]{1,0:T(8,128)(2,1)S(1)} %get-tuple-element.145.refs_2_.dup, bf16[2048,1536]{1,0:T(8,128)(2,1)} %gate.1, ...), custom_call_target="tpu_custom_call" | custom-call | flops 1 | bytes 1 | tf_op jit(solution)/shard_map/unit_back/pallas_call | solution.py:656
  169.1 11.8 %collective-permute-done.18.refs_4_ = bf16[256,2304]{1,0:T(8,128)(2,1)S(1)} collective-permute-done((bf16[256,2304]{1,0:T(8,128)(2,1)S(1)}, bf16[256,2304]{1,0:T(8,128)(2,1)S(1)}, u32[]{:S(2)}, u32[]{:S(2)}) %collective-permute-start.18) | collective-permute-done | bytes 1179680 | tf_op jit(solution)/shard_map/ppermute | solution.py:952
  187.7 18.4 %collective-permute-done.23.refs_4_ = bf16[256,2304]{1,0:T(8,128)(2,1)S(1)} collective-permute-done((bf16[256,2304]{1,0:T(8,128)(2,1)S(1)}, bf16[256,2304]{1,0:T(8,128)(2,1)S(1)}, u32[]{:S(2)}, u32[]{:S(2)}) %collective-permute-start.23) | collective-permute-done | bytes 1179680 | tf_op jit(solution)/shard_map/ppermute | solution.py:952
  211.4 20.0 %collective-permute-done.21.refs_4_ = bf16[256,2304]{1,0:T(8,128)(2,1)S(1)} collective-permute-done((bf16[256,2304]{1,0:T(8,128)(2,1)S(1)}, bf16[256,2304]{1,0:T(8,128)(2,1)S(1)}, u32[]{:S(2)}, u32[]{:S(2)}) %collective-permute-start.21) | collective-permute-done | bytes 1179680 | tf_op jit(solution)/shard_map/ppermute | solution.py:952
  233.0 2.4 unit_term.12
  239.4 17.2 %collective-permute-done.26.refs_4_ = bf16[256,2304]{1,0:T(8,128)(2,1)S(1)} collective-permute-done((bf16[256,2304]{1,0:T(8,128)(2,1)S(1)}, bf16[256,2304]{1,0:T(8,128)(2,1)S(1)}, u32[]{:S(2)}, u32[]{:S(2)}) %collective-permute-start.26) | collective-permute-done | bytes 1179680 | tf_op jit(solution)/shard_map/ppermute | solution.py:952
  258.4 2.0 unit_term.13
  267.6 13.8 %mixer_backward.1 = (bf16[512,704]{1,0:T(8,128)(2,1)S(1)}, bf16[512,704]{1,0:T(8,128)(2,1)S(1)}, bf16[384,704]{1,0:T(8,128)(2,1)S(1)}) custom-call(bf16[8,512,256]{2,1,0:T(8,128)(2,1)S(1)} %constant_dynamic-update-slice_fusion.refs_0_.refs_5_, bf16[1024,256]{1,0:T(8,128)(2,1)S(1)} %copy-done.11, bf16[1024,256]{1,0:T(8,128)(2,1)S(1)} %copy-done.24, ...), custom_call_target="tpu_custom_call" | custom-call | flops 1 | bytes 1 | tf_op jit(solution)/shard_map/mixer_backward/pallas_call | solution.py:73
  281.4 7.8 %unit_out.1 = (f32[256,2048]{1,0:T(8,128)S(1)}, bf16[256,2048]{1,0:T(8,128)(2,1)S(1)}) custom-call(bf16[512,1536]{1,0:T(8,128)(2,1)S(1)} %get-tuple-element.143.refs_3_.refs_0_, bf16[1536,2048]{1,0:T(8,128)(2,1)} %refs_1_.3, bf16[512,704]{1,0:T(8,128)(2,1)S(1)} %get-tuple-element.166.refs_2_.refs_0_.refs_6_), custom_call_target="tpu_custom_call" | custom-call | flops 1 | bytes 1 | tf_op jit(solution)/shard_map/unit_out/pallas_call | solution.py:73
  291.6 3.2 unit_term.14
  297.3 5.0 %input_out.1 = (f32[8,256,256]{2,1,0:T(8,128)S(1)}, bf16[8,256,256]{2,1,0:T(8,128)(2,1)S(1)}) custom-call(bf16[512,704]{1,0:T(8,128)(2,1)S(1)} %get-tuple-element.166.refs_2_.refs_0_.refs_6_, bf16[512,704]{1,0:T(8,128)(2,1)S(1)} %get-tuple-element.175.refs_1_.refs_6_, bf16[1104,256]{1,0:T(8,128)(2,1)S(1)} %copy-done.14, ...), custom_call_target="tpu_custom_call" | custom-call | flops 1 | bytes 1 | tf_op jit(solution)/shard_map/input_out/pallas_call | solution.py:73
  304.0 13.6 %collective-permute-done.32.refs_4_ = bf16[256,2304]{1,0:T(8,128)(2,1)S(1)} collective-permute-done((bf16[256,2304]{1,0:T(8,128)(2,1)S(1)}, bf16[256,2304]{1,0:T(8,128)(2,1)S(1)}, u32[]{:S(2)}, u32[]{:S(2)}) %collective-permute-start.32) | collective-permute-done | bytes 1179680 | tf_op jit(solution)/shard_map/ppermute | solution.py:952
  324.2 19.3 %collective-permute-done.35.refs_2_ = bf16[256,2304]{1,0:T(8,128)(2,1)S(1)} collective-permute-done((bf16[256,2304]{1,0:T(8,128)(2,1)S(1)}, bf16[256,2304]{1,0:T(8,128)(2,1)S(1)}, u32[]{:S(2)}, u32[]{:S(2)}) %collective-permute-start.35) | collective-permute-done | bytes 1179680 | tf_op jit(solution)/shard_map/ppermute | solution.py:952
  344.9 1.9 collective-permute-done.34.refs_2_
  359.8 11.5 %collective-permute-done.39.refs_9_ = bf16[1104,256]{1,0:T(8,128)(2,1)S(1)} collective-permute-done((bf16[1104,256]{1,0:T(8,128)(2,1)S(1)}, bf16[1104,256]{1,0:T(8,128)(2,1)S(1)}, u32[]{:S(2)}, u32[]{:S(2)}) %collective-permute-start.39) | collective-permute-done | bytes 565280 | tf_op jit(solution)/shard_map/ppermute | solution.py:952
  375.9 8.1 %collective-permute-done.37.refs_8_ = bf16[1152,256]{1,0:T(8,128)(2,1)S(1)} collective-permute-done((bf16[1152,256]{1,0:T(8,128)(2,1)S(1)}, bf16[1152,256]{1,0:T(8,128)(2,1)S(1)}, u32[]{:S(2)}, u32[]{:S(2)}) %collective-permute-start.37) | collective-permute-done | bytes 589856 | tf_op jit(solution)/shard_map/ppermute | solution.py:952
  388.7 2.8 arrange.2.refs_11_
  391.6 4.6 collective-permute-done.44.refs_9_
  396.1 3.9 collective-permute-done.45.refs_10_
  400.0 2.2 copy-done.8
  403.5 4.8 %collective-permute-done.42.refs_8_ = bf16[1152,256]{1,0:T(8,128)(2,1)S(1)} collective-permute-done((bf16[1152,256]{1,0:T(8,128)(2,1)S(1)}, bf16[1152,256]{1,0:T(8,128)(2,1)S(1)}, u32[]{:S(2)}, u32[]{:S(2)}) %collective-permute-start.42) | collective-permute-done | bytes 589856 | tf_op jit(solution)/shard_map/ppermute | solution.py:952
  408.3 2.5 collective-permute-done.43.refs_9_
  417.5 11.5 %collective-permute-done.50.refs_9_ = bf16[1104,256]{1,0:T(8,128)(2,1)S(1)} collective-permute-done((bf16[1104,256]{1,0:T(8,128)(2,1)S(1)}, bf16[1104,256]{1,0:T(8,128)(2,1)S(1)}, u32[]{:S(2)}, u32[]{:S(2)}) %collective-permute-start.50) | collective-permute-done | bytes 565280 | tf_op jit(solution)/shard_map/ppermute | solution.py:952
  430.7 2.1 mixer_term.14
  434.3 8.2 %collective-permute-done.48.refs_8_ = bf16[1152,256]{1,0:T(8,128)(2,1)S(1)} collective-permute-done((bf16[1152,256]{1,0:T(8,128)(2,1)S(1)}, bf16[1152,256]{1,0:T(8,128)(2,1)S(1)}, u32[]{:S(2)}, u32[]{:S(2)}) %collective-permute-start.48) | collective-permute-done | bytes 589856 | tf_op jit(solution)/shard_map/ppermute | solution.py:952
  442.5 2.0 mixer_term.15
  446.7 3.9 arrange.3.refs_4_
  450.6 2.9 collective-permute-done.52.refs_3_
  453.5 2.2 copy-done.9
  455.7 2.1 mixer_end.2
  459.9 2.6 collective-permute-done.57.refs_8_
  468.7 2.0 mixer_end.3
  (334 shorter events, 129.3 us)
Async XLA Ops:
  4.2 28.6 %collective-permute-start = (bf16[1104,256]{1,0:T(8,128)(2,1)S(1)}, bf16[1104,256]{1,0:T(8,128)(2,1)S(1)}, u32[]{:S(2)}, u32[]{:S(2)}) collective-permute-start(bf16[1104,256]{1,0:T(8,128)(2,1)S(1)} %pad_maximum_fusion.3.refs_2_.refs_1_), channel_id=1, source_target_pairs={{0,8},{8,16},{16,24},{24,28},{28,20},{20,12},{12,4},{4,0},{1,9},{9... | collective-permute-start | bytes 1695752 | tf_op jit(solution)/shard_map/ppermute | solution.py:928
  7.3 25.5 %collective-permute-start.1 = (bf16[1104,256]{1,0:T(8,128)(2,1)S(1)}, bf16[1104,256]{1,0:T(8,128)(2,1)}, u32[]{:S(2)}, u32[]{:S(2)}) collective-permute-start(bf16[1104,256]{1,0:T(8,128)(2,1)S(1)} %pad_maximum_fusion.3.refs_2_.refs_1_), channel_id=1, source_target_pairs={{8,0},{16,8},{24,16},{28,24},{20,28},{12,20},{4,12},{0,4},{9,1},{1... | collective-permute-start | bytes 1695752 | tf_op jit(solution)/shard_map/ppermute | solution.py:928
  8.3 23.0 %collective-permute-start.2 = (bf16[1024,256]{1,0:T(8,128)(2,1)S(1)}, bf16[1024,256]{1,0:T(8,128)(2,1)S(1)}, u32[]{:S(2)}, u32[]{:S(2)}) collective-permute-start(bf16[1024,256]{1,0:T(8,128)(2,1)S(1)} %pad_maximum_fusion.4.refs_5_.refs_9_.refs_1_.refs_10_), channel_id=1, source_target_pairs={{0,8},{8,16},{16,24},{24,28},{28,20},{20,12},{12,4},{4,0},{1,9},{9... | collective-permute-start | bytes 1572872 | tf_op jit(solution)/shard_map/ppermute | solution.py:928
  10.3 22.4 %collective-permute-start.3 = (bf16[1024,256]{1,0:T(8,128)(2,1)S(1)}, bf16[1024,256]{1,0:T(8,128)(2,1)S(1)}, u32[]{:S(2)}, u32[]{:S(2)}) collective-permute-start(bf16[1024,256]{1,0:T(8,128)(2,1)S(1)} %pad_maximum_fusion.4.refs_5_.refs_9_.refs_1_.refs_10_), channel_id=1, source_target_pairs={{8,0},{16,8},{24,16},{28,24},{20,28},{12,20},{4,12},{0,4},{9,1},{1... | collective-permute-start | bytes 1572872 | tf_op jit(solution)/shard_map/ppermute | solution.py:928
  34.8 26.5 %collective-permute-start.10 = (bf16[1104,256]{1,0:T(8,128)(2,1)}, bf16[1104,256]{1,0:T(8,128)(2,1)S(1)}, u32[]{:S(2)}, u32[]{:S(2)}) collective-permute-start(bf16[1104,256]{1,0:T(8,128)(2,1)} %collective-permute-done.1.refs_3_.refs_2_), channel_id=1, source_target_pairs={{8,0},{16,8},{24,16},{28,24},{20,28},{12,20},{4,12},{0,4},{9,1},{1... | collective-permute-start | bytes 1695752 | tf_op jit(solution)/shard_map/ppermute | solution.py:928
  46.2 15.7 %collective-permute-start.5 = (bf16[1104,256]{1,0:T(8,128)(2,1)S(1)}, bf16[1104,256]{1,0:T(8,128)(2,1)S(1)}, u32[]{:S(2)}, u32[]{:S(2)}) collective-permute-start(bf16[1104,256]{1,0:T(8,128)(2,1)S(1)} %collective-permute-done.4.refs_3_.refs_7_.refs_8_), channel_id=1, source_target_pairs={{0,8},{8,16},{16,24},{24,28},{28,20},{20,12},{12,4},{4,0},{1,9},{9... | collective-permute-start | bytes 1695752 | tf_op jit(solution)/shard_map/ppermute | solution.py:928
  47.8 25.4 %collective-permute-start.12 = (bf16[1024,256]{1,0:T(8,128)(2,1)S(1)}, bf16[1024,256]{1,0:T(8,128)(2,1)S(1)}, u32[]{:S(2)}, u32[]{:S(2)}) collective-permute-start(bf16[1024,256]{1,0:T(8,128)(2,1)S(1)} %collective-permute-done.2.refs_7_.refs_16_.refs_8_.refs_17_), channel_id=1, source_target_pairs={{0,8},{8,16},{16,24},{24,28},{28,20},{20,12},{12,4},{4,0},{1,9},{9... | collective-permute-start | bytes 1572872 | tf_op jit(solution)/shard_map/ppermute | solution.py:928
  49.3 25.4 %collective-permute-start.8 = (bf16[1024,256]{1,0:T(8,128)(2,1)S(1)}, bf16[1024,256]{1,0:T(8,128)(2,1)S(1)}, u32[]{:S(2)}, u32[]{:S(2)}) collective-permute-start(bf16[1024,256]{1,0:T(8,128)(2,1)S(1)} %collective-permute-done.7.refs_4_.refs_11_.refs_3_.refs_12_), channel_id=1, source_target_pairs={{8,0},{16,8},{24,16},{28,24},{20,28},{12,20},{4,12},{0,4},{9,1},{1... | collective-permute-start | bytes 1572872 | tf_op jit(solution)/shard_map/ppermute | solution.py:928
  61.4 31.8 %collective-permute-start.11 = (bf16[1104,256]{1,0:T(8,128)(2,1)S(1)}, bf16[1104,256]{1,0:T(8,128)(2,1)S(1)}, u32[]{:S(2)}, u32[]{:S(2)}) collective-permute-start(bf16[1104,256]{1,0:T(8,128)(2,1)S(1)} %collective-permute-done.10.refs_2_.refs_3_.refs_4_), channel_id=1, source_target_pairs={{8,0},{16,8},{24,16},{28,24},{20,28},{12,20},{4,12},{0,4},{9,1},{1... | collective-permute-start | bytes 1695752 | tf_op jit(solution)/shard_map/ppermute | solution.py:928
  61.9 32.8 %collective-permute-start.6 = (bf16[1104,256]{1,0:T(8,128)(2,1)S(1)}, bf16[1104,256]{1,0:T(8,128)(2,1)S(1)}, u32[]{:S(2)}, u32[]{:S(2)}) collective-permute-start(bf16[1104,256]{1,0:T(8,128)(2,1)S(1)} %collective-permute-done.5.refs_3_.refs_6_.refs_7_), channel_id=1, source_target_pairs={{0,8},{8,16},{16,24},{24,28},{28,20},{20,12},{12,4},{4,0},{1,9},{9... | collective-permute-start | bytes 1695752 | tf_op jit(solution)/shard_map/ppermute | solution.py:928
  73.2 20.0 %collective-permute-start.13 = (bf16[1024,256]{1,0:T(8,128)(2,1)S(1)}, bf16[1024,256]{1,0:T(8,128)(2,1)S(1)}, u32[]{:S(2)}, u32[]{:S(2)}) collective-permute-start(bf16[1024,256]{1,0:T(8,128)(2,1)S(1)} %collective-permute-done.12.refs_5_.refs_15_.refs_7_.refs_16_), channel_id=1, source_target_pairs={{0,8},{8,16},{16,24},{24,28},{28,20},{20,12},{12,4},{4,0},{1,9},{9... | collective-permute-start | bytes 1572872 | tf_op jit(solution)/shard_map/ppermute | solution.py:928
  74.7 20.0 %collective-permute-start.9 = (bf16[1024,256]{1,0:T(8,128)(2,1)S(1)}, bf16[1024,256]{1,0:T(8,128)(2,1)S(1)}, u32[]{:S(2)}, u32[]{:S(2)}) collective-permute-start(bf16[1024,256]{1,0:T(8,128)(2,1)S(1)} %collective-permute-done.8.refs_4_.refs_12_.refs_13_), channel_id=1, source_target_pairs={{8,0},{16,8},{24,16},{28,24},{20,28},{12,20},{4,12},{0,4},{9,1},{1... | collective-permute-start | bytes 1572872 | tf_op jit(solution)/shard_map/ppermute | solution.py:928
  109.3 25.3 %collective-permute-start.15 = (bf16[8,256,256]{2,1,0:T(8,128)(2,1)S(1)}, bf16[8,256,256]{2,1,0:T(8,128)(2,1)S(1)}, u32[]{:S(2)}, u32[]{:S(2)}) collective-permute-start(bf16[8,256,256]{2,1,0:T(8,128)(2,1)S(1)} %pair_sum.4.refs_2_.refs_3_.refs_4_), channel_id=1, source_target_pairs={{0,2},{1,3},{2,0},{3,1},{4,6},{5,7},{6,4},{7,5},{8,10},{9,11},{10,... | collective-permute-start | bytes 3145736 | tf_op jit(solution)/shard_map/ppermute | solution.py:966
  152.0 28.9 %collective-permute-start.18 = (bf16[256,2304]{1,0:T(8,128)(2,1)S(1)}, bf16[256,2304]{1,0:T(8,128)(2,1)S(1)}, u32[]{:S(2)}, u32[]{:S(2)}) collective-permute-start(bf16[256,2304]{1,0:T(8,128)(2,1)S(1)} %get-tuple-element.148.refs_4_), channel_id=1, source_target_pairs={{0,8},{8,16},{16,24},{24,28},{28,20},{20,12},{12,4},{4,0},{1,9},{9... | collective-permute-start | bytes 3538952 | tf_op jit(solution)/shard_map/ppermute | solution.py:952
  153.6 28.9 %collective-permute-start.19 = (bf16[256,2304]{1,0:T(8,128)(2,1)S(1)}, bf16[256,2304]{1,0:T(8,128)(2,1)S(1)}, u32[]{:S(2)}, u32[]{:S(2)}) collective-permute-start(bf16[256,2304]{1,0:T(8,128)(2,1)S(1)} %get-tuple-element.152), channel_id=1, source_target_pairs={{8,0},{16,8},{24,16},{28,24},{20,28},{12,20},{4,12},{0,4},{9,1},{1... | collective-permute-start | bytes 3538952 | tf_op jit(solution)/shard_map/ppermute | solution.py:952
  166.9 19.1 %collective-permute-start.17 = (bf16[8,256,256]{2,1,0:T(8,128)(2,1)S(1)}, bf16[8,256,256]{2,1,0:T(8,128)(2,1)S(1)}, u32[]{:S(2)}, u32[]{:S(2)}) collective-permute-start(bf16[8,256,256]{2,1,0:T(8,128)(2,1)S(1)} %get-tuple-element.151), channel_id=1, source_target_pairs={{0,1},{1,0},{2,3},{3,2},{4,5},{5,4},{6,7},{7,6},{8,9},{9,8},{10,11... | collective-permute-start | bytes 3145736 | tf_op jit(solution)/shard_map/ppermute | solution.py:961
  167.0 39.2 %collective-permute-start.23 = (bf16[256,2304]{1,0:T(8,128)(2,1)S(1)}, bf16[256,2304]{1,0:T(8,128)(2,1)S(1)}, u32[]{:S(2)}, u32[]{:S(2)}) collective-permute-start(bf16[256,2304]{1,0:T(8,128)(2,1)S(1)} %get-tuple-element.149.refs_0_), channel_id=1, source_target_pairs={{0,8},{8,16},{16,24},{24,28},{28,20},{20,12},{12,4},{4,0},{1,9},{9... | collective-permute-start | bytes 3538952 | tf_op jit(solution)/shard_map/ppermute | solution.py:952
  168.6 39.1 %collective-permute-start.24 = (bf16[256,2304]{1,0:T(8,128)(2,1)S(1)}, bf16[256,2304]{1,0:T(8,128)(2,1)S(1)}, u32[]{:S(2)}, u32[]{:S(2)}) collective-permute-start(bf16[256,2304]{1,0:T(8,128)(2,1)S(1)} %get-tuple-element.156), channel_id=1, source_target_pairs={{8,0},{16,8},{24,16},{28,24},{20,28},{12,20},{4,12},{0,4},{9,1},{1... | collective-permute-start | bytes 3538952 | tf_op jit(solution)/shard_map/ppermute | solution.py:952
  183.9 47.5 %collective-permute-start.21 = (bf16[256,2304]{1,0:T(8,128)(2,1)S(1)}, bf16[256,2304]{1,0:T(8,128)(2,1)S(1)}, u32[]{:S(2)}, u32[]{:S(2)}) collective-permute-start(bf16[256,2304]{1,0:T(8,128)(2,1)S(1)} %get-tuple-element.153.refs_2_), channel_id=1, source_target_pairs={{0,8},{8,16},{16,24},{24,28},{28,20},{20,12},{12,4},{4,0},{1,9},{9... | collective-permute-start | bytes 3538952 | tf_op jit(solution)/shard_map/ppermute | solution.py:952
  185.5 47.5 %collective-permute-start.22 = (bf16[256,2304]{1,0:T(8,128)(2,1)S(1)}, bf16[256,2304]{1,0:T(8,128)(2,1)S(1)}, u32[]{:S(2)}, u32[]{:S(2)}) collective-permute-start(bf16[256,2304]{1,0:T(8,128)(2,1)S(1)} %get-tuple-element.155), channel_id=1, source_target_pairs={{8,0},{16,8},{24,16},{28,24},{20,28},{12,20},{4,12},{0,4},{9,1},{1... | collective-permute-start | bytes 3538952 | tf_op jit(solution)/shard_map/ppermute | solution.py:952
  186.1 49.3 %collective-permute-start.20 = (bf16[8,256,256]{2,1,0:T(8,128)(2,1)S(1)}, bf16[8,256,256]{2,1,0:T(8,128)(2,1)S(1)}, u32[]{:S(2)}, u32[]{:S(2)}) collective-permute-start(bf16[8,256,256]{2,1,0:T(8,128)(2,1)S(1)} %pair_sum.5.refs_6_.refs_0_), channel_id=1, source_target_pairs={{0,2},{1,3},{2,0},{3,1},{4,6},{5,7},{6,4},{7,5},{8,10},{9,11},{10,... | collective-permute-start | bytes 3145736 | tf_op jit(solution)/shard_map/ppermute | solution.py:966
  209.2 47.5 %collective-permute-start.26 = (bf16[256,2304]{1,0:T(8,128)(2,1)S(1)}, bf16[256,2304]{1,0:T(8,128)(2,1)S(1)}, u32[]{:S(2)}, u32[]{:S(2)}) collective-permute-start(bf16[256,2304]{1,0:T(8,128)(2,1)S(1)} %get-tuple-element.157.refs_6_), channel_id=1, source_target_pairs={{0,8},{8,16},{16,24},{24,28},{28,20},{20,12},{12,4},{4,0},{1,9},{9... | collective-permute-start | bytes 3538952 | tf_op jit(solution)/shard_map/ppermute | solution.py:952
  210.8 47.5 %collective-permute-start.27 = (bf16[256,2304]{1,0:T(8,128)(2,1)S(1)}, bf16[256,2304]{1,0:T(8,128)(2,1)S(1)}, u32[]{:S(2)}, u32[]{:S(2)}) collective-permute-start(bf16[256,2304]{1,0:T(8,128)(2,1)S(1)} %get-tuple-element.164), channel_id=1, source_target_pairs={{8,0},{16,8},{24,16},{28,24},{20,28},{12,20},{4,12},{0,4},{9,1},{1... | collective-permute-start | bytes 3538952 | tf_op jit(solution)/shard_map/ppermute | solution.py:952
  237.2 24.3 %collective-permute-start.25 = (bf16[8,256,256]{2,1,0:T(8,128)(2,1)S(1)}, bf16[8,256,256]{2,1,0:T(8,128)(2,1)S(1)}, u32[]{:S(2)}, u32[]{:S(2)}) collective-permute-start(bf16[8,256,256]{2,1,0:T(8,128)(2,1)S(1)} %get-tuple-element.159.refs_6_), channel_id=1, source_target_pairs={{0,1},{1,0},{2,3},{3,2},{4,5},{5,4},{6,7},{7,6},{8,9},{9,8},{10,11... | collective-permute-start | bytes 3145736 | tf_op jit(solution)/shard_map/ppermute | solution.py:969
  237.3 54.2 %collective-permute-start.29 = (bf16[256,2304]{1,0:T(8,128)(2,1)}, bf16[256,2304]{1,0:T(8,128)(2,1)}, u32[]{:S(2)}, u32[]{:S(2)}) collective-permute-start(bf16[256,2304]{1,0:T(8,128)(2,1)} %get-tuple-element.158.refs_6_), channel_id=1, source_target_pairs={{0,8},{8,16},{16,24},{24,28},{28,20},{20,12},{12,4},{4,0},{1,9},{9... | collective-permute-start | bytes 3538952 | tf_op jit(solution)/shard_map/ppermute | solution.py:952
  238.9 52.6 %collective-permute-start.30 = (bf16[256,2304]{1,0:T(8,128)(2,1)}, bf16[256,2304]{1,0:T(8,128)(2,1)}, u32[]{:S(2)}, u32[]{:S(2)}) collective-permute-start(bf16[256,2304]{1,0:T(8,128)(2,1)} %get-tuple-element.169), channel_id=1, source_target_pairs={{8,0},{16,8},{24,16},{28,24},{20,28},{12,20},{4,12},{0,4},{9,1},{1... | collective-permute-start | bytes 3538952 | tf_op jit(solution)/shard_map/ppermute | solution.py:952
  289.3 28.4 %collective-permute-start.32 = (bf16[256,2304]{1,0:T(8,128)(2,1)S(1)}, bf16[256,2304]{1,0:T(8,128)(2,1)S(1)}, u32[]{:S(2)}, u32[]{:S(2)}) collective-permute-start(bf16[256,2304]{1,0:T(8,128)(2,1)S(1)} %copy-done.80), channel_id=1, source_target_pairs={{8,0},{16,8},{24,16},{28,24},{20,28},{12,20},{4,12},{0,4},{9,1},{1... | collective-permute-start | bytes 3538952 | tf_op jit(solution)/shard_map/ppermute | solution.py:952
  289.8 29.2 %collective-permute-start.33 = (bf16[256,2304]{1,0:T(8,128)(2,1)}, bf16[256,2304]{1,0:T(8,128)(2,1)S(1)}, u32[]{:S(2)}, u32[]{:S(2)}) collective-permute-start(bf16[256,2304]{1,0:T(8,128)(2,1)} %get-tuple-element.165.refs_18_), channel_id=1, source_target_pairs={{0,8},{8,16},{16,24},{24,28},{28,20},{20,12},{12,4},{4,0},{1,9},{9... | collective-permute-start | bytes 3538952 | tf_op jit(solution)/shard_map/ppermute | solution.py:952
  302.3 19.1 %collective-permute-start.36 = (bf16[8,256,256]{2,1,0:T(8,128)(2,1)S(1)}, bf16[8,256,256]{2,1,0:T(8,128)(2,1)S(1)}, u32[]{:S(2)}, u32[]{:S(2)}) collective-permute-start(bf16[8,256,256]{2,1,0:T(8,128)(2,1)S(1)} %get-tuple-element.184), channel_id=1, source_target_pairs={{0,1},{1,0},{2,3},{3,2},{4,5},{5,4},{6,7},{7,6},{8,9},{9,8},{10,11... | collective-permute-start | bytes 3145736 | tf_op jit(solution)/shard_map/ppermute | solution.py:961
  302.4 41.1 %collective-permute-start.35 = (bf16[256,2304]{1,0:T(8,128)(2,1)S(1)}, bf16[256,2304]{1,0:T(8,128)(2,1)S(1)}, u32[]{:S(2)}, u32[]{:S(2)}) collective-permute-start(bf16[256,2304]{1,0:T(8,128)(2,1)S(1)} %get-tuple-element.170.refs_2_), channel_id=1, source_target_pairs={{0,8},{8,16},{16,24},{24,28},{28,20},{20,12},{12,4},{4,0},{1,9},{9... | collective-permute-start | bytes 3538952 | tf_op jit(solution)/shard_map/ppermute | solution.py:952
  320.4 26.5 %collective-permute-start.34 = (bf16[256,2304]{1,0:T(8,128)(2,1)S(1)}, bf16[256,2304]{1,0:T(8,128)(2,1)S(1)}, u32[]{:S(2)}, u32[]{:S(2)}) collective-permute-start(bf16[256,2304]{1,0:T(8,128)(2,1)S(1)} %get-tuple-element.180.refs_2_), channel_id=1, source_target_pairs={{8,0},{16,8},{24,16},{28,24},{20,28},{12,20},{4,12},{0,4},{9,1},{1... | collective-permute-start | bytes 3538952 | tf_op jit(solution)/shard_map/ppermute | solution.py:952
  321.6 32.0 %collective-permute-start.41 = (bf16[8,256,256]{2,1,0:T(8,128)(2,1)S(1)}, bf16[8,256,256]{2,1,0:T(8,128)(2,1)S(1)}, u32[]{:S(2)}, u32[]{:S(2)}) collective-permute-start(bf16[8,256,256]{2,1,0:T(8,128)(2,1)S(1)} %pair_sum.7.refs_9_.refs_1_), channel_id=1, source_target_pairs={{0,2},{1,3},{2,0},{3,1},{4,6},{5,7},{6,4},{7,5},{8,10},{9,11},{10,... | collective-permute-start | bytes 3145736 | tf_op jit(solution)/shard_map/ppermute | solution.py:966
  355.6 32.3 %collective-permute-start.46 = (f32[256,2048]{1,0:T(8,128)S(1)}, f32[256,2048]{1,0:T(8,128)S(1)}, u32[]{:S(2)}, u32[]{:S(2)}) collective-permute-start(f32[256,2048]{1,0:T(8,128)S(1)} %get-tuple-element.193.refs_11_.refs_1_), channel_id=1, source_target_pairs={{0,1},{1,0},{2,3},{3,2},{4,5},{5,4},{6,7},{7,6},{8,9},{9,8},{10,11... | collective-permute-start | bytes 6291464 | tf_op jit(solution)/shard_map/ppermute | solution.py:961
  355.7 15.7 %collective-permute-start.39 = (bf16[1104,256]{1,0:T(8,128)(2,1)S(1)}, bf16[1104,256]{1,0:T(8,128)(2,1)S(1)}, u32[]{:S(2)}, u32[]{:S(2)}) collective-permute-start(bf16[1104,256]{1,0:T(8,128)(2,1)S(1)} %get-tuple-element.185.refs_3_), channel_id=1, source_target_pairs={{0,8},{8,16},{16,24},{24,28},{28,20},{20,12},{12,4},{4,0},{1,9},{9... | collective-permute-start | bytes 1695752 | tf_op jit(solution)/shard_map/ppermute | solution.py:952
  357.4 15.6 %collective-permute-start.40 = (bf16[1104,256]{1,0:T(8,128)(2,1)S(1)}, bf16[1104,256]{1,0:T(8,128)(2,1)S(1)}, u32[]{:S(2)}, u32[]{:S(2)}) collective-permute-start(bf16[1104,256]{1,0:T(8,128)(2,1)S(1)} %get-tuple-element.190), channel_id=1, source_target_pairs={{8,0},{16,8},{24,16},{28,24},{20,28},{12,20},{4,12},{0,4},{9,1},{1... | collective-permute-start | bytes 1695752 | tf_op jit(solution)/shard_map/ppermute | solution.py:952
  357.8 26.2 %collective-permute-start.37 = (bf16[1152,256]{1,0:T(8,128)(2,1)S(1)}, bf16[1152,256]{1,0:T(8,128)(2,1)S(1)}, u32[]{:S(2)}, u32[]{:S(2)}) collective-permute-start(bf16[1152,256]{1,0:T(8,128)(2,1)S(1)} %get-tuple-element.188.refs_8_), channel_id=1, source_target_pairs={{0,8},{8,16},{16,24},{24,28},{28,20},{20,12},{12,4},{4,0},{1,9},{9... | collective-permute-start | bytes 1769480 | tf_op jit(solution)/shard_map/ppermute | solution.py:952
  359.4 25.8 %collective-permute-start.38 = (bf16[1152,256]{1,0:T(8,128)(2,1)S(1)}, bf16[1152,256]{1,0:T(8,128)(2,1)S(1)}, u32[]{:S(2)}, u32[]{:S(2)}) collective-permute-start(bf16[1152,256]{1,0:T(8,128)(2,1)S(1)} %get-tuple-element.189), channel_id=1, source_target_pairs={{8,0},{16,8},{24,16},{28,24},{20,28},{12,20},{4,12},{0,4},{9,1},{1... | collective-permute-start | bytes 1769480 | tf_op jit(solution)/shard_map/ppermute | solution.py:952
  371.4 40.9 %collective-permute-start.31 = (bf16[256,2048]{1,0:T(8,128)(2,1)S(1)}, bf16[256,2048]{1,0:T(8,128)(2,1)S(1)}, u32[]{:S(2)}, u32[]{:S(2)}) collective-permute-start(bf16[256,2048]{1,0:T(8,128)(2,1)S(1)} %pair_sum.6.refs_18_.refs_2_), channel_id=1, source_target_pairs={{0,2},{1,3},{2,0},{3,1},{4,6},{5,7},{6,4},{7,5},{8,10},{9,11},{10,... | collective-permute-start | bytes 3145736 | tf_op jit(solution)/shard_map/ppermute | solution.py:1059
  374.3 21.8 %collective-permute-start.44 = (bf16[1104,256]{1,0:T(8,128)(2,1)S(1)}, bf16[1104,256]{1,0:T(8,128)(2,1)S(1)}, u32[]{:S(2)}, u32[]{:S(2)}) collective-permute-start(bf16[1104,256]{1,0:T(8,128)(2,1)S(1)} %get-tuple-element.194.refs_10_), channel_id=1, source_target_pairs={{0,8},{8,16},{16,24},{24,28},{28,20},{20,12},{12,4},{4,0},{1,9},{9... | collective-permute-start | bytes 1695752 | tf_op jit(solution)/shard_map/ppermute | solution.py:952
  384.0 16.0 %collective-permute-start.45 = (bf16[1104,256]{1,0:T(8,128)(2,1)S(1)}, bf16[1104,256]{1,0:T(8,128)(2,1)S(1)}, u32[]{:S(2)}, u32[]{:S(2)}) collective-permute-start(bf16[1104,256]{1,0:T(8,128)(2,1)S(1)} %get-tuple-element.197), channel_id=1, source_target_pairs={{8,0},{16,8},{24,16},{28,24},{20,28},{12,20},{4,12},{0,4},{9,1},{1... | collective-permute-start | bytes 1695752 | tf_op jit(solution)/shard_map/ppermute | solution.py:952
  386.7 21.7 %collective-permute-start.42 = (bf16[1152,256]{1,0:T(8,128)(2,1)S(1)}, bf16[1152,256]{1,0:T(8,128)(2,1)S(1)}, u32[]{:S(2)}, u32[]{:S(2)}) collective-permute-start(bf16[1152,256]{1,0:T(8,128)(2,1)S(1)} %get-tuple-element.195.refs_3_), channel_id=1, source_target_pairs={{0,8},{8,16},{16,24},{24,28},{28,20},{20,12},{12,4},{4,0},{1,9},{9... | collective-permute-start | bytes 1769480 | tf_op jit(solution)/shard_map/ppermute | solution.py:952
  388.0 22.8 %collective-permute-start.43 = (bf16[1152,256]{1,0:T(8,128)(2,1)S(1)}, bf16[1152,256]{1,0:T(8,128)(2,1)S(1)}, u32[]{:S(2)}, u32[]{:S(2)}) collective-permute-start(bf16[1152,256]{1,0:T(8,128)(2,1)S(1)} %get-tuple-element.196), channel_id=1, source_target_pairs={{8,0},{16,8},{24,16},{28,24},{20,28},{12,20},{4,12},{0,4},{9,1},{1... | collective-permute-start | bytes 1769480 | tf_op jit(solution)/shard_map/ppermute | solution.py:952
  413.3 33.4 %collective-permute-start.47 = (f32[256,2048]{1,0:T(8,128)S(1)}, f32[256,2048]{1,0:T(8,128)}, u32[]{:S(2)}, u32[]{:S(2)}) collective-permute-start(f32[256,2048]{1,0:T(8,128)S(1)} %finish.1.refs_11_.refs_1_), channel_id=1, source_target_pairs={{0,1},{1,0},{2,3},{3,2},{4,5},{5,4},{6,7},{7,6},{8,9},{9,8},{10,11... | collective-permute-start | bytes 6291464 | tf_op jit(solution)/shard_map/ppermute | solution.py:961
  413.4 15.7 %collective-permute-start.50 = (bf16[1104,256]{1,0:T(8,128)(2,1)S(1)}, bf16[1104,256]{1,0:T(8,128)(2,1)S(1)}, u32[]{:S(2)}, u32[]{:S(2)}) collective-permute-start(bf16[1104,256]{1,0:T(8,128)(2,1)S(1)} %get-tuple-element.198.refs_10_), channel_id=1, source_target_pairs={{0,8},{8,16},{16,24},{24,28},{28,20},{20,12},{12,4},{4,0},{1,9},{9... | collective-permute-start | bytes 1695752 | tf_op jit(solution)/shard_map/ppermute | solution.py:952
  415.5 27.1 %collective-permute-start.48 = (bf16[1152,256]{1,0:T(8,128)(2,1)S(1)}, bf16[1152,256]{1,0:T(8,128)(2,1)S(1)}, u32[]{:S(2)}, u32[]{:S(2)}) collective-permute-start(bf16[1152,256]{1,0:T(8,128)(2,1)S(1)} %get-tuple-element.200), channel_id=1, source_target_pairs={{8,0},{16,8},{24,16},{28,24},{20,28},{12,20},{4,12},{0,4},{9,1},{1... | collective-permute-start | bytes 1769480 | tf_op jit(solution)/shard_map/ppermute | solution.py:952
  416.4 26.1 %collective-permute-start.49 = (bf16[1152,256]{1,0:T(8,128)(2,1)S(1)}, bf16[1152,256]{1,0:T(8,128)(2,1)S(1)}, u32[]{:S(2)}, u32[]{:S(2)}) collective-permute-start(bf16[1152,256]{1,0:T(8,128)(2,1)S(1)} %get-tuple-element.199.refs_4_), channel_id=1, source_target_pairs={{0,8},{8,16},{16,24},{24,28},{28,20},{20,12},{12,4},{4,0},{1,9},{9... | collective-permute-start | bytes 1769480 | tf_op jit(solution)/shard_map/ppermute | solution.py:952
  432.7 20.7 %collective-permute-start.52 = (bf16[1104,256]{1,0:T(8,128)(2,1)}, bf16[1104,256]{1,0:T(8,128)(2,1)}, u32[]{:S(2)}, u32[]{:S(2)}) collective-permute-start(bf16[1104,256]{1,0:T(8,128)(2,1)} %get-tuple-element.202.refs_10_), channel_id=1, source_target_pairs={{0,8},{8,16},{16,24},{24,28},{28,20},{20,12},{12,4},{4,0},{1,9},{9... | collective-permute-start | bytes 1695752 | tf_op jit(solution)/shard_map/ppermute | solution.py:952
  446.2 22.5 %collective-permute-start.61 = (bf16[1152,256]{1,0:T(8,128)(2,1)}, bf16[1152,256]{1,0:T(8,128)(2,1)}, u32[]{:S(2)}, u32[]{:S(2)}) collective-permute-start(bf16[1152,256]{1,0:T(8,128)(2,1)} %get-tuple-element.203.refs_3_), channel_id=1, source_target_pairs={{8,0},{16,8},{24,16},{28,24},{20,28},{12,20},{4,12},{0,4},{9,1},{1... | collective-permute-start | bytes 1769480 | tf_op jit(solution)/shard_map/ppermute | solution.py:952
  (107 other events, 2088.7 us)

commit v3 on v2

--- a/solution.py
+++ b/solution.py
@@ -291,6 +291,27 @@
     )
 
 
+def pack_kernel(split, value, gelu_w, output, gain_one, gain_two, one_o, two_o):
+    width = value.shape[0]
+    one_o[:width, :] = value[...]
+    spare = jnp.zeros((14, value.shape[1]), F32)
+    lines = jnp.concatenate([gain_one[...].astype(F32), gain_two[...].astype(F32), spare], 0)
+    one_o[width : width + 16, :] = lines.astype(BF16)
+    one_o[width + 16 :, :] = gelu_w[:split, :]
+    two_o[: width - split, :] = gelu_w[split:, :]
+    two_o[width - split :, :] = output[...]
+
+
+def pack(split, value, gelu_w, output, gain_one, gain_two):
+    width, block = value.shape
+    return launch(
+        lambda *refs: pack_kernel(split, *refs),
+        (value, gelu_w, output, gain_one, gain_two),
+        (shaped((width + 16 + split, block), BF16), shaped((2 * width - split, block), BF16)),
+        "pack",
+    )
+
+
 def prepare_kernel(scalars, slots, tokens, cotangent, gate_i, gate_r, x_o, g_o, flat_o, r_o, blocks_i, blocks_r):
     ring_size, total, block = x_o.shape
     half = total // 2
@@ -439,6 +460,14 @@
     return launch(pair_kernel, (own, got), shaped(own.shape, BF16), "pair_sum", after=after)
 
 
+def relay_kernel(source, out):
+    out[...] = source[...]
+
+
+def relay(source, after):
+    return launch(relay_kernel, (source,), shaped(source.shape, source.dtype), "relay", after=after)
+
+
 def norm_kernel(slots, x, gains, pair, other, h_o, n_o, r_o):
     ring_size, half, block = h_o.shape
     squares = jnp.zeros((half, block), F32)
@@ -525,28 +554,38 @@
     )
 
 
-def finish_kernel(slots, h1, pair, other, out_o):
+def finish_kernel(slots, h1, pair, other, beside, out_o):
     ring_size, half, block = h1.shape
+    out_o[0] = beside[...]
     for k in range(ring_size):
         columns = slice(k * block, (k + 1) * block)
-        out_o[:, columns] = h1[slots[k]] + (pair[:, columns].astype(F32) + other[:, columns].astype(F32))
-
-
-def finish(slots, h1, pair, other, after):
-    return launch(
-        finish_kernel, (slots, h1, pair, other), shaped(pair.shape, F32), "finish", scalars=1, after=after
-    )
-
-
-def arrange_kernel(scalars, own, got, out):
+        summed = pair[:, columns].astype(F32) + other[:, columns].astype(F32)
+        out_o[1, :, columns] = h1[slots[k]] + summed
+
+
+def finish(slots, h1, pair, other, beside, after):
+    return launch(
+        finish_kernel,
+        (slots, h1, pair, other, beside),
+        shaped((2, *beside.shape), F32),
+        "finish",
+        scalars=1,
+        after=after,
+        mib=24,
+    )
+
+
+def arrange_kernel(scalars, own, got, *outs):
     core = scalars[0]
-    out[core] = own[...]
-    out[1 - core] = got[...]
+    for i, out in enumerate(outs):
+        out[core] = own[i]
+        out[1 - core] = got[i]
 
 
 def arrange(scalars, own, got, after):
-    return launch(
-        arrange_kernel, (scalars, own, got), shaped((2, *own.shape), own.dtype), "arrange", scalars=1, after=after
+    out = shaped((2, *own.shape[1:]), own.dtype)
+    return launch(
+        arrange_kernel, (scalars, own, got), (out,) * own.shape[0], "arrange", scalars=1, after=after, mib=24
     )
 
 
@@ -566,13 +605,15 @@
     return launch(unit_grad_kernel, (g, in_hbm(down)), shaped((total, units), F32), "unit_grad", after=after, grid=grid)
 
 
-def unit_kernel(slots, n2, gate, up, dq, q_o, dga_o, dup_o, rel_o):
-    ring_size, total, block = rel_o.shape
-
-    @pl.when(pl.program_id(0) == 0)
-    def _():
-        for k in range(ring_size):
-            rel_o[slots[k]] = n2[:, k * block : (k + 1) * block]
+def unit_kernel(with_rel, slots, n2, gate, up, dq, q_o, dga_o, dup_o, *rel):
+    if with_rel:
+        rel_o = rel[0]
+        ring_size, total, block = rel_o.shape
+
+        @pl.when(pl.program_id(0) == 0)
+        def _():
+            for k in range(ring_size):
+                rel_o[slots[k]] = n2[:, k * block : (k + 1) * block]
 
     ga = jnp.dot(n2[...], gate[...], preferred_element_type=F32)
     upward = jnp.dot(n2[...], up[...], preferred_element_type=F32)
@@ -583,52 +624,57 @@
     dup_o[...] = (grad * value).astype(BF16)
 
 
-def unit_pass(slots, n2, gate, up, dq):
+def unit_pass(part, slots, n2, gate, up, dq, after):
     total, model = n2.shape
     ring_size = slots.shape[0]
-    units = gate.shape[1]
+    share = gate.shape[1] // 2
     tile = 256
+    first = part * (share // tile)
     rel = (ring_size, total, model // ring_size)
     wide = pl.BlockSpec((total, tile), lambda i: (0, i))
-    tall = pl.BlockSpec((model, tile), lambda i: (0, i))
-    out = shaped((total, units), BF16)
+    out = shaped((total, share), BF16)
     grid = (
-        (units // tile,),
-        [pl.BlockSpec((total, model), lambda i: (0, 0)), tall, tall, wide],
-        [wide, wide, wide, pl.BlockSpec(rel, lambda i: (0, 0, 0))],
-    )
-    return launch(
-        unit_kernel,
+        (share // tile,),
+        [
+            pl.BlockSpec((total, model), lambda i: (0, 0)),
+            pl.BlockSpec((model, tile), lambda i: (0, i + first)),
+            pl.BlockSpec((model, tile), lambda i: (0, i + first)),
+            pl.BlockSpec((total, tile), lambda i: (0, i + first)),
+        ],
+        [wide, wide, wide] + [pl.BlockSpec(rel, lambda i: (0, 0, 0))] * (1 - part),
+    )
+    return launch(
+        lambda *refs: unit_kernel(part == 0, *refs),
         (slots, n2, in_hbm(gate), in_hbm(up), dq),
-        (out, out, out, shaped(rel, BF16)),
+        (out, out, out) + (shaped(rel, BF16),) * (1 - part),
         "unit_pass",
         scalars=1,
+        after=after,
         mib=28,
         grid=grid,
     )
 
 
-def unit_out_kernel(q, down, own_o, other_o):
+def unit_out_kernel(q_a, q_b, down, own_o, other_o):
     half = own_o.shape[0]
-    part = jnp.dot(q[...], down[...], preferred_element_type=F32)
+    share = q_a.shape[1]
+    part = jnp.dot(q_a[...], down[:share, :], preferred_element_type=F32)
+    part = part + jnp.dot(q_b[...], down[share:, :], preferred_element_type=F32)
     own_o[...] = part[:half]
     other_o[...] = part[half:].astype(BF16)
 
 
-def unit_out(q, down, after):
-    total, units = q.shape
-    model = down.shape[1]
+def unit_out(q_a, q_b, down, after):
+    total, share = q_a.shape
+    units, model = down.shape
     half = total // 2
     tile = 256
     out = pl.BlockSpec((half, tile), lambda i: (0, i))
-    grid = (
-        (model // tile,),
-        [pl.BlockSpec((total, units), lambda i: (0, 0)), pl.BlockSpec((units, tile), lambda i: (0, i))],
-        [out, out],
-    )
+    left = pl.BlockSpec((total, share), lambda i: (0, 0))
+    grid = ((model // tile,), [left, left, pl.BlockSpec((units, tile), lambda i: (0, i))], [out, out])
     return launch(
         unit_out_kernel,
-        (q, in_hbm(down)),
+        (q_a, q_b, in_hbm(down)),
         (shaped((half, model), F32), shaped((half, model), BF16)),
         "unit_out",
         after=after,
@@ -636,21 +682,30 @@
     )
 
 
-def unit_back_kernel(owners, dga, dup, gate, up, *refs):
+def unit_back_kernel(owners, dga_a, dga_b, dup_a, dup_b, gate, up, *refs):
     own_o, other_o = refs[-2:]
     half = other_o.shape[1]
-    part = lax.dot_general(dga[...], gate[...], NT, preferred_element_type=F32)
-    part = part + lax.dot_general(dup[...], up[...], NT, preferred_element_type=F32)
+    share = dga_a.shape[1]
+    part = None
+    for left, right in (
+        (dga_a, gate[:, :share]),
+        (dga_b, gate[:, share:]),
+        (dup_a, up[:, :share]),
+        (dup_b, up[:, share:]),
+    ):
+        term = lax.dot_general(left[...], right, NT, preferred_element_type=F32)
+        part = term if part is None else part + term
     own_o[0] = part[:half]
     other_o[0] = part[half:].astype(BF16)
 
 
-def unit_back(owners, dga, dup, gate, up, after):
+def unit_back(owners, grads, gate, up, after):
     ring_size = owners.shape[0]
-    total, units = dga.shape
+    total, share = grads[0].shape
+    model, units = gate.shape
     half = total // 2
-    block = gate.shape[0] // ring_size
-    left = pl.BlockSpec((total, units), lambda o, owners: (0, 0))
+    block = model // ring_size
+    left = pl.BlockSpec((total, share), lambda o, owners: (0, 0))
     weight = pl.BlockSpec((block, units), lambda o, owners: (owners[o], 0))
     out = pl.BlockSpec((1, half, block), lambda o, owners: (o, 0, 0))
     return pl.pallas_call(
@@ -658,73 +713,91 @@
         grid_spec=pltpu.PrefetchScalarGridSpec(
             num_scalar_prefetch=1,
             grid=(ring_size,),
-            in_specs=[left, left, weight, weight, *[pl.BlockSpec(memory_space=pl.ANY)] * len(after)],
+            in_specs=[left] * 4 + [weight, weight, *[pl.BlockSpec(memory_space=pl.ANY)] * len(after)],
             out_specs=[out, out],
         ),
         out_shape=(shaped((ring_size, half, block), F32), shaped((ring_size, half, block), BF16)),
         compiler_params=pltpu.CompilerParams(vmem_limit_bytes=24 << 20),
         cost_estimate=pl.CostEstimate(flops=1, bytes_accessed=1, transcendentals=0),
         name="unit_back",
-    )(owners, dga, dup, in_hbm(gate), in_hbm(up), *after)
-
-
-def unit_term_kernel(part, turns, fold, n2, g, right, q, *refs):
-    units = right.shape[1]
-    share = units // 2
-    columns = slice(part * share, (part + 1) * share)
+    )(owners, *grads, in_hbm(gate), in_hbm(up), *after)
+
+
+def unit_term_kernel(turns, fold, n2, g, dga, dup, q, *refs):
+    share = q.shape[1]
     rest = list(refs)
-    outs = rest[len(rest) - len(turns) - (2 if fold else 0) :]
+    outs = rest[len(rest) - len(turns) - (3 if fold else 0) :]
+    parts = [slice(i * share, (i + 1) * share) for i in range(3)]
+
+    def terms(o):
+        return (
+            lax.dot_general(n2[o], dga[...], TN, preferred_element_type=F32),
+            lax.dot_general(n2[o], dup[...], TN, preferred_element_type=F32),
+        )
+
     for (o, has), out in zip(turns, outs):
         recv = rest.pop(0) if has else None
-        grad = lax.dot_general(n2[o], right[...], TN, preferred_element_type=F32)
-        down = lax.dot_general(g[o], q[:, columns], TN, preferred_element_type=F32)
-        if recv is not None:
-            grad = grad + recv[:, :units].astype(F32)
-            down = down + recv[:, units:].astype(F32)
-        out[:, :units] = grad.astype(BF16)
-        out[:, units:] = down.astype(BF16)
+        down = lax.dot_general(g[o], q[...], TN, preferred_element_type=F32)
+        for grad, columns in zip((*terms(o), down), parts):
+            if recv is not None:
+                grad = grad + recv[:, columns].astype(F32)
+            out[:, columns] = grad.astype(BF16)
     if fold:
         recv = rest.pop(0)
-        grad_o, down_o = outs[len(turns) :]
-        grad = lax.dot_general(n2[0], right[...], TN, preferred_element_type=F32)
-        grad_o[...] = grad + recv[:, :units].astype(F32)
-        down = lax.dot_general(q[:, columns], g[0], TN, preferred_element_type=F32)
-        down_o[...] = down + recv[:, units:].astype(F32).T
-
-
-def unit_term(part, n2, g, right, q, turns, fold, after):
-    block, units = n2.shape[2], right.shape[1]
+        gate_o, up_o, down_o = outs[len(turns) :]
+        for grad, columns, out in zip(terms(0), parts, (gate_o, up_o)):
+            out[...] = grad + recv[:, columns].astype(F32)
+        down = lax.dot_general(q[...], g[0], TN, preferred_element_type=F32)
+        down_o[...] = down + recv[:, parts[2]].astype(F32).T
+
+
+def unit_term(n2, g, dga, dup, q, turns, fold, after, weight=100 * 10**9):
+    block, share = n2.shape[2], q.shape[1]
     arrived = [item for _, item in turns if item is not None] + ([] if fold is None else [fold])
     plan = [(o, item is not None) for o, item in turns]
-    out = [shaped((block, units + units // 2), BF16) for _ in turns]
+    out = [shaped((block, 3 * share), BF16) for _ in turns]
     if fold is not None:
-        out += [shaped((block, units), F32), shaped((units // 2, block), F32)]
-    return launch(
-        lambda *refs: unit_term_kernel(part, plan, fold is not None, *refs),
-        (n2, g, right, q, *arrived),
+        out += [shaped((block, share), F32), shaped((block, share), F32), shaped((share, block), F32)]
+    return launch(
+        lambda *refs: unit_term_kernel(plan, fold is not None, *refs),
+        (n2, g, dga, dup, q, *arrived),
         tuple(out),
         "unit_term",
         after=after,
         mib=24,
-        flops=10**9,
-    )
-
-
-def unit_end_kernel(grad, down, item, grad_o, down_o):
-    units = grad.shape[1]
-    grad_o[...] = grad[...] + item[:, :units].astype(F32)
-    down_o[...] = down[...] + item[:, units:].astype(F32).T
-
-
-def unit_end(own, item, after):
-    grad, down = own
-    return launch(
-        unit_end_kernel,
-        (grad, down, item),
-        (shaped(grad.shape, F32), shaped(down.shape, F32)),
+        flops=weight if arrived else 1,
+    )
+
+
+def unit_end_kernel(count, *refs):
+    own, item, low, outs = refs[:3], refs[3], refs[4 : 4 + count], refs[4 + count :]
+    share = own[0].shape[1]
+    for i in range(2):
+        total = own[i][...] + item[:, i * share : (i + 1) * share].astype(F32)
+        if count:
+            outs[i][:, :share] = low[i][...]
+            outs[i][:, share:] = total
+        else:
+            outs[i][...] = total
+    total = own[2][...] + item[:, 2 * share :].astype(F32).T
+    if count:
+        outs[2][:share, :] = low[2][...]
+        outs[2][share:, :] = total
+    else:
+        outs[2][...] = total
+
+
+def unit_end(low, own, item, after):
+    block, share = own[0].shape
+    wide = 2 if low else 1
+    grad = shaped((block, wide * share), F32)
+    return launch(
+        lambda *refs: unit_end_kernel(len(low), *refs),
+        (*own, item, *low),
+        (grad, grad, shaped((wide * share, block), F32)),
         "unit_end",
         after=after,
-        flops=10**9,
+        flops=100 * 10**9,
     )
 
 
@@ -801,30 +874,49 @@
         scalars=1,
         after=after,
         mib=24,
-        flops=10**9,
+        flops=100 * 10**9,
     )
 
 
 def mixer_end_kernel(part, *refs):
-    own, item, outs = refs[: 3 - part], refs[3 - part], refs[4 - part :]
+    own, item = refs[: 3 - part], refs[3 - part]
+    extra, outs = refs[4 - part : 6 - 2 * part], refs[6 - 2 * part :]
     width, block = own[0].shape
     at = width + own[1].shape[0]
     outs[0][...] = own[0][...] + item[:width, :].astype(F32)
-    outs[1][...] = own[1][...] + item[width:at, :].astype(F32)
+    total = own[1][...] + item[width:at, :].astype(F32)
+    if part == 1:
+        low = extra[0]
+        split = low.shape[0]
+        outs[1][:split, :] = low[...]
+        outs[1][split:, :] = total
+        return
+    outs[1][...] = total
+    chunk = own[2].shape[0]
+    for i, piece in enumerate(small_pieces(width, block)):
+        rows = slice(at + i * chunk, at + (i + 1) * chunk)
+        total = own[2][:, piece] + item[rows, : piece.stop - piece.start].astype(F32)
+        outs[2][:chunk, piece] = total.astype(BF16)
+    ring_size = extra[0].shape[0]
+    lines = jnp.concatenate([extra[0][o] + extra[1][o] for o in range(ring_size)], 0)
+    outs[2][chunk:, :block] = lines.astype(BF16)
+    outs[2][chunk:, block:] = jnp.zeros((2 * ring_size, width - block), BF16)
+
+
+def mixer_end(part, extra, own, item, after):
+    width, block = own[0].shape
     if part == 0:
-        chunk = own[2].shape[0]
-        for i, piece in enumerate(small_pieces(width, block)):
-            rows = slice(at + i * chunk, at + (i + 1) * chunk)
-            total = own[2][:, piece] + item[rows, : piece.stop - piece.start].astype(F32)
-            outs[2][:, piece] = total.astype(BF16)
-
-
-def mixer_end(part, own, item, after):
-    shapes = [shaped(own[0].shape, F32), shaped(own[1].shape, F32)]
-    if part == 0:
-        shapes.append(shaped(own[2].shape, BF16))
-    return launch(
-        lambda *refs: mixer_end_kernel(part, *refs), (*own, item), tuple(shapes), "mixer_end", after=after, flops=10**9
+        rows = own[2].shape[0] + 2 * extra[0].shape[0]
+        shapes = [own[0].shape, own[1].shape, (rows, width)]
+    else:
+        shapes = [own[0].shape, own[0].shape]
+    return launch(
+        lambda *refs: mixer_end_kernel(part, *refs),
+        (*own, item, *extra),
+        tuple(shaped(shape, BF16 if i == 2 else F32) for i, shape in enumerate(shapes)),
+        "mixer_end",
+        after=after,
+        flops=100 * 10**9,
     )
 
 
@@ -951,9 +1043,9 @@
             for d, part in zip(ways, parts):
                 self.moving[d] = lax.ppermute(part, "dp", (onward, backward)[d])
 
-        def end(self):
+        def end(self, *low):
             last = 0 if self.hops[0] > self.hops[1] else 1
-            out = self.ending(self.own, self.moving[last], tuple(token))
+            out = self.ending(low, self.own, self.moving[last], tuple(token))
             mark(out[0])
             return out
 
@@ -969,10 +1061,10 @@
         return jnp.concatenate([own, lax.ppermute(own, "mp", core_pair)], dim)
 
     scalars = jnp.concatenate([core[None], row_length.reshape(-1)]).astype(jnp.int32)
-    gain_lines = jnp.pad(jnp.stack([first_gain, second_gain]), ((0, 14), (0, 0)))
-    gelu_t = gelu_weight.T
-    ring_one = Gather(jnp.concatenate([value_weight.T, gain_lines, gelu_t[:split]]), True)
-    ring_two = Gather(jnp.concatenate([gelu_t[split:], output_weight]), False)
+    shard_one, shard_two = pack(
+        split, value_weight.T, gelu_weight.T, output_weight, first_gain[None], second_gain[None]
+    )
+    ring_one, ring_two = Gather(shard_one, True), Gather(shard_two, False)
     ring_one.step(1)
     ring_two.step(1)
 
@@ -1022,18 +1114,19 @@
     pair, other = chip_swap(own, core_swap(other), ())
     dq = unit_grad(g_flat, mlp_down, (pair,))
     h1, n2_own, r2 = norm(slots, x, gains, pair, other, (dq,))
-    q, dga, dup, n2 = unit_pass(slots, both_halves(n2_own, 0), mlp_gate, mlp_up, dq)
-
-    unit_a = Scatter(lambda *a: unit_term(0, n2, g, dga, q, *a), unit_end, True)
-    unit_b = Scatter(lambda *a: unit_term(1, n2, g, dup, q, *a), unit_end, False)
+    n2 = both_halves(n2_own, 0)
+    q_a, dga_a, dup_a, n2_rel = unit_pass(0, slots, n2, mlp_gate, mlp_up, dq, ())
+    unit_a = Scatter(lambda *a: unit_term(n2_rel, g, dga_a, dup_a, q_a, *a), unit_end, True)
+    unit_a.step(0)
+    q_b, dga_b, dup_b = unit_pass(1, slots, n2, mlp_gate, mlp_up, dq, tuple(token))
+    unit_b = Scatter(lambda *a: unit_term(n2_rel, g, dga_b, dup_b, q_b, *a), unit_end, False)
+    unit_b.step(0)
     last = middle - 1
 
     def now():
         return tuple(token)
 
-    unit_a.step(0)
-    unit_b.step(0)
-    own, other = unit_back(owners, dga, dup, mlp_gate, mlp_up, now())
+    own, other = unit_back(owners, (dga_a, dga_b, dup_a, dup_b), mlp_gate, mlp_up, now())
     mark(own)
     got = core_swap(other)
     for s in range(1, max(last - 1, 1)):
@@ -1050,60 +1143,54 @@
         seqs, head, count, split, small_rows, dhr, two, (bx, by, cx, lx, lr, h, lines, blocks_i, blocks_r), now()
     )
     mark(dbx)
-    out_own, out_other = unit_out(q, mlp_down, now())
+    half_split = width // 2 // 128 * 128
+    mixer_a = Scatter(
+        lambda *a: mixer_term(0, places, half_split, chunk, owners, n1, dhr, dbx, p, small, *a),
+        lambda *a: mixer_end(0, *a),
+        True,
+    )
+    mixer_b = Scatter(
+        lambda *a: mixer_term(1, places, half_split, chunk, owners, n1, dhr, dby, p, None, *a),
+        lambda *a: mixer_end(1, *a),
+        False,
+    )
+    mixer_a.step(0)
+    unit_a.step(last)
+    out_own, out_other = unit_out(q_a, q_b, mlp_down, now())
     mark(out_own)
-    out_got = core_swap(out_other)
-    unit_a.step(last)
-    layer_pair = pair_sum(out_own, out_got, now())
+    layer_pair = pair_sum(out_own, core_swap(out_other), now())
     mark(layer_pair)
-    layer_other = lax.ppermute(layer_pair, "mp", chip_pair)
     own, other = input_out(dbx, dby, one, two, split, now())
     mark(own)
     got = core_swap(other)
     unit_b.step(last)
     pair, other = chip_swap(own, got, now())
-
-    half_split = width // 2 // 128 * 128
-    mixer_a = Scatter(
-        lambda *a: mixer_term(0, places, half_split, chunk, owners, n1, dhr, dbx, p, small, *a),
-        lambda *a: mixer_end(0, *a),
-        True,
-    )
-    mixer_b = Scatter(
-        lambda *a: mixer_term(1, places, half_split, chunk, owners, n1, dhr, dby, p, None, *a),
-        lambda *a: mixer_end(1, *a),
-        False,
-    )
-    mixer_a.step(0)
-    gate_grad, down_low = unit_a.end()
-    up_grad, down_high = unit_b.end()
+    mixer_a.step(1)
+    low = unit_a.end()
     mixer_b.step(0)
+    gate_grad, up_grad, down_grad = unit_b.end(*low)
     input_own, gain_grads = input_back(slots, pair, other, x, r1, gains, dh1, second_grad, now())
     mark(input_own)
-    input_got = core_swap(input_own)
-    for s in range(1, middle):
+    layer_pair = relay(layer_pair, now())
+    mark(layer_pair)
+    layer_other = lax.ppermute(layer_pair, "mp", chip_pair)
+    gain_got = core_swap(gain_grads)
+    for s in range(2, middle):
         mixer_a.step(s)
-        mixer_b.step(s)
-        if s == 1:
-            input_grad = arrange(scalars, input_own, input_got, now())
-            mark(input_grad)
-        elif s == 2:
-            layer_own = finish(slots, h1, layer_pair, layer_other, now())
-            mark(layer_own)
-            layer_got = core_swap(layer_own)
-        elif s == 3:
-            layer_out = arrange(scalars, layer_own, layer_got, now())
-            mark(layer_out)
-    value_grad, output_low, small = mixer_a.end()
-    gain_grads = gain_grads + core_swap(gain_grads)
-    gain_rows = jnp.pad(gain_grads.reshape(2 * ring_size, block), ((0, 0), (0, width - block)))
-    small_ring = Gather(jnp.concatenate([small, gain_rows.astype(BF16)]), True)
-    for s in range(1, middle + 1):
+        if s == middle - 1:
+            both_own = finish(slots, h1, layer_pair, layer_other, input_own, now())
+            mark(both_own)
+        mixer_b.step(s - 1)
+    input_grad, layer_out = arrange(scalars, both_own, core_swap(both_own), now())
+    mark(layer_out)
+    value_grad, output_low, small = mixer_a.end(gain_grads, gain_got)
+    small_ring = Gather(small, True)
+    small_ring.step(1)
+    mark(*token, *small_ring.moving)
+    mixer_b.step(last)
+    for s in range(2, middle + 1):
         small_ring.step(s)
-    gelu_grad, output_high = mixer_b.end()
-    output_grad = jnp.concatenate([output_low, output_high], 0)
-    down_grad = jnp.concatenate([down_low, down_high], 0)
-    down_grad = jnp.concatenate([down_low, down_high], 0)
+    gelu_grad, output_grad = mixer_b.end(output_low)
     gate_i, gate_r, sums, gain_grads = spread(head, block, owners, small_ring.got, now())
 
     return (

time: 488 us -> 451 us (0.924)
  waiting for transfers between devices: 261 us -> 204 us
  starting transfers between devices: 59.9 us -> 70.8 us
  Pallas kernels: 125 us -> 135 us
    ppermute x28, waiting for transfers between devices: 170 us -> 108 us  [step(): self.moving[d] = lax.ppermute(part, 'dp', (onward, backward)[d])]
    ppermute x28, starting transfers between devices: 30.5 us -> 42.5 us  [step(): self.moving[d] = lax.ppermute(part, 'dp', (onward, backward)[d])]
    pallas_call x43 -> x45, Pallas kernels: 114 us -> 124 us  [launch(): pl.pallas_call(lambda *refs: kernel(*refs[:count], *refs[count + extra:])...]
    unnamed x187 -> x176, local copies, waits for them, and re-layouts: 23.6 us -> 23.7 us
  transfers between devices with their start and end apart: 62 -> 61, of which waited for: 38 -> 37; matrix products, arithmetic and copies ran while one was open for 1% -> 1% of each run, Pallas kernels for 20% -> 25%
where the time goes in v3:
time: 451 us; the launch traced here: 443 us
  waiting for transfers between devices  204 us (45%)
  Pallas kernels  135 us (30%)
  starting transfers between devices  70.8 us (16%)
  local copies, waits for them, and re-layouts  29.7 us (7%)
    pallas_call x45, Pallas kernels, launch(): pl.pallas_call(lambda *refs: kernel(*refs[:count], *refs[count + extra:])...  124 us
    ppermute x28, waiting for transfers between devices, step(): self.moving[d] = lax.ppermute(part, 'dp', (onward, backward)[d])  108 us
    ppermute x21, waiting for transfers between devices, step(): self.moving[d] = lax.ppermute(self.moving[d], 'dp', way)  73.7 us
    ppermute x28, starting transfers between devices, step(): self.moving[d] = lax.ppermute(part, 'dp', (onward, backward)[d])  42.5 us
    unnamed x176, local copies, waits for them, and re-layouts  23.7 us
    ppermute x21, starting transfers between devices, step(): self.moving[d] = lax.ppermute(self.moving[d], 'dp', way)  22.2 us
    ppermute x3, waiting for transfers between devices, chip_swap(): return (pair, lax.ppermute(pair, 'mp', chip_pair))  16.8 us
    pallas_call x1, Pallas kernels, unit_back(): pl.pallas_call(unit_back_kernel, grid_spec=pltpu.PrefetchScalarGridSpec(n...  11.4 us
  transfers between devices with their start and end apart: 61, of which 37 were waited for; matrix products, arithmetic and copies ran while one was open for 1% of the time, Pallas kernels for 25%

profile of v3, /device:TPU:0, one launch (start us, length us, event | category | flops | bytes accessed | tf_op | source)
XLA Modules:
  0.0 443.5 jit_solution(17514328077127499319)
XLA Ops:
  5.0 3.1 collective-permute-start
  8.1 2.0 collective-permute-start.2
  19.5 2.1 prepare.1
  21.6 10.4 %collective-permute-done.2.refs_7_.refs_16_.refs_8_.refs_17_ = bf16[1024,256]{1,0:T(8,128)(2,1)S(1)} collective-permute-done((bf16[1024,256]{1,0:T(8,128)(2,1)S(1)}, bf16[1024,256]{1,0:T(8,128)(2,1)S(1)}, u32[]{:S(2)}, u32[]{:S(2)}) %collective-permute-start.2) | collective-permute-done | bytes 524320 | tf_op jit(solution)/shard_map/ppermute | solution.py:1020
  35.9 11.0 %collective-permute-done.4.refs_3_.refs_7_.refs_8_ = bf16[1104,256]{1,0:T(8,128)(2,1)S(1)} collective-permute-done((bf16[1104,256]{1,0:T(8,128)(2,1)S(1)}, bf16[1104,256]{1,0:T(8,128)(2,1)S(1)}, u32[]{:S(2)}, u32[]{:S(2)}) %collective-permute-start.4) | collective-permute-done | bytes 565280 | tf_op jit(solution)/shard_map/ppermute | solution.py:1020
  50.5 11.6 %collective-permute-done.10.refs_2_.refs_3_.refs_4_ = bf16[1104,256]{1,0:T(8,128)(2,1)S(1)} collective-permute-done((bf16[1104,256]{1,0:T(8,128)(2,1)S(1)}, bf16[1104,256]{1,0:T(8,128)(2,1)S(1)}, u32[]{:S(2)}, u32[]{:S(2)}) %collective-permute-start.10) | collective-permute-done | bytes 565280 | tf_op jit(solution)/shard_map/ppermute | solution.py:1020
  64.3 9.7 %collective-permute-done.12.refs_5_.refs_15_.refs_7_.refs_16_ = bf16[1024,256]{1,0:T(8,128)(2,1)S(1)} collective-permute-done((bf16[1024,256]{1,0:T(8,128)(2,1)S(1)}, bf16[1024,256]{1,0:T(8,128)(2,1)S(1)}, u32[]{:S(2)}, u32[]{:S(2)}) %collective-permute-start.12) | collective-permute-done | bytes 524320 | tf_op jit(solution)/shard_map/ppermute | solution.py:1020
  79.3 14.7 %collective-permute-done.13.refs_5_.refs_14_.refs_6_.refs_15_ = bf16[1024,256]{1,0:T(8,128)(2,1)S(1)} collective-permute-done((bf16[1024,256]{1,0:T(8,128)(2,1)S(1)}, bf16[1024,256]{1,0:T(8,128)(2,1)S(1)}, u32[]{:S(2)}, u32[]{:S(2)}) %collective-permute-start.13) | collective-permute-done | bytes 524320 | tf_op jit(solution)/shard_map/ppermute | solution.py:1020
  96.4 7.3 %mixer_forward.1 = (bf16[512,704]{1,0:T(8,128)(2,1)S(1)}, bf16[512,704]{1,0:T(8,128)(2,1)S(1)}, f32[512,704]{1,0:T(8,128)S(1)}, f32[512,704]{1,0:T(8,128)S(1)}, f32[512,704]{1,0:T(8,128)S(1)}) custom-call(f32[512,704]{1,0:T(8,128)S(1)} %get-tuple-element.145.refs_0_.refs_9_, f32[512,704]{1,0:T(8,128)S(1)} %get-tuple-element.146.refs_1_.refs_10_, ...), custom_call_target="tpu_custom_call" | custom-call | flops 1 | bytes 1 | tf_op jit(solution)/shard_map/mixer_forward/pallas_call | solution.py:73
  106.5 2.7 collective-permute-done.14.refs_1_
  110.9 6.9 %unit_grad.1.refs_5_.refs_4_ = f32[512,1536]{1,0:T(8,128)S(1)} custom-call(bf16[512,2048]{1,0:T(8,128)(2,1)S(1)} %get-tuple-element.153.refs_0_, bf16[1536,2048]{1,0:T(8,128)(2,1)} %refs_2_.7, bf16[8,256,256]{2,1,0:T(8,128)(2,1)S(1)} %pair_sum.4.refs_2_.refs_3_.refs_5_), custom_call_target="tpu_custom_call" | custom-call | flops 1 | bytes 1 | tf_op jit(solution)/shard_map/unit_grad/pallas_call | solution.py:73
  117.8 16.7 %collective-permute-done.15.refs_4_ = bf16[8,256,256]{2,1,0:T(8,128)(2,1)S(1)} collective-permute-done((bf16[8,256,256]{2,1,0:T(8,128)(2,1)S(1)}, bf16[8,256,256]{2,1,0:T(8,128)(2,1)S(1)}, u32[]{:S(2)}, u32[]{:S(2)}) %collective-permute-start.15) | collective-permute-done | bytes 1048608 | tf_op jit(solution)/shard_map/ppermute | solution.py:1058
  136.1 2.6 collective-permute-done.16
  138.8 6.6 %unit_pass.2 = (bf16[512,768]{1,0:T(8,128)(2,1)S(1)}, bf16[512,768]{1,0:T(8,128)(2,1)S(1)}, bf16[512,768]{1,0:T(8,128)(2,1)S(1)}, bf16[8,512,256]{2,1,0:T(8,128)(2,1)S(1)}) custom-call(s32[8]{0:T(128)S(1)} %and_select_fusion.1.refs_1_.refs_0_, bf16[512,2048]{1,0:T(8,128)(2,1)S(1)} %constant_dynamic-update-slice_fusion.refs_1_, bf16[2048,1536]{1,0:T(8,128)(2,1)} %gate.1, ...), custom_call_target="tpu_custom_call" | custom-call | flops 1 | bytes 1 | tf_op jit(solution)/shard_map/unit_pass/pallas_call | solution.py:73
  149.0 6.5 %unit_pass.3 = (bf16[512,768]{1,0:T(8,128)(2,1)S(1)}, bf16[512,768]{1,0:T(8,128)(2,1)S(1)}, bf16[512,768]{1,0:T(8,128)(2,1)S(1)}) custom-call(s32[8]{0:T(128)S(1)} %and_select_fusion.1.refs_1_.refs_0_, bf16[512,2048]{1,0:T(8,128)(2,1)S(1)} %constant_dynamic-update-slice_fusion.refs_1_, bf16[2048,1536]{1,0:T(8,128)(2,1)} %gate.1, bf16[2048,1536]{1,0:T(8,128)(2,1)} %up.1, ...), custom_call_target="tpu_custom_call" | custom-call | flops 1 | bytes 1 | tf_op jit(solution)/shard_map/unit_pass/pallas_call | solution.py:73
  158.5 11.4 %unit_back.1 = (f32[8,256,256]{2,1,0:T(8,128)S(1)}, bf16[8,256,256]{2,1,0:T(8,128)(2,1)S(1)}) custom-call(s32[8]{0:T(128)S(1)} %compare_select_fusion.5.owners.refs_0_, bf16[512,768]{1,0:T(8,128)(2,1)S(1)} %get-tuple-element.159.refs_2_.dga_a, bf16[512,768]{1,0:T(8,128)(2,1)S(1)} %get-tuple-element.164.refs_2_.dga_b, ...), custom_call_target="tpu_custom_call" | custom-call | flops 1 | bytes 1 | tf_op jit(solution)/shard_map/unit_back/pallas_call | solution.py:711
  170.5 5.2 %collective-permute-done.17.refs_5_ = bf16[256,2304]{1,0:T(8,128)(2,1)S(1)} collective-permute-done((bf16[256,2304]{1,0:T(8,128)(2,1)S(1)}, bf16[256,2304]{1,0:T(8,128)(2,1)S(1)}, u32[]{:S(2)}, u32[]{:S(2)}) %collective-permute-start.17) | collective-permute-done | bytes 1179680 | tf_op jit(solution)/shard_map/ppermute | solution.py:1044
  177.5 2.7 unit_term.10
  181.8 12.9 %collective-permute-start.20 = (bf16[256,2304]{1,0:T(8,128)(2,1)S(1)}, bf16[256,2304]{1,0:T(8,128)(2,1)S(1)}, u32[]{:S(2)}, u32[]{:S(2)}) collective-permute-start(bf16[256,2304]{1,0:T(8,128)(2,1)S(1)} %get-tuple-element.169), channel_id=1, source_target_pairs={{8,0},{16,8},{24,16},{28,24},{20,28},{12,20},{4,12},{0,4},{9,1},{1... | collective-permute-start | bytes 3538952 | tf_op jit(solution)/shard_map/ppermute | solution.py:1044
  197.3 3.7 collective-permute-done.21.refs_5_
  206.1 20.1 %collective-permute-done.19.refs_5_ = bf16[256,2304]{1,0:T(8,128)(2,1)S(1)} collective-permute-done((bf16[256,2304]{1,0:T(8,128)(2,1)S(1)}, bf16[256,2304]{1,0:T(8,128)(2,1)S(1)}, u32[]{:S(2)}, u32[]{:S(2)}) %collective-permute-start.19) | collective-permute-done | bytes 1179680 | tf_op jit(solution)/shard_map/ppermute | solution.py:1044
  227.9 2.5 unit_term.12
  231.9 3.3 norm_back.1
  237.0 14.5 %collective-permute-done.28.refs_5_ = bf16[256,2304]{1,0:T(8,128)(2,1)S(1)} collective-permute-done((bf16[256,2304]{1,0:T(8,128)(2,1)S(1)}, bf16[256,2304]{1,0:T(8,128)(2,1)S(1)}, u32[]{:S(2)}, u32[]{:S(2)}) %collective-permute-start.28) | collective-permute-done | bytes 1179680 | tf_op jit(solution)/shard_map/ppermute | solution.py:1044
  253.3 2.5 unit_term.13
  262.5 13.8 %mixer_backward.1 = (bf16[512,704]{1,0:T(8,128)(2,1)S(1)}, bf16[512,704]{1,0:T(8,128)(2,1)S(1)}, bf16[384,704]{1,0:T(8,128)(2,1)S(1)}) custom-call(bf16[8,512,256]{2,1,0:T(8,128)(2,1)S(1)} %constant_dynamic-update-slice_fusion.2.refs_0_.refs_5_, bf16[1024,256]{1,0:T(8,128)(2,1)S(1)} %get-tuple-element.132.refs_5_.refs_9_.refs_1_.refs_10_, ...), custom_call_target="tpu_custom_call" | custom-call | flops 1 | bytes 1 | tf_op jit(solution)/shard_map/mixer_backward/pallas_call | solution.py:73
  278.6 3.5 unit_term.14
  282.1 7.7 %unit_out.1 = (f32[256,2048]{1,0:T(8,128)S(1)}, bf16[256,2048]{1,0:T(8,128)(2,1)S(1)}) custom-call(bf16[512,768]{1,0:T(8,128)(2,1)S(1)} %copy-done.41, bf16[512,768]{1,0:T(8,128)(2,1)S(1)} %get-tuple-element.162.refs_4_.refs_1_, bf16[1536,2048]{1,0:T(8,128)(2,1)} %refs_2_.7, bf16[256,2304]{1,0:T(8,128)(2,1)} %get-tuple-element.190.refs_3_), custom_call_target="tpu_custom_call" | custom-call | flops 1 | bytes 1 | tf_op jit(solution)/shard_map/unit_out/pallas_call | solution.py:73
  295.7 4.0 input_out.1
  299.7 4.2 collective-permute-done.32.refs_5_
  303.9 3.5 unit_term.15
  310.8 3.4 collective-permute-done.37.refs_9_
  315.9 2.1 mixer_term.9
  319.6 20.1 %collective-permute-done.36.refs_3_ = bf16[256,2304]{1,0:T(8,128)(2,1)} collective-permute-done((bf16[256,2304]{1,0:T(8,128)(2,1)}, bf16[256,2304]{1,0:T(8,128)(2,1)}, u32[]{:S(2)}, u32[]{:S(2)}) %collective-permute-start.36) | collective-permute-done | bytes 1179680 | tf_op jit(solution)/shard_map/ppermute | solution.py:1044
  341.2 2.3 mixer_term.10
  346.5 3.9 unit_end.3
  351.9 3.6 input_back.1
  364.4 7.7 %collective-permute-done.45.refs_9_ = bf16[1152,256]{1,0:T(8,128)(2,1)} collective-permute-done((bf16[1152,256]{1,0:T(8,128)(2,1)}, bf16[1152,256]{1,0:T(8,128)(2,1)}, u32[]{:S(2)}, u32[]{:S(2)}) %collective-permute-start.45) | collective-permute-done | bytes 589856 | tf_op jit(solution)/shard_map/ppermute | solution.py:1044
  373.0 2.2 mixer_term.12
  377.3 6.8 %collective-permute-done.43.refs_10_ = bf16[1104,256]{1,0:T(8,128)(2,1)S(1)} collective-permute-done((bf16[1104,256]{1,0:T(8,128)(2,1)S(1)}, bf16[1104,256]{1,0:T(8,128)(2,1)S(1)}, u32[]{:S(2)}, u32[]{:S(2)}) %collective-permute-start.43) | collective-permute-done | bytes 565280 | tf_op jit(solution)/shard_map/ppermute | solution.py:1044
  387.0 2.1 finish.1.refs_10_.refs_1_
  389.2 2.3 collective-permute-done.47.refs_8_
  391.5 2.6 collective-permute-done.48.refs_9_
  397.8 4.5 %arrange.1 = (f32[2,256,2048]{2,1,0:T(8,128)}, f32[2,256,2048]{2,1,0:T(8,128)}) custom-call(s32[3]{0:T(128)S(1)} %copy-done.70, f32[2,256,2048]{2,1,0:T(8,128)S(1)} %finish.1.refs_10_.refs_1_, f32[2,256,2048]{2,1,0:T(8,128)S(1)} %collective-permute-done.46.refs_2_, bf16[1152,256]{1,0:T(8,128)(2,1)S(1)} %get-tuple-element.221.refs_3_), custom_call_target="tpu_custom_call" | custom-call | flops 1 | bytes 1 | tf_op jit(solution)/shard_map/arrange/pallas_call | solution.py:73
  403.6 2.2 copy-done.71
  409.6 4.4 %collective-permute-done.59.refs_9_ = bf16[1152,256]{1,0:T(8,128)(2,1)S(1)} collective-permute-done((bf16[1152,256]{1,0:T(8,128)(2,1)S(1)}, bf16[1152,256]{1,0:T(8,128)(2,1)S(1)}, u32[]{:S(2)}, u32[]{:S(2)}) %collective-permute-start.59) | collective-permute-done | bytes 589856 | tf_op jit(solution)/shard_map/ppermute | solution.py:1044
  420.7 2.8 collective-permute-done.55.refs_7_
  424.4 8.5 %collective-permute-done.52.refs_3_ = bf16[64,704]{1,0:T(8,128)(2,1)S(1)} collective-permute-done((bf16[64,704]{1,0:T(8,128)(2,1)S(1)}, bf16[64,704]{1,0:T(8,128)(2,1)S(1)}, u32[]{:S(2)}, u32[]{:S(2)}) %collective-permute-start.52) | collective-permute-done | bytes 90144 | tf_op jit(solution)/shard_map/ppermute | solution.py:1020
  (313 shorter events, 130.7 us)
Async XLA Ops:
  5.0 28.6 %collective-permute-start = (bf16[1104,256]{1,0:T(8,128)(2,1)S(1)}, bf16[1104,256]{1,0:T(8,128)(2,1)S(1)}, u32[]{:S(2)}, u32[]{:S(2)}) collective-permute-start(bf16[1104,256]{1,0:T(8,128)(2,1)S(1)} %get-tuple-element.131.refs_2_.refs_1_), channel_id=1, source_target_pairs={{0,8},{8,16},{16,24},{24,28},{28,20},{20,12},{12,4},{4,0},{1,9},{9... | collective-permute-start | bytes 1695752 | tf_op jit(solution)/shard_map/ppermute | solution.py:1020
  8.1 25.5 %collective-permute-start.1 = (bf16[1104,256]{1,0:T(8,128)(2,1)S(1)}, bf16[1104,256]{1,0:T(8,128)(2,1)S(1)}, u32[]{:S(2)}, u32[]{:S(2)}) collective-permute-start(bf16[1104,256]{1,0:T(8,128)(2,1)S(1)} %get-tuple-element.131.refs_2_.refs_1_), channel_id=1, source_target_pairs={{8,0},{16,8},{24,16},{28,24},{20,28},{12,20},{4,12},{0,4},{9,1},{1... | collective-permute-start | bytes 1695752 | tf_op jit(solution)/shard_map/ppermute | solution.py:1020
  8.1 23.9 %collective-permute-start.2 = (bf16[1024,256]{1,0:T(8,128)(2,1)S(1)}, bf16[1024,256]{1,0:T(8,128)(2,1)S(1)}, u32[]{:S(2)}, u32[]{:S(2)}) collective-permute-start(bf16[1024,256]{1,0:T(8,128)(2,1)S(1)} %get-tuple-element.132.refs_5_.refs_9_.refs_1_.refs_10_), channel_id=1, source_target_pairs={{0,8},{8,16},{16,24},{24,28},{28,20},{20,12},{12,4},{4,0},{1,9},{9... | collective-permute-start | bytes 1572872 | tf_op jit(solution)/shard_map/ppermute | solution.py:1020
  10.1 23.5 %collective-permute-start.3 = (bf16[1024,256]{1,0:T(8,128)(2,1)S(1)}, bf16[1024,256]{1,0:T(8,128)(2,1)S(1)}, u32[]{:S(2)}, u32[]{:S(2)}) collective-permute-start(bf16[1024,256]{1,0:T(8,128)(2,1)S(1)} %get-tuple-element.132.refs_5_.refs_9_.refs_1_.refs_10_), channel_id=1, source_target_pairs={{8,0},{16,8},{24,16},{28,24},{20,28},{12,20},{4,12},{0,4},{9,1},{1... | collective-permute-start | bytes 1572872 | tf_op jit(solution)/shard_map/ppermute | solution.py:1020
  35.2 14.9 %collective-permute-start.7 = (bf16[1024,256]{1,0:T(8,128)(2,1)S(1)}, bf16[1024,256]{1,0:T(8,128)(2,1)S(1)}, u32[]{:S(2)}, u32[]{:S(2)}) collective-permute-start(bf16[1024,256]{1,0:T(8,128)(2,1)S(1)} %collective-permute-done.3.refs_6_.refs_10_.refs_2_.refs_11_), channel_id=1, source_target_pairs={{8,0},{16,8},{24,16},{28,24},{20,28},{12,20},{4,12},{0,4},{9,1},{1... | collective-permute-start | bytes 1572872 | tf_op jit(solution)/shard_map/ppermute | solution.py:1020
  35.6 26.5 %collective-permute-start.10 = (bf16[1104,256]{1,0:T(8,128)(2,1)S(1)}, bf16[1104,256]{1,0:T(8,128)(2,1)S(1)}, u32[]{:S(2)}, u32[]{:S(2)}) collective-permute-start(bf16[1104,256]{1,0:T(8,128)(2,1)S(1)} %collective-permute-done.1.refs_3_.refs_2_), channel_id=1, source_target_pairs={{8,0},{16,8},{24,16},{28,24},{20,28},{12,20},{4,12},{0,4},{9,1},{1... | collective-permute-start | bytes 1695752 | tf_op jit(solution)/shard_map/ppermute | solution.py:1020
  46.9 15.7 %collective-permute-start.5 = (bf16[1104,256]{1,0:T(8,128)(2,1)S(1)}, bf16[1104,256]{1,0:T(8,128)(2,1)S(1)}, u32[]{:S(2)}, u32[]{:S(2)}) collective-permute-start(bf16[1104,256]{1,0:T(8,128)(2,1)S(1)} %collective-permute-done.4.refs_3_.refs_7_.refs_8_), channel_id=1, source_target_pairs={{0,8},{8,16},{16,24},{24,28},{28,20},{20,12},{12,4},{4,0},{1,9},{9... | collective-permute-start | bytes 1695752 | tf_op jit(solution)/shard_map/ppermute | solution.py:1020
  48.5 25.4 %collective-permute-start.12 = (bf16[1024,256]{1,0:T(8,128)(2,1)S(1)}, bf16[1024,256]{1,0:T(8,128)(2,1)S(1)}, u32[]{:S(2)}, u32[]{:S(2)}) collective-permute-start(bf16[1024,256]{1,0:T(8,128)(2,1)S(1)} %collective-permute-done.2.refs_7_.refs_16_.refs_8_.refs_17_), channel_id=1, source_target_pairs={{0,8},{8,16},{16,24},{24,28},{28,20},{20,12},{12,4},{4,0},{1,9},{9... | collective-permute-start | bytes 1572872 | tf_op jit(solution)/shard_map/ppermute | solution.py:1020
  50.1 25.4 %collective-permute-start.8 = (bf16[1024,256]{1,0:T(8,128)(2,1)S(1)}, bf16[1024,256]{1,0:T(8,128)(2,1)S(1)}, u32[]{:S(2)}, u32[]{:S(2)}) collective-permute-start(bf16[1024,256]{1,0:T(8,128)(2,1)S(1)} %collective-permute-done.7.refs_4_.refs_11_.refs_3_.refs_12_), channel_id=1, source_target_pairs={{8,0},{16,8},{24,16},{28,24},{20,28},{12,20},{4,12},{0,4},{9,1},{1... | collective-permute-start | bytes 1572872 | tf_op jit(solution)/shard_map/ppermute | solution.py:1020
  62.1 31.8 %collective-permute-start.11 = (bf16[1104,256]{1,0:T(8,128)(2,1)S(1)}, bf16[1104,256]{1,0:T(8,128)(2,1)S(1)}, u32[]{:S(2)}, u32[]{:S(2)}) collective-permute-start(bf16[1104,256]{1,0:T(8,128)(2,1)S(1)} %collective-permute-done.10.refs_2_.refs_3_.refs_4_), channel_id=1, source_target_pairs={{8,0},{16,8},{24,16},{28,24},{20,28},{12,20},{4,12},{0,4},{9,1},{1... | collective-permute-start | bytes 1695752 | tf_op jit(solution)/shard_map/ppermute | solution.py:1020
  62.7 32.8 %collective-permute-start.6 = (bf16[1104,256]{1,0:T(8,128)(2,1)S(1)}, bf16[1104,256]{1,0:T(8,128)(2,1)S(1)}, u32[]{:S(2)}, u32[]{:S(2)}) collective-permute-start(bf16[1104,256]{1,0:T(8,128)(2,1)S(1)} %collective-permute-done.5.refs_3_.refs_6_.refs_7_), channel_id=1, source_target_pairs={{0,8},{8,16},{16,24},{24,28},{28,20},{20,12},{12,4},{4,0},{1,9},{9... | collective-permute-start | bytes 1695752 | tf_op jit(solution)/shard_map/ppermute | solution.py:1020
  73.9 20.0 %collective-permute-start.13 = (bf16[1024,256]{1,0:T(8,128)(2,1)S(1)}, bf16[1024,256]{1,0:T(8,128)(2,1)S(1)}, u32[]{:S(2)}, u32[]{:S(2)}) collective-permute-start(bf16[1024,256]{1,0:T(8,128)(2,1)S(1)} %collective-permute-done.12.refs_5_.refs_15_.refs_7_.refs_16_), channel_id=1, source_target_pairs={{0,8},{8,16},{16,24},{24,28},{28,20},{20,12},{12,4},{4,0},{1,9},{9... | collective-permute-start | bytes 1572872 | tf_op jit(solution)/shard_map/ppermute | solution.py:1020
  75.5 20.0 %collective-permute-start.9 = (bf16[1024,256]{1,0:T(8,128)(2,1)S(1)}, bf16[1024,256]{1,0:T(8,128)(2,1)S(1)}, u32[]{:S(2)}, u32[]{:S(2)}) collective-permute-start(bf16[1024,256]{1,0:T(8,128)(2,1)S(1)} %collective-permute-done.8.refs_4_.refs_12_.refs_13_), channel_id=1, source_target_pairs={{8,0},{16,8},{24,16},{28,24},{20,28},{12,20},{4,12},{0,4},{9,1},{1... | collective-permute-start | bytes 1572872 | tf_op jit(solution)/shard_map/ppermute | solution.py:1020
  109.3 25.3 %collective-permute-start.15 = (bf16[8,256,256]{2,1,0:T(8,128)(2,1)S(1)}, bf16[8,256,256]{2,1,0:T(8,128)(2,1)S(1)}, u32[]{:S(2)}, u32[]{:S(2)}) collective-permute-start(bf16[8,256,256]{2,1,0:T(8,128)(2,1)S(1)} %pair_sum.4.refs_2_.refs_3_.refs_5_), channel_id=1, source_target_pairs={{0,2},{1,3},{2,0},{3,1},{4,6},{5,7},{6,4},{7,5},{8,10},{9,11},{10,... | collective-permute-start | bytes 3145736 | tf_op jit(solution)/shard_map/ppermute | solution.py:1058
  146.9 28.9 %collective-permute-start.17 = (bf16[256,2304]{1,0:T(8,128)(2,1)S(1)}, bf16[256,2304]{1,0:T(8,128)(2,1)S(1)}, u32[]{:S(2)}, u32[]{:S(2)}) collective-permute-start(bf16[256,2304]{1,0:T(8,128)(2,1)S(1)} %get-tuple-element.161.refs_5_), channel_id=1, source_target_pairs={{0,8},{8,16},{16,24},{24,28},{28,20},{20,12},{12,4},{4,0},{1,9},{9... | collective-permute-start | bytes 3538952 | tf_op jit(solution)/shard_map/ppermute | solution.py:1044
  148.5 29.0 %collective-permute-start.18 = (bf16[256,2304]{1,0:T(8,128)(2,1)S(1)}, bf16[256,2304]{1,0:T(8,128)(2,1)}, u32[]{:S(2)}, u32[]{:S(2)}) collective-permute-start(bf16[256,2304]{1,0:T(8,128)(2,1)S(1)} %get-tuple-element.163), channel_id=1, source_target_pairs={{8,0},{16,8},{24,16},{28,24},{20,28},{12,20},{4,12},{0,4},{9,1},{1... | collective-permute-start | bytes 3538952 | tf_op jit(solution)/shard_map/ppermute | solution.py:1044
  156.9 44.1 %collective-permute-start.21 = (bf16[256,2304]{1,0:T(8,128)(2,1)S(1)}, bf16[256,2304]{1,0:T(8,128)(2,1)S(1)}, u32[]{:S(2)}, u32[]{:S(2)}) collective-permute-start(bf16[256,2304]{1,0:T(8,128)(2,1)S(1)} %get-tuple-element.166.refs_0_), channel_id=1, source_target_pairs={{0,8},{8,16},{16,24},{24,28},{28,20},{20,12},{12,4},{4,0},{1,9},{9... | collective-permute-start | bytes 3538952 | tf_op jit(solution)/shard_map/ppermute | solution.py:1044
  169.9 24.7 %collective-permute-start.23 = (bf16[8,256,256]{2,1,0:T(8,128)(2,1)S(1)}, bf16[8,256,256]{2,1,0:T(8,128)(2,1)S(1)}, u32[]{:S(2)}, u32[]{:S(2)}) collective-permute-start(bf16[8,256,256]{2,1,0:T(8,128)(2,1)S(1)} %get-tuple-element.171), channel_id=1, source_target_pairs={{0,1},{1,0},{2,3},{3,2},{4,5},{5,4},{6,7},{7,6},{8,9},{9,8},{10,11... | collective-permute-start | bytes 3145736 | tf_op jit(solution)/shard_map/ppermute | solution.py:1053
  170.0 32.6 %collective-permute-start.22 = (bf16[256,2304]{1,0:T(8,128)(2,1)S(1)}, bf16[256,2304]{1,0:T(8,128)(2,1)S(1)}, u32[]{:S(2)}, u32[]{:S(2)}) collective-permute-start(bf16[256,2304]{1,0:T(8,128)(2,1)S(1)} %get-tuple-element.170), channel_id=1, source_target_pairs={{8,0},{16,8},{24,16},{28,24},{20,28},{12,20},{4,12},{0,4},{9,1},{1... | collective-permute-start | bytes 3538952 | tf_op jit(solution)/shard_map/ppermute | solution.py:1044
  180.2 46.1 %collective-permute-start.19 = (bf16[256,2304]{1,0:T(8,128)(2,1)S(1)}, bf16[256,2304]{1,0:T(8,128)(2,1)S(1)}, u32[]{:S(2)}, u32[]{:S(2)}) collective-permute-start(bf16[256,2304]{1,0:T(8,128)(2,1)S(1)} %get-tuple-element.168.refs_2_), channel_id=1, source_target_pairs={{0,8},{8,16},{16,24},{24,28},{28,20},{20,12},{12,4},{4,0},{1,9},{9... | collective-permute-start | bytes 3538952 | tf_op jit(solution)/shard_map/ppermute | solution.py:1044
  181.8 46.1 %collective-permute-start.20 = (bf16[256,2304]{1,0:T(8,128)(2,1)S(1)}, bf16[256,2304]{1,0:T(8,128)(2,1)S(1)}, u32[]{:S(2)}, u32[]{:S(2)}) collective-permute-start(bf16[256,2304]{1,0:T(8,128)(2,1)S(1)} %get-tuple-element.169), channel_id=1, source_target_pairs={{8,0},{16,8},{24,16},{28,24},{20,28},{12,20},{4,12},{0,4},{9,1},{1... | collective-permute-start | bytes 3538952 | tf_op jit(solution)/shard_map/ppermute | solution.py:1044
  195.8 36.1 %collective-permute-start.26 = (bf16[8,256,256]{2,1,0:T(8,128)(2,1)}, bf16[8,256,256]{2,1,0:T(8,128)(2,1)}, u32[]{:S(2)}, u32[]{:S(2)}) collective-permute-start(bf16[8,256,256]{2,1,0:T(8,128)(2,1)} %pair_sum.5.refs_7_.refs_0_), channel_id=1, source_target_pairs={{0,2},{1,3},{2,0},{3,1},{4,6},{5,7},{6,4},{7,5},{8,10},{9,11},{10,... | collective-permute-start | bytes 3145736 | tf_op jit(solution)/shard_map/ppermute | solution.py:1058
  204.1 47.5 %collective-permute-start.28 = (bf16[256,2304]{1,0:T(8,128)(2,1)S(1)}, bf16[256,2304]{1,0:T(8,128)(2,1)S(1)}, u32[]{:S(2)}, u32[]{:S(2)}) collective-permute-start(bf16[256,2304]{1,0:T(8,128)(2,1)S(1)} %get-tuple-element.172.refs_7_), channel_id=1, source_target_pairs={{0,8},{8,16},{16,24},{24,28},{28,20},{20,12},{12,4},{4,0},{1,9},{9... | collective-permute-start | bytes 3538952 | tf_op jit(solution)/shard_map/ppermute | solution.py:1044
  205.7 47.5 %collective-permute-start.29 = (bf16[256,2304]{1,0:T(8,128)(2,1)S(1)}, bf16[256,2304]{1,0:T(8,128)(2,1)S(1)}, u32[]{:S(2)}, u32[]{:S(2)}) collective-permute-start(bf16[256,2304]{1,0:T(8,128)(2,1)S(1)} %get-tuple-element.185), channel_id=1, source_target_pairs={{8,0},{16,8},{24,16},{28,24},{20,28},{12,20},{4,12},{0,4},{9,1},{1... | collective-permute-start | bytes 3538952 | tf_op jit(solution)/shard_map/ppermute | solution.py:1044
  230.4 47.3 %collective-permute-start.24 = (bf16[256,2304]{1,0:T(8,128)(2,1)}, bf16[256,2304]{1,0:T(8,128)(2,1)}, u32[]{:S(2)}, u32[]{:S(2)}) collective-permute-start(bf16[256,2304]{1,0:T(8,128)(2,1)} %get-tuple-element.173.refs_6_), channel_id=1, source_target_pairs={{0,8},{8,16},{16,24},{24,28},{28,20},{20,12},{12,4},{4,0},{1,9},{9... | collective-permute-start | bytes 3538952 | tf_op jit(solution)/shard_map/ppermute | solution.py:1044
  236.5 21.3 %collective-permute-start.27 = (bf16[8,256,256]{2,1,0:T(8,128)(2,1)S(1)}, bf16[8,256,256]{2,1,0:T(8,128)(2,1)S(1)}, u32[]{:S(2)}, u32[]{:S(2)}) collective-permute-start(bf16[8,256,256]{2,1,0:T(8,128)(2,1)S(1)} %get-tuple-element.180.refs_7_), channel_id=1, source_target_pairs={{0,1},{1,0},{2,3},{3,2},{4,5},{5,4},{6,7},{7,6},{8,9},{9,8},{10,11... | collective-permute-start | bytes 3145736 | tf_op jit(solution)/shard_map/ppermute | solution.py:1061
  236.5 42.0 %collective-permute-start.25 = (bf16[256,2304]{1,0:T(8,128)(2,1)}, bf16[256,2304]{1,0:T(8,128)(2,1)}, u32[]{:S(2)}, u32[]{:S(2)}) collective-permute-start(bf16[256,2304]{1,0:T(8,128)(2,1)} %get-tuple-element.174), channel_id=1, source_target_pairs={{8,0},{16,8},{24,16},{28,24},{20,28},{12,20},{4,12},{0,4},{9,1},{1... | collective-permute-start | bytes 3538952 | tf_op jit(solution)/shard_map/ppermute | solution.py:1044
  255.8 48.1 %collective-permute-start.32 = (bf16[256,2304]{1,0:T(8,128)(2,1)}, bf16[256,2304]{1,0:T(8,128)(2,1)}, u32[]{:S(2)}, u32[]{:S(2)}) collective-permute-start(bf16[256,2304]{1,0:T(8,128)(2,1)} %get-tuple-element.196), channel_id=1, source_target_pairs={{8,0},{16,8},{24,16},{28,24},{20,28},{12,20},{4,12},{0,4},{9,1},{1... | collective-permute-start | bytes 3538952 | tf_op jit(solution)/shard_map/ppermute | solution.py:1044
  256.2 47.7 %collective-permute-start.33 = (bf16[256,2304]{1,0:T(8,128)(2,1)}, bf16[256,2304]{1,0:T(8,128)(2,1)}, u32[]{:S(2)}, u32[]{:S(2)}) collective-permute-start(bf16[256,2304]{1,0:T(8,128)(2,1)} %get-tuple-element.186.refs_18_), channel_id=1, source_target_pairs={{0,8},{8,16},{16,24},{24,28},{28,20},{20,12},{12,4},{4,0},{1,9},{9... | collective-permute-start | bytes 3538952 | tf_op jit(solution)/shard_map/ppermute | solution.py:1044
  289.9 24.3 %collective-permute-start.37 = (bf16[1104,256]{1,0:T(8,128)(2,1)S(1)}, bf16[1104,256]{1,0:T(8,128)(2,1)S(1)}, u32[]{:S(2)}, u32[]{:S(2)}) collective-permute-start(bf16[1104,256]{1,0:T(8,128)(2,1)S(1)} %get-tuple-element.189.refs_7_), channel_id=1, source_target_pairs={{0,8},{8,16},{16,24},{24,28},{28,20},{20,12},{12,4},{4,0},{1,9},{9... | collective-permute-start | bytes 1695752 | tf_op jit(solution)/shard_map/ppermute | solution.py:1044
  291.5 24.3 %collective-permute-start.38 = (bf16[1104,256]{1,0:T(8,128)(2,1)S(1)}, bf16[1104,256]{1,0:T(8,128)(2,1)S(1)}, u32[]{:S(2)}, u32[]{:S(2)}) collective-permute-start(bf16[1104,256]{1,0:T(8,128)(2,1)S(1)} %get-tuple-element.206), channel_id=1, source_target_pairs={{8,0},{16,8},{24,16},{28,24},{20,28},{12,20},{4,12},{0,4},{9,1},{1... | collective-permute-start | bytes 1695752 | tf_op jit(solution)/shard_map/ppermute | solution.py:1044
  292.6 47.1 %collective-permute-start.36 = (bf16[256,2304]{1,0:T(8,128)(2,1)}, bf16[256,2304]{1,0:T(8,128)(2,1)}, u32[]{:S(2)}, u32[]{:S(2)}) collective-permute-start(bf16[256,2304]{1,0:T(8,128)(2,1)} %get-tuple-element.190.refs_3_), channel_id=1, source_target_pairs={{0,8},{8,16},{16,24},{24,28},{28,20},{20,12},{12,4},{4,0},{1,9},{9... | collective-permute-start | bytes 3538952 | tf_op jit(solution)/shard_map/ppermute | solution.py:1044
  307.4 38.2 %collective-permute-start.35 = (bf16[256,2304]{1,0:T(8,128)(2,1)}, bf16[256,2304]{1,0:T(8,128)(2,1)}, u32[]{:S(2)}, u32[]{:S(2)}) collective-permute-start(bf16[256,2304]{1,0:T(8,128)(2,1)} %get-tuple-element.197.refs_2_), channel_id=1, source_target_pairs={{8,0},{16,8},{24,16},{28,24},{20,28},{12,20},{4,12},{0,4},{9,1},{1... | collective-permute-start | bytes 3538952 | tf_op jit(solution)/shard_map/ppermute | solution.py:1044
  309.3 41.2 %collective-permute-start.34 = (bf16[8,256,256]{2,1,0:T(8,128)(2,1)}, bf16[8,256,256]{2,1,0:T(8,128)(2,1)}, u32[]{:S(2)}, u32[]{:S(2)}) collective-permute-start(bf16[8,256,256]{2,1,0:T(8,128)(2,1)} %pair_sum.7.refs_11_.refs_1_), channel_id=1, source_target_pairs={{0,2},{1,3},{2,0},{3,1},{4,6},{5,7},{6,4},{7,5},{8,10},{9,11},{10,... | collective-permute-start | bytes 3145736 | tf_op jit(solution)/shard_map/ppermute | solution.py:1058
  318.0 40.5 %collective-permute-start.40 = (bf16[1104,256]{1,0:T(8,128)(2,1)}, bf16[1104,256]{1,0:T(8,128)(2,1)}, u32[]{:S(2)}, u32[]{:S(2)}) collective-permute-start(bf16[1104,256]{1,0:T(8,128)(2,1)} %get-tuple-element.207.refs_4_), channel_id=1, source_target_pairs={{0,8},{8,16},{16,24},{24,28},{28,20},{20,12},{12,4},{4,0},{1,9},{9... | collective-permute-start | bytes 1695752 | tf_op jit(solution)/shard_map/ppermute | solution.py:1044
  343.6 15.7 %collective-permute-start.41 = (bf16[1104,256]{1,0:T(8,128)(2,1)S(1)}, bf16[1104,256]{1,0:T(8,128)(2,1)S(1)}, u32[]{:S(2)}, u32[]{:S(2)}) collective-permute-start(bf16[1104,256]{1,0:T(8,128)(2,1)S(1)} %get-tuple-element.214), channel_id=1, source_target_pairs={{8,0},{16,8},{24,16},{28,24},{20,28},{12,20},{4,12},{0,4},{9,1},{1... | collective-permute-start | bytes 1695752 | tf_op jit(solution)/shard_map/ppermute | solution.py:1044
  344.5 19.9 %collective-permute-start.44 = (bf16[1152,256]{1,0:T(8,128)(2,1)}, bf16[1152,256]{1,0:T(8,128)(2,1)}, u32[]{:S(2)}, u32[]{:S(2)}) collective-permute-start(bf16[1152,256]{1,0:T(8,128)(2,1)} %get-tuple-element.211.refs_7_), channel_id=1, source_target_pairs={{0,8},{8,16},{16,24},{24,28},{28,20},{20,12},{12,4},{4,0},{1,9},{9... | collective-permute-start | bytes 1769480 | tf_op jit(solution)/shard_map/ppermute | solution.py:1044
  345.6 26.5 %collective-permute-start.45 = (bf16[1152,256]{1,0:T(8,128)(2,1)}, bf16[1152,256]{1,0:T(8,128)(2,1)}, u32[]{:S(2)}, u32[]{:S(2)}) collective-permute-start(bf16[1152,256]{1,0:T(8,128)(2,1)} %get-tuple-element.217), channel_id=1, source_target_pairs={{8,0},{16,8},{24,16},{28,24},{20,28},{12,20},{4,12},{0,4},{9,1},{1... | collective-permute-start | bytes 1769480 | tf_op jit(solution)/shard_map/ppermute | solution.py:1044
  357.2 29.9 %collective-permute-start.39 = (bf16[256,2048]{1,0:T(8,128)(2,1)}, bf16[256,2048]{1,0:T(8,128)(2,1)}, u32[]{:S(2)}, u32[]{:S(2)}) collective-permute-start(bf16[256,2048]{1,0:T(8,128)(2,1)} %relay.1.refs_11_.refs_2_), channel_id=1, source_target_pairs={{0,2},{1,3},{2,0},{3,1},{4,6},{5,7},{6,4},{7,5},{8,10},{9,11},{10,... | collective-permute-start | bytes 3145736 | tf_op jit(solution)/shard_map/ppermute | solution.py:1176
  361.2 16.1 %collective-permute-start.42 = (bf16[1104,256]{1,0:T(8,128)(2,1)S(1)}, bf16[1104,256]{1,0:T(8,128)(2,1)S(1)}, u32[]{:S(2)}, u32[]{:S(2)}) collective-permute-start(bf16[1104,256]{1,0:T(8,128)(2,1)S(1)} %get-tuple-element.215.refs_10_), channel_id=1, source_target_pairs={{0,8},{8,16},{16,24},{24,28},{28,20},{20,12},{12,4},{4,0},{1,9},{9... | collective-permute-start | bytes 1695752 | tf_op jit(solution)/shard_map/ppermute | solution.py:1044
  362.8 21.3 %collective-permute-start.43 = (bf16[1104,256]{1,0:T(8,128)(2,1)S(1)}, bf16[1104,256]{1,0:T(8,128)(2,1)S(1)}, u32[]{:S(2)}, u32[]{:S(2)}) collective-permute-start(bf16[1104,256]{1,0:T(8,128)(2,1)S(1)} %get-tuple-element.216), channel_id=1, source_target_pairs={{8,0},{16,8},{24,16},{28,24},{20,28},{12,20},{4,12},{0,4},{9,1},{1... | collective-permute-start | bytes 1695752 | tf_op jit(solution)/shard_map/ppermute | solution.py:1044
  375.2 16.3 %collective-permute-start.47 = (bf16[1152,256]{1,0:T(8,128)(2,1)S(1)}, bf16[1152,256]{1,0:T(8,128)(2,1)S(1)}, u32[]{:S(2)}, u32[]{:S(2)}) collective-permute-start(bf16[1152,256]{1,0:T(8,128)(2,1)S(1)} %get-tuple-element.218.refs_11_), channel_id=1, source_target_pairs={{0,8},{8,16},{16,24},{24,28},{28,20},{20,12},{12,4},{4,0},{1,9},{9... | collective-permute-start | bytes 1769480 | tf_op jit(solution)/shard_map/ppermute | solution.py:1044
  376.9 17.3 %collective-permute-start.48 = (bf16[1152,256]{1,0:T(8,128)(2,1)S(1)}, bf16[1152,256]{1,0:T(8,128)(2,1)S(1)}, u32[]{:S(2)}, u32[]{:S(2)}) collective-permute-start(bf16[1152,256]{1,0:T(8,128)(2,1)S(1)} %get-tuple-element.220), channel_id=1, source_target_pairs={{8,0},{16,8},{24,16},{28,24},{20,28},{12,20},{4,12},{0,4},{9,1},{1... | collective-permute-start | bytes 1769480 | tf_op jit(solution)/shard_map/ppermute | solution.py:1044
  377.3 24.9 %collective-permute-start.50 = (f32[8,2,256]{2,1,0:T(2,128)}, f32[8,2,256]{2,1,0:T(2,128)}, u32[]{:S(2)}, u32[]{:S(2)}) collective-permute-start(f32[8,2,256]{2,1,0:T(2,128)} %get-tuple-element.227.refs_4_), channel_id=1, source_target_pairs={{0,1},{1,0},{2,3},{3,2},{4,5},{5,4},{6,7},{7,6},{8,9},{9,8},{10,11... | collective-permute-start | bytes 49160 | tf_op jit(solution)/shard_map/ppermute | solution.py:1053
  385.4 18.3 %collective-permute-start.49 = (bf16[1104,256]{1,0:T(8,128)(2,1)S(1)}, bf16[1104,256]{1,0:T(8,128)(2,1)S(1)}, u32[]{:S(2)}, u32[]{:S(2)}) collective-permute-start(bf16[1104,256]{1,0:T(8,128)(2,1)S(1)} %get-tuple-element.219.refs_5_), channel_id=1, source_target_pairs={{0,8},{8,16},{16,24},{24,28},{28,20},{20,12},{12,4},{4,0},{1,9},{9... | collective-permute-start | bytes 1695752 | tf_op jit(solution)/shard_map/ppermute | solution.py:1044
  395.7 13.9 %collective-permute-start.58 = (bf16[1152,256]{1,0:T(8,128)(2,1)S(1)}, bf16[1152,256]{1,0:T(8,128)(2,1)S(1)}, u32[]{:S(2)}, u32[]{:S(2)}) collective-permute-start(bf16[1152,256]{1,0:T(8,128)(2,1)S(1)} %get-tuple-element.229), channel_id=1, source_target_pairs={{8,0},{16,8},{24,16},{28,24},{20,28},{12,20},{4,12},{0,4},{9,1},{1... | collective-permute-start | bytes 1769480 | tf_op jit(solution)/shard_map/ppermute | solution.py:1044
  396.7 17.4 %collective-permute-start.59 = (bf16[1152,256]{1,0:T(8,128)(2,1)S(1)}, bf16[1152,256]{1,0:T(8,128)(2,1)S(1)}, u32[]{:S(2)}, u32[]{:S(2)}) collective-permute-start(bf16[1152,256]{1,0:T(8,128)(2,1)S(1)} %get-tuple-element.221.refs_3_), channel_id=1, source_target_pairs={{0,8},{8,16},{16,24},{24,28},{28,20},{20,12},{12,4},{4,0},{1,9},{9... | collective-permute-start | bytes 1769480 | tf_op jit(solution)/shard_map/ppermute | solution.py:1044
  417.7 17.3 %collective-permute-start.60 = (bf16[1152,256]{1,0:T(8,128)(2,1)S(1)}, bf16[1152,256]{1,0:T(8,128)(2,1)S(1)}, u32[]{:S(2)}, u32[]{:S(2)}) collective-permute-start(bf16[1152,256]{1,0:T(8,128)(2,1)S(1)} %get-tuple-element.233.refs_4_), channel_id=1, source_target_pairs={{8,0},{16,8},{24,16},{28,24},{20,28},{12,20},{4,12},{0,4},{9,1},{1... | collective-permute-start | bytes 1769480 | tf_op jit(solution)/shard_map/ppermute | solution.py:1044
  (100 other events, 1908.3 us)

commit v4 on v3

--- a/solution.py
+++ b/solution.py
@@ -14,6 +14,8 @@
 STEP = 16
 HALF = 8
 SUMS = 8
+HEAVY = 100 * 10**9
+END_WEIGHT = 1
 TN = (((0,), (0,)), ((), ()))
 NT = (((1,), (1,)), ((), ()))
 
@@ -291,24 +293,39 @@
     )
 
 
-def pack_kernel(split, value, gelu_w, output, gain_one, gain_two, one_o, two_o):
+def pack_kernel(split, gain_one, gain_two, value, gelu_w, output, one_o, two_o, sems):
     width = value.shape[0]
-    one_o[:width, :] = value[...]
+    copies = [
+        pltpu.make_async_copy(source, target, sems.at[i])
+        for i, (source, target) in enumerate(
+            (
+                (value, one_o.at[pl.ds(0, width)]),
+                (gelu_w.at[pl.ds(0, split)], one_o.at[pl.ds(width + 16, split)]),
+                (gelu_w.at[pl.ds(split, width - split)], two_o.at[pl.ds(0, width - split)]),
+                (output, two_o.at[pl.ds(width - split, width)]),
+            )
+        )
+    ]
+    for copy in copies:
+        copy.start()
     spare = jnp.zeros((14, value.shape[1]), F32)
     lines = jnp.concatenate([gain_one[...].astype(F32), gain_two[...].astype(F32), spare], 0)
     one_o[width : width + 16, :] = lines.astype(BF16)
-    one_o[width + 16 :, :] = gelu_w[:split, :]
-    two_o[: width - split, :] = gelu_w[split:, :]
-    two_o[width - split :, :] = output[...]
+    for copy in copies:
+        copy.wait()
 
 
 def pack(split, value, gelu_w, output, gain_one, gain_two):
     width, block = value.shape
+    whole = pl.BlockSpec(memory_space=pltpu.VMEM)
+    anywhere = pl.BlockSpec(memory_space=pl.ANY)
     return launch(
         lambda *refs: pack_kernel(split, *refs),
-        (value, gelu_w, output, gain_one, gain_two),
+        (gain_one, gain_two, in_hbm(value), in_hbm(gelu_w), in_hbm(output)),
         (shaped((width + 16 + split, block), BF16), shaped((2 * width - split, block), BF16)),
         "pack",
+        scratch=[pltpu.SemaphoreType.DMA((4,))],
+        grid=((), [whole, whole, anywhere, anywhere, anywhere], [whole, whole]),
     )
 
 
@@ -605,50 +622,96 @@
     return launch(unit_grad_kernel, (g, in_hbm(down)), shaped((total, units), F32), "unit_grad", after=after, grid=grid)
 
 
-def unit_kernel(with_rel, slots, n2, gate, up, dq, q_o, dga_o, dup_o, *rel):
-    if with_rel:
-        rel_o = rel[0]
-        ring_size, total, block = rel_o.shape
-
-        @pl.when(pl.program_id(0) == 0)
-        def _():
-            for k in range(ring_size):
-                rel_o[slots[k]] = n2[:, k * block : (k + 1) * block]
-
+def fetch_kernel(gate, up, gate_o, up_o, sems):
+    columns = pl.ds(0, gate_o.shape[1])
+    copies = [
+        pltpu.make_async_copy(source.at[:, columns], target, sems.at[i])
+        for i, (source, target) in enumerate(((gate, gate_o), (up, up_o)))
+    ]
+    for copy in copies:
+        copy.start()
+    for copy in copies:
+        copy.wait()
+
+
+def fetch(gate, up, after):
+    model, units = gate.shape
+    whole = pl.BlockSpec(memory_space=pltpu.VMEM)
+    anywhere = pl.BlockSpec(memory_space=pl.ANY)
+    half = shaped((model, units // 2), BF16)
+    return launch(
+        fetch_kernel,
+        (in_hbm(gate), in_hbm(up)),
+        (half, half),
+        "fetch",
+        after=after,
+        scratch=[pltpu.SemaphoreType.DMA((2,))],
+        grid=((), [anywhere, anywhere], [whole, whole]),
+    )
+
+
+def unit_products(ga, upward, grad):
+    value, slope = gelu_both(ga)
+    return value * upward, grad * upward * slope, grad * value
+
+
+def unit_first_kernel(slots, n2, gate, up, dq, q_o, dga_o, dup_o, rel_o):
+    ring_size, total, block = rel_o.shape
+    tile = 256
+    for i in range(0, gate.shape[1], tile):
+        columns = slice(i, i + tile)
+        ga = jnp.dot(n2[...], gate[:, columns], preferred_element_type=F32)
+        upward = jnp.dot(n2[...], up[:, columns], preferred_element_type=F32)
+        for out, item in zip((q_o, dga_o, dup_o), unit_products(ga, upward, dq[:, columns])):
+            out[:, columns] = item.astype(BF16)
+    for k in range(ring_size):
+        rel_o[slots[k]] = n2[:, k * block : (k + 1) * block]
+
+
+def unit_first(slots, n2, gate, up, dq):
+    total, model = n2.shape
+    ring_size = slots.shape[0]
+    out = shaped((total, gate.shape[1]), BF16)
+    return launch(
+        unit_first_kernel,
+        (slots, n2, gate, up, dq),
+        (out, out, out, shaped((ring_size, total, model // ring_size), BF16)),
+        "unit_first",
+        scalars=1,
+        mib=28,
+    )
+
+
+def unit_kernel(n2, gate, up, dq, q_o, dga_o, dup_o):
     ga = jnp.dot(n2[...], gate[...], preferred_element_type=F32)
     upward = jnp.dot(n2[...], up[...], preferred_element_type=F32)
-    value, slope = gelu_both(ga)
-    grad = dq[...]
-    q_o[...] = (value * upward).astype(BF16)
-    dga_o[...] = (grad * upward * slope).astype(BF16)
-    dup_o[...] = (grad * value).astype(BF16)
-
-
-def unit_pass(part, slots, n2, gate, up, dq, after):
+    for out, item in zip((q_o, dga_o, dup_o), unit_products(ga, upward, dq[...])):
+        out[...] = item.astype(BF16)
+
+
+def unit_second(n2, gate, up, dq, after):
     total, model = n2.shape
-    ring_size = slots.shape[0]
     share = gate.shape[1] // 2
     tile = 256
-    first = part * (share // tile)
-    rel = (ring_size, total, model // ring_size)
+    first = share // tile
     wide = pl.BlockSpec((total, tile), lambda i: (0, i))
+    tall = pl.BlockSpec((model, tile), lambda i: (0, i + first))
     out = shaped((total, share), BF16)
     grid = (
         (share // tile,),
         [
             pl.BlockSpec((total, model), lambda i: (0, 0)),
-            pl.BlockSpec((model, tile), lambda i: (0, i + first)),
-            pl.BlockSpec((model, tile), lambda i: (0, i + first)),
+            tall,
+            tall,
             pl.BlockSpec((total, tile), lambda i: (0, i + first)),
         ],
-        [wide, wide, wide] + [pl.BlockSpec(rel, lambda i: (0, 0, 0))] * (1 - part),
-    )
-    return launch(
-        lambda *refs: unit_kernel(part == 0, *refs),
-        (slots, n2, in_hbm(gate), in_hbm(up), dq),
-        (out, out, out) + (shaped(rel, BF16),) * (1 - part),
-        "unit_pass",
-        scalars=1,
+        [wide, wide, wide],
+    )
+    return launch(
+        unit_kernel,
+        (n2, in_hbm(gate), in_hbm(up), dq),
+        (out, out, out),
+        "unit_second",
         after=after,
         mib=28,
         grid=grid,
@@ -751,7 +814,7 @@
         down_o[...] = down + recv[:, parts[2]].astype(F32).T
 
 
-def unit_term(n2, g, dga, dup, q, turns, fold, after, weight=100 * 10**9):
+def unit_term(n2, g, dga, dup, q, turns, fold, after, weight):
     block, share = n2.shape[2], q.shape[1]
     arrived = [item for _, item in turns if item is not None] + ([] if fold is None else [fold])
     plan = [(o, item is not None) for o, item in turns]
@@ -765,7 +828,7 @@
         "unit_term",
         after=after,
         mib=24,
-        flops=weight if arrived else 1,
+        flops=weight,
     )
 
 
@@ -797,7 +860,7 @@
         (grad, grad, shaped((wide * share, block), F32)),
         "unit_end",
         after=after,
-        flops=100 * 10**9,
+        flops=END_WEIGHT,
     )
 
 
@@ -856,7 +919,7 @@
                 outs[len(turns) + 2][:, piece] = total
 
 
-def mixer_term(part, places, split, chunk, owners, n1, dhr, grads, p, extra, turns, fold, after):
+def mixer_term(part, places, split, chunk, owners, n1, dhr, grads, p, extra, turns, fold, after, weight):
     block, width = dhr.shape[2], grads.shape[1]
     size = split if part == 0 else width - split
     arrived = [item for _, item in turns if item is not None] + ([] if fold is None else [fold])
@@ -874,7 +937,7 @@
         scalars=1,
         after=after,
         mib=24,
-        flops=100 * 10**9,
+        flops=weight,
     )
 
 
@@ -916,13 +979,13 @@
         tuple(shaped(shape, BF16 if i == 2 else F32) for i, shape in enumerate(shapes)),
         "mixer_end",
         after=after,
-        flops=100 * 10**9,
+        flops=HEAVY,
     )
 
 
 def spread_kernel(head, owners, *refs):
     ring_size = owners.shape[0]
-    gate_i, gate_r, sums, gain_o, whole = refs[ring_size:]
+    gate_i, gate_r, taps, sums, gain_o, whole = refs[ring_size:]
     block = gain_o.shape[1]
     chunk = refs[0].shape[0] - 2 * ring_size
     gain = jnp.zeros((2, block), F32)
@@ -933,18 +996,20 @@
         gain = gain + refs[o][chunk:, :block].astype(F32)[mine : mine + 2, :]
     gate_i[...] = whole[:head, :]
     gate_r[...] = whole[head : 2 * head, :]
-    sums[...] = whole[2 * head : 2 * head + SUMS, :]
+    count = taps.shape[0]
+    taps[...] = whole[2 * head : 2 * head + count, :]
+    sums[...] = whole[2 * head + count : 2 * head + SUMS, :]
     gain_o[...] = gain
 
 
-def spread(head, block, owners, chunks, after):
+def spread(head, count, block, owners, chunks, after):
     ring_size = len(chunks)
     rows, width = chunks[0].shape
     gate = shaped((head, width), F32)
     return launch(
         lambda *refs: spread_kernel(head, *refs),
         (owners, *chunks),
-        (gate, gate, shaped((SUMS, width), F32), shaped((2, block), F32)),
+        (gate, gate, shaped((count, width), F32), shaped((SUMS - count, width), F32), shaped((2, block), F32)),
         "spread",
         scalars=1,
         after=after,
@@ -1027,7 +1092,7 @@
             self.moving = [None, None]
             self.own = None
 
-        def step(self, s):
+        def step(self, s, weight=HEAVY, apart=False):
             turns, ways, fold = [], [], None
             for d in range(2):
                 far = self.hops[d] - s
@@ -1036,12 +1101,15 @@
                     ways.append(d)
                 elif far == 0:
                     fold = self.moving[d]
-            parts = self.term(turns, fold, tuple(token))
-            if fold is not None:
-                self.own = parts[len(turns) :]
+            parts = self.term(turns, None if apart else fold, tuple(token), weight)
             mark(parts[0])
             for d, part in zip(ways, parts):
                 self.moving[d] = lax.ppermute(part, "dp", (onward, backward)[d])
+            if fold is not None:
+                self.own = parts[len(turns) :]
+                if apart:
+                    self.own = self.term([], fold, tuple(token), weight)
+                    mark(self.own[0])
 
         def end(self, *low):
             last = 0 if self.hops[0] > self.hops[1] else 1
@@ -1113,14 +1181,15 @@
     own, other, gains = mixer_out(p, one, two, split)
     pair, other = chip_swap(own, core_swap(other), ())
     dq = unit_grad(g_flat, mlp_down, (pair,))
-    h1, n2_own, r2 = norm(slots, x, gains, pair, other, (dq,))
+    fetched = fetch(mlp_gate, mlp_up, (dq,))
+    h1, n2_own, r2 = norm(slots, x, gains, pair, other, (fetched[0],))
     n2 = both_halves(n2_own, 0)
-    q_a, dga_a, dup_a, n2_rel = unit_pass(0, slots, n2, mlp_gate, mlp_up, dq, ())
+    q_a, dga_a, dup_a, n2_rel = unit_first(slots, n2, *fetched, dq)
     unit_a = Scatter(lambda *a: unit_term(n2_rel, g, dga_a, dup_a, q_a, *a), unit_end, True)
     unit_a.step(0)
-    q_b, dga_b, dup_b = unit_pass(1, slots, n2, mlp_gate, mlp_up, dq, tuple(token))
+    q_b, dga_b, dup_b = unit_second(n2, mlp_gate, mlp_up, dq, tuple(token))
     unit_b = Scatter(lambda *a: unit_term(n2_rel, g, dga_b, dup_b, q_b, *a), unit_end, False)
-    unit_b.step(0)
+    unit_b.step(0, 1)
     last = middle - 1
 
     def now():
@@ -1167,7 +1236,7 @@
     pair, other = chip_swap(own, got, now())
     mixer_a.step(1)
     low = unit_a.end()
-    mixer_b.step(0)
+    mixer_b.step(0, 1)
     gate_grad, up_grad, down_grad = unit_b.end(*low)
     input_own, gain_grads = input_back(slots, pair, other, x, r1, gains, dh1, second_grad, now())
     mark(input_own)
@@ -1185,13 +1254,11 @@
     mark(layer_out)
     value_grad, output_low, small = mixer_a.end(gain_grads, gain_got)
     small_ring = Gather(small, True)
-    small_ring.step(1)
-    mark(*token, *small_ring.moving)
-    mixer_b.step(last)
-    for s in range(2, middle + 1):
+    mixer_b.step(last, 1, True)
+    for s in range(1, middle + 1):
         small_ring.step(s)
     gelu_grad, output_grad = mixer_b.end(output_low)
-    gate_i, gate_r, sums, gain_grads = spread(head, block, owners, small_ring.got, now())
+    gate_i, gate_r, taps_grad, sums, gain_grads = spread(head, count, block, owners, small_ring.got, now())
 
     return (
         layer_out.reshape(tokens.shape),
@@ -1199,13 +1266,13 @@
         gain_grads[0],
         value_grad.T,
         gelu_grad.T,
-        sums[:count],
-        sums[count],
+        taps_grad,
+        sums[0],
         gate_i.T,
-        sums[count + 1],
+        sums[1],
         gate_r.T,
-        sums[count + 2],
-        sums[count + 3],
+        sums[2],
+        sums[3],
         output_grad,
         gain_grads[1],
         gate_grad,

time: 451 us -> 443 us (0.982)
  starting transfers between devices: 70.8 us -> 58.8 us
  waiting for transfers between devices: 204 us -> 211 us
    ppermute x28, starting transfers between devices: 42.5 us -> 29.5 us  [step(): self.moving[d] = lax.ppermute(part, 'dp', (onward, backward)[d])]
    ppermute x28, waiting for transfers between devices: 108 us -> 116 us  [step(): self.moving[d] = lax.ppermute(part, 'dp', (onward, backward)[d])]
    pallas_call x45 -> x47, Pallas kernels: 124 us -> 120 us  [launch(): pl.pallas_call(lambda *refs: kernel(*refs[:count], *refs[count + extra:])...]
    unnamed x176 -> x166, local copies, waits for them, and re-layouts: 23.7 us -> 25.4 us
where the time goes in v4:
time: 443 us; the launch traced here: 436 us
  waiting for transfers between devices  211 us (48%)
  Pallas kernels  132 us (30%)
  starting transfers between devices  58.8 us (13%)
  local copies, waits for them, and re-layouts  30.8 us (7%)
    pallas_call x47, Pallas kernels, launch(): pl.pallas_call(lambda *refs: kernel(*refs[:count], *refs[count + extra:])...  120 us
    ppermute x28, waiting for transfers between devices, step(): self.moving[d] = lax.ppermute(part, 'dp', (onward, backward)[d])  116 us
    ppermute x21, waiting for transfers between devices, step(): self.moving[d] = lax.ppermute(self.moving[d], 'dp', way)  75.1 us
    ppermute x28, starting transfers between devices, step(): self.moving[d] = lax.ppermute(part, 'dp', (onward, backward)[d])  29.5 us
    unnamed x166, local copies, waits for them, and re-layouts  25.4 us
    ppermute x21, starting transfers between devices, step(): self.moving[d] = lax.ppermute(self.moving[d], 'dp', way)  22.7 us
    ppermute x3, waiting for transfers between devices, chip_swap(): return (pair, lax.ppermute(pair, 'mp', chip_pair))  13.9 us
    pallas_call x1, Pallas kernels, unit_back(): pl.pallas_call(unit_back_kernel, grid_spec=pltpu.PrefetchScalarGridSpec(n...  11.5 us
  transfers between devices with their start and end apart: 61, of which 37 were waited for; matrix products, arithmetic and copies ran while one was open for 1% of the time, Pallas kernels for 25%

profile of v4, /device:TPU:0, one launch (start us, length us, event | category | flops | bytes accessed | tf_op | source)
XLA Modules:
  0.0 435.6 jit_solution(9467919964667376411)
XLA Ops:
  3.3 3.1 collective-permute-start
  6.3 2.0 collective-permute-start.2
  17.7 2.1 prepare.1
  19.8 10.5 %collective-permute-done.2.refs_7_.refs_16_.refs_8_.refs_17_ = bf16[1024,256]{1,0:T(8,128)(2,1)S(1)} collective-permute-done((bf16[1024,256]{1,0:T(8,128)(2,1)S(1)}, bf16[1024,256]{1,0:T(8,128)(2,1)S(1)}, u32[]{:S(2)}, u32[]{:S(2)}) %collective-permute-start.2) | collective-permute-done | bytes 524320 | tf_op jit(solution)/shard_map/ppermute | solution.py:1085
  34.2 11.0 %collective-permute-done.4.refs_3_.refs_7_.refs_8_ = bf16[1104,256]{1,0:T(8,128)(2,1)S(1)} collective-permute-done((bf16[1104,256]{1,0:T(8,128)(2,1)S(1)}, bf16[1104,256]{1,0:T(8,128)(2,1)S(1)}, u32[]{:S(2)}, u32[]{:S(2)}) %collective-permute-start.4) | collective-permute-done | bytes 565280 | tf_op jit(solution)/shard_map/ppermute | solution.py:1085
  48.8 11.6 %collective-permute-done.10.refs_2_.refs_3_.refs_4_ = bf16[1104,256]{1,0:T(8,128)(2,1)S(1)} collective-permute-done((bf16[1104,256]{1,0:T(8,128)(2,1)S(1)}, bf16[1104,256]{1,0:T(8,128)(2,1)S(1)}, u32[]{:S(2)}, u32[]{:S(2)}) %collective-permute-start.10) | collective-permute-done | bytes 565280 | tf_op jit(solution)/shard_map/ppermute | solution.py:1085
  62.5 9.7 %collective-permute-done.12.refs_5_.refs_15_.refs_7_.refs_16_ = bf16[1024,256]{1,0:T(8,128)(2,1)S(1)} collective-permute-done((bf16[1024,256]{1,0:T(8,128)(2,1)S(1)}, bf16[1024,256]{1,0:T(8,128)(2,1)S(1)}, u32[]{:S(2)}, u32[]{:S(2)}) %collective-permute-start.12) | collective-permute-done | bytes 524320 | tf_op jit(solution)/shard_map/ppermute | solution.py:1085
  74.2 1.8 project.4
  77.5 14.7 %collective-permute-done.13.refs_5_.refs_14_.refs_6_.refs_15_ = bf16[1024,256]{1,0:T(8,128)(2,1)S(1)} collective-permute-done((bf16[1024,256]{1,0:T(8,128)(2,1)S(1)}, bf16[1024,256]{1,0:T(8,128)(2,1)S(1)}, u32[]{:S(2)}, u32[]{:S(2)}) %collective-permute-start.13) | collective-permute-done | bytes 524320 | tf_op jit(solution)/shard_map/ppermute | solution.py:1085
  94.7 7.5 %mixer_forward.1 = (bf16[512,704]{1,0:T(8,128)(2,1)S(1)}, bf16[512,704]{1,0:T(8,128)(2,1)S(1)}, f32[512,704]{1,0:T(8,128)S(1)}, f32[512,704]{1,0:T(8,128)S(1)}, f32[512,704]{1,0:T(8,128)S(1)}) custom-call(f32[512,704]{1,0:T(8,128)S(1)} %get-tuple-element.147.refs_0_.refs_9_, f32[512,704]{1,0:T(8,128)S(1)} %get-tuple-element.148.refs_1_.refs_10_, ...), custom_call_target="tpu_custom_call" | custom-call | flops 1 | bytes 1 | tf_op jit(solution)/shard_map/mixer_forward/pallas_call | solution.py:75
  102.3 1.8 mixer_out.1
  104.9 2.7 collective-permute-done.14.refs_1_
  109.3 6.9 %unit_grad.1.refs_2_.refs_4_.refs_3_ = f32[512,1536]{1,0:T(8,128)S(1)} custom-call(bf16[512,2048]{1,0:T(8,128)(2,1)S(1)} %get-tuple-element.155.refs_0_, bf16[1536,2048]{1,0:T(8,128)(2,1)} %refs_2_.3, bf16[8,256,256]{2,1,0:T(8,128)(2,1)S(1)} %pair_sum.4.refs_2_.refs_3_.refs_5_), custom_call_target="tpu_custom_call" | custom-call | flops 1 | bytes 1 | tf_op jit(solution)/shard_map/unit_grad/pallas_call | solution.py:75
  116.3 2.9 fetch.1
  119.1 13.9 %collective-permute-done.15.refs_4_ = bf16[8,256,256]{2,1,0:T(8,128)(2,1)S(1)} collective-permute-done((bf16[8,256,256]{2,1,0:T(8,128)(2,1)S(1)}, bf16[8,256,256]{2,1,0:T(8,128)(2,1)S(1)}, u32[]{:S(2)}, u32[]{:S(2)}) %collective-permute-start.15) | collective-permute-done | bytes 1048608 | tf_op jit(solution)/shard_map/ppermute | solution.py:1126
  134.6 2.5 collective-permute-done.16
  137.2 5.0 %unit_first.1 = (bf16[512,768]{1,0:T(8,128)(2,1)S(1)}, bf16[512,768]{1,0:T(8,128)(2,1)S(1)}, bf16[512,768]{1,0:T(8,128)(2,1)S(1)}, bf16[8,512,256]{2,1,0:T(8,128)(2,1)S(1)}) custom-call(s32[8]{0:T(128)S(1)} %and_select_fusion.1.refs_1_.refs_0_, bf16[512,2048]{1,0:T(8,128)(2,1)S(1)} %constant_dynamic-update-slice_fusion.refs_1_.refs_0_, ...), custom_call_target="tpu_custom_call" | custom-call | flops 1 | bytes 1 | tf_op jit(solution)/shard_map/unit_first/pallas_call | solution.py:75
  145.8 6.5 %unit_second.1 = (bf16[512,768]{1,0:T(8,128)(2,1)S(1)}, bf16[512,768]{1,0:T(8,128)(2,1)S(1)}, bf16[512,768]{1,0:T(8,128)(2,1)S(1)}) custom-call(bf16[512,2048]{1,0:T(8,128)(2,1)S(1)} %constant_dynamic-update-slice_fusion.refs_1_.refs_0_, bf16[2048,1536]{1,0:T(8,128)(2,1)} %gate.1, bf16[2048,1536]{1,0:T(8,128)(2,1)} %up.1, ...), custom_call_target="tpu_custom_call" | custom-call | flops 1 | bytes 1 | tf_op jit(solution)/shard_map/unit_second/pallas_call | solution.py:75
  155.5 11.5 %unit_back.1 = (f32[8,256,256]{2,1,0:T(8,128)S(1)}, bf16[8,256,256]{2,1,0:T(8,128)(2,1)S(1)}) custom-call(s32[8]{0:T(128)S(1)} %compare_select_fusion.5.owners.refs_0_, bf16[512,768]{1,0:T(8,128)(2,1)S(1)} %get-tuple-element.163.refs_2_.dga_a, bf16[512,768]{1,0:T(8,128)(2,1)S(1)} %get-tuple-element.168.refs_2_.dga_b, ...), custom_call_target="tpu_custom_call" | custom-call | flops 1 | bytes 1 | tf_op jit(solution)/shard_map/unit_back/pallas_call | solution.py:774
  167.6 5.0 %collective-permute-done.17.refs_5_ = bf16[256,2304]{1,0:T(8,128)(2,1)S(1)} collective-permute-done((bf16[256,2304]{1,0:T(8,128)(2,1)S(1)}, bf16[256,2304]{1,0:T(8,128)(2,1)S(1)}, u32[]{:S(2)}, u32[]{:S(2)}) %collective-permute-start.17) | collective-permute-done | bytes 1179680 | tf_op jit(solution)/shard_map/ppermute | solution.py:1107
  182.8 15.1 %collective-permute-done.21.refs_5_ = bf16[256,2304]{1,0:T(8,128)(2,1)S(1)} collective-permute-done((bf16[256,2304]{1,0:T(8,128)(2,1)S(1)}, bf16[256,2304]{1,0:T(8,128)(2,1)S(1)}, u32[]{:S(2)}, u32[]{:S(2)}) %collective-permute-start.21) | collective-permute-done | bytes 1179680 | tf_op jit(solution)/shard_map/ppermute | solution.py:1107
  203.0 20.1 %collective-permute-done.19.refs_5_ = bf16[256,2304]{1,0:T(8,128)(2,1)S(1)} collective-permute-done((bf16[256,2304]{1,0:T(8,128)(2,1)S(1)}, bf16[256,2304]{1,0:T(8,128)(2,1)S(1)}, u32[]{:S(2)}, u32[]{:S(2)}) %collective-permute-start.19) | collective-permute-done | bytes 1179680 | tf_op jit(solution)/shard_map/ppermute | solution.py:1107
  224.8 2.5 unit_term.12
  228.8 3.4 norm_back.1
  234.0 14.4 %collective-permute-done.28.refs_5_ = bf16[256,2304]{1,0:T(8,128)(2,1)S(1)} collective-permute-done((bf16[256,2304]{1,0:T(8,128)(2,1)S(1)}, bf16[256,2304]{1,0:T(8,128)(2,1)S(1)}, u32[]{:S(2)}, u32[]{:S(2)}) %collective-permute-start.28) | collective-permute-done | bytes 1179680 | tf_op jit(solution)/shard_map/ppermute | solution.py:1107
  250.1 2.5 unit_term.13
  259.4 14.0 %mixer_backward.1 = (bf16[512,704]{1,0:T(8,128)(2,1)S(1)}, bf16[512,704]{1,0:T(8,128)(2,1)S(1)}, bf16[384,704]{1,0:T(8,128)(2,1)S(1)}) custom-call(bf16[8,512,256]{2,1,0:T(8,128)(2,1)S(1)} %constant_dynamic-update-slice_fusion.2.refs_0_.refs_5_, bf16[1024,256]{1,0:T(8,128)(2,1)S(1)} %get-tuple-element.134.refs_5_.refs_9_.refs_1_.refs_10_, ...), custom_call_target="tpu_custom_call" | custom-call | flops 1 | bytes 1 | tf_op jit(solution)/shard_map/mixer_backward/pallas_call | solution.py:75
  276.2 3.6 unit_term.14
  279.8 7.7 %unit_out.1 = (f32[256,2048]{1,0:T(8,128)S(1)}, bf16[256,2048]{1,0:T(8,128)(2,1)S(1)}) custom-call(bf16[512,768]{1,0:T(8,128)(2,1)S(1)} %copy-done.60, bf16[512,768]{1,0:T(8,128)(2,1)S(1)} %copy-done.39, bf16[1536,2048]{1,0:T(8,128)(2,1)} %refs_2_.3, bf16[256,2304]{1,0:T(8,128)(2,1)} %get-tuple-element.194.refs_3_), custom_call_target="tpu_custom_call" | custom-call | flops 1 | bytes 1 | tf_op jit(solution)/shard_map/unit_out/pallas_call | solution.py:75
  293.4 4.0 input_out.1
  297.3 3.4 collective-permute-done.32.refs_5_
  300.8 3.1 unit_term.15
  306.1 5.0 %collective-permute-done.37.refs_9_ = bf16[1104,256]{1,0:T(8,128)(2,1)S(1)} collective-permute-done((bf16[1104,256]{1,0:T(8,128)(2,1)S(1)}, bf16[1104,256]{1,0:T(8,128)(2,1)S(1)}, u32[]{:S(2)}, u32[]{:S(2)}) %collective-permute-start.37) | collective-permute-done | bytes 565280 | tf_op jit(solution)/shard_map/ppermute | solution.py:1107
  316.4 20.1 %collective-permute-done.36.refs_3_ = bf16[256,2304]{1,0:T(8,128)(2,1)} collective-permute-done((bf16[256,2304]{1,0:T(8,128)(2,1)}, bf16[256,2304]{1,0:T(8,128)(2,1)}, u32[]{:S(2)}, u32[]{:S(2)}) %collective-permute-start.36) | collective-permute-done | bytes 1179680 | tf_op jit(solution)/shard_map/ppermute | solution.py:1107
  341.7 2.7 unit_end.3
  347.1 2.5 input_back.1
  356.2 4.9 %collective-permute-done.44.refs_8_ = bf16[1152,256]{1,0:T(8,128)(2,1)S(1)} collective-permute-done((bf16[1152,256]{1,0:T(8,128)(2,1)S(1)}, bf16[1152,256]{1,0:T(8,128)(2,1)S(1)}, u32[]{:S(2)}, u32[]{:S(2)}) %collective-permute-start.44) | collective-permute-done | bytes 589856 | tf_op jit(solution)/shard_map/ppermute | solution.py:1107
  366.3 6.9 %collective-permute-done.42.refs_9_ = bf16[1104,256]{1,0:T(8,128)(2,1)S(1)} collective-permute-done((bf16[1104,256]{1,0:T(8,128)(2,1)S(1)}, bf16[1104,256]{1,0:T(8,128)(2,1)S(1)}, u32[]{:S(2)}, u32[]{:S(2)}) %collective-permute-start.42) | collective-permute-done | bytes 565280 | tf_op jit(solution)/shard_map/ppermute | solution.py:1107
  377.8 2.0 finish.1.refs_10_.refs_1_
  380.0 5.9 %collective-permute-done.47.refs_8_ = bf16[1152,256]{1,0:T(8,128)(2,1)S(1)} collective-permute-done((bf16[1152,256]{1,0:T(8,128)(2,1)S(1)}, bf16[1152,256]{1,0:T(8,128)(2,1)S(1)}, u32[]{:S(2)}, u32[]{:S(2)}) %collective-permute-start.47) | collective-permute-done | bytes 589856 | tf_op jit(solution)/shard_map/ppermute | solution.py:1107
  390.0 4.5 %arrange.1 = (f32[2,256,2048]{2,1,0:T(8,128)}, f32[2,256,2048]{2,1,0:T(8,128)}) custom-call(s32[3]{0:T(128)S(1)} %copy-done.76, f32[2,256,2048]{2,1,0:T(8,128)S(1)} %finish.1.refs_10_.refs_1_, f32[2,256,2048]{2,1,0:T(8,128)S(1)} %collective-permute-done.46.refs_2_, bf16[1152,256]{1,0:T(8,128)(2,1)S(1)} %get-tuple-element.225.refs_3_), custom_call_target="tpu_custom_call" | custom-call | flops 1 | bytes 1 | tf_op jit(solution)/shard_map/arrange/pallas_call | solution.py:75
  394.5 3.6 collective-permute-done.49.refs_3_
  398.0 2.2 copy-done.77
  400.2 1.7 mixer_end.2
  407.2 4.8 %collective-permute-done.54.refs_8_ = bf16[64,704]{1,0:T(8,128)(2,1)S(1)} collective-permute-done((bf16[64,704]{1,0:T(8,128)(2,1)S(1)}, bf16[64,704]{1,0:T(8,128)(2,1)S(1)}, u32[]{:S(2)}, u32[]{:S(2)}) %collective-permute-start.54) | collective-permute-done | bytes 90144 | tf_op jit(solution)/shard_map/ppermute | solution.py:1085
  413.5 6.5 %collective-permute-done.51.refs_2_ = bf16[64,704]{1,0:T(8,128)(2,1)S(1)} collective-permute-done((bf16[64,704]{1,0:T(8,128)(2,1)S(1)}, bf16[64,704]{1,0:T(8,128)(2,1)S(1)}, u32[]{:S(2)}, u32[]{:S(2)}) %collective-permute-start.51) | collective-permute-done | bytes 90144 | tf_op jit(solution)/shard_map/ppermute | solution.py:1085
  423.2 2.4 collective-permute-done.52.refs_3_
  432.3 1.6 spread.1
  (304 shorter events, 129.8 us)
Async XLA Ops:
  3.3 28.6 %collective-permute-start = (bf16[1104,256]{1,0:T(8,128)(2,1)S(1)}, bf16[1104,256]{1,0:T(8,128)(2,1)S(1)}, u32[]{:S(2)}, u32[]{:S(2)}) collective-permute-start(bf16[1104,256]{1,0:T(8,128)(2,1)S(1)} %get-tuple-element.133.refs_2_.refs_1_), channel_id=1, source_target_pairs={{0,8},{8,16},{16,24},{24,28},{28,20},{20,12},{12,4},{4,0},{1,9},{9... | collective-permute-start | bytes 1695752 | tf_op jit(solution)/shard_map/ppermute | solution.py:1085
  6.3 25.5 %collective-permute-start.1 = (bf16[1104,256]{1,0:T(8,128)(2,1)S(1)}, bf16[1104,256]{1,0:T(8,128)(2,1)S(1)}, u32[]{:S(2)}, u32[]{:S(2)}) collective-permute-start(bf16[1104,256]{1,0:T(8,128)(2,1)S(1)} %get-tuple-element.133.refs_2_.refs_1_), channel_id=1, source_target_pairs={{8,0},{16,8},{24,16},{28,24},{20,28},{12,20},{4,12},{0,4},{9,1},{1... | collective-permute-start | bytes 1695752 | tf_op jit(solution)/shard_map/ppermute | solution.py:1085
  6.3 23.9 %collective-permute-start.2 = (bf16[1024,256]{1,0:T(8,128)(2,1)S(1)}, bf16[1024,256]{1,0:T(8,128)(2,1)S(1)}, u32[]{:S(2)}, u32[]{:S(2)}) collective-permute-start(bf16[1024,256]{1,0:T(8,128)(2,1)S(1)} %get-tuple-element.134.refs_5_.refs_9_.refs_1_.refs_10_), channel_id=1, source_target_pairs={{0,8},{8,16},{16,24},{24,28},{28,20},{20,12},{12,4},{4,0},{1,9},{9... | collective-permute-start | bytes 1572872 | tf_op jit(solution)/shard_map/ppermute | solution.py:1085
  8.4 23.5 %collective-permute-start.3 = (bf16[1024,256]{1,0:T(8,128)(2,1)S(1)}, bf16[1024,256]{1,0:T(8,128)(2,1)S(1)}, u32[]{:S(2)}, u32[]{:S(2)}) collective-permute-start(bf16[1024,256]{1,0:T(8,128)(2,1)S(1)} %get-tuple-element.134.refs_5_.refs_9_.refs_1_.refs_10_), channel_id=1, source_target_pairs={{8,0},{16,8},{24,16},{28,24},{20,28},{12,20},{4,12},{0,4},{9,1},{1... | collective-permute-start | bytes 1572872 | tf_op jit(solution)/shard_map/ppermute | solution.py:1085
  33.4 14.9 %collective-permute-start.7 = (bf16[1024,256]{1,0:T(8,128)(2,1)S(1)}, bf16[1024,256]{1,0:T(8,128)(2,1)S(1)}, u32[]{:S(2)}, u32[]{:S(2)}) collective-permute-start(bf16[1024,256]{1,0:T(8,128)(2,1)S(1)} %collective-permute-done.3.refs_6_.refs_10_.refs_2_.refs_11_), channel_id=1, source_target_pairs={{8,0},{16,8},{24,16},{28,24},{20,28},{12,20},{4,12},{0,4},{9,1},{1... | collective-permute-start | bytes 1572872 | tf_op jit(solution)/shard_map/ppermute | solution.py:1085
  33.9 26.5 %collective-permute-start.10 = (bf16[1104,256]{1,0:T(8,128)(2,1)S(1)}, bf16[1104,256]{1,0:T(8,128)(2,1)S(1)}, u32[]{:S(2)}, u32[]{:S(2)}) collective-permute-start(bf16[1104,256]{1,0:T(8,128)(2,1)S(1)} %collective-permute-done.1.refs_3_.refs_2_), channel_id=1, source_target_pairs={{8,0},{16,8},{24,16},{28,24},{20,28},{12,20},{4,12},{0,4},{9,1},{1... | collective-permute-start | bytes 1695752 | tf_op jit(solution)/shard_map/ppermute | solution.py:1085
  45.2 15.7 %collective-permute-start.5 = (bf16[1104,256]{1,0:T(8,128)(2,1)S(1)}, bf16[1104,256]{1,0:T(8,128)(2,1)S(1)}, u32[]{:S(2)}, u32[]{:S(2)}) collective-permute-start(bf16[1104,256]{1,0:T(8,128)(2,1)S(1)} %collective-permute-done.4.refs_3_.refs_7_.refs_8_), channel_id=1, source_target_pairs={{0,8},{8,16},{16,24},{24,28},{28,20},{20,12},{12,4},{4,0},{1,9},{9... | collective-permute-start | bytes 1695752 | tf_op jit(solution)/shard_map/ppermute | solution.py:1085
  46.8 25.4 %collective-permute-start.12 = (bf16[1024,256]{1,0:T(8,128)(2,1)S(1)}, bf16[1024,256]{1,0:T(8,128)(2,1)S(1)}, u32[]{:S(2)}, u32[]{:S(2)}) collective-permute-start(bf16[1024,256]{1,0:T(8,128)(2,1)S(1)} %collective-permute-done.2.refs_7_.refs_16_.refs_8_.refs_17_), channel_id=1, source_target_pairs={{0,8},{8,16},{16,24},{24,28},{28,20},{20,12},{12,4},{4,0},{1,9},{9... | collective-permute-start | bytes 1572872 | tf_op jit(solution)/shard_map/ppermute | solution.py:1085
  48.3 25.4 %collective-permute-start.8 = (bf16[1024,256]{1,0:T(8,128)(2,1)S(1)}, bf16[1024,256]{1,0:T(8,128)(2,1)S(1)}, u32[]{:S(2)}, u32[]{:S(2)}) collective-permute-start(bf16[1024,256]{1,0:T(8,128)(2,1)S(1)} %collective-permute-done.7.refs_4_.refs_11_.refs_3_.refs_12_), channel_id=1, source_target_pairs={{8,0},{16,8},{24,16},{28,24},{20,28},{12,20},{4,12},{0,4},{9,1},{1... | collective-permute-start | bytes 1572872 | tf_op jit(solution)/shard_map/ppermute | solution.py:1085
  60.4 31.8 %collective-permute-start.11 = (bf16[1104,256]{1,0:T(8,128)(2,1)S(1)}, bf16[1104,256]{1,0:T(8,128)(2,1)S(1)}, u32[]{:S(2)}, u32[]{:S(2)}) collective-permute-start(bf16[1104,256]{1,0:T(8,128)(2,1)S(1)} %collective-permute-done.10.refs_2_.refs_3_.refs_4_), channel_id=1, source_target_pairs={{8,0},{16,8},{24,16},{28,24},{20,28},{12,20},{4,12},{0,4},{9,1},{1... | collective-permute-start | bytes 1695752 | tf_op jit(solution)/shard_map/ppermute | solution.py:1085
  60.9 32.8 %collective-permute-start.6 = (bf16[1104,256]{1,0:T(8,128)(2,1)S(1)}, bf16[1104,256]{1,0:T(8,128)(2,1)S(1)}, u32[]{:S(2)}, u32[]{:S(2)}) collective-permute-start(bf16[1104,256]{1,0:T(8,128)(2,1)S(1)} %collective-permute-done.5.refs_3_.refs_6_.refs_7_), channel_id=1, source_target_pairs={{0,8},{8,16},{16,24},{24,28},{28,20},{20,12},{12,4},{4,0},{1,9},{9... | collective-permute-start | bytes 1695752 | tf_op jit(solution)/shard_map/ppermute | solution.py:1085
  72.2 20.0 %collective-permute-start.13 = (bf16[1024,256]{1,0:T(8,128)(2,1)S(1)}, bf16[1024,256]{1,0:T(8,128)(2,1)S(1)}, u32[]{:S(2)}, u32[]{:S(2)}) collective-permute-start(bf16[1024,256]{1,0:T(8,128)(2,1)S(1)} %collective-permute-done.12.refs_5_.refs_15_.refs_7_.refs_16_), channel_id=1, source_target_pairs={{0,8},{8,16},{16,24},{24,28},{28,20},{20,12},{12,4},{4,0},{1,9},{9... | collective-permute-start | bytes 1572872 | tf_op jit(solution)/shard_map/ppermute | solution.py:1085
  73.7 20.0 %collective-permute-start.9 = (bf16[1024,256]{1,0:T(8,128)(2,1)S(1)}, bf16[1024,256]{1,0:T(8,128)(2,1)S(1)}, u32[]{:S(2)}, u32[]{:S(2)}) collective-permute-start(bf16[1024,256]{1,0:T(8,128)(2,1)S(1)} %collective-permute-done.8.refs_4_.refs_12_.refs_13_), channel_id=1, source_target_pairs={{8,0},{16,8},{24,16},{28,24},{20,28},{12,20},{4,12},{0,4},{9,1},{1... | collective-permute-start | bytes 1572872 | tf_op jit(solution)/shard_map/ppermute | solution.py:1085
  107.7 25.3 %collective-permute-start.15 = (bf16[8,256,256]{2,1,0:T(8,128)(2,1)S(1)}, bf16[8,256,256]{2,1,0:T(8,128)(2,1)S(1)}, u32[]{:S(2)}, u32[]{:S(2)}) collective-permute-start(bf16[8,256,256]{2,1,0:T(8,128)(2,1)S(1)} %pair_sum.4.refs_2_.refs_3_.refs_5_), channel_id=1, source_target_pairs={{0,2},{1,3},{2,0},{3,1},{4,6},{5,7},{6,4},{7,5},{8,10},{9,11},{10,... | collective-permute-start | bytes 3145736 | tf_op jit(solution)/shard_map/ppermute | solution.py:1126
  143.7 28.9 %collective-permute-start.17 = (bf16[256,2304]{1,0:T(8,128)(2,1)S(1)}, bf16[256,2304]{1,0:T(8,128)(2,1)S(1)}, u32[]{:S(2)}, u32[]{:S(2)}) collective-permute-start(bf16[256,2304]{1,0:T(8,128)(2,1)S(1)} %get-tuple-element.165.refs_4_.refs_5_), channel_id=1, source_target_pairs={{0,8},{8,16},{16,24},{24,28},{28,20},{20,12},{12,4},{4,0},{1,9},{9... | collective-permute-start | bytes 3538952 | tf_op jit(solution)/shard_map/ppermute | solution.py:1107
  145.4 28.9 %collective-permute-start.18 = (bf16[256,2304]{1,0:T(8,128)(2,1)S(1)}, bf16[256,2304]{1,0:T(8,128)(2,1)S(1)}, u32[]{:S(2)}, u32[]{:S(2)}) collective-permute-start(bf16[256,2304]{1,0:T(8,128)(2,1)S(1)} %get-tuple-element.167), channel_id=1, source_target_pairs={{8,0},{16,8},{24,16},{28,24},{20,28},{12,20},{4,12},{0,4},{9,1},{1... | collective-permute-start | bytes 3538952 | tf_op jit(solution)/shard_map/ppermute | solution.py:1107
  153.8 44.1 %collective-permute-start.21 = (bf16[256,2304]{1,0:T(8,128)(2,1)S(1)}, bf16[256,2304]{1,0:T(8,128)(2,1)S(1)}, u32[]{:S(2)}, u32[]{:S(2)}) collective-permute-start(bf16[256,2304]{1,0:T(8,128)(2,1)S(1)} %get-tuple-element.170.refs_0_), channel_id=1, source_target_pairs={{0,8},{8,16},{16,24},{24,28},{28,20},{20,12},{12,4},{4,0},{1,9},{9... | collective-permute-start | bytes 3538952 | tf_op jit(solution)/shard_map/ppermute | solution.py:1107
  167.1 32.4 %collective-permute-start.22 = (bf16[256,2304]{1,0:T(8,128)(2,1)S(1)}, bf16[256,2304]{1,0:T(8,128)(2,1)S(1)}, u32[]{:S(2)}, u32[]{:S(2)}) collective-permute-start(bf16[256,2304]{1,0:T(8,128)(2,1)S(1)} %get-tuple-element.174), channel_id=1, source_target_pairs={{8,0},{16,8},{24,16},{28,24},{20,28},{12,20},{4,12},{0,4},{9,1},{1... | collective-permute-start | bytes 3538952 | tf_op jit(solution)/shard_map/ppermute | solution.py:1107
  178.1 45.1 %collective-permute-start.19 = (bf16[256,2304]{1,0:T(8,128)(2,1)S(1)}, bf16[256,2304]{1,0:T(8,128)(2,1)S(1)}, u32[]{:S(2)}, u32[]{:S(2)}) collective-permute-start(bf16[256,2304]{1,0:T(8,128)(2,1)S(1)} %get-tuple-element.172.refs_2_), channel_id=1, source_target_pairs={{0,8},{8,16},{16,24},{24,28},{28,20},{20,12},{12,4},{4,0},{1,9},{9... | collective-permute-start | bytes 3538952 | tf_op jit(solution)/shard_map/ppermute | solution.py:1107
  179.7 45.1 %collective-permute-start.20 = (bf16[256,2304]{1,0:T(8,128)(2,1)S(1)}, bf16[256,2304]{1,0:T(8,128)(2,1)S(1)}, u32[]{:S(2)}, u32[]{:S(2)}) collective-permute-start(bf16[256,2304]{1,0:T(8,128)(2,1)S(1)} %get-tuple-element.173), channel_id=1, source_target_pairs={{8,0},{16,8},{24,16},{28,24},{20,28},{12,20},{4,12},{0,4},{9,1},{1... | collective-permute-start | bytes 3538952 | tf_op jit(solution)/shard_map/ppermute | solution.py:1107
  181.3 47.5 %collective-permute-start.26 = (bf16[8,256,256]{2,1,0:T(8,128)(2,1)}, bf16[8,256,256]{2,1,0:T(8,128)(2,1)}, u32[]{:S(2)}, u32[]{:S(2)}) collective-permute-start(bf16[8,256,256]{2,1,0:T(8,128)(2,1)} %pair_sum.5.refs_7_.refs_0_), channel_id=1, source_target_pairs={{0,2},{1,3},{2,0},{3,1},{4,6},{5,7},{6,4},{7,5},{8,10},{9,11},{10,... | collective-permute-start | bytes 3145736 | tf_op jit(solution)/shard_map/ppermute | solution.py:1126
  200.9 47.5 %collective-permute-start.28 = (bf16[256,2304]{1,0:T(8,128)(2,1)S(1)}, bf16[256,2304]{1,0:T(8,128)(2,1)S(1)}, u32[]{:S(2)}, u32[]{:S(2)}) collective-permute-start(bf16[256,2304]{1,0:T(8,128)(2,1)S(1)} %get-tuple-element.176.refs_7_), channel_id=1, source_target_pairs={{0,8},{8,16},{16,24},{24,28},{28,20},{20,12},{12,4},{4,0},{1,9},{9... | collective-permute-start | bytes 3538952 | tf_op jit(solution)/shard_map/ppermute | solution.py:1107
  202.6 47.5 %collective-permute-start.29 = (bf16[256,2304]{1,0:T(8,128)(2,1)S(1)}, bf16[256,2304]{1,0:T(8,128)(2,1)S(1)}, u32[]{:S(2)}, u32[]{:S(2)}) collective-permute-start(bf16[256,2304]{1,0:T(8,128)(2,1)S(1)} %get-tuple-element.189), channel_id=1, source_target_pairs={{8,0},{16,8},{24,16},{28,24},{20,28},{12,20},{4,12},{0,4},{9,1},{1... | collective-permute-start | bytes 3538952 | tf_op jit(solution)/shard_map/ppermute | solution.py:1107
  227.2 47.6 %collective-permute-start.24 = (bf16[256,2304]{1,0:T(8,128)(2,1)}, bf16[256,2304]{1,0:T(8,128)(2,1)}, u32[]{:S(2)}, u32[]{:S(2)}) collective-permute-start(bf16[256,2304]{1,0:T(8,128)(2,1)} %get-tuple-element.177.refs_6_), channel_id=1, source_target_pairs={{0,8},{8,16},{16,24},{24,28},{28,20},{20,12},{12,4},{4,0},{1,9},{9... | collective-permute-start | bytes 3538952 | tf_op jit(solution)/shard_map/ppermute | solution.py:1107
  233.6 21.1 %collective-permute-start.27 = (bf16[8,256,256]{2,1,0:T(8,128)(2,1)S(1)}, bf16[8,256,256]{2,1,0:T(8,128)(2,1)S(1)}, u32[]{:S(2)}, u32[]{:S(2)}) collective-permute-start(bf16[8,256,256]{2,1,0:T(8,128)(2,1)S(1)} %get-tuple-element.184.refs_7_), channel_id=1, source_target_pairs={{0,1},{1,0},{2,3},{3,2},{4,5},{5,4},{6,7},{7,6},{8,9},{9,8},{10,11... | collective-permute-start | bytes 3145736 | tf_op jit(solution)/shard_map/ppermute | solution.py:1129
  233.6 41.9 %collective-permute-start.25 = (bf16[256,2304]{1,0:T(8,128)(2,1)}, bf16[256,2304]{1,0:T(8,128)(2,1)}, u32[]{:S(2)}, u32[]{:S(2)}) collective-permute-start(bf16[256,2304]{1,0:T(8,128)(2,1)} %get-tuple-element.178), channel_id=1, source_target_pairs={{8,0},{16,8},{24,16},{28,24},{20,28},{12,20},{4,12},{0,4},{9,1},{1... | collective-permute-start | bytes 3538952 | tf_op jit(solution)/shard_map/ppermute | solution.py:1107
  252.6 48.1 %collective-permute-start.32 = (bf16[256,2304]{1,0:T(8,128)(2,1)}, bf16[256,2304]{1,0:T(8,128)(2,1)}, u32[]{:S(2)}, u32[]{:S(2)}) collective-permute-start(bf16[256,2304]{1,0:T(8,128)(2,1)} %get-tuple-element.200), channel_id=1, source_target_pairs={{8,0},{16,8},{24,16},{28,24},{20,28},{12,20},{4,12},{0,4},{9,1},{1... | collective-permute-start | bytes 3538952 | tf_op jit(solution)/shard_map/ppermute | solution.py:1107
  253.0 47.7 %collective-permute-start.33 = (bf16[256,2304]{1,0:T(8,128)(2,1)}, bf16[256,2304]{1,0:T(8,128)(2,1)}, u32[]{:S(2)}, u32[]{:S(2)}) collective-permute-start(bf16[256,2304]{1,0:T(8,128)(2,1)} %get-tuple-element.190.refs_18_), channel_id=1, source_target_pairs={{0,8},{8,16},{16,24},{24,28},{28,20},{20,12},{12,4},{4,0},{1,9},{9... | collective-permute-start | bytes 3538952 | tf_op jit(solution)/shard_map/ppermute | solution.py:1107
  287.6 23.6 %collective-permute-start.37 = (bf16[1104,256]{1,0:T(8,128)(2,1)S(1)}, bf16[1104,256]{1,0:T(8,128)(2,1)S(1)}, u32[]{:S(2)}, u32[]{:S(2)}) collective-permute-start(bf16[1104,256]{1,0:T(8,128)(2,1)S(1)} %get-tuple-element.193.refs_7_), channel_id=1, source_target_pairs={{0,8},{8,16},{16,24},{24,28},{28,20},{20,12},{12,4},{4,0},{1,9},{9... | collective-permute-start | bytes 1695752 | tf_op jit(solution)/shard_map/ppermute | solution.py:1107
  289.2 23.6 %collective-permute-start.38 = (bf16[1104,256]{1,0:T(8,128)(2,1)S(1)}, bf16[1104,256]{1,0:T(8,128)(2,1)S(1)}, u32[]{:S(2)}, u32[]{:S(2)}) collective-permute-start(bf16[1104,256]{1,0:T(8,128)(2,1)S(1)} %get-tuple-element.210), channel_id=1, source_target_pairs={{8,0},{16,8},{24,16},{28,24},{20,28},{12,20},{4,12},{0,4},{9,1},{1... | collective-permute-start | bytes 1695752 | tf_op jit(solution)/shard_map/ppermute | solution.py:1107
  290.2 46.3 %collective-permute-start.36 = (bf16[256,2304]{1,0:T(8,128)(2,1)}, bf16[256,2304]{1,0:T(8,128)(2,1)}, u32[]{:S(2)}, u32[]{:S(2)}) collective-permute-start(bf16[256,2304]{1,0:T(8,128)(2,1)} %get-tuple-element.194.refs_3_), channel_id=1, source_target_pairs={{0,8},{8,16},{16,24},{24,28},{28,20},{20,12},{12,4},{4,0},{1,9},{9... | collective-permute-start | bytes 3538952 | tf_op jit(solution)/shard_map/ppermute | solution.py:1107
  303.9 37.4 %collective-permute-start.35 = (bf16[256,2304]{1,0:T(8,128)(2,1)S(1)}, bf16[256,2304]{1,0:T(8,128)(2,1)S(1)}, u32[]{:S(2)}, u32[]{:S(2)}) collective-permute-start(bf16[256,2304]{1,0:T(8,128)(2,1)S(1)} %get-tuple-element.201.refs_2_), channel_id=1, source_target_pairs={{8,0},{16,8},{24,16},{28,24},{20,28},{12,20},{4,12},{0,4},{9,1},{1... | collective-permute-start | bytes 3538952 | tf_op jit(solution)/shard_map/ppermute | solution.py:1107
  304.6 39.9 %collective-permute-start.34 = (bf16[8,256,256]{2,1,0:T(8,128)(2,1)S(1)}, bf16[8,256,256]{2,1,0:T(8,128)(2,1)S(1)}, u32[]{:S(2)}, u32[]{:S(2)}) collective-permute-start(bf16[8,256,256]{2,1,0:T(8,128)(2,1)S(1)} %pair_sum.7.refs_11_.refs_1_), channel_id=1, source_target_pairs={{0,2},{1,3},{2,0},{3,1},{4,6},{5,7},{6,4},{7,5},{8,10},{9,11},{10,... | collective-permute-start | bytes 3145736 | tf_op jit(solution)/shard_map/ppermute | solution.py:1126
  314.1 38.7 %collective-permute-start.40 = (bf16[1104,256]{1,0:T(8,128)(2,1)S(1)}, bf16[1104,256]{1,0:T(8,128)(2,1)S(1)}, u32[]{:S(2)}, u32[]{:S(2)}) collective-permute-start(bf16[1104,256]{1,0:T(8,128)(2,1)S(1)} %get-tuple-element.211.refs_4_), channel_id=1, source_target_pairs={{0,8},{8,16},{16,24},{24,28},{28,20},{20,12},{12,4},{4,0},{1,9},{9... | collective-permute-start | bytes 1695752 | tf_op jit(solution)/shard_map/ppermute | solution.py:1107
  315.7 37.1 %collective-permute-start.41 = (bf16[1104,256]{1,0:T(8,128)(2,1)S(1)}, bf16[1104,256]{1,0:T(8,128)(2,1)S(1)}, u32[]{:S(2)}, u32[]{:S(2)}) collective-permute-start(bf16[1104,256]{1,0:T(8,128)(2,1)S(1)} %get-tuple-element.218), channel_id=1, source_target_pairs={{8,0},{16,8},{24,16},{28,24},{20,28},{12,20},{4,12},{0,4},{9,1},{1... | collective-permute-start | bytes 1695752 | tf_op jit(solution)/shard_map/ppermute | solution.py:1107
  339.6 21.5 %collective-permute-start.44 = (bf16[1152,256]{1,0:T(8,128)(2,1)S(1)}, bf16[1152,256]{1,0:T(8,128)(2,1)S(1)}, u32[]{:S(2)}, u32[]{:S(2)}) collective-permute-start(bf16[1152,256]{1,0:T(8,128)(2,1)S(1)} %get-tuple-element.215.refs_7_), channel_id=1, source_target_pairs={{0,8},{8,16},{16,24},{24,28},{28,20},{20,12},{12,4},{4,0},{1,9},{9... | collective-permute-start | bytes 1769480 | tf_op jit(solution)/shard_map/ppermute | solution.py:1107
  341.3 21.5 %collective-permute-start.45 = (bf16[1152,256]{1,0:T(8,128)(2,1)S(1)}, bf16[1152,256]{1,0:T(8,128)(2,1)S(1)}, u32[]{:S(2)}, u32[]{:S(2)}) collective-permute-start(bf16[1152,256]{1,0:T(8,128)(2,1)S(1)} %get-tuple-element.221), channel_id=1, source_target_pairs={{8,0},{16,8},{24,16},{28,24},{20,28},{12,20},{4,12},{0,4},{9,1},{1... | collective-permute-start | bytes 1769480 | tf_op jit(solution)/shard_map/ppermute | solution.py:1107
  351.3 26.5 %collective-permute-start.39 = (bf16[256,2048]{1,0:T(8,128)(2,1)}, bf16[256,2048]{1,0:T(8,128)(2,1)}, u32[]{:S(2)}, u32[]{:S(2)}) collective-permute-start(bf16[256,2048]{1,0:T(8,128)(2,1)} %relay.1.refs_11_.refs_2_), channel_id=1, source_target_pairs={{0,2},{1,3},{2,0},{3,1},{4,6},{5,7},{6,4},{7,5},{8,10},{9,11},{10,... | collective-permute-start | bytes 3145736 | tf_op jit(solution)/shard_map/ppermute | solution.py:1245
  354.2 19.1 %collective-permute-start.42 = (bf16[1104,256]{1,0:T(8,128)(2,1)S(1)}, bf16[1104,256]{1,0:T(8,128)(2,1)S(1)}, u32[]{:S(2)}, u32[]{:S(2)}) collective-permute-start(bf16[1104,256]{1,0:T(8,128)(2,1)S(1)} %get-tuple-element.219.refs_10_), channel_id=1, source_target_pairs={{0,8},{8,16},{16,24},{24,28},{28,20},{20,12},{12,4},{4,0},{1,9},{9... | collective-permute-start | bytes 1695752 | tf_op jit(solution)/shard_map/ppermute | solution.py:1107
  355.8 19.1 %collective-permute-start.43 = (bf16[1104,256]{1,0:T(8,128)(2,1)S(1)}, bf16[1104,256]{1,0:T(8,128)(2,1)S(1)}, u32[]{:S(2)}, u32[]{:S(2)}) collective-permute-start(bf16[1104,256]{1,0:T(8,128)(2,1)S(1)} %get-tuple-element.220), channel_id=1, source_target_pairs={{8,0},{16,8},{24,16},{28,24},{20,28},{12,20},{4,12},{0,4},{9,1},{1... | collective-permute-start | bytes 1695752 | tf_op jit(solution)/shard_map/ppermute | solution.py:1107
  364.3 21.6 %collective-permute-start.47 = (bf16[1152,256]{1,0:T(8,128)(2,1)S(1)}, bf16[1152,256]{1,0:T(8,128)(2,1)S(1)}, u32[]{:S(2)}, u32[]{:S(2)}) collective-permute-start(bf16[1152,256]{1,0:T(8,128)(2,1)S(1)} %get-tuple-element.222.refs_11_), channel_id=1, source_target_pairs={{0,8},{8,16},{16,24},{24,28},{28,20},{20,12},{12,4},{4,0},{1,9},{9... | collective-permute-start | bytes 1769480 | tf_op jit(solution)/shard_map/ppermute | solution.py:1107
  365.9 20.5 %collective-permute-start.48 = (bf16[1152,256]{1,0:T(8,128)(2,1)S(1)}, bf16[1152,256]{1,0:T(8,128)(2,1)S(1)}, u32[]{:S(2)}, u32[]{:S(2)}) collective-permute-start(bf16[1152,256]{1,0:T(8,128)(2,1)S(1)} %get-tuple-element.224), channel_id=1, source_target_pairs={{8,0},{16,8},{24,16},{28,24},{20,28},{12,20},{4,12},{0,4},{9,1},{1... | collective-permute-start | bytes 1769480 | tf_op jit(solution)/shard_map/ppermute | solution.py:1107
  373.3 21.2 %collective-permute-start.50 = (f32[8,2,256]{2,1,0:T(2,128)}, f32[8,2,256]{2,1,0:T(2,128)}, u32[]{:S(2)}, u32[]{:S(2)}) collective-permute-start(f32[8,2,256]{2,1,0:T(2,128)} %get-tuple-element.231.refs_4_), channel_id=1, source_target_pairs={{0,1},{1,0},{2,3},{3,2},{4,5},{5,4},{6,7},{7,6},{8,9},{9,8},{10,11... | collective-permute-start | bytes 49160 | tf_op jit(solution)/shard_map/ppermute | solution.py:1121
  376.2 21.8 %collective-permute-start.49 = (bf16[1104,256]{1,0:T(8,128)(2,1)S(1)}, bf16[1104,256]{1,0:T(8,128)(2,1)S(1)}, u32[]{:S(2)}, u32[]{:S(2)}) collective-permute-start(bf16[1104,256]{1,0:T(8,128)(2,1)S(1)} %get-tuple-element.223.refs_5_), channel_id=1, source_target_pairs={{0,8},{8,16},{16,24},{24,28},{28,20},{20,12},{12,4},{4,0},{1,9},{9... | collective-permute-start | bytes 1695752 | tf_op jit(solution)/shard_map/ppermute | solution.py:1107
  387.9 14.3 %collective-permute-start.59 = (bf16[1152,256]{1,0:T(8,128)(2,1)S(1)}, bf16[1152,256]{1,0:T(8,128)(2,1)S(1)}, u32[]{:S(2)}, u32[]{:S(2)}) collective-permute-start(bf16[1152,256]{1,0:T(8,128)(2,1)S(1)} %get-tuple-element.233), channel_id=1, source_target_pairs={{8,0},{16,8},{24,16},{28,24},{20,28},{12,20},{4,12},{0,4},{9,1},{1... | collective-permute-start | bytes 1769480 | tf_op jit(solution)/shard_map/ppermute | solution.py:1107
  388.4 33.7 %collective-permute-start.58 = (bf16[1152,256]{1,0:T(8,128)(2,1)S(1)}, bf16[1152,256]{1,0:T(8,128)(2,1)S(1)}, u32[]{:S(2)}, u32[]{:S(2)}) collective-permute-start(bf16[1152,256]{1,0:T(8,128)(2,1)S(1)} %get-tuple-element.225.refs_3_), channel_id=1, source_target_pairs={{0,8},{8,16},{16,24},{24,28},{28,20},{20,12},{12,4},{4,0},{1,9},{9... | collective-permute-start | bytes 1769480 | tf_op jit(solution)/shard_map/ppermute | solution.py:1107
  404.4 23.3 %collective-permute-start.60 = (bf16[1152,256]{1,0:T(8,128)(2,1)S(1)}, bf16[1152,256]{1,0:T(8,128)(2,1)S(1)}, u32[]{:S(2)}, u32[]{:S(2)}) collective-permute-start(bf16[1152,256]{1,0:T(8,128)(2,1)S(1)} %mixer_term.16.refs_9_), channel_id=1, source_target_pairs={{8,0},{16,8},{24,16},{28,24},{20,28},{12,20},{4,12},{0,4},{9,1},{1... | collective-permute-start | bytes 1769480 | tf_op jit(solution)/shard_map/ppermute | solution.py:1107
  406.5 13.6 %collective-permute-start.51 = (bf16[64,704]{1,0:T(8,128)(2,1)S(1)}, bf16[64,704]{1,0:T(8,128)(2,1)S(1)}, u32[]{:S(2)}, u32[]{:S(2)}) collective-permute-start(bf16[64,704]{1,0:T(8,128)(2,1)S(1)} %get-tuple-element.232.refs_1_), channel_id=1, source_target_pairs={{8,0},{16,8},{24,16},{28,24},{20,28},{12,20},{4,12},{0,4},{9,1},{1... | collective-permute-start | bytes 270344 | tf_op jit(solution)/shard_map/ppermute | solution.py:1085
  (95 other events, 1515.6 us)

commit v5 on v4

--- a/solution.py
+++ b/solution.py
@@ -61,7 +61,7 @@
 
 
 def launch(
-    kernel, inputs, out_shape, name, scalars=0, after=(), mib=20, scratch=(), aliases=None, grid=None, flops=1
+    kernel, inputs, out_shape, name, scalars=0, after=(), mib=10, scratch=(), aliases=None, grid=None, flops=1
 ):
     count, extra = len(inputs), len(after)
     waits = [pl.BlockSpec(memory_space=pl.ANY)] * extra
@@ -111,7 +111,7 @@
             cx_o[at, :] = mixed.astype(BF16)
             return now
 
-        lax.fori_loop(0, steps, conv, jnp.zeros((STEP, width), F32))
+        lax.fori_loop(0, steps, conv, jnp.zeros((STEP, width), F32), unroll=2)
     lx_o[...] = lax.dot_general(cx_o[...], blocks_i[...], NT, preferred_element_type=F32) + bias_i
     lr_o[...] = lax.dot_general(cx_o[...], blocks_r[...], NT, preferred_element_type=F32) + bias_r
     rows8 = rows_of((HALF, width))
@@ -146,7 +146,7 @@
             out.append(carry)
         return tuple(out)
 
-    lax.fori_loop(0, steps, scan, tuple(jnp.zeros((HALF, width), F32) for _ in range(seqs)))
+    lax.fori_loop(0, steps, scan, tuple(jnp.zeros((HALF, width), F32) for _ in range(seqs)), unroll=4)
 
 
 def mixer_forward(seqs, count, bx, by, lines, blocks_i, blocks_r):
@@ -283,7 +283,7 @@
         (low, low, shaped((small_rows, width), BF16)),
         "mixer_backward",
         after=after,
-        mib=32,
+        mib=18,
         scratch=[
             pltpu.VMEM((total, width), BF16),
             pltpu.VMEM((total, width), BF16),
@@ -293,21 +293,32 @@
     )
 
 
-def pack_kernel(split, gain_one, gain_two, value, gelu_w, output, one_o, two_o, sems):
-    width = value.shape[0]
+def copy_all(pairs, sems):
     copies = [
-        pltpu.make_async_copy(source, target, sems.at[i])
-        for i, (source, target) in enumerate(
-            (
-                (value, one_o.at[pl.ds(0, width)]),
-                (gelu_w.at[pl.ds(0, split)], one_o.at[pl.ds(width + 16, split)]),
-                (gelu_w.at[pl.ds(split, width - split)], two_o.at[pl.ds(0, width - split)]),
-                (output, two_o.at[pl.ds(width - split, width)]),
-            )
-        )
+        pltpu.make_async_copy(source, target, sems.at[i]) for i, (source, target) in enumerate(pairs)
     ]
     for copy in copies:
         copy.start()
+    return copies
+
+
+def pack_two_kernel(split, gelu_w, output, two_o, sems):
+    width = gelu_w.shape[0]
+    pairs = (
+        (gelu_w.at[pl.ds(split, width - split)], two_o.at[pl.ds(0, width - split)]),
+        (output, two_o.at[pl.ds(width - split, width)]),
+    )
+    for copy in copy_all(pairs, sems):
+        copy.wait()
+
+
+def pack_one_kernel(split, gain_one, gain_two, value, gelu_w, one_o, sems):
+    width = value.shape[0]
+    pairs = (
+        (value, one_o.at[pl.ds(0, width)]),
+        (gelu_w.at[pl.ds(0, split)], one_o.at[pl.ds(width + 16, split)]),
+    )
+    copies = copy_all(pairs, sems)
     spare = jnp.zeros((14, value.shape[1]), F32)
     lines = jnp.concatenate([gain_one[...].astype(F32), gain_two[...].astype(F32), spare], 0)
     one_o[width : width + 16, :] = lines.astype(BF16)
@@ -319,14 +330,25 @@
     width, block = value.shape
     whole = pl.BlockSpec(memory_space=pltpu.VMEM)
     anywhere = pl.BlockSpec(memory_space=pl.ANY)
-    return launch(
-        lambda *refs: pack_kernel(split, *refs),
-        (gain_one, gain_two, in_hbm(value), in_hbm(gelu_w), in_hbm(output)),
-        (shaped((width + 16 + split, block), BF16), shaped((2 * width - split, block), BF16)),
-        "pack",
-        scratch=[pltpu.SemaphoreType.DMA((4,))],
-        grid=((), [whole, whole, anywhere, anywhere, anywhere], [whole, whole]),
-    )
+    value, gelu_w, output = in_hbm(value), in_hbm(gelu_w), in_hbm(output)
+    two = launch(
+        lambda *refs: pack_two_kernel(split, *refs),
+        (gelu_w, output),
+        shaped((2 * width - split, block), BF16),
+        "pack_two",
+        scratch=[pltpu.SemaphoreType.DMA((2,))],
+        grid=((), [anywhere, anywhere], whole),
+    )
+    one = launch(
+        lambda *refs: pack_one_kernel(split, *refs),
+        (gain_one, gain_two, value, gelu_w),
+        shaped((width + 16 + split, block), BF16),
+        "pack_one",
+        after=(two,),
+        scratch=[pltpu.SemaphoreType.DMA((2,))],
+        grid=((), [whole, whole, anywhere, anywhere], whole),
+    )
+    return one, two
 
 
 def prepare_kernel(scalars, slots, tokens, cotangent, gate_i, gate_r, x_o, g_o, flat_o, r_o, blocks_i, blocks_r):
@@ -429,7 +451,7 @@
         gains_o[o] = refs[o][width : width + 16, :].astype(F32)[0:2, :]
 
 
-def mixer_out(p, one, two, split):
+def mixer_out(p, one, two, split, after):
     total, width = p.shape
     count, block = len(one), one[0].shape[1]
     shape = (count, total // 2, block)
@@ -438,7 +460,8 @@
         (p, *one, *two),
         (shaped(shape, F32), shaped(shape, BF16), shaped((count, 2, block), F32)),
         "mixer_out",
-        mib=24,
+        after=after,
+        mib=10,
     )
 
 
@@ -465,7 +488,7 @@
         (shaped(shape, F32), shaped(shape, BF16)),
         "input_out",
         after=after,
-        mib=24,
+        mib=10,
     )
 
 
@@ -485,11 +508,16 @@
     return launch(relay_kernel, (source,), shaped(source.shape, source.dtype), "relay", after=after)
 
 
-def norm_kernel(slots, x, gains, pair, other, h_o, n_o, r_o):
+def norm_kernel(slots, x, full_gains, *refs):
+    h_o, n_o, r_o = refs[-3:]
     ring_size, half, block = h_o.shape
+    cut = ring_size // 2 + 1
+    groups = [refs[0:2], refs[2:4]]
     squares = jnp.zeros((half, block), F32)
     for o in range(ring_size):
-        h = x[o, 0:half, :].astype(F32) + (pair[o].astype(F32) + other[o].astype(F32))
+        pair, other = groups[o // cut]
+        i = o % cut
+        h = x[o, 0:half, :].astype(F32) + (pair[i].astype(F32) + other[i].astype(F32))
         h_o[o] = h
         squares = squares + h * h
     mean = jnp.sum(squares, 1, keepdims=True) * (1.0 / (ring_size * block))
@@ -497,15 +525,21 @@
     r_o[...] = scale
     for k in range(ring_size):
         o = slots[k]
-        n_o[:, k * block : (k + 1) * block] = (h_o[o] * scale * gains[o, 1:2, :]).astype(BF16)
-
-
-def norm(slots, x, gains, pair, other, after):
-    ring_size, half, block = pair.shape
+        gain = full_gains[o, 1:2, :]
+        n_o[:, k * block : (k + 1) * block] = (h_o[o] * scale * gain).astype(BF16)
+
+
+def norm(slots, x, gains, sums, after):
+    ring_size, total, block = x.shape
+    half = total // 2
     return launch(
         norm_kernel,
-        (slots, x, gains, pair, other),
-        (shaped(pair.shape, F32), shaped((half, ring_size * block), BF16), shaped((half, 1), F32)),
+        (slots, x, gains, *sums),
+        (
+            shaped((ring_size, half, block), F32),
+            shaped((half, ring_size * block), BF16),
+            shaped((half, 1), F32),
+        ),
         "norm",
         scalars=1,
         after=after,
@@ -588,7 +622,7 @@
         "finish",
         scalars=1,
         after=after,
-        mib=24,
+        mib=10,
     )
 
 
@@ -827,7 +861,7 @@
         tuple(out),
         "unit_term",
         after=after,
-        mib=24,
+        mib=10,
         flops=weight,
     )
 
@@ -936,7 +970,7 @@
         "mixer_term",
         scalars=1,
         after=after,
-        mib=24,
+        mib=10,
         flops=weight,
     )
 
@@ -1061,7 +1095,7 @@
     block = model // ring_size
     width, head = input_gate.shape
     count = conv_weight.shape[0]
-    split = (width // 2 + 127) // 128 * 128
+    split = width // 2 // 128 * 128
     chunk = -(-(2 * head + SUMS) // (16 * ring_size)) * 16
     small_rows = chunk * ring_size
 
@@ -1178,11 +1212,16 @@
         places |= {o: (place, i) for i, o in enumerate(offsets)}
 
     p, cx, lx, lr, h = mixer_forward(seqs, count, bx, by, lines, blocks_i, blocks_r)
-    own, other, gains = mixer_out(p, one, two, split)
-    pair, other = chip_swap(own, core_swap(other), ())
-    dq = unit_grad(g_flat, mlp_down, (pair,))
+    cut = ring_size // 2 + 1
+    own_a, other_a, gains_a = mixer_out(p, one[:cut], two[:cut], split, ())
+    got_a = core_swap(other_a)
+    own_b, other_b, gains_b = mixer_out(p, one[cut:], two[cut:], split, (own_a,))
+    sums_a = chip_swap(own_a, got_a, (own_b,))
+    sums_b = chip_swap(own_b, core_swap(other_b), tuple(token))
+    gains = jnp.concatenate([gains_a, gains_b])
+    dq = unit_grad(g_flat, mlp_down, tuple(token))
     fetched = fetch(mlp_gate, mlp_up, (dq,))
-    h1, n2_own, r2 = norm(slots, x, gains, pair, other, (fetched[0],))
+    h1, n2_own, r2 = norm(slots, x, gains, (*sums_a, *sums_b), (fetched[0],))
     n2 = both_halves(n2_own, 0)
     q_a, dga_a, dup_a, n2_rel = unit_first(slots, n2, *fetched, dq)
     unit_a = Scatter(lambda *a: unit_term(n2_rel, g, dga_a, dup_a, q_a, *a), unit_end, True)

time: 443 us -> 440 us (level)
  local copies, waits for them, and re-layouts: 30.8 us -> 19.8 us
  waiting for transfers between devices: 211 us -> 220 us
    ppermute x28, waiting for transfers between devices: 116 us -> 126 us  [step(): self.moving[d] = lax.ppermute(part, 'dp', (onward, backward)[d])]
    unnamed x166 -> x137, local copies, waits for them, and re-layouts: 25.4 us -> 17 us
    ppermute x3 -> x4, waiting for transfers between devices: 13.9 us -> 13.1 us  [chip_swap(): return (pair, lax.ppermute(pair, 'mp', chip_pair))]
    pallas_call x47 -> x50, Pallas kernels: 120 us -> 120 us  [launch(): pl.pallas_call(lambda *refs: kernel(*refs[:count], *refs[count + extra:])...]
  transfers between devices with their start and end apart: 61 -> 63, of which waited for: 37 -> 38; matrix products, arithmetic and copies ran while one was open for 1% -> 0% of each run, Pallas kernels for 25% -> 26%
where the time goes in v5:
time: 440 us; the launch traced here: 434 us
  waiting for transfers between devices  220 us (50%)
  Pallas kernels  131 us (30%)
  starting transfers between devices  60.7 us (14%)
  local copies, waits for them, and re-layouts  19.8 us (4%)
    ppermute x28, waiting for transfers between devices, step(): self.moving[d] = lax.ppermute(part, 'dp', (onward, backward)[d])  126 us
    pallas_call x50, Pallas kernels, launch(): pl.pallas_call(lambda *refs: kernel(*refs[:count], *refs[count + extra:])...  120 us
    ppermute x21, waiting for transfers between devices, step(): self.moving[d] = lax.ppermute(self.moving[d], 'dp', way)  77 us
    ppermute x28, starting transfers between devices, step(): self.moving[d] = lax.ppermute(part, 'dp', (onward, backward)[d])  29.8 us
    ppermute x21, starting transfers between devices, step(): self.moving[d] = lax.ppermute(self.moving[d], 'dp', way)  23.4 us
    unnamed x137, local copies, waits for them, and re-layouts  17 us
    ppermute x4, waiting for transfers between devices, chip_swap(): return (pair, lax.ppermute(pair, 'mp', chip_pair))  13.1 us
    pallas_call x1, Pallas kernels, unit_back(): pl.pallas_call(unit_back_kernel, grid_spec=pltpu.PrefetchScalarGridSpec(n...  11.4 us
  transfers between devices with their start and end apart: 63, of which 38 were waited for; matrix products, arithmetic and copies ran while one was open for 0% of the time, Pallas kernels for 26%

profile of v5, /device:TPU:0, one launch (start us, length us, event | category | flops | bytes accessed | tf_op | source)
XLA Modules:
  0.0 433.8 jit_solution(9602275330060129852)
XLA Ops:
  1.9 3.1 collective-permute-start.2
  7.3 2.1 collective-permute-start
  14.8 2.1 prepare.1
  16.9 12.0 %collective-permute-done.refs_4_.refs_3_.refs_9_ = bf16[976,256]{1,0:T(8,128)(2,1)S(1)} collective-permute-done((bf16[976,256]{1,0:T(8,128)(2,1)S(1)}, bf16[976,256]{1,0:T(8,128)(2,1)S(1)}, u32[]{:S(2)}, u32[]{:S(2)}) %collective-permute-start) | collective-permute-done | bytes 499744 | tf_op jit(solution)/shard_map/ppermute | solution.py:1119
  30.7 1.7 collective-permute-start.4
  34.1 10.3 %collective-permute-done.7.refs_4_.refs_8_.refs_3_.refs_12_ = bf16[1152,256]{1,0:T(8,128)(2,1)S(1)} collective-permute-done((bf16[1152,256]{1,0:T(8,128)(2,1)S(1)}, bf16[1152,256]{1,0:T(8,128)(2,1)S(1)}, u32[]{:S(2)}, u32[]{:S(2)}) %collective-permute-start.7) | collective-permute-done | bytes 589856 | tf_op jit(solution)/shard_map/ppermute | solution.py:1119
  47.0 10.7 %collective-permute-done.12.refs_5_.refs_7_.refs_16_ = bf16[1152,256]{1,0:T(8,128)(2,1)S(1)} collective-permute-done((bf16[1152,256]{1,0:T(8,128)(2,1)S(1)}, bf16[1152,256]{1,0:T(8,128)(2,1)S(1)}, u32[]{:S(2)}, u32[]{:S(2)}) %collective-permute-start.12) | collective-permute-done | bytes 589856 | tf_op jit(solution)/shard_map/ppermute | solution.py:1119
  57.7 1.7 collective-permute-start.13
  61.2 10.1 %collective-permute-done.10.refs_2_.refs_3_.refs_4_ = bf16[976,256]{1,0:T(8,128)(2,1)S(1)} collective-permute-done((bf16[976,256]{1,0:T(8,128)(2,1)S(1)}, bf16[976,256]{1,0:T(8,128)(2,1)S(1)}, u32[]{:S(2)}, u32[]{:S(2)}) %collective-permute-start.10) | collective-permute-done | bytes 499744 | tf_op jit(solution)/shard_map/ppermute | solution.py:1119
  76.2 15.1 %collective-permute-done.11.refs_2_.refs_4_.refs_5_ = bf16[976,256]{1,0:T(8,128)(2,1)S(1)} collective-permute-done((bf16[976,256]{1,0:T(8,128)(2,1)S(1)}, bf16[976,256]{1,0:T(8,128)(2,1)S(1)}, u32[]{:S(2)}, u32[]{:S(2)}) %collective-permute-start.11) | collective-permute-done | bytes 499744 | tf_op jit(solution)/shard_map/ppermute | solution.py:1119
  93.6 7.2 %mixer_forward.1 = (bf16[512,704]{1,0:T(8,128)(2,1)S(1)}, bf16[512,704]{1,0:T(8,128)(2,1)S(1)}, f32[512,704]{1,0:T(8,128)S(1)}, f32[512,704]{1,0:T(8,128)S(1)}, f32[512,704]{1,0:T(8,128)S(1)}) custom-call(f32[512,704]{1,0:T(8,128)S(1)} %get-tuple-element.146.refs_0_.refs_9_, f32[512,704]{1,0:T(8,128)S(1)} %get-tuple-element.147.refs_1_.refs_10_, ...), custom_call_target="tpu_custom_call" | custom-call | flops 1 | bytes 1 | tf_op jit(solution)/shard_map/mixer_forward/pallas_call | solution.py:75
  108.2 7.0 %unit_grad.1.refs_2_.refs_4_.refs_3_ = f32[512,1536]{1,0:T(8,128)S(1)} custom-call(bf16[512,2048]{1,0:T(8,128)(2,1)S(1)} %get-tuple-element.157.refs_0_, bf16[1536,2048]{1,0:T(8,128)(2,1)} %refs_2_.3, bf16[3,256,256]{2,1,0:T(8,128)(2,1)S(1)} %pair_sum.6.refs_2_.refs_5_), custom_call_target="tpu_custom_call" | custom-call | flops 1 | bytes 1 | tf_op jit(solution)/shard_map/unit_grad/pallas_call | solution.py:75
  115.1 2.9 fetch.1
  118.0 13.1 %collective-permute-done.17.refs_6_ = bf16[3,256,256]{2,1,0:T(8,128)(2,1)S(1)} collective-permute-done((bf16[3,256,256]{2,1,0:T(8,128)(2,1)S(1)}, bf16[3,256,256]{2,1,0:T(8,128)(2,1)S(1)}, u32[]{:S(2)}, u32[]{:S(2)}) %collective-permute-start.17) | collective-permute-done | bytes 393248 | tf_op jit(solution)/shard_map/ppermute | solution.py:1160
  132.7 2.6 collective-permute-done.18
  135.4 5.1 %unit_first.1 = (bf16[512,768]{1,0:T(8,128)(2,1)S(1)}, bf16[512,768]{1,0:T(8,128)(2,1)S(1)}, bf16[512,768]{1,0:T(8,128)(2,1)S(1)}, bf16[8,512,256]{2,1,0:T(8,128)(2,1)S(1)}) custom-call(s32[8]{0:T(128)S(1)} %and_select_fusion.1.refs_1_.refs_0_, bf16[512,2048]{1,0:T(8,128)(2,1)S(1)} %constant_dynamic-update-slice_fusion.2.refs_1_.refs_0_, ...), custom_call_target="tpu_custom_call" | custom-call | flops 1 | bytes 1 | tf_op jit(solution)/shard_map/unit_first/pallas_call | solution.py:75
  144.1 6.7 %unit_second.1 = (bf16[512,768]{1,0:T(8,128)(2,1)S(1)}, bf16[512,768]{1,0:T(8,128)(2,1)S(1)}, bf16[512,768]{1,0:T(8,128)(2,1)S(1)}) custom-call(bf16[512,2048]{1,0:T(8,128)(2,1)S(1)} %constant_dynamic-update-slice_fusion.2.refs_1_.refs_0_, bf16[2048,1536]{1,0:T(8,128)(2,1)} %gate.1, bf16[2048,1536]{1,0:T(8,128)(2,1)} %up.1, ...), custom_call_target="tpu_custom_call" | custom-call | flops 1 | bytes 1 | tf_op jit(solution)/shard_map/unit_second/pallas_call | solution.py:75
  153.9 11.4 %unit_back.1 = (f32[8,256,256]{2,1,0:T(8,128)S(1)}, bf16[8,256,256]{2,1,0:T(8,128)(2,1)S(1)}) custom-call(s32[8]{0:T(128)S(1)} %compare_select_fusion.5.owners.refs_0_, bf16[512,768]{1,0:T(8,128)(2,1)S(1)} %get-tuple-element.165.refs_2_.dga_a, bf16[512,768]{1,0:T(8,128)(2,1)S(1)} %get-tuple-element.170.refs_2_.dga_b, ...), custom_call_target="tpu_custom_call" | custom-call | flops 1 | bytes 1 | tf_op jit(solution)/shard_map/unit_back/pallas_call | solution.py:808
  165.8 5.0 %collective-permute-done.19.refs_5_ = bf16[256,2304]{1,0:T(8,128)(2,1)S(1)} collective-permute-done((bf16[256,2304]{1,0:T(8,128)(2,1)S(1)}, bf16[256,2304]{1,0:T(8,128)(2,1)S(1)}, u32[]{:S(2)}, u32[]{:S(2)}) %collective-permute-start.19) | collective-permute-done | bytes 1179680 | tf_op jit(solution)/shard_map/ppermute | solution.py:1141
  178.7 17.5 %collective-permute-done.23.refs_5_ = bf16[256,2304]{1,0:T(8,128)(2,1)S(1)} collective-permute-done((bf16[256,2304]{1,0:T(8,128)(2,1)S(1)}, bf16[256,2304]{1,0:T(8,128)(2,1)S(1)}, u32[]{:S(2)}, u32[]{:S(2)}) %collective-permute-start.23) | collective-permute-done | bytes 1179680 | tf_op jit(solution)/shard_map/ppermute | solution.py:1141
  201.3 20.1 %collective-permute-done.21.refs_5_ = bf16[256,2304]{1,0:T(8,128)(2,1)S(1)} collective-permute-done((bf16[256,2304]{1,0:T(8,128)(2,1)S(1)}, bf16[256,2304]{1,0:T(8,128)(2,1)S(1)}, u32[]{:S(2)}, u32[]{:S(2)}) %collective-permute-start.21) | collective-permute-done | bytes 1179680 | tf_op jit(solution)/shard_map/ppermute | solution.py:1141
  223.0 2.5 unit_term.12
  227.1 3.4 norm_back.1
  231.1 15.6 %collective-permute-done.30.refs_5_ = bf16[256,2304]{1,0:T(8,128)(2,1)S(1)} collective-permute-done((bf16[256,2304]{1,0:T(8,128)(2,1)S(1)}, bf16[256,2304]{1,0:T(8,128)(2,1)S(1)}, u32[]{:S(2)}, u32[]{:S(2)}) %collective-permute-start.30) | collective-permute-done | bytes 1179680 | tf_op jit(solution)/shard_map/ppermute | solution.py:1141
  248.4 2.5 unit_term.13
  251.3 1.8 collective-permute-start.35
  255.1 13.8 %mixer_backward.1 = (bf16[512,704]{1,0:T(8,128)(2,1)S(1)}, bf16[512,704]{1,0:T(8,128)(2,1)S(1)}, bf16[384,704]{1,0:T(8,128)(2,1)S(1)}) custom-call(bf16[8,512,256]{2,1,0:T(8,128)(2,1)S(1)} %constant_dynamic-update-slice_fusion.4.refs_0_.refs_5_, bf16[1152,256]{1,0:T(8,128)(2,1)S(1)} %pack_two.1.refs_4_.refs_5_.refs_6_.refs_1_.refs_10_, ...), custom_call_target="tpu_custom_call" | custom-call | flops 1 | bytes 1 | tf_op jit(solution)/shard_map/mixer_backward/pallas_call | solution.py:75
  270.3 1.8 collective-permute-done.26.refs_5_
  273.7 3.6 unit_term.14
  277.3 7.7 %unit_out.1 = (f32[256,2048]{1,0:T(8,128)S(1)}, bf16[256,2048]{1,0:T(8,128)(2,1)S(1)}) custom-call(bf16[512,768]{1,0:T(8,128)(2,1)S(1)} %copy-done.49, bf16[512,768]{1,0:T(8,128)(2,1)S(1)} %copy-done.36, bf16[1536,2048]{1,0:T(8,128)(2,1)} %refs_2_.3, bf16[256,2304]{1,0:T(8,128)(2,1)} %get-tuple-element.196.refs_3_), custom_call_target="tpu_custom_call" | custom-call | flops 1 | bytes 1 | tf_op jit(solution)/shard_map/unit_out/pallas_call | solution.py:75
  291.1 3.4 input_out.1
  294.5 4.5 %collective-permute-done.34.refs_5_ = bf16[256,2304]{1,0:T(8,128)(2,1)} collective-permute-done((bf16[256,2304]{1,0:T(8,128)(2,1)}, bf16[256,2304]{1,0:T(8,128)(2,1)}, u32[]{:S(2)}, u32[]{:S(2)}) %collective-permute-start.34) | collective-permute-done | bytes 1179680 | tf_op jit(solution)/shard_map/ppermute | solution.py:1141
  299.0 3.1 unit_term.15
  304.7 4.7 %collective-permute-done.39.refs_9_ = bf16[1104,256]{1,0:T(8,128)(2,1)S(1)} collective-permute-done((bf16[1104,256]{1,0:T(8,128)(2,1)S(1)}, bf16[1104,256]{1,0:T(8,128)(2,1)S(1)}, u32[]{:S(2)}, u32[]{:S(2)}) %collective-permute-start.39) | collective-permute-done | bytes 565280 | tf_op jit(solution)/shard_map/ppermute | solution.py:1141
  314.4 20.4 %collective-permute-done.38.refs_3_ = bf16[256,2304]{1,0:T(8,128)(2,1)} collective-permute-done((bf16[256,2304]{1,0:T(8,128)(2,1)}, bf16[256,2304]{1,0:T(8,128)(2,1)}, u32[]{:S(2)}, u32[]{:S(2)}) %collective-permute-start.38) | collective-permute-done | bytes 1179680 | tf_op jit(solution)/shard_map/ppermute | solution.py:1141
  340.0 2.5 unit_end.3
  343.9 2.5 input_back.1
  353.0 6.4 %collective-permute-done.46.refs_8_ = bf16[1152,256]{1,0:T(8,128)(2,1)S(1)} collective-permute-done((bf16[1152,256]{1,0:T(8,128)(2,1)S(1)}, bf16[1152,256]{1,0:T(8,128)(2,1)S(1)}, u32[]{:S(2)}, u32[]{:S(2)}) %collective-permute-start.46) | collective-permute-done | bytes 589856 | tf_op jit(solution)/shard_map/ppermute | solution.py:1141
  364.6 6.9 %collective-permute-done.44.refs_9_ = bf16[1104,256]{1,0:T(8,128)(2,1)S(1)} collective-permute-done((bf16[1104,256]{1,0:T(8,128)(2,1)S(1)}, bf16[1104,256]{1,0:T(8,128)(2,1)S(1)}, u32[]{:S(2)}, u32[]{:S(2)}) %collective-permute-start.44) | collective-permute-done | bytes 565280 | tf_op jit(solution)/shard_map/ppermute | solution.py:1141
  376.1 2.0 finish.1.refs_10_.refs_1_
  378.2 5.9 %collective-permute-done.49.refs_8_ = bf16[1152,256]{1,0:T(8,128)(2,1)S(1)} collective-permute-done((bf16[1152,256]{1,0:T(8,128)(2,1)S(1)}, bf16[1152,256]{1,0:T(8,128)(2,1)S(1)}, u32[]{:S(2)}, u32[]{:S(2)}) %collective-permute-start.49) | collective-permute-done | bytes 589856 | tf_op jit(solution)/shard_map/ppermute | solution.py:1141
  388.2 4.5 %arrange.1 = (f32[2,256,2048]{2,1,0:T(8,128)}, f32[2,256,2048]{2,1,0:T(8,128)}) custom-call(s32[3]{0:T(128)S(1)} %copy-done.57, f32[2,256,2048]{2,1,0:T(8,128)S(1)} %finish.1.refs_10_.refs_1_, f32[2,256,2048]{2,1,0:T(8,128)S(1)} %collective-permute-done.48.refs_2_, bf16[1152,256]{1,0:T(8,128)(2,1)S(1)} %get-tuple-element.227.refs_3_), custom_call_target="tpu_custom_call" | custom-call | flops 1 | bytes 1 | tf_op jit(solution)/shard_map/arrange/pallas_call | solution.py:75
  392.7 3.6 collective-permute-done.51.refs_3_
  396.3 2.2 copy-done.58
  398.4 1.7 mixer_end.2
  405.4 4.8 %collective-permute-done.56.refs_8_ = bf16[64,704]{1,0:T(8,128)(2,1)S(1)} collective-permute-done((bf16[64,704]{1,0:T(8,128)(2,1)S(1)}, bf16[64,704]{1,0:T(8,128)(2,1)S(1)}, u32[]{:S(2)}, u32[]{:S(2)}) %collective-permute-start.56) | collective-permute-done | bytes 90144 | tf_op jit(solution)/shard_map/ppermute | solution.py:1119
  411.8 6.5 %collective-permute-done.53.refs_2_ = bf16[64,704]{1,0:T(8,128)(2,1)S(1)} collective-permute-done((bf16[64,704]{1,0:T(8,128)(2,1)S(1)}, bf16[64,704]{1,0:T(8,128)(2,1)S(1)}, u32[]{:S(2)}, u32[]{:S(2)}) %collective-permute-start.53) | collective-permute-done | bytes 90144 | tf_op jit(solution)/shard_map/ppermute | solution.py:1119
  421.4 2.4 collective-permute-done.54.refs_3_
  (283 shorter events, 123.8 us)
Async XLA Ops:
  1.9 28.6 %collective-permute-start.2 = (bf16[1152,256]{1,0:T(8,128)(2,1)S(1)}, bf16[1152,256]{1,0:T(8,128)(2,1)S(1)}, u32[]{:S(2)}, u32[]{:S(2)}) collective-permute-start(bf16[1152,256]{1,0:T(8,128)(2,1)S(1)} %pack_two.1.refs_4_.refs_5_.refs_6_.refs_1_.refs_10_), channel_id=1, source_target_pairs={{0,8},{8,16},{16,24},{24,28},{28,20},{20,12},{12,4},{4,0},{1,9},{9... | collective-permute-start | bytes 1769480 | tf_op jit(solution)/shard_map/ppermute | solution.py:1119
  5.0 25.5 %collective-permute-start.3 = (bf16[1152,256]{1,0:T(8,128)(2,1)S(1)}, bf16[1152,256]{1,0:T(8,128)(2,1)S(1)}, u32[]{:S(2)}, u32[]{:S(2)}) collective-permute-start(bf16[1152,256]{1,0:T(8,128)(2,1)S(1)} %pack_two.1.refs_4_.refs_5_.refs_6_.refs_1_.refs_10_), channel_id=1, source_target_pairs={{8,0},{16,8},{24,16},{28,24},{20,28},{12,20},{4,12},{0,4},{9,1},{1... | collective-permute-start | bytes 1769480 | tf_op jit(solution)/shard_map/ppermute | solution.py:1119
  7.3 21.6 %collective-permute-start = (bf16[976,256]{1,0:T(8,128)(2,1)S(1)}, bf16[976,256]{1,0:T(8,128)(2,1)S(1)}, u32[]{:S(2)}, u32[]{:S(2)}) collective-permute-start(bf16[976,256]{1,0:T(8,128)(2,1)S(1)} %pack_one.1.refs_2_.refs_1_), channel_id=1, source_target_pairs={{0,8},{8,16},{16,24},{24,28},{28,20},{20,12},{12,4},{4,0},{1,9},{9... | collective-permute-start | bytes 1499144 | tf_op jit(solution)/shard_map/ppermute | solution.py:1119
  9.4 21.1 %collective-permute-start.1 = (bf16[976,256]{1,0:T(8,128)(2,1)S(1)}, bf16[976,256]{1,0:T(8,128)(2,1)S(1)}, u32[]{:S(2)}, u32[]{:S(2)}) collective-permute-start(bf16[976,256]{1,0:T(8,128)(2,1)S(1)} %pack_one.1.refs_2_.refs_1_), channel_id=1, source_target_pairs={{8,0},{16,8},{24,16},{28,24},{20,28},{12,20},{4,12},{0,4},{9,1},{1... | collective-permute-start | bytes 1499144 | tf_op jit(solution)/shard_map/ppermute | solution.py:1119
  30.7 15.7 %collective-permute-start.4 = (bf16[976,256]{1,0:T(8,128)(2,1)S(1)}, bf16[976,256]{1,0:T(8,128)(2,1)S(1)}, u32[]{:S(2)}, u32[]{:S(2)}) collective-permute-start(bf16[976,256]{1,0:T(8,128)(2,1)S(1)} %collective-permute-done.refs_4_.refs_3_.refs_9_), channel_id=1, source_target_pairs={{0,8},{8,16},{16,24},{24,28},{28,20},{20,12},{12,4},{4,0},{1,9},{9... | collective-permute-start | bytes 1499144 | tf_op jit(solution)/shard_map/ppermute | solution.py:1119
  32.5 25.2 %collective-permute-start.12 = (bf16[1152,256]{1,0:T(8,128)(2,1)S(1)}, bf16[1152,256]{1,0:T(8,128)(2,1)S(1)}, u32[]{:S(2)}, u32[]{:S(2)}) collective-permute-start(bf16[1152,256]{1,0:T(8,128)(2,1)S(1)} %collective-permute-done.2.refs_7_.refs_6_.refs_8_.refs_17_), channel_id=1, source_target_pairs={{0,8},{8,16},{16,24},{24,28},{28,20},{20,12},{12,4},{4,0},{1,9},{9... | collective-permute-start | bytes 1769480 | tf_op jit(solution)/shard_map/ppermute | solution.py:1119
  44.3 16.3 %collective-permute-start.8 = (bf16[1152,256]{1,0:T(8,128)(2,1)S(1)}, bf16[1152,256]{1,0:T(8,128)(2,1)S(1)}, u32[]{:S(2)}, u32[]{:S(2)}) collective-permute-start(bf16[1152,256]{1,0:T(8,128)(2,1)S(1)} %collective-permute-done.7.refs_4_.refs_8_.refs_3_.refs_12_), channel_id=1, source_target_pairs={{8,0},{16,8},{24,16},{28,24},{20,28},{12,20},{4,12},{0,4},{9,1},{1... | collective-permute-start | bytes 1769480 | tf_op jit(solution)/shard_map/ppermute | solution.py:1119
  44.9 26.4 %collective-permute-start.10 = (bf16[976,256]{1,0:T(8,128)(2,1)S(1)}, bf16[976,256]{1,0:T(8,128)(2,1)S(1)}, u32[]{:S(2)}, u32[]{:S(2)}) collective-permute-start(bf16[976,256]{1,0:T(8,128)(2,1)S(1)} %collective-permute-done.1.refs_3_.refs_2_), channel_id=1, source_target_pairs={{8,0},{16,8},{24,16},{28,24},{20,28},{12,20},{4,12},{0,4},{9,1},{1... | collective-permute-start | bytes 1499144 | tf_op jit(solution)/shard_map/ppermute | solution.py:1119
  46.5 25.4 %collective-permute-start.5 = (bf16[976,256]{1,0:T(8,128)(2,1)S(1)}, bf16[976,256]{1,0:T(8,128)(2,1)S(1)}, u32[]{:S(2)}, u32[]{:S(2)}) collective-permute-start(bf16[976,256]{1,0:T(8,128)(2,1)S(1)} %collective-permute-done.4.refs_3_.refs_2_.refs_8_), channel_id=1, source_target_pairs={{0,8},{8,16},{16,24},{24,28},{28,20},{20,12},{12,4},{4,0},{1,9},{9... | collective-permute-start | bytes 1499144 | tf_op jit(solution)/shard_map/ppermute | solution.py:1119
  57.7 33.6 %collective-permute-start.13 = (bf16[1152,256]{1,0:T(8,128)(2,1)S(1)}, bf16[1152,256]{1,0:T(8,128)(2,1)S(1)}, u32[]{:S(2)}, u32[]{:S(2)}) collective-permute-start(bf16[1152,256]{1,0:T(8,128)(2,1)S(1)} %collective-permute-done.12.refs_5_.refs_7_.refs_16_), channel_id=1, source_target_pairs={{0,8},{8,16},{16,24},{24,28},{28,20},{20,12},{12,4},{4,0},{1,9},{9... | collective-permute-start | bytes 1769480 | tf_op jit(solution)/shard_map/ppermute | solution.py:1119
  60.6 32.1 %collective-permute-start.9 = (bf16[1152,256]{1,0:T(8,128)(2,1)S(1)}, bf16[1152,256]{1,0:T(8,128)(2,1)S(1)}, u32[]{:S(2)}, u32[]{:S(2)}) collective-permute-start(bf16[1152,256]{1,0:T(8,128)(2,1)S(1)} %collective-permute-done.8.refs_4_.refs_9_.refs_13_), channel_id=1, source_target_pairs={{8,0},{16,8},{24,16},{28,24},{20,28},{12,20},{4,12},{0,4},{9,1},{1... | collective-permute-start | bytes 1769480 | tf_op jit(solution)/shard_map/ppermute | solution.py:1119
  71.3 20.0 %collective-permute-start.11 = (bf16[976,256]{1,0:T(8,128)(2,1)S(1)}, bf16[976,256]{1,0:T(8,128)(2,1)S(1)}, u32[]{:S(2)}, u32[]{:S(2)}) collective-permute-start(bf16[976,256]{1,0:T(8,128)(2,1)S(1)} %collective-permute-done.10.refs_2_.refs_3_.refs_4_), channel_id=1, source_target_pairs={{8,0},{16,8},{24,16},{28,24},{20,28},{12,20},{4,12},{0,4},{9,1},{1... | collective-permute-start | bytes 1499144 | tf_op jit(solution)/shard_map/ppermute | solution.py:1119
  71.9 20.8 %collective-permute-start.6 = (bf16[976,256]{1,0:T(8,128)(2,1)S(1)}, bf16[976,256]{1,0:T(8,128)(2,1)S(1)}, u32[]{:S(2)}, u32[]{:S(2)}) collective-permute-start(bf16[976,256]{1,0:T(8,128)(2,1)S(1)} %collective-permute-done.5.refs_3_.refs_1_.refs_7_), channel_id=1, source_target_pairs={{0,8},{8,16},{16,24},{24,28},{28,20},{20,12},{12,4},{4,0},{1,9},{9... | collective-permute-start | bytes 1499144 | tf_op jit(solution)/shard_map/ppermute | solution.py:1119
  105.9 25.3 %collective-permute-start.15 = (bf16[5,256,256]{2,1,0:T(8,128)(2,1)S(1)}, bf16[5,256,256]{2,1,0:T(8,128)(2,1)S(1)}, u32[]{:S(2)}, u32[]{:S(2)}) collective-permute-start(bf16[5,256,256]{2,1,0:T(8,128)(2,1)S(1)} %pair_sum.5.refs_2_.refs_3_), channel_id=1, source_target_pairs={{0,2},{1,3},{2,0},{3,1},{4,6},{5,7},{6,4},{7,5},{8,10},{9,11},{10,... | collective-permute-start | bytes 1966088 | tf_op jit(solution)/shard_map/ppermute | solution.py:1160
  107.6 23.6 %collective-permute-start.17 = (bf16[3,256,256]{2,1,0:T(8,128)(2,1)S(1)}, bf16[3,256,256]{2,1,0:T(8,128)(2,1)S(1)}, u32[]{:S(2)}, u32[]{:S(2)}) collective-permute-start(bf16[3,256,256]{2,1,0:T(8,128)(2,1)S(1)} %pair_sum.6.refs_2_.refs_5_), channel_id=1, source_target_pairs={{0,2},{1,3},{2,0},{3,1},{4,6},{5,7},{6,4},{7,5},{8,10},{9,11},{10,... | collective-permute-start | bytes 1179656 | tf_op jit(solution)/shard_map/ppermute | solution.py:1160
  142.0 28.9 %collective-permute-start.19 = (bf16[256,2304]{1,0:T(8,128)(2,1)S(1)}, bf16[256,2304]{1,0:T(8,128)(2,1)S(1)}, u32[]{:S(2)}, u32[]{:S(2)}) collective-permute-start(bf16[256,2304]{1,0:T(8,128)(2,1)S(1)} %get-tuple-element.167.refs_4_.refs_5_), channel_id=1, source_target_pairs={{0,8},{8,16},{16,24},{24,28},{28,20},{20,12},{12,4},{4,0},{1,9},{9... | collective-permute-start | bytes 3538952 | tf_op jit(solution)/shard_map/ppermute | solution.py:1141
  143.6 28.9 %collective-permute-start.20 = (bf16[256,2304]{1,0:T(8,128)(2,1)S(1)}, bf16[256,2304]{1,0:T(8,128)(2,1)S(1)}, u32[]{:S(2)}, u32[]{:S(2)}) collective-permute-start(bf16[256,2304]{1,0:T(8,128)(2,1)S(1)} %get-tuple-element.169), channel_id=1, source_target_pairs={{8,0},{16,8},{24,16},{28,24},{20,28},{12,20},{4,12},{0,4},{9,1},{1... | collective-permute-start | bytes 3538952 | tf_op jit(solution)/shard_map/ppermute | solution.py:1141
  152.2 43.9 %collective-permute-start.23 = (bf16[256,2304]{1,0:T(8,128)(2,1)S(1)}, bf16[256,2304]{1,0:T(8,128)(2,1)S(1)}, u32[]{:S(2)}, u32[]{:S(2)}) collective-permute-start(bf16[256,2304]{1,0:T(8,128)(2,1)S(1)} %get-tuple-element.172.refs_0_), channel_id=1, source_target_pairs={{0,8},{8,16},{16,24},{24,28},{28,20},{20,12},{12,4},{4,0},{1,9},{9... | collective-permute-start | bytes 3538952 | tf_op jit(solution)/shard_map/ppermute | solution.py:1141
  165.3 32.4 %collective-permute-start.24 = (bf16[256,2304]{1,0:T(8,128)(2,1)S(1)}, bf16[256,2304]{1,0:T(8,128)(2,1)S(1)}, u32[]{:S(2)}, u32[]{:S(2)}) collective-permute-start(bf16[256,2304]{1,0:T(8,128)(2,1)S(1)} %get-tuple-element.176), channel_id=1, source_target_pairs={{8,0},{16,8},{24,16},{28,24},{20,28},{12,20},{4,12},{0,4},{9,1},{1... | collective-permute-start | bytes 3538952 | tf_op jit(solution)/shard_map/ppermute | solution.py:1141
  173.9 47.5 %collective-permute-start.21 = (bf16[256,2304]{1,0:T(8,128)(2,1)S(1)}, bf16[256,2304]{1,0:T(8,128)(2,1)S(1)}, u32[]{:S(2)}, u32[]{:S(2)}) collective-permute-start(bf16[256,2304]{1,0:T(8,128)(2,1)S(1)} %get-tuple-element.174.refs_2_), channel_id=1, source_target_pairs={{0,8},{8,16},{16,24},{24,28},{28,20},{20,12},{12,4},{4,0},{1,9},{9... | collective-permute-start | bytes 3538952 | tf_op jit(solution)/shard_map/ppermute | solution.py:1141
  175.5 47.5 %collective-permute-start.22 = (bf16[256,2304]{1,0:T(8,128)(2,1)S(1)}, bf16[256,2304]{1,0:T(8,128)(2,1)S(1)}, u32[]{:S(2)}, u32[]{:S(2)}) collective-permute-start(bf16[256,2304]{1,0:T(8,128)(2,1)S(1)} %get-tuple-element.175), channel_id=1, source_target_pairs={{8,0},{16,8},{24,16},{28,24},{20,28},{12,20},{4,12},{0,4},{9,1},{1... | collective-permute-start | bytes 3538952 | tf_op jit(solution)/shard_map/ppermute | solution.py:1141
  177.2 49.9 %collective-permute-start.28 = (bf16[8,256,256]{2,1,0:T(8,128)(2,1)}, bf16[8,256,256]{2,1,0:T(8,128)(2,1)}, u32[]{:S(2)}, u32[]{:S(2)}) collective-permute-start(bf16[8,256,256]{2,1,0:T(8,128)(2,1)} %pair_sum.7.refs_7_.refs_0_), channel_id=1, source_target_pairs={{0,2},{1,3},{2,0},{3,1},{4,6},{5,7},{6,4},{7,5},{8,10},{9,11},{10,... | collective-permute-start | bytes 3145736 | tf_op jit(solution)/shard_map/ppermute | solution.py:1160
  199.2 47.5 %collective-permute-start.30 = (bf16[256,2304]{1,0:T(8,128)(2,1)S(1)}, bf16[256,2304]{1,0:T(8,128)(2,1)S(1)}, u32[]{:S(2)}, u32[]{:S(2)}) collective-permute-start(bf16[256,2304]{1,0:T(8,128)(2,1)S(1)} %get-tuple-element.178.refs_7_), channel_id=1, source_target_pairs={{0,8},{8,16},{16,24},{24,28},{28,20},{20,12},{12,4},{4,0},{1,9},{9... | collective-permute-start | bytes 3538952 | tf_op jit(solution)/shard_map/ppermute | solution.py:1141
  200.8 47.5 %collective-permute-start.31 = (bf16[256,2304]{1,0:T(8,128)(2,1)S(1)}, bf16[256,2304]{1,0:T(8,128)(2,1)S(1)}, u32[]{:S(2)}, u32[]{:S(2)}) collective-permute-start(bf16[256,2304]{1,0:T(8,128)(2,1)S(1)} %get-tuple-element.191), channel_id=1, source_target_pairs={{8,0},{16,8},{24,16},{28,24},{20,28},{12,20},{4,12},{0,4},{9,1},{1... | collective-permute-start | bytes 3538952 | tf_op jit(solution)/shard_map/ppermute | solution.py:1141
  225.5 46.5 %collective-permute-start.26 = (bf16[256,2304]{1,0:T(8,128)(2,1)}, bf16[256,2304]{1,0:T(8,128)(2,1)}, u32[]{:S(2)}, u32[]{:S(2)}) collective-permute-start(bf16[256,2304]{1,0:T(8,128)(2,1)} %get-tuple-element.179.refs_6_), channel_id=1, source_target_pairs={{0,8},{8,16},{16,24},{24,28},{28,20},{20,12},{12,4},{4,0},{1,9},{9... | collective-permute-start | bytes 3538952 | tf_op jit(solution)/shard_map/ppermute | solution.py:1141
  230.5 22.7 %collective-permute-start.29 = (bf16[8,256,256]{2,1,0:T(8,128)(2,1)S(1)}, bf16[8,256,256]{2,1,0:T(8,128)(2,1)S(1)}, u32[]{:S(2)}, u32[]{:S(2)}) collective-permute-start(bf16[8,256,256]{2,1,0:T(8,128)(2,1)S(1)} %get-tuple-element.186.refs_7_), channel_id=1, source_target_pairs={{0,1},{1,0},{2,3},{3,2},{4,5},{5,4},{6,7},{7,6},{8,9},{9,8},{10,11... | collective-permute-start | bytes 3145736 | tf_op jit(solution)/shard_map/ppermute | solution.py:1163
  230.6 43.1 %collective-permute-start.27 = (bf16[256,2304]{1,0:T(8,128)(2,1)}, bf16[256,2304]{1,0:T(8,128)(2,1)}, u32[]{:S(2)}, u32[]{:S(2)}) collective-permute-start(bf16[256,2304]{1,0:T(8,128)(2,1)} %get-tuple-element.180), channel_id=1, source_target_pairs={{8,0},{16,8},{24,16},{28,24},{20,28},{12,20},{4,12},{0,4},{9,1},{1... | collective-permute-start | bytes 3538952 | tf_op jit(solution)/shard_map/ppermute | solution.py:1141
  250.8 48.1 %collective-permute-start.34 = (bf16[256,2304]{1,0:T(8,128)(2,1)}, bf16[256,2304]{1,0:T(8,128)(2,1)}, u32[]{:S(2)}, u32[]{:S(2)}) collective-permute-start(bf16[256,2304]{1,0:T(8,128)(2,1)} %get-tuple-element.202), channel_id=1, source_target_pairs={{8,0},{16,8},{24,16},{28,24},{20,28},{12,20},{4,12},{0,4},{9,1},{1... | collective-permute-start | bytes 3538952 | tf_op jit(solution)/shard_map/ppermute | solution.py:1141
  251.3 47.7 %collective-permute-start.35 = (bf16[256,2304]{1,0:T(8,128)(2,1)}, bf16[256,2304]{1,0:T(8,128)(2,1)}, u32[]{:S(2)}, u32[]{:S(2)}) collective-permute-start(bf16[256,2304]{1,0:T(8,128)(2,1)} %get-tuple-element.192.refs_18_), channel_id=1, source_target_pairs={{0,8},{8,16},{16,24},{24,28},{28,20},{20,12},{12,4},{4,0},{1,9},{9... | collective-permute-start | bytes 3538952 | tf_op jit(solution)/shard_map/ppermute | solution.py:1141
  285.1 24.3 %collective-permute-start.39 = (bf16[1104,256]{1,0:T(8,128)(2,1)S(1)}, bf16[1104,256]{1,0:T(8,128)(2,1)S(1)}, u32[]{:S(2)}, u32[]{:S(2)}) collective-permute-start(bf16[1104,256]{1,0:T(8,128)(2,1)S(1)} %get-tuple-element.195.refs_7_), channel_id=1, source_target_pairs={{0,8},{8,16},{16,24},{24,28},{28,20},{20,12},{12,4},{4,0},{1,9},{9... | collective-permute-start | bytes 1695752 | tf_op jit(solution)/shard_map/ppermute | solution.py:1141
  286.7 24.2 %collective-permute-start.40 = (bf16[1104,256]{1,0:T(8,128)(2,1)S(1)}, bf16[1104,256]{1,0:T(8,128)(2,1)S(1)}, u32[]{:S(2)}, u32[]{:S(2)}) collective-permute-start(bf16[1104,256]{1,0:T(8,128)(2,1)S(1)} %get-tuple-element.212), channel_id=1, source_target_pairs={{8,0},{16,8},{24,16},{28,24},{20,28},{12,20},{4,12},{0,4},{9,1},{1... | collective-permute-start | bytes 1695752 | tf_op jit(solution)/shard_map/ppermute | solution.py:1141
  287.8 47.0 %collective-permute-start.38 = (bf16[256,2304]{1,0:T(8,128)(2,1)}, bf16[256,2304]{1,0:T(8,128)(2,1)}, u32[]{:S(2)}, u32[]{:S(2)}) collective-permute-start(bf16[256,2304]{1,0:T(8,128)(2,1)} %get-tuple-element.196.refs_3_), channel_id=1, source_target_pairs={{0,8},{8,16},{16,24},{24,28},{28,20},{20,12},{12,4},{4,0},{1,9},{9... | collective-permute-start | bytes 3538952 | tf_op jit(solution)/shard_map/ppermute | solution.py:1141
  302.1 37.4 %collective-permute-start.37 = (bf16[256,2304]{1,0:T(8,128)(2,1)S(1)}, bf16[256,2304]{1,0:T(8,128)(2,1)S(1)}, u32[]{:S(2)}, u32[]{:S(2)}) collective-permute-start(bf16[256,2304]{1,0:T(8,128)(2,1)S(1)} %get-tuple-element.203.refs_2_), channel_id=1, source_target_pairs={{8,0},{16,8},{24,16},{28,24},{20,28},{12,20},{4,12},{0,4},{9,1},{1... | collective-permute-start | bytes 3538952 | tf_op jit(solution)/shard_map/ppermute | solution.py:1141
  303.1 39.3 %collective-permute-start.36 = (bf16[8,256,256]{2,1,0:T(8,128)(2,1)S(1)}, bf16[8,256,256]{2,1,0:T(8,128)(2,1)S(1)}, u32[]{:S(2)}, u32[]{:S(2)}) collective-permute-start(bf16[8,256,256]{2,1,0:T(8,128)(2,1)S(1)} %pair_sum.9.refs_11_.refs_1_), channel_id=1, source_target_pairs={{0,2},{1,3},{2,0},{3,1},{4,6},{5,7},{6,4},{7,5},{8,10},{9,11},{10,... | collective-permute-start | bytes 3145736 | tf_op jit(solution)/shard_map/ppermute | solution.py:1160
  312.3 37.3 %collective-permute-start.42 = (bf16[1104,256]{1,0:T(8,128)(2,1)S(1)}, bf16[1104,256]{1,0:T(8,128)(2,1)S(1)}, u32[]{:S(2)}, u32[]{:S(2)}) collective-permute-start(bf16[1104,256]{1,0:T(8,128)(2,1)S(1)} %get-tuple-element.213.refs_4_), channel_id=1, source_target_pairs={{0,8},{8,16},{16,24},{24,28},{28,20},{20,12},{12,4},{4,0},{1,9},{9... | collective-permute-start | bytes 1695752 | tf_op jit(solution)/shard_map/ppermute | solution.py:1141
  313.9 35.7 %collective-permute-start.43 = (bf16[1104,256]{1,0:T(8,128)(2,1)S(1)}, bf16[1104,256]{1,0:T(8,128)(2,1)S(1)}, u32[]{:S(2)}, u32[]{:S(2)}) collective-permute-start(bf16[1104,256]{1,0:T(8,128)(2,1)S(1)} %get-tuple-element.220), channel_id=1, source_target_pairs={{8,0},{16,8},{24,16},{28,24},{20,28},{12,20},{4,12},{0,4},{9,1},{1... | collective-permute-start | bytes 1695752 | tf_op jit(solution)/shard_map/ppermute | solution.py:1141
  337.9 21.5 %collective-permute-start.46 = (bf16[1152,256]{1,0:T(8,128)(2,1)S(1)}, bf16[1152,256]{1,0:T(8,128)(2,1)S(1)}, u32[]{:S(2)}, u32[]{:S(2)}) collective-permute-start(bf16[1152,256]{1,0:T(8,128)(2,1)S(1)} %get-tuple-element.217.refs_7_), channel_id=1, source_target_pairs={{0,8},{8,16},{16,24},{24,28},{28,20},{20,12},{12,4},{4,0},{1,9},{9... | collective-permute-start | bytes 1769480 | tf_op jit(solution)/shard_map/ppermute | solution.py:1141
  339.5 21.5 %collective-permute-start.47 = (bf16[1152,256]{1,0:T(8,128)(2,1)S(1)}, bf16[1152,256]{1,0:T(8,128)(2,1)S(1)}, u32[]{:S(2)}, u32[]{:S(2)}) collective-permute-start(bf16[1152,256]{1,0:T(8,128)(2,1)S(1)} %get-tuple-element.223), channel_id=1, source_target_pairs={{8,0},{16,8},{24,16},{28,24},{20,28},{12,20},{4,12},{0,4},{9,1},{1... | collective-permute-start | bytes 1769480 | tf_op jit(solution)/shard_map/ppermute | solution.py:1141
  348.1 28.0 %collective-permute-start.41 = (bf16[256,2048]{1,0:T(8,128)(2,1)}, bf16[256,2048]{1,0:T(8,128)(2,1)}, u32[]{:S(2)}, u32[]{:S(2)}) collective-permute-start(bf16[256,2048]{1,0:T(8,128)(2,1)} %relay.1.refs_11_.refs_2_), channel_id=1, source_target_pairs={{0,2},{1,3},{2,0},{3,1},{4,6},{5,7},{6,4},{7,5},{8,10},{9,11},{10,... | collective-permute-start | bytes 3145736 | tf_op jit(solution)/shard_map/ppermute | solution.py:1284
  350.9 20.6 %collective-permute-start.44 = (bf16[1104,256]{1,0:T(8,128)(2,1)S(1)}, bf16[1104,256]{1,0:T(8,128)(2,1)S(1)}, u32[]{:S(2)}, u32[]{:S(2)}) collective-permute-start(bf16[1104,256]{1,0:T(8,128)(2,1)S(1)} %get-tuple-element.221.refs_10_), channel_id=1, source_target_pairs={{0,8},{8,16},{16,24},{24,28},{28,20},{20,12},{12,4},{4,0},{1,9},{9... | collective-permute-start | bytes 1695752 | tf_op jit(solution)/shard_map/ppermute | solution.py:1141
  352.5 20.6 %collective-permute-start.45 = (bf16[1104,256]{1,0:T(8,128)(2,1)S(1)}, bf16[1104,256]{1,0:T(8,128)(2,1)S(1)}, u32[]{:S(2)}, u32[]{:S(2)}) collective-permute-start(bf16[1104,256]{1,0:T(8,128)(2,1)S(1)} %get-tuple-element.222), channel_id=1, source_target_pairs={{8,0},{16,8},{24,16},{28,24},{20,28},{12,20},{4,12},{0,4},{9,1},{1... | collective-permute-start | bytes 1695752 | tf_op jit(solution)/shard_map/ppermute | solution.py:1141
  362.5 21.6 %collective-permute-start.49 = (bf16[1152,256]{1,0:T(8,128)(2,1)S(1)}, bf16[1152,256]{1,0:T(8,128)(2,1)S(1)}, u32[]{:S(2)}, u32[]{:S(2)}) collective-permute-start(bf16[1152,256]{1,0:T(8,128)(2,1)S(1)} %get-tuple-element.224.refs_11_), channel_id=1, source_target_pairs={{0,8},{8,16},{16,24},{24,28},{28,20},{20,12},{12,4},{4,0},{1,9},{9... | collective-permute-start | bytes 1769480 | tf_op jit(solution)/shard_map/ppermute | solution.py:1141
  364.1 20.5 %collective-permute-start.50 = (bf16[1152,256]{1,0:T(8,128)(2,1)S(1)}, bf16[1152,256]{1,0:T(8,128)(2,1)S(1)}, u32[]{:S(2)}, u32[]{:S(2)}) collective-permute-start(bf16[1152,256]{1,0:T(8,128)(2,1)S(1)} %get-tuple-element.226), channel_id=1, source_target_pairs={{8,0},{16,8},{24,16},{28,24},{20,28},{12,20},{4,12},{0,4},{9,1},{1... | collective-permute-start | bytes 1769480 | tf_op jit(solution)/shard_map/ppermute | solution.py:1141
  371.5 21.2 %collective-permute-start.52 = (f32[8,2,256]{2,1,0:T(2,128)}, f32[8,2,256]{2,1,0:T(2,128)}, u32[]{:S(2)}, u32[]{:S(2)}) collective-permute-start(f32[8,2,256]{2,1,0:T(2,128)} %get-tuple-element.233.refs_4_), channel_id=1, source_target_pairs={{0,1},{1,0},{2,3},{3,2},{4,5},{5,4},{6,7},{7,6},{8,9},{9,8},{10,11... | collective-permute-start | bytes 49160 | tf_op jit(solution)/shard_map/ppermute | solution.py:1155
  374.5 21.8 %collective-permute-start.51 = (bf16[1104,256]{1,0:T(8,128)(2,1)S(1)}, bf16[1104,256]{1,0:T(8,128)(2,1)S(1)}, u32[]{:S(2)}, u32[]{:S(2)}) collective-permute-start(bf16[1104,256]{1,0:T(8,128)(2,1)S(1)} %get-tuple-element.225.refs_5_), channel_id=1, source_target_pairs={{0,8},{8,16},{16,24},{24,28},{28,20},{20,12},{12,4},{4,0},{1,9},{9... | collective-permute-start | bytes 1695752 | tf_op jit(solution)/shard_map/ppermute | solution.py:1141
  386.1 14.3 %collective-permute-start.61 = (bf16[1152,256]{1,0:T(8,128)(2,1)S(1)}, bf16[1152,256]{1,0:T(8,128)(2,1)S(1)}, u32[]{:S(2)}, u32[]{:S(2)}) collective-permute-start(bf16[1152,256]{1,0:T(8,128)(2,1)S(1)} %get-tuple-element.235), channel_id=1, source_target_pairs={{8,0},{16,8},{24,16},{28,24},{20,28},{12,20},{4,12},{0,4},{9,1},{1... | collective-permute-start | bytes 1769480 | tf_op jit(solution)/shard_map/ppermute | solution.py:1141
  386.6 33.7 %collective-permute-start.60 = (bf16[1152,256]{1,0:T(8,128)(2,1)S(1)}, bf16[1152,256]{1,0:T(8,128)(2,1)S(1)}, u32[]{:S(2)}, u32[]{:S(2)}) collective-permute-start(bf16[1152,256]{1,0:T(8,128)(2,1)S(1)} %get-tuple-element.227.refs_3_), channel_id=1, source_target_pairs={{0,8},{8,16},{16,24},{24,28},{28,20},{20,12},{12,4},{4,0},{1,9},{9... | collective-permute-start | bytes 1769480 | tf_op jit(solution)/shard_map/ppermute | solution.py:1141
  402.6 23.2 %collective-permute-start.62 = (bf16[1152,256]{1,0:T(8,128)(2,1)S(1)}, bf16[1152,256]{1,0:T(8,128)(2,1)S(1)}, u32[]{:S(2)}, u32[]{:S(2)}) collective-permute-start(bf16[1152,256]{1,0:T(8,128)(2,1)S(1)} %mixer_term.16.refs_9_), channel_id=1, source_target_pairs={{8,0},{16,8},{24,16},{28,24},{20,28},{12,20},{4,12},{0,4},{9,1},{1... | collective-permute-start | bytes 1769480 | tf_op jit(solution)/shard_map/ppermute | solution.py:1141
  (82 other events, 1555.9 us)

commit v6 on v5

--- a/solution.py
+++ b/solution.py
@@ -995,15 +995,17 @@
         total = own[2][:, piece] + item[rows, : piece.stop - piece.start].astype(F32)
         outs[2][:chunk, piece] = total.astype(BF16)
     ring_size = extra[0].shape[0]
-    lines = jnp.concatenate([extra[0][o] + extra[1][o] for o in range(ring_size)], 0)
-    outs[2][chunk:, :block] = lines.astype(BF16)
-    outs[2][chunk:, block:] = jnp.zeros((2 * ring_size, width - block), BF16)
+    lines = [extra[0][o] + extra[1][o] for o in range(ring_size)]
+    for g in range(2):
+        gain = jnp.concatenate([line[g : g + 1, :] for line in lines], 0)
+        outs[2][chunk:, g * block : (g + 1) * block] = gain.astype(BF16)
+    outs[2][chunk:, 2 * block :] = jnp.zeros((ring_size, width - 2 * block), BF16)
 
 
 def mixer_end(part, extra, own, item, after):
     width, block = own[0].shape
     if part == 0:
-        rows = own[2].shape[0] + 2 * extra[0].shape[0]
+        rows = own[2].shape[0] + extra[0].shape[0]
         shapes = [own[0].shape, own[1].shape, (rows, width)]
     else:
         shapes = [own[0].shape, own[0].shape]
@@ -1021,19 +1023,20 @@
     ring_size = owners.shape[0]
     gate_i, gate_r, taps, sums, gain_o, whole = refs[ring_size:]
     block = gain_o.shape[1]
-    chunk = refs[0].shape[0] - 2 * ring_size
-    gain = jnp.zeros((2, block), F32)
+    chunk = refs[0].shape[0] - ring_size
+    gains = [jnp.zeros((1, block), F32) for _ in range(2)]
     for o in range(ring_size):
         at = pl.ds(pl.multiple_of(owners[o] * chunk, 16), chunk)
         whole[at, :] = refs[o][:chunk, :].astype(F32)
-        mine = 2 * ((ring_size - o) % ring_size)
-        gain = gain + refs[o][chunk:, :block].astype(F32)[mine : mine + 2, :]
+        mine = (ring_size - o) % ring_size
+        lines = refs[o][chunk:, : 2 * block].astype(F32)[mine : mine + 1, :]
+        gains = [gains[g] + lines[:, g * block : (g + 1) * block] for g in range(2)]
     gate_i[...] = whole[:head, :]
     gate_r[...] = whole[head : 2 * head, :]
     count = taps.shape[0]
     taps[...] = whole[2 * head : 2 * head + count, :]
     sums[...] = whole[2 * head + count : 2 * head + SUMS, :]
-    gain_o[...] = gain
+    gain_o[...] = jnp.concatenate(gains, 0)
 
 
 def spread(head, count, block, owners, chunks, after):
@@ -1047,7 +1050,7 @@
         "spread",
         scalars=1,
         after=after,
-        scratch=[pltpu.VMEM(((rows - 2 * ring_size) * ring_size, width), F32)],
+        scratch=[pltpu.VMEM(((rows - ring_size) * ring_size, width), F32)],
     )
 
 

time: 440 us -> 440 us (level)
  no operation moved by 1% of the time
where the time goes in v6:
time: 440 us; the launch traced here: 433 us
  waiting for transfers between devices  219 us (50%)
  Pallas kernels  131 us (30%)
  starting transfers between devices  60.7 us (14%)
  local copies, waits for them, and re-layouts  19.8 us (4%)
    ppermute x28, waiting for transfers between devices, step(): self.moving[d] = lax.ppermute(part, 'dp', (onward, backward)[d])  126 us
    pallas_call x50, Pallas kernels, launch(): pl.pallas_call(lambda *refs: kernel(*refs[:count], *refs[count + extra:])...  120 us
    ppermute x21, waiting for transfers between devices, step(): self.moving[d] = lax.ppermute(self.moving[d], 'dp', way)  76.4 us
    ppermute x28, starting transfers between devices, step(): self.moving[d] = lax.ppermute(part, 'dp', (onward, backward)[d])  29.8 us
    ppermute x21, starting transfers between devices, step(): self.moving[d] = lax.ppermute(self.moving[d], 'dp', way)  23.4 us
    unnamed x137, local copies, waits for them, and re-layouts  17 us
    ppermute x4, waiting for transfers between devices, chip_swap(): return (pair, lax.ppermute(pair, 'mp', chip_pair))  13.1 us
    pallas_call x1, Pallas kernels, unit_back(): pl.pallas_call(unit_back_kernel, grid_spec=pltpu.PrefetchScalarGridSpec(n...  11.4 us
  transfers between devices with their start and end apart: 63, of which 38 were waited for; matrix products, arithmetic and copies ran while one was open for 0% of the time, Pallas kernels for 26%

profile of v6, /device:TPU:0, one launch (start us, length us, event | category | flops | bytes accessed | tf_op | source)
XLA Modules:
  0.0 433.2 jit_solution(11340704593378591866)
XLA Ops:
  1.9 3.1 collective-permute-start.2
  7.3 2.1 collective-permute-start
  14.8 2.1 prepare.1
  16.9 12.0 %collective-permute-done.refs_4_.refs_3_.refs_9_ = bf16[976,256]{1,0:T(8,128)(2,1)S(1)} collective-permute-done((bf16[976,256]{1,0:T(8,128)(2,1)S(1)}, bf16[976,256]{1,0:T(8,128)(2,1)S(1)}, u32[]{:S(2)}, u32[]{:S(2)}) %collective-permute-start) | collective-permute-done | bytes 499744 | tf_op jit(solution)/shard_map/ppermute | solution.py:1122
  30.7 1.7 collective-permute-start.4
  34.1 10.3 %collective-permute-done.7.refs_4_.refs_8_.refs_3_.refs_12_ = bf16[1152,256]{1,0:T(8,128)(2,1)S(1)} collective-permute-done((bf16[1152,256]{1,0:T(8,128)(2,1)S(1)}, bf16[1152,256]{1,0:T(8,128)(2,1)S(1)}, u32[]{:S(2)}, u32[]{:S(2)}) %collective-permute-start.7) | collective-permute-done | bytes 589856 | tf_op jit(solution)/shard_map/ppermute | solution.py:1122
  47.0 10.7 %collective-permute-done.12.refs_5_.refs_7_.refs_16_ = bf16[1152,256]{1,0:T(8,128)(2,1)S(1)} collective-permute-done((bf16[1152,256]{1,0:T(8,128)(2,1)S(1)}, bf16[1152,256]{1,0:T(8,128)(2,1)S(1)}, u32[]{:S(2)}, u32[]{:S(2)}) %collective-permute-start.12) | collective-permute-done | bytes 589856 | tf_op jit(solution)/shard_map/ppermute | solution.py:1122
  57.7 1.7 collective-permute-start.13
  61.2 10.1 %collective-permute-done.10.refs_2_.refs_3_.refs_4_ = bf16[976,256]{1,0:T(8,128)(2,1)S(1)} collective-permute-done((bf16[976,256]{1,0:T(8,128)(2,1)S(1)}, bf16[976,256]{1,0:T(8,128)(2,1)S(1)}, u32[]{:S(2)}, u32[]{:S(2)}) %collective-permute-start.10) | collective-permute-done | bytes 499744 | tf_op jit(solution)/shard_map/ppermute | solution.py:1122
  76.2 15.1 %collective-permute-done.11.refs_2_.refs_4_.refs_5_ = bf16[976,256]{1,0:T(8,128)(2,1)S(1)} collective-permute-done((bf16[976,256]{1,0:T(8,128)(2,1)S(1)}, bf16[976,256]{1,0:T(8,128)(2,1)S(1)}, u32[]{:S(2)}, u32[]{:S(2)}) %collective-permute-start.11) | collective-permute-done | bytes 499744 | tf_op jit(solution)/shard_map/ppermute | solution.py:1122
  93.6 7.2 %mixer_forward.1 = (bf16[512,704]{1,0:T(8,128)(2,1)S(1)}, bf16[512,704]{1,0:T(8,128)(2,1)S(1)}, f32[512,704]{1,0:T(8,128)S(1)}, f32[512,704]{1,0:T(8,128)S(1)}, f32[512,704]{1,0:T(8,128)S(1)}) custom-call(f32[512,704]{1,0:T(8,128)S(1)} %get-tuple-element.146.refs_0_.refs_9_, f32[512,704]{1,0:T(8,128)S(1)} %get-tuple-element.147.refs_1_.refs_10_, ...), custom_call_target="tpu_custom_call" | custom-call | flops 1 | bytes 1 | tf_op jit(solution)/shard_map/mixer_forward/pallas_call | solution.py:75
  108.2 7.0 %unit_grad.1.refs_2_.refs_4_.refs_3_ = f32[512,1536]{1,0:T(8,128)S(1)} custom-call(bf16[512,2048]{1,0:T(8,128)(2,1)S(1)} %get-tuple-element.157.refs_0_, bf16[1536,2048]{1,0:T(8,128)(2,1)} %refs_2_.3, bf16[3,256,256]{2,1,0:T(8,128)(2,1)S(1)} %pair_sum.6.refs_2_.refs_5_), custom_call_target="tpu_custom_call" | custom-call | flops 1 | bytes 1 | tf_op jit(solution)/shard_map/unit_grad/pallas_call | solution.py:75
  115.1 2.9 fetch.1
  118.0 13.1 %collective-permute-done.17.refs_6_ = bf16[3,256,256]{2,1,0:T(8,128)(2,1)S(1)} collective-permute-done((bf16[3,256,256]{2,1,0:T(8,128)(2,1)S(1)}, bf16[3,256,256]{2,1,0:T(8,128)(2,1)S(1)}, u32[]{:S(2)}, u32[]{:S(2)}) %collective-permute-start.17) | collective-permute-done | bytes 393248 | tf_op jit(solution)/shard_map/ppermute | solution.py:1163
  132.7 2.6 collective-permute-done.18
  135.4 5.1 %unit_first.1 = (bf16[512,768]{1,0:T(8,128)(2,1)S(1)}, bf16[512,768]{1,0:T(8,128)(2,1)S(1)}, bf16[512,768]{1,0:T(8,128)(2,1)S(1)}, bf16[8,512,256]{2,1,0:T(8,128)(2,1)S(1)}) custom-call(s32[8]{0:T(128)S(1)} %and_select_fusion.1.refs_1_.refs_0_, bf16[512,2048]{1,0:T(8,128)(2,1)S(1)} %constant_dynamic-update-slice_fusion.2.refs_1_.refs_0_, ...), custom_call_target="tpu_custom_call" | custom-call | flops 1 | bytes 1 | tf_op jit(solution)/shard_map/unit_first/pallas_call | solution.py:75
  144.1 6.7 %unit_second.1 = (bf16[512,768]{1,0:T(8,128)(2,1)S(1)}, bf16[512,768]{1,0:T(8,128)(2,1)S(1)}, bf16[512,768]{1,0:T(8,128)(2,1)S(1)}) custom-call(bf16[512,2048]{1,0:T(8,128)(2,1)S(1)} %constant_dynamic-update-slice_fusion.2.refs_1_.refs_0_, bf16[2048,1536]{1,0:T(8,128)(2,1)} %gate.1, bf16[2048,1536]{1,0:T(8,128)(2,1)} %up.1, ...), custom_call_target="tpu_custom_call" | custom-call | flops 1 | bytes 1 | tf_op jit(solution)/shard_map/unit_second/pallas_call | solution.py:75
  153.9 11.4 %unit_back.1 = (f32[8,256,256]{2,1,0:T(8,128)S(1)}, bf16[8,256,256]{2,1,0:T(8,128)(2,1)S(1)}) custom-call(s32[8]{0:T(128)S(1)} %compare_select_fusion.5.owners.refs_0_, bf16[512,768]{1,0:T(8,128)(2,1)S(1)} %get-tuple-element.165.refs_2_.dga_a, bf16[512,768]{1,0:T(8,128)(2,1)S(1)} %get-tuple-element.170.refs_2_.dga_b, ...), custom_call_target="tpu_custom_call" | custom-call | flops 1 | bytes 1 | tf_op jit(solution)/shard_map/unit_back/pallas_call | solution.py:808
  165.8 5.0 %collective-permute-done.19.refs_5_ = bf16[256,2304]{1,0:T(8,128)(2,1)S(1)} collective-permute-done((bf16[256,2304]{1,0:T(8,128)(2,1)S(1)}, bf16[256,2304]{1,0:T(8,128)(2,1)S(1)}, u32[]{:S(2)}, u32[]{:S(2)}) %collective-permute-start.19) | collective-permute-done | bytes 1179680 | tf_op jit(solution)/shard_map/ppermute | solution.py:1144
  178.7 17.5 %collective-permute-done.23.refs_5_ = bf16[256,2304]{1,0:T(8,128)(2,1)S(1)} collective-permute-done((bf16[256,2304]{1,0:T(8,128)(2,1)S(1)}, bf16[256,2304]{1,0:T(8,128)(2,1)S(1)}, u32[]{:S(2)}, u32[]{:S(2)}) %collective-permute-start.23) | collective-permute-done | bytes 1179680 | tf_op jit(solution)/shard_map/ppermute | solution.py:1144
  201.3 20.1 %collective-permute-done.21.refs_5_ = bf16[256,2304]{1,0:T(8,128)(2,1)S(1)} collective-permute-done((bf16[256,2304]{1,0:T(8,128)(2,1)S(1)}, bf16[256,2304]{1,0:T(8,128)(2,1)S(1)}, u32[]{:S(2)}, u32[]{:S(2)}) %collective-permute-start.21) | collective-permute-done | bytes 1179680 | tf_op jit(solution)/shard_map/ppermute | solution.py:1144
  223.0 2.5 unit_term.12
  227.1 3.4 norm_back.1
  231.1 15.6 %collective-permute-done.30.refs_5_ = bf16[256,2304]{1,0:T(8,128)(2,1)S(1)} collective-permute-done((bf16[256,2304]{1,0:T(8,128)(2,1)S(1)}, bf16[256,2304]{1,0:T(8,128)(2,1)S(1)}, u32[]{:S(2)}, u32[]{:S(2)}) %collective-permute-start.30) | collective-permute-done | bytes 1179680 | tf_op jit(solution)/shard_map/ppermute | solution.py:1144
  248.4 2.5 unit_term.13
  251.3 1.8 collective-permute-start.35
  255.1 13.8 %mixer_backward.1 = (bf16[512,704]{1,0:T(8,128)(2,1)S(1)}, bf16[512,704]{1,0:T(8,128)(2,1)S(1)}, bf16[384,704]{1,0:T(8,128)(2,1)S(1)}) custom-call(bf16[8,512,256]{2,1,0:T(8,128)(2,1)S(1)} %constant_dynamic-update-slice_fusion.4.refs_0_.refs_5_, bf16[1152,256]{1,0:T(8,128)(2,1)S(1)} %pack_two.1.refs_4_.refs_5_.refs_6_.refs_1_.refs_10_, ...), custom_call_target="tpu_custom_call" | custom-call | flops 1 | bytes 1 | tf_op jit(solution)/shard_map/mixer_backward/pallas_call | solution.py:75
  270.3 1.8 collective-permute-done.26.refs_5_
  273.7 3.6 unit_term.14
  277.3 7.7 %unit_out.1 = (f32[256,2048]{1,0:T(8,128)S(1)}, bf16[256,2048]{1,0:T(8,128)(2,1)S(1)}) custom-call(bf16[512,768]{1,0:T(8,128)(2,1)S(1)} %copy-done.49, bf16[512,768]{1,0:T(8,128)(2,1)S(1)} %copy-done.36, bf16[1536,2048]{1,0:T(8,128)(2,1)} %refs_2_.3, bf16[256,2304]{1,0:T(8,128)(2,1)} %get-tuple-element.196.refs_3_), custom_call_target="tpu_custom_call" | custom-call | flops 1 | bytes 1 | tf_op jit(solution)/shard_map/unit_out/pallas_call | solution.py:75
  291.1 3.4 input_out.1
  294.5 4.5 %collective-permute-done.34.refs_5_ = bf16[256,2304]{1,0:T(8,128)(2,1)} collective-permute-done((bf16[256,2304]{1,0:T(8,128)(2,1)}, bf16[256,2304]{1,0:T(8,128)(2,1)}, u32[]{:S(2)}, u32[]{:S(2)}) %collective-permute-start.34) | collective-permute-done | bytes 1179680 | tf_op jit(solution)/shard_map/ppermute | solution.py:1144
  299.0 3.1 unit_term.15
  304.7 4.7 %collective-permute-done.39.refs_9_ = bf16[1104,256]{1,0:T(8,128)(2,1)S(1)} collective-permute-done((bf16[1104,256]{1,0:T(8,128)(2,1)S(1)}, bf16[1104,256]{1,0:T(8,128)(2,1)S(1)}, u32[]{:S(2)}, u32[]{:S(2)}) %collective-permute-start.39) | collective-permute-done | bytes 565280 | tf_op jit(solution)/shard_map/ppermute | solution.py:1144
  314.4 20.4 %collective-permute-done.38.refs_3_ = bf16[256,2304]{1,0:T(8,128)(2,1)} collective-permute-done((bf16[256,2304]{1,0:T(8,128)(2,1)}, bf16[256,2304]{1,0:T(8,128)(2,1)}, u32[]{:S(2)}, u32[]{:S(2)}) %collective-permute-start.38) | collective-permute-done | bytes 1179680 | tf_op jit(solution)/shard_map/ppermute | solution.py:1144
  340.0 2.5 unit_end.3
  343.9 2.5 input_back.1
  353.0 6.4 %collective-permute-done.46.refs_8_ = bf16[1152,256]{1,0:T(8,128)(2,1)S(1)} collective-permute-done((bf16[1152,256]{1,0:T(8,128)(2,1)S(1)}, bf16[1152,256]{1,0:T(8,128)(2,1)S(1)}, u32[]{:S(2)}, u32[]{:S(2)}) %collective-permute-start.46) | collective-permute-done | bytes 589856 | tf_op jit(solution)/shard_map/ppermute | solution.py:1144
  364.6 6.9 %collective-permute-done.44.refs_9_ = bf16[1104,256]{1,0:T(8,128)(2,1)S(1)} collective-permute-done((bf16[1104,256]{1,0:T(8,128)(2,1)S(1)}, bf16[1104,256]{1,0:T(8,128)(2,1)S(1)}, u32[]{:S(2)}, u32[]{:S(2)}) %collective-permute-start.44) | collective-permute-done | bytes 565280 | tf_op jit(solution)/shard_map/ppermute | solution.py:1144
  376.1 2.0 finish.1.refs_10_.refs_1_
  378.2 5.9 %collective-permute-done.49.refs_8_ = bf16[1152,256]{1,0:T(8,128)(2,1)S(1)} collective-permute-done((bf16[1152,256]{1,0:T(8,128)(2,1)S(1)}, bf16[1152,256]{1,0:T(8,128)(2,1)S(1)}, u32[]{:S(2)}, u32[]{:S(2)}) %collective-permute-start.49) | collective-permute-done | bytes 589856 | tf_op jit(solution)/shard_map/ppermute | solution.py:1144
  388.2 4.5 %arrange.1 = (f32[2,256,2048]{2,1,0:T(8,128)}, f32[2,256,2048]{2,1,0:T(8,128)}) custom-call(s32[3]{0:T(128)S(1)} %copy-done.57, f32[2,256,2048]{2,1,0:T(8,128)S(1)} %finish.1.refs_10_.refs_1_, f32[2,256,2048]{2,1,0:T(8,128)S(1)} %collective-permute-done.48.refs_2_, bf16[1152,256]{1,0:T(8,128)(2,1)S(1)} %get-tuple-element.227.refs_3_), custom_call_target="tpu_custom_call" | custom-call | flops 1 | bytes 1 | tf_op jit(solution)/shard_map/arrange/pallas_call | solution.py:75
  392.7 3.6 collective-permute-done.51.refs_3_
  396.3 2.2 copy-done.58
  398.4 1.7 mixer_end.2
  405.4 4.5 %collective-permute-done.56.refs_8_ = bf16[56,704]{1,0:T(8,128)(2,1)S(1)} collective-permute-done((bf16[56,704]{1,0:T(8,128)(2,1)S(1)}, bf16[56,704]{1,0:T(8,128)(2,1)S(1)}, u32[]{:S(2)}, u32[]{:S(2)}) %collective-permute-start.56) | collective-permute-done | bytes 78880 | tf_op jit(solution)/shard_map/ppermute | solution.py:1122
  411.5 6.5 %collective-permute-done.53.refs_2_ = bf16[56,704]{1,0:T(8,128)(2,1)S(1)} collective-permute-done((bf16[56,704]{1,0:T(8,128)(2,1)S(1)}, bf16[56,704]{1,0:T(8,128)(2,1)S(1)}, u32[]{:S(2)}, u32[]{:S(2)}) %collective-permute-start.53) | collective-permute-done | bytes 78880 | tf_op jit(solution)/shard_map/ppermute | solution.py:1122
  421.2 2.0 collective-permute-done.54.refs_3_
  (283 shorter events, 123.8 us)
Async XLA Ops:
  1.9 28.6 %collective-permute-start.2 = (bf16[1152,256]{1,0:T(8,128)(2,1)S(1)}, bf16[1152,256]{1,0:T(8,128)(2,1)S(1)}, u32[]{:S(2)}, u32[]{:S(2)}) collective-permute-start(bf16[1152,256]{1,0:T(8,128)(2,1)S(1)} %pack_two.1.refs_4_.refs_5_.refs_6_.refs_1_.refs_10_), channel_id=1, source_target_pairs={{0,8},{8,16},{16,24},{24,28},{28,20},{20,12},{12,4},{4,0},{1,9},{9... | collective-permute-start | bytes 1769480 | tf_op jit(solution)/shard_map/ppermute | solution.py:1122
  5.0 25.5 %collective-permute-start.3 = (bf16[1152,256]{1,0:T(8,128)(2,1)S(1)}, bf16[1152,256]{1,0:T(8,128)(2,1)S(1)}, u32[]{:S(2)}, u32[]{:S(2)}) collective-permute-start(bf16[1152,256]{1,0:T(8,128)(2,1)S(1)} %pack_two.1.refs_4_.refs_5_.refs_6_.refs_1_.refs_10_), channel_id=1, source_target_pairs={{8,0},{16,8},{24,16},{28,24},{20,28},{12,20},{4,12},{0,4},{9,1},{1... | collective-permute-start | bytes 1769480 | tf_op jit(solution)/shard_map/ppermute | solution.py:1122
  7.3 21.6 %collective-permute-start = (bf16[976,256]{1,0:T(8,128)(2,1)S(1)}, bf16[976,256]{1,0:T(8,128)(2,1)S(1)}, u32[]{:S(2)}, u32[]{:S(2)}) collective-permute-start(bf16[976,256]{1,0:T(8,128)(2,1)S(1)} %pack_one.1.refs_2_.refs_1_), channel_id=1, source_target_pairs={{0,8},{8,16},{16,24},{24,28},{28,20},{20,12},{12,4},{4,0},{1,9},{9... | collective-permute-start | bytes 1499144 | tf_op jit(solution)/shard_map/ppermute | solution.py:1122
  9.4 21.1 %collective-permute-start.1 = (bf16[976,256]{1,0:T(8,128)(2,1)S(1)}, bf16[976,256]{1,0:T(8,128)(2,1)S(1)}, u32[]{:S(2)}, u32[]{:S(2)}) collective-permute-start(bf16[976,256]{1,0:T(8,128)(2,1)S(1)} %pack_one.1.refs_2_.refs_1_), channel_id=1, source_target_pairs={{8,0},{16,8},{24,16},{28,24},{20,28},{12,20},{4,12},{0,4},{9,1},{1... | collective-permute-start | bytes 1499144 | tf_op jit(solution)/shard_map/ppermute | solution.py:1122
  30.7 15.7 %collective-permute-start.4 = (bf16[976,256]{1,0:T(8,128)(2,1)S(1)}, bf16[976,256]{1,0:T(8,128)(2,1)S(1)}, u32[]{:S(2)}, u32[]{:S(2)}) collective-permute-start(bf16[976,256]{1,0:T(8,128)(2,1)S(1)} %collective-permute-done.refs_4_.refs_3_.refs_9_), channel_id=1, source_target_pairs={{0,8},{8,16},{16,24},{24,28},{28,20},{20,12},{12,4},{4,0},{1,9},{9... | collective-permute-start | bytes 1499144 | tf_op jit(solution)/shard_map/ppermute | solution.py:1122
  32.5 25.2 %collective-permute-start.12 = (bf16[1152,256]{1,0:T(8,128)(2,1)S(1)}, bf16[1152,256]{1,0:T(8,128)(2,1)S(1)}, u32[]{:S(2)}, u32[]{:S(2)}) collective-permute-start(bf16[1152,256]{1,0:T(8,128)(2,1)S(1)} %collective-permute-done.2.refs_7_.refs_6_.refs_8_.refs_17_), channel_id=1, source_target_pairs={{0,8},{8,16},{16,24},{24,28},{28,20},{20,12},{12,4},{4,0},{1,9},{9... | collective-permute-start | bytes 1769480 | tf_op jit(solution)/shard_map/ppermute | solution.py:1122
  44.3 16.3 %collective-permute-start.8 = (bf16[1152,256]{1,0:T(8,128)(2,1)S(1)}, bf16[1152,256]{1,0:T(8,128)(2,1)S(1)}, u32[]{:S(2)}, u32[]{:S(2)}) collective-permute-start(bf16[1152,256]{1,0:T(8,128)(2,1)S(1)} %collective-permute-done.7.refs_4_.refs_8_.refs_3_.refs_12_), channel_id=1, source_target_pairs={{8,0},{16,8},{24,16},{28,24},{20,28},{12,20},{4,12},{0,4},{9,1},{1... | collective-permute-start | bytes 1769480 | tf_op jit(solution)/shard_map/ppermute | solution.py:1122
  44.9 26.4 %collective-permute-start.10 = (bf16[976,256]{1,0:T(8,128)(2,1)S(1)}, bf16[976,256]{1,0:T(8,128)(2,1)S(1)}, u32[]{:S(2)}, u32[]{:S(2)}) collective-permute-start(bf16[976,256]{1,0:T(8,128)(2,1)S(1)} %collective-permute-done.1.refs_3_.refs_2_), channel_id=1, source_target_pairs={{8,0},{16,8},{24,16},{28,24},{20,28},{12,20},{4,12},{0,4},{9,1},{1... | collective-permute-start | bytes 1499144 | tf_op jit(solution)/shard_map/ppermute | solution.py:1122
  46.5 25.4 %collective-permute-start.5 = (bf16[976,256]{1,0:T(8,128)(2,1)S(1)}, bf16[976,256]{1,0:T(8,128)(2,1)S(1)}, u32[]{:S(2)}, u32[]{:S(2)}) collective-permute-start(bf16[976,256]{1,0:T(8,128)(2,1)S(1)} %collective-permute-done.4.refs_3_.refs_2_.refs_8_), channel_id=1, source_target_pairs={{0,8},{8,16},{16,24},{24,28},{28,20},{20,12},{12,4},{4,0},{1,9},{9... | collective-permute-start | bytes 1499144 | tf_op jit(solution)/shard_map/ppermute | solution.py:1122
  57.7 33.6 %collective-permute-start.13 = (bf16[1152,256]{1,0:T(8,128)(2,1)S(1)}, bf16[1152,256]{1,0:T(8,128)(2,1)S(1)}, u32[]{:S(2)}, u32[]{:S(2)}) collective-permute-start(bf16[1152,256]{1,0:T(8,128)(2,1)S(1)} %collective-permute-done.12.refs_5_.refs_7_.refs_16_), channel_id=1, source_target_pairs={{0,8},{8,16},{16,24},{24,28},{28,20},{20,12},{12,4},{4,0},{1,9},{9... | collective-permute-start | bytes 1769480 | tf_op jit(solution)/shard_map/ppermute | solution.py:1122
  60.6 32.1 %collective-permute-start.9 = (bf16[1152,256]{1,0:T(8,128)(2,1)S(1)}, bf16[1152,256]{1,0:T(8,128)(2,1)S(1)}, u32[]{:S(2)}, u32[]{:S(2)}) collective-permute-start(bf16[1152,256]{1,0:T(8,128)(2,1)S(1)} %collective-permute-done.8.refs_4_.refs_9_.refs_13_), channel_id=1, source_target_pairs={{8,0},{16,8},{24,16},{28,24},{20,28},{12,20},{4,12},{0,4},{9,1},{1... | collective-permute-start | bytes 1769480 | tf_op jit(solution)/shard_map/ppermute | solution.py:1122
  71.3 20.0 %collective-permute-start.11 = (bf16[976,256]{1,0:T(8,128)(2,1)S(1)}, bf16[976,256]{1,0:T(8,128)(2,1)S(1)}, u32[]{:S(2)}, u32[]{:S(2)}) collective-permute-start(bf16[976,256]{1,0:T(8,128)(2,1)S(1)} %collective-permute-done.10.refs_2_.refs_3_.refs_4_), channel_id=1, source_target_pairs={{8,0},{16,8},{24,16},{28,24},{20,28},{12,20},{4,12},{0,4},{9,1},{1... | collective-permute-start | bytes 1499144 | tf_op jit(solution)/shard_map/ppermute | solution.py:1122
  71.9 20.8 %collective-permute-start.6 = (bf16[976,256]{1,0:T(8,128)(2,1)S(1)}, bf16[976,256]{1,0:T(8,128)(2,1)S(1)}, u32[]{:S(2)}, u32[]{:S(2)}) collective-permute-start(bf16[976,256]{1,0:T(8,128)(2,1)S(1)} %collective-permute-done.5.refs_3_.refs_1_.refs_7_), channel_id=1, source_target_pairs={{0,8},{8,16},{16,24},{24,28},{28,20},{20,12},{12,4},{4,0},{1,9},{9... | collective-permute-start | bytes 1499144 | tf_op jit(solution)/shard_map/ppermute | solution.py:1122
  105.9 25.3 %collective-permute-start.15 = (bf16[5,256,256]{2,1,0:T(8,128)(2,1)S(1)}, bf16[5,256,256]{2,1,0:T(8,128)(2,1)S(1)}, u32[]{:S(2)}, u32[]{:S(2)}) collective-permute-start(bf16[5,256,256]{2,1,0:T(8,128)(2,1)S(1)} %pair_sum.5.refs_2_.refs_3_), channel_id=1, source_target_pairs={{0,2},{1,3},{2,0},{3,1},{4,6},{5,7},{6,4},{7,5},{8,10},{9,11},{10,... | collective-permute-start | bytes 1966088 | tf_op jit(solution)/shard_map/ppermute | solution.py:1163
  107.6 23.6 %collective-permute-start.17 = (bf16[3,256,256]{2,1,0:T(8,128)(2,1)S(1)}, bf16[3,256,256]{2,1,0:T(8,128)(2,1)S(1)}, u32[]{:S(2)}, u32[]{:S(2)}) collective-permute-start(bf16[3,256,256]{2,1,0:T(8,128)(2,1)S(1)} %pair_sum.6.refs_2_.refs_5_), channel_id=1, source_target_pairs={{0,2},{1,3},{2,0},{3,1},{4,6},{5,7},{6,4},{7,5},{8,10},{9,11},{10,... | collective-permute-start | bytes 1179656 | tf_op jit(solution)/shard_map/ppermute | solution.py:1163
  142.0 28.9 %collective-permute-start.19 = (bf16[256,2304]{1,0:T(8,128)(2,1)S(1)}, bf16[256,2304]{1,0:T(8,128)(2,1)S(1)}, u32[]{:S(2)}, u32[]{:S(2)}) collective-permute-start(bf16[256,2304]{1,0:T(8,128)(2,1)S(1)} %get-tuple-element.167.refs_4_.refs_5_), channel_id=1, source_target_pairs={{0,8},{8,16},{16,24},{24,28},{28,20},{20,12},{12,4},{4,0},{1,9},{9... | collective-permute-start | bytes 3538952 | tf_op jit(solution)/shard_map/ppermute | solution.py:1144
  143.6 28.9 %collective-permute-start.20 = (bf16[256,2304]{1,0:T(8,128)(2,1)S(1)}, bf16[256,2304]{1,0:T(8,128)(2,1)S(1)}, u32[]{:S(2)}, u32[]{:S(2)}) collective-permute-start(bf16[256,2304]{1,0:T(8,128)(2,1)S(1)} %get-tuple-element.169), channel_id=1, source_target_pairs={{8,0},{16,8},{24,16},{28,24},{20,28},{12,20},{4,12},{0,4},{9,1},{1... | collective-permute-start | bytes 3538952 | tf_op jit(solution)/shard_map/ppermute | solution.py:1144
  152.2 43.9 %collective-permute-start.23 = (bf16[256,2304]{1,0:T(8,128)(2,1)S(1)}, bf16[256,2304]{1,0:T(8,128)(2,1)S(1)}, u32[]{:S(2)}, u32[]{:S(2)}) collective-permute-start(bf16[256,2304]{1,0:T(8,128)(2,1)S(1)} %get-tuple-element.172.refs_0_), channel_id=1, source_target_pairs={{0,8},{8,16},{16,24},{24,28},{28,20},{20,12},{12,4},{4,0},{1,9},{9... | collective-permute-start | bytes 3538952 | tf_op jit(solution)/shard_map/ppermute | solution.py:1144
  165.3 32.4 %collective-permute-start.24 = (bf16[256,2304]{1,0:T(8,128)(2,1)S(1)}, bf16[256,2304]{1,0:T(8,128)(2,1)S(1)}, u32[]{:S(2)}, u32[]{:S(2)}) collective-permute-start(bf16[256,2304]{1,0:T(8,128)(2,1)S(1)} %get-tuple-element.176), channel_id=1, source_target_pairs={{8,0},{16,8},{24,16},{28,24},{20,28},{12,20},{4,12},{0,4},{9,1},{1... | collective-permute-start | bytes 3538952 | tf_op jit(solution)/shard_map/ppermute | solution.py:1144
  173.9 47.5 %collective-permute-start.21 = (bf16[256,2304]{1,0:T(8,128)(2,1)S(1)}, bf16[256,2304]{1,0:T(8,128)(2,1)S(1)}, u32[]{:S(2)}, u32[]{:S(2)}) collective-permute-start(bf16[256,2304]{1,0:T(8,128)(2,1)S(1)} %get-tuple-element.174.refs_2_), channel_id=1, source_target_pairs={{0,8},{8,16},{16,24},{24,28},{28,20},{20,12},{12,4},{4,0},{1,9},{9... | collective-permute-start | bytes 3538952 | tf_op jit(solution)/shard_map/ppermute | solution.py:1144
  175.5 47.5 %collective-permute-start.22 = (bf16[256,2304]{1,0:T(8,128)(2,1)S(1)}, bf16[256,2304]{1,0:T(8,128)(2,1)S(1)}, u32[]{:S(2)}, u32[]{:S(2)}) collective-permute-start(bf16[256,2304]{1,0:T(8,128)(2,1)S(1)} %get-tuple-element.175), channel_id=1, source_target_pairs={{8,0},{16,8},{24,16},{28,24},{20,28},{12,20},{4,12},{0,4},{9,1},{1... | collective-permute-start | bytes 3538952 | tf_op jit(solution)/shard_map/ppermute | solution.py:1144
  177.2 49.9 %collective-permute-start.28 = (bf16[8,256,256]{2,1,0:T(8,128)(2,1)}, bf16[8,256,256]{2,1,0:T(8,128)(2,1)}, u32[]{:S(2)}, u32[]{:S(2)}) collective-permute-start(bf16[8,256,256]{2,1,0:T(8,128)(2,1)} %pair_sum.7.refs_7_.refs_0_), channel_id=1, source_target_pairs={{0,2},{1,3},{2,0},{3,1},{4,6},{5,7},{6,4},{7,5},{8,10},{9,11},{10,... | collective-permute-start | bytes 3145736 | tf_op jit(solution)/shard_map/ppermute | solution.py:1163
  199.2 47.5 %collective-permute-start.30 = (bf16[256,2304]{1,0:T(8,128)(2,1)S(1)}, bf16[256,2304]{1,0:T(8,128)(2,1)S(1)}, u32[]{:S(2)}, u32[]{:S(2)}) collective-permute-start(bf16[256,2304]{1,0:T(8,128)(2,1)S(1)} %get-tuple-element.178.refs_7_), channel_id=1, source_target_pairs={{0,8},{8,16},{16,24},{24,28},{28,20},{20,12},{12,4},{4,0},{1,9},{9... | collective-permute-start | bytes 3538952 | tf_op jit(solution)/shard_map/ppermute | solution.py:1144
  200.8 47.5 %collective-permute-start.31 = (bf16[256,2304]{1,0:T(8,128)(2,1)S(1)}, bf16[256,2304]{1,0:T(8,128)(2,1)S(1)}, u32[]{:S(2)}, u32[]{:S(2)}) collective-permute-start(bf16[256,2304]{1,0:T(8,128)(2,1)S(1)} %get-tuple-element.191), channel_id=1, source_target_pairs={{8,0},{16,8},{24,16},{28,24},{20,28},{12,20},{4,12},{0,4},{9,1},{1... | collective-permute-start | bytes 3538952 | tf_op jit(solution)/shard_map/ppermute | solution.py:1144
  225.5 46.5 %collective-permute-start.26 = (bf16[256,2304]{1,0:T(8,128)(2,1)}, bf16[256,2304]{1,0:T(8,128)(2,1)}, u32[]{:S(2)}, u32[]{:S(2)}) collective-permute-start(bf16[256,2304]{1,0:T(8,128)(2,1)} %get-tuple-element.179.refs_6_), channel_id=1, source_target_pairs={{0,8},{8,16},{16,24},{24,28},{28,20},{20,12},{12,4},{4,0},{1,9},{9... | collective-permute-start | bytes 3538952 | tf_op jit(solution)/shard_map/ppermute | solution.py:1144
  230.5 22.7 %collective-permute-start.29 = (bf16[8,256,256]{2,1,0:T(8,128)(2,1)S(1)}, bf16[8,256,256]{2,1,0:T(8,128)(2,1)S(1)}, u32[]{:S(2)}, u32[]{:S(2)}) collective-permute-start(bf16[8,256,256]{2,1,0:T(8,128)(2,1)S(1)} %get-tuple-element.186.refs_7_), channel_id=1, source_target_pairs={{0,1},{1,0},{2,3},{3,2},{4,5},{5,4},{6,7},{7,6},{8,9},{9,8},{10,11... | collective-permute-start | bytes 3145736 | tf_op jit(solution)/shard_map/ppermute | solution.py:1166
  230.6 43.1 %collective-permute-start.27 = (bf16[256,2304]{1,0:T(8,128)(2,1)}, bf16[256,2304]{1,0:T(8,128)(2,1)}, u32[]{:S(2)}, u32[]{:S(2)}) collective-permute-start(bf16[256,2304]{1,0:T(8,128)(2,1)} %get-tuple-element.180), channel_id=1, source_target_pairs={{8,0},{16,8},{24,16},{28,24},{20,28},{12,20},{4,12},{0,4},{9,1},{1... | collective-permute-start | bytes 3538952 | tf_op jit(solution)/shard_map/ppermute | solution.py:1144
  250.8 48.1 %collective-permute-start.34 = (bf16[256,2304]{1,0:T(8,128)(2,1)}, bf16[256,2304]{1,0:T(8,128)(2,1)}, u32[]{:S(2)}, u32[]{:S(2)}) collective-permute-start(bf16[256,2304]{1,0:T(8,128)(2,1)} %get-tuple-element.202), channel_id=1, source_target_pairs={{8,0},{16,8},{24,16},{28,24},{20,28},{12,20},{4,12},{0,4},{9,1},{1... | collective-permute-start | bytes 3538952 | tf_op jit(solution)/shard_map/ppermute | solution.py:1144
  251.3 47.7 %collective-permute-start.35 = (bf16[256,2304]{1,0:T(8,128)(2,1)}, bf16[256,2304]{1,0:T(8,128)(2,1)}, u32[]{:S(2)}, u32[]{:S(2)}) collective-permute-start(bf16[256,2304]{1,0:T(8,128)(2,1)} %get-tuple-element.192.refs_18_), channel_id=1, source_target_pairs={{0,8},{8,16},{16,24},{24,28},{28,20},{20,12},{12,4},{4,0},{1,9},{9... | collective-permute-start | bytes 3538952 | tf_op jit(solution)/shard_map/ppermute | solution.py:1144
  285.1 24.3 %collective-permute-start.39 = (bf16[1104,256]{1,0:T(8,128)(2,1)S(1)}, bf16[1104,256]{1,0:T(8,128)(2,1)S(1)}, u32[]{:S(2)}, u32[]{:S(2)}) collective-permute-start(bf16[1104,256]{1,0:T(8,128)(2,1)S(1)} %get-tuple-element.195.refs_7_), channel_id=1, source_target_pairs={{0,8},{8,16},{16,24},{24,28},{28,20},{20,12},{12,4},{4,0},{1,9},{9... | collective-permute-start | bytes 1695752 | tf_op jit(solution)/shard_map/ppermute | solution.py:1144
  286.7 24.2 %collective-permute-start.40 = (bf16[1104,256]{1,0:T(8,128)(2,1)S(1)}, bf16[1104,256]{1,0:T(8,128)(2,1)S(1)}, u32[]{:S(2)}, u32[]{:S(2)}) collective-permute-start(bf16[1104,256]{1,0:T(8,128)(2,1)S(1)} %get-tuple-element.212), channel_id=1, source_target_pairs={{8,0},{16,8},{24,16},{28,24},{20,28},{12,20},{4,12},{0,4},{9,1},{1... | collective-permute-start | bytes 1695752 | tf_op jit(solution)/shard_map/ppermute | solution.py:1144
  287.8 47.0 %collective-permute-start.38 = (bf16[256,2304]{1,0:T(8,128)(2,1)}, bf16[256,2304]{1,0:T(8,128)(2,1)}, u32[]{:S(2)}, u32[]{:S(2)}) collective-permute-start(bf16[256,2304]{1,0:T(8,128)(2,1)} %get-tuple-element.196.refs_3_), channel_id=1, source_target_pairs={{0,8},{8,16},{16,24},{24,28},{28,20},{20,12},{12,4},{4,0},{1,9},{9... | collective-permute-start | bytes 3538952 | tf_op jit(solution)/shard_map/ppermute | solution.py:1144
  302.1 37.4 %collective-permute-start.37 = (bf16[256,2304]{1,0:T(8,128)(2,1)S(1)}, bf16[256,2304]{1,0:T(8,128)(2,1)S(1)}, u32[]{:S(2)}, u32[]{:S(2)}) collective-permute-start(bf16[256,2304]{1,0:T(8,128)(2,1)S(1)} %get-tuple-element.203.refs_2_), channel_id=1, source_target_pairs={{8,0},{16,8},{24,16},{28,24},{20,28},{12,20},{4,12},{0,4},{9,1},{1... | collective-permute-start | bytes 3538952 | tf_op jit(solution)/shard_map/ppermute | solution.py:1144
  303.1 39.3 %collective-permute-start.36 = (bf16[8,256,256]{2,1,0:T(8,128)(2,1)S(1)}, bf16[8,256,256]{2,1,0:T(8,128)(2,1)S(1)}, u32[]{:S(2)}, u32[]{:S(2)}) collective-permute-start(bf16[8,256,256]{2,1,0:T(8,128)(2,1)S(1)} %pair_sum.9.refs_11_.refs_1_), channel_id=1, source_target_pairs={{0,2},{1,3},{2,0},{3,1},{4,6},{5,7},{6,4},{7,5},{8,10},{9,11},{10,... | collective-permute-start | bytes 3145736 | tf_op jit(solution)/shard_map/ppermute | solution.py:1163
  312.3 37.3 %collective-permute-start.42 = (bf16[1104,256]{1,0:T(8,128)(2,1)S(1)}, bf16[1104,256]{1,0:T(8,128)(2,1)S(1)}, u32[]{:S(2)}, u32[]{:S(2)}) collective-permute-start(bf16[1104,256]{1,0:T(8,128)(2,1)S(1)} %get-tuple-element.213.refs_4_), channel_id=1, source_target_pairs={{0,8},{8,16},{16,24},{24,28},{28,20},{20,12},{12,4},{4,0},{1,9},{9... | collective-permute-start | bytes 1695752 | tf_op jit(solution)/shard_map/ppermute | solution.py:1144
  313.9 35.7 %collective-permute-start.43 = (bf16[1104,256]{1,0:T(8,128)(2,1)S(1)}, bf16[1104,256]{1,0:T(8,128)(2,1)S(1)}, u32[]{:S(2)}, u32[]{:S(2)}) collective-permute-start(bf16[1104,256]{1,0:T(8,128)(2,1)S(1)} %get-tuple-element.220), channel_id=1, source_target_pairs={{8,0},{16,8},{24,16},{28,24},{20,28},{12,20},{4,12},{0,4},{9,1},{1... | collective-permute-start | bytes 1695752 | tf_op jit(solution)/shard_map/ppermute | solution.py:1144
  337.9 21.5 %collective-permute-start.46 = (bf16[1152,256]{1,0:T(8,128)(2,1)S(1)}, bf16[1152,256]{1,0:T(8,128)(2,1)S(1)}, u32[]{:S(2)}, u32[]{:S(2)}) collective-permute-start(bf16[1152,256]{1,0:T(8,128)(2,1)S(1)} %get-tuple-element.217.refs_7_), channel_id=1, source_target_pairs={{0,8},{8,16},{16,24},{24,28},{28,20},{20,12},{12,4},{4,0},{1,9},{9... | collective-permute-start | bytes 1769480 | tf_op jit(solution)/shard_map/ppermute | solution.py:1144
  339.5 21.5 %collective-permute-start.47 = (bf16[1152,256]{1,0:T(8,128)(2,1)S(1)}, bf16[1152,256]{1,0:T(8,128)(2,1)S(1)}, u32[]{:S(2)}, u32[]{:S(2)}) collective-permute-start(bf16[1152,256]{1,0:T(8,128)(2,1)S(1)} %get-tuple-element.223), channel_id=1, source_target_pairs={{8,0},{16,8},{24,16},{28,24},{20,28},{12,20},{4,12},{0,4},{9,1},{1... | collective-permute-start | bytes 1769480 | tf_op jit(solution)/shard_map/ppermute | solution.py:1144
  348.1 28.0 %collective-permute-start.41 = (bf16[256,2048]{1,0:T(8,128)(2,1)}, bf16[256,2048]{1,0:T(8,128)(2,1)}, u32[]{:S(2)}, u32[]{:S(2)}) collective-permute-start(bf16[256,2048]{1,0:T(8,128)(2,1)} %relay.1.refs_11_.refs_2_), channel_id=1, source_target_pairs={{0,2},{1,3},{2,0},{3,1},{4,6},{5,7},{6,4},{7,5},{8,10},{9,11},{10,... | collective-permute-start | bytes 3145736 | tf_op jit(solution)/shard_map/ppermute | solution.py:1287
  350.9 20.6 %collective-permute-start.44 = (bf16[1104,256]{1,0:T(8,128)(2,1)S(1)}, bf16[1104,256]{1,0:T(8,128)(2,1)S(1)}, u32[]{:S(2)}, u32[]{:S(2)}) collective-permute-start(bf16[1104,256]{1,0:T(8,128)(2,1)S(1)} %get-tuple-element.221.refs_10_), channel_id=1, source_target_pairs={{0,8},{8,16},{16,24},{24,28},{28,20},{20,12},{12,4},{4,0},{1,9},{9... | collective-permute-start | bytes 1695752 | tf_op jit(solution)/shard_map/ppermute | solution.py:1144
  352.5 20.6 %collective-permute-start.45 = (bf16[1104,256]{1,0:T(8,128)(2,1)S(1)}, bf16[1104,256]{1,0:T(8,128)(2,1)S(1)}, u32[]{:S(2)}, u32[]{:S(2)}) collective-permute-start(bf16[1104,256]{1,0:T(8,128)(2,1)S(1)} %get-tuple-element.222), channel_id=1, source_target_pairs={{8,0},{16,8},{24,16},{28,24},{20,28},{12,20},{4,12},{0,4},{9,1},{1... | collective-permute-start | bytes 1695752 | tf_op jit(solution)/shard_map/ppermute | solution.py:1144
  362.5 21.6 %collective-permute-start.49 = (bf16[1152,256]{1,0:T(8,128)(2,1)S(1)}, bf16[1152,256]{1,0:T(8,128)(2,1)S(1)}, u32[]{:S(2)}, u32[]{:S(2)}) collective-permute-start(bf16[1152,256]{1,0:T(8,128)(2,1)S(1)} %get-tuple-element.224.refs_11_), channel_id=1, source_target_pairs={{0,8},{8,16},{16,24},{24,28},{28,20},{20,12},{12,4},{4,0},{1,9},{9... | collective-permute-start | bytes 1769480 | tf_op jit(solution)/shard_map/ppermute | solution.py:1144
  364.1 20.5 %collective-permute-start.50 = (bf16[1152,256]{1,0:T(8,128)(2,1)S(1)}, bf16[1152,256]{1,0:T(8,128)(2,1)S(1)}, u32[]{:S(2)}, u32[]{:S(2)}) collective-permute-start(bf16[1152,256]{1,0:T(8,128)(2,1)S(1)} %get-tuple-element.226), channel_id=1, source_target_pairs={{8,0},{16,8},{24,16},{28,24},{20,28},{12,20},{4,12},{0,4},{9,1},{1... | collective-permute-start | bytes 1769480 | tf_op jit(solution)/shard_map/ppermute | solution.py:1144
  371.5 21.2 %collective-permute-start.52 = (f32[8,2,256]{2,1,0:T(2,128)}, f32[8,2,256]{2,1,0:T(2,128)}, u32[]{:S(2)}, u32[]{:S(2)}) collective-permute-start(f32[8,2,256]{2,1,0:T(2,128)} %get-tuple-element.233.refs_4_), channel_id=1, source_target_pairs={{0,1},{1,0},{2,3},{3,2},{4,5},{5,4},{6,7},{7,6},{8,9},{9,8},{10,11... | collective-permute-start | bytes 49160 | tf_op jit(solution)/shard_map/ppermute | solution.py:1158
  374.5 21.8 %collective-permute-start.51 = (bf16[1104,256]{1,0:T(8,128)(2,1)S(1)}, bf16[1104,256]{1,0:T(8,128)(2,1)S(1)}, u32[]{:S(2)}, u32[]{:S(2)}) collective-permute-start(bf16[1104,256]{1,0:T(8,128)(2,1)S(1)} %get-tuple-element.225.refs_5_), channel_id=1, source_target_pairs={{0,8},{8,16},{16,24},{24,28},{28,20},{20,12},{12,4},{4,0},{1,9},{9... | collective-permute-start | bytes 1695752 | tf_op jit(solution)/shard_map/ppermute | solution.py:1144
  386.1 14.3 %collective-permute-start.61 = (bf16[1152,256]{1,0:T(8,128)(2,1)S(1)}, bf16[1152,256]{1,0:T(8,128)(2,1)S(1)}, u32[]{:S(2)}, u32[]{:S(2)}) collective-permute-start(bf16[1152,256]{1,0:T(8,128)(2,1)S(1)} %get-tuple-element.235), channel_id=1, source_target_pairs={{8,0},{16,8},{24,16},{28,24},{20,28},{12,20},{4,12},{0,4},{9,1},{1... | collective-permute-start | bytes 1769480 | tf_op jit(solution)/shard_map/ppermute | solution.py:1144
  386.6 33.4 %collective-permute-start.60 = (bf16[1152,256]{1,0:T(8,128)(2,1)S(1)}, bf16[1152,256]{1,0:T(8,128)(2,1)S(1)}, u32[]{:S(2)}, u32[]{:S(2)}) collective-permute-start(bf16[1152,256]{1,0:T(8,128)(2,1)S(1)} %get-tuple-element.227.refs_3_), channel_id=1, source_target_pairs={{0,8},{8,16},{16,24},{24,28},{28,20},{20,12},{12,4},{4,0},{1,9},{9... | collective-permute-start | bytes 1769480 | tf_op jit(solution)/shard_map/ppermute | solution.py:1144
  402.6 22.6 %collective-permute-start.62 = (bf16[1152,256]{1,0:T(8,128)(2,1)S(1)}, bf16[1152,256]{1,0:T(8,128)(2,1)S(1)}, u32[]{:S(2)}, u32[]{:S(2)}) collective-permute-start(bf16[1152,256]{1,0:T(8,128)(2,1)S(1)} %mixer_term.16.refs_9_), channel_id=1, source_target_pairs={{8,0},{16,8},{24,16},{28,24},{20,28},{12,20},{4,12},{0,4},{9,1},{1... | collective-permute-start | bytes 1769480 | tf_op jit(solution)/shard_map/ppermute | solution.py:1144
  (82 other events, 1554.5 us)
